TPU v7x, 32 devices: a whole 2x2x4 slice. The times are simulated.
32 devices in a mesh: pipe: 2 (over core), dp: 4 (over y, x), tensor: 4 (over z).
Axes of the slice: x: 2, y: 2, z: 4, core: 2. Of those that a mesh axis runs over, the one named last changes fastest.
Arguments:
- enc_input: bfloat16 [8, 2048, 1024], P('dp', 'tensor'), may hold values from -6 to 6
- dec_input: bfloat16 [8, 256, 1024], P('dp', 'tensor'), may hold values from -6 to 6
- dec_cotangent: bfloat16 [8, 256, 1024], P('dp', 'tensor'), may hold values from -6 to 6
- enc_lengths: int32 [8, 3], P('dp'), may hold values from 1 to 1024, 2048 in all within a row
- dec_lengths: int32 [8, 3], P('dp'), may hold values from 1 to 128, 256 in all within a row
- attn_weights: float32 [2, 1024, 4, 1024], P('pipe', None, None, 'tensor'), as said below
- cross_weights: float32 [2, 1024, 2, 1024], P('pipe', None, None, 'tensor'), as said below
- ffn_weights: float32 [2, 1024, 2, 4096], P('pipe', None, None, 'tensor'), may hold values from -0.1875 to 0.1875
- norm_gains: float32 [2, 3, 1024], P('pipe'), may hold values from 0.25 to 1.75
- norm_biases: float32 [2, 3, 1024], P('pipe'), may hold values from -2.5 to 2.5
Outputs:
- dec_output: bfloat16 [8, 256, 1024], P('dp', 'tensor', 'pipe')
- enc_input_grad: float32 [8, 2048, 1024], P('dp', 'tensor', 'pipe')
- dec_input_grad: float32 [8, 256, 1024], P('dp', 'tensor', 'pipe')
- attn_weights_grad: float32 [2, 1024, 4, 1024], P('pipe', 'dp', None, 'tensor')
- cross_weights_grad: float32 [2, 1024, 2, 1024], P('pipe', 'dp', None, 'tensor')
- ffn_weights_grad: float32 [2, 1024, 2, 4096], P('pipe', 'dp', None, 'tensor')
- norm_gains_grad: float32 [2, 3, 1024], P('pipe', None, ('dp', 'tensor'))
- norm_biases_grad: float32 [2, 3, 1024], P('pipe', None, ('dp', 'tensor'))
Inputs may be any that keep to these rules, and one draw needn't show every extreme that they name: `enc_lengths`: each row sums to 2048; entry j is the encoder length of table j. `dec_lengths`: each row sums to 256; entry j is the decoder length of table j. `attn_weights`: independent entries. `cross_weights`: independent entries.
All inputs are finite; a program needn't handle non-finite values.
Results may differ from a plain program's by a relative error of at most 0.034.
Values may be sent and summed in bfloat16 or wider, within the bound.
A program may use at most 320 MiB of HBM per device.

v0:
```python
from functools import partial

import jax
import jax.numpy as jnp
from jax import lax
from jax.sharding import PartitionSpec as P

HEAD = 64


EPSILON = 1e-05
NEGATIVE = -1e30
HALF_TYPE = jnp.bfloat16
WIDE_TYPE = jnp.float32


def shifted(value, axis, steps):
    count = lax.axis_size(axis)
    initial, last = (max(0, -steps), min(count, count - steps))
    return lax.ppermute(value, axis, [(source, source + steps) for source in range(initial, last)])


def gather_rows(values):
    return lax.all_gather(values, "tensor", axis=1, tiled=True)


def sum_rows(terms):
    return lax.psum_scatter(
        terms.astype(jnp.bfloat16), "tensor", scatter_dimension=1, tiled=True
    ).astype(jnp.float32)


def blanks(specs):
    return tuple((jnp.zeros(spec_shape, spec_type) for spec_shape, spec_type in specs))


def segments(lengths, row_count):
    seg_ends = jnp.cumsum(lengths, axis=-1)
    places = jnp.arange(row_count, dtype=jnp.int32)
    return jnp.sum((places[None, None, :] >= seg_ends[:, :, None]).astype(jnp.int32), axis=1)


def norm_forward(values, gain_vec, bias_vec):
    center = values - jnp.mean(values, axis=-1, keepdims=True)
    inv_scale = lax.rsqrt(jnp.mean(center * center, axis=-1, keepdims=True) + EPSILON)
    normed = center * inv_scale
    return (normed * gain_vec + bias_vec, normed, inv_scale)


def norm_backward(grad_out, normed, inv_scale, gain_vec):
    grad_gain = jnp.sum(grad_out * normed, axis=(0, 1))
    grad_bias = jnp.sum(grad_out, axis=(0, 1))
    grad_normed = grad_out * gain_vec
    grad_in = inv_scale * (
        grad_normed
        - jnp.mean(grad_normed, axis=-1, keepdims=True)
        - normed * jnp.mean(grad_normed * normed, axis=-1, keepdims=True)
    )
    return (grad_in, grad_gain, grad_bias)


def pick_rows(values, batch_index, start_row, block_rows):
    return lax.dynamic_slice_in_dim(
        lax.dynamic_index_in_dim(values, batch_index, 0, False), start_row, block_rows, 0
    )


def add_batch(totals, batch_index, addition):
    current = lax.dynamic_index_in_dim(totals, batch_index, 0, False)
    return lax.dynamic_update_index_in_dim(totals, current + addition, batch_index, 0)


def block_allowed(query_seg, key_seg, batch_index, start_row, block_rows, causal):
    query_ids = pick_rows(query_seg, batch_index, start_row, block_rows)
    key_ids = lax.dynamic_index_in_dim(key_seg, batch_index, 0, False)
    allowed = query_ids[:, None] == key_ids[None, :]
    if causal:
        places = start_row + jnp.arange(block_rows)
        allowed = allowed & (places[:, None] >= jnp.arange(key_ids.shape[0])[None, :])
    return allowed


def block_scores(query_part, key_here, allowed):
    raw_scores = jnp.einsum(
        "qhd,khd->hqk", query_part, key_here, preferred_element_type=jnp.float32
    )
    return jnp.where(allowed[None], raw_scores * HEAD ** (-0.5), NEGATIVE)


def attend_forward(queries, key_vecs, value_vecs, query_seg, key_seg, causal):
    batch_count, row_count, row_width = queries.shape
    head_count = row_width // HEAD
    key_count = key_vecs.shape[1]
    block_rows = min(512, row_count)
    block_count = row_count // block_rows

    def one_block(flat_index):
        batch_index = flat_index // block_count
        start_row = flat_index % block_count * block_rows
        query_part = pick_rows(queries, batch_index, start_row, block_rows).reshape(
            block_rows, head_count, HEAD
        )
        key_here = lax.dynamic_index_in_dim(key_vecs, batch_index, 0, False).reshape(
            key_count, head_count, HEAD
        )
        value_here = lax.dynamic_index_in_dim(value_vecs, batch_index, 0, False).reshape(
            key_count, head_count, HEAD
        )
        allowed = block_allowed(query_seg, key_seg, batch_index, start_row, block_rows, causal)
        scores = block_scores(query_part, key_here, allowed)
        row_top = jnp.max(scores, axis=-1, keepdims=True)
        expo_vals = jnp.exp(scores - row_top)
        row_total = jnp.sum(expo_vals, axis=-1, keepdims=True)
        probabilities = (expo_vals / row_total).astype(HALF_TYPE)
        head_out = jnp.einsum(
            "hqk,khd->qhd", probabilities, value_here, preferred_element_type=jnp.float32
        )
        log_total = (row_top + jnp.log(row_total))[:, :, 0].T
        return (head_out.reshape(block_rows, row_width), log_total)

    outputs, log_totals = lax.map(one_block, jnp.arange(batch_count * block_count))
    return (
        outputs.reshape(batch_count, row_count, row_width),
        log_totals.reshape(batch_count, row_count, head_count),
    )


def attend_backward(
    queries, key_vecs, value_vecs, log_totals, grad_heads, query_seg, key_seg, causal
):
    batch_count, row_count, row_width = queries.shape
    head_count = row_width // HEAD
    key_count = key_vecs.shape[1]
    block_rows = min(512, row_count)
    block_count = row_count // block_rows

    def one_block(carried, flat_index):
        grad_keys, grad_values = carried
        batch_index = flat_index // block_count
        start_row = flat_index % block_count * block_rows
        query_part = pick_rows(queries, batch_index, start_row, block_rows).reshape(
            block_rows, head_count, HEAD
        )
        grad_part = pick_rows(grad_heads, batch_index, start_row, block_rows).reshape(
            block_rows, head_count, HEAD
        )
        total_part = pick_rows(log_totals, batch_index, start_row, block_rows)
        key_here = lax.dynamic_index_in_dim(key_vecs, batch_index, 0, False).reshape(
            key_count, head_count, HEAD
        )
        value_here = lax.dynamic_index_in_dim(value_vecs, batch_index, 0, False).reshape(
            key_count, head_count, HEAD
        )
        allowed = block_allowed(query_seg, key_seg, batch_index, start_row, block_rows, causal)
        scores = block_scores(query_part, key_here, allowed)
        probabilities = jnp.exp(scores - total_part.T[:, :, None])
        grad_probs = jnp.einsum(
            "qhd,khd->hqk", grad_part, value_here, preferred_element_type=jnp.float32
        )
        grad_scores = probabilities * (
            grad_probs - jnp.sum(probabilities * grad_probs, axis=-1, keepdims=True)
        )
        grad_raw = (grad_scores * HEAD ** (-0.5)).astype(HALF_TYPE)
        grad_query = jnp.einsum(
            "hqk,khd->qhd", grad_raw, key_here, preferred_element_type=jnp.float32
        )
        key_term = jnp.einsum(
            "hqk,qhd->khd", grad_raw, query_part, preferred_element_type=jnp.float32
        )
        value_term = jnp.einsum(
            "hqk,qhd->khd",
            probabilities.astype(HALF_TYPE),
            grad_part,
            preferred_element_type=jnp.float32,
        )
        grad_keys = add_batch(grad_keys, batch_index, key_term.reshape(key_count, row_width))
        grad_values = add_batch(grad_values, batch_index, value_term.reshape(key_count, row_width))
        return ((grad_keys, grad_values), grad_query.reshape(block_rows, row_width))

    empty_sums = jnp.zeros((batch_count, key_count, row_width), WIDE_TYPE)
    (grad_keys, grad_values), grad_query = lax.scan(
        one_block, (empty_sums, empty_sums), jnp.arange(batch_count * block_count)
    )
    return (grad_query.reshape(batch_count, row_count, row_width), grad_keys, grad_values)


def self_forward(inputs, attn_low, seg_ids, causal):
    inputs_full = gather_rows(inputs.astype(HALF_TYPE))
    proj_qkv = jnp.einsum(
        "bsd,dkc->bskc", inputs_full, attn_low[:, :3], preferred_element_type=jnp.float32
    ).astype(HALF_TYPE)
    head_out, log_totals = attend_forward(
        proj_qkv[:, :, 0], proj_qkv[:, :, 1], proj_qkv[:, :, 2], seg_ids, seg_ids, causal
    )
    head_out = head_out.astype(HALF_TYPE)
    branch = sum_rows(
        jnp.einsum("bsc,dc->bsd", head_out, attn_low[:, 3], preferred_element_type=jnp.float32)
    )
    return (branch, (inputs_full, proj_qkv, log_totals, head_out))


def self_backward(grad_branch, saved, attn_low, seg_ids, causal):
    inputs_full, proj_qkv, log_totals, head_out = saved
    grad_full = gather_rows(grad_branch.astype(HALF_TYPE))
    grad_out_w = jnp.einsum("bsd,bsc->dc", grad_full, head_out, preferred_element_type=jnp.float32)
    grad_heads = jnp.einsum(
        "bsd,dc->bsc", grad_full, attn_low[:, 3], preferred_element_type=jnp.float32
    ).astype(HALF_TYPE)
    grad_query, grad_keys, grad_values = attend_backward(
        proj_qkv[:, :, 0],
        proj_qkv[:, :, 1],
        proj_qkv[:, :, 2],
        log_totals,
        grad_heads,
        seg_ids,
        seg_ids,
        causal,
    )
    grad_proj = jnp.stack([grad_query, grad_keys, grad_values], axis=2).astype(HALF_TYPE)
    grad_in_w = jnp.einsum(
        "bsd,bskc->dkc", inputs_full, grad_proj, preferred_element_type=jnp.float32
    )
    grad_inputs = sum_rows(
        jnp.einsum("bskc,dkc->bsd", grad_proj, attn_low[:, :3], preferred_element_type=jnp.float32)
    )
    return (grad_inputs, jnp.concatenate([grad_in_w, grad_out_w[:, None]], axis=1))


def cross_forward(inputs, cross_low, key_vecs, value_vecs, dec_seg, enc_seg):
    inputs_full = gather_rows(inputs.astype(HALF_TYPE))
    queries = jnp.einsum(
        "bsd,dc->bsc", inputs_full, cross_low[:, 0], preferred_element_type=jnp.float32
    ).astype(HALF_TYPE)
    head_out, log_totals = attend_forward(queries, key_vecs, value_vecs, dec_seg, enc_seg, False)
    head_out = head_out.astype(HALF_TYPE)
    branch = sum_rows(
        jnp.einsum("bsc,dc->bsd", head_out, cross_low[:, 1], preferred_element_type=jnp.float32)
    )
    return (branch, (inputs_full, queries, log_totals, head_out))


def cross_backward(grad_branch, saved, cross_low, key_vecs, value_vecs, dec_seg, enc_seg):
    inputs_full, queries, log_totals, head_out = saved
    grad_full = gather_rows(grad_branch.astype(HALF_TYPE))
    grad_out_w = jnp.einsum("bsd,bsc->dc", grad_full, head_out, preferred_element_type=jnp.float32)
    grad_heads = jnp.einsum(
        "bsd,dc->bsc", grad_full, cross_low[:, 1], preferred_element_type=jnp.float32
    ).astype(HALF_TYPE)
    grad_query, grad_keys, grad_values = attend_backward(
        queries, key_vecs, value_vecs, log_totals, grad_heads, dec_seg, enc_seg, False
    )
    grad_query = grad_query.astype(HALF_TYPE)
    grad_in_w = jnp.einsum(
        "bsd,bsc->dc", inputs_full, grad_query, preferred_element_type=jnp.float32
    )
    grad_inputs = sum_rows(
        jnp.einsum("bsc,dc->bsd", grad_query, cross_low[:, 0], preferred_element_type=jnp.float32)
    )
    grad_pairs = jnp.stack([grad_keys, grad_values], axis=2).astype(HALF_TYPE)
    return (grad_inputs, jnp.stack([grad_in_w, grad_out_w], axis=1), grad_pairs)


def ffn_forward(inputs, ffn_low):
    inputs_full = gather_rows(inputs.astype(HALF_TYPE))
    hidden = jnp.einsum(
        "bsd,df->bsf", inputs_full, ffn_low[:, 0], preferred_element_type=jnp.float32
    )
    active = jax.nn.gelu(hidden, approximate=False).astype(HALF_TYPE)
    branch = sum_rows(
        jnp.einsum("bsf,df->bsd", active, ffn_low[:, 1], preferred_element_type=jnp.float32)
    )
    return (branch, (inputs_full, hidden))


def ffn_backward(grad_branch, saved, ffn_low):
    inputs_full, hidden = saved
    grad_full = gather_rows(grad_branch.astype(HALF_TYPE))
    active, gelu_back = jax.vjp(partial(jax.nn.gelu, approximate=False), hidden)
    grad_out_w = jnp.einsum(
        "bsd,bsf->df", grad_full, active.astype(HALF_TYPE), preferred_element_type=jnp.float32
    )
    grad_active = jnp.einsum(
        "bsd,df->bsf", grad_full, ffn_low[:, 1], preferred_element_type=jnp.float32
    )
    grad_hidden = gelu_back(grad_active)[0].astype(HALF_TYPE)
    grad_in_w = jnp.einsum(
        "bsd,bsf->df", inputs_full, grad_hidden, preferred_element_type=jnp.float32
    )
    grad_inputs = sum_rows(
        jnp.einsum("bsf,df->bsd", grad_hidden, ffn_low[:, 0], preferred_element_type=jnp.float32)
    )
    return (grad_inputs, jnp.stack([grad_in_w, grad_out_w], axis=1))


def project_memory(memory_full, pair_low):
    return jnp.einsum(
        "bsd,dkc->bskc", memory_full, pair_low, preferred_element_type=jnp.float32
    ).astype(HALF_TYPE)


def project_back(grad_pairs, memory_full, pair_low):
    grad_w = jnp.einsum(
        "bsd,bskc->dkc", memory_full, grad_pairs, preferred_element_type=jnp.float32
    )
    grad_memory = sum_rows(
        jnp.einsum("bskc,dkc->bsd", grad_pairs, pair_low, preferred_element_type=jnp.float32)
    )
    return (grad_memory, grad_w)


def encoder_forward(enc_input, enc_seg, attn_low, ffn_low, gain_vecs, bias_vecs):
    start_rows = enc_input.astype(WIDE_TYPE)
    embed_norm, _, _ = norm_forward(start_rows, gain_vecs[0], bias_vecs[0])
    attn_branch, attn_saved = self_forward(embed_norm, attn_low, enc_seg, False)
    attn_resid = embed_norm + attn_branch
    attn_norm, _, _ = norm_forward(attn_resid, gain_vecs[1], bias_vecs[1])
    ffn_branch, ffn_saved = ffn_forward(attn_norm, ffn_low)
    ffn_resid = attn_norm + ffn_branch
    memory, _, _ = norm_forward(ffn_resid, gain_vecs[2], bias_vecs[2])
    return (memory, attn_saved + (attn_resid,) + ffn_saved + (ffn_resid,))


def encoder_backward(
    grad_memory, stash, enc_input, enc_seg, attn_low, ffn_low, gain_vecs, bias_vecs
):
    attn_saved = stash[:4]
    attn_resid = stash[4]
    ffn_saved = stash[5:7]
    ffn_resid = stash[7]
    _, normed, inv_scale = norm_forward(ffn_resid, gain_vecs[2], bias_vecs[2])
    grad_resid, gain_last, bias_last = norm_backward(grad_memory, normed, inv_scale, gain_vecs[2])
    grad_ffn_in, ffn_grad = ffn_backward(grad_resid, ffn_saved, ffn_low)
    _, normed, inv_scale = norm_forward(attn_resid, gain_vecs[1], bias_vecs[1])
    grad_resid, gain_middle, bias_middle = norm_backward(
        grad_resid + grad_ffn_in, normed, inv_scale, gain_vecs[1]
    )
    grad_attn_in, attn_grad = self_backward(grad_resid, attn_saved, attn_low, enc_seg, False)
    _, normed, inv_scale = norm_forward(enc_input.astype(WIDE_TYPE), gain_vecs[0], bias_vecs[0])
    grad_start, gain_first, bias_first = norm_backward(
        grad_resid + grad_attn_in, normed, inv_scale, gain_vecs[0]
    )
    return (
        grad_start,
        attn_grad,
        ffn_grad,
        jnp.stack([gain_first, gain_middle, gain_last]),
        jnp.stack([bias_first, bias_middle, bias_last]),
    )


def decoder_pass(
    dec_input,
    dec_cotangent,
    dec_seg,
    enc_seg,
    key_vecs,
    value_vecs,
    attn_low,
    cross_low,
    ffn_low,
    gain_vecs,
    bias_vecs,
):
    start_rows = dec_input.astype(WIDE_TYPE)
    self_branch, self_saved = self_forward(start_rows, attn_low, dec_seg, True)
    self_norm, self_normed, self_scale = norm_forward(
        start_rows + self_branch, gain_vecs[0], bias_vecs[0]
    )
    cross_branch, cross_saved = cross_forward(
        self_norm, cross_low, key_vecs, value_vecs, dec_seg, enc_seg
    )
    cross_norm, cross_normed, cross_scale = norm_forward(
        self_norm + cross_branch, gain_vecs[1], bias_vecs[1]
    )
    ffn_branch, ffn_saved = ffn_forward(cross_norm, ffn_low)
    result, result_normed, result_scale = norm_forward(
        cross_norm + ffn_branch, gain_vecs[2], bias_vecs[2]
    )
    grad_resid, gain_last, bias_last = norm_backward(
        dec_cotangent.astype(WIDE_TYPE), result_normed, result_scale, gain_vecs[2]
    )
    grad_ffn_in, ffn_grad = ffn_backward(grad_resid, ffn_saved, ffn_low)
    grad_resid, gain_middle, bias_middle = norm_backward(
        grad_resid + grad_ffn_in, cross_normed, cross_scale, gain_vecs[1]
    )
    grad_cross_in, cross_grad, grad_pairs = cross_backward(
        grad_resid, cross_saved, cross_low, key_vecs, value_vecs, dec_seg, enc_seg
    )
    grad_resid, gain_first, bias_first = norm_backward(
        grad_resid + grad_cross_in, self_normed, self_scale, gain_vecs[0]
    )
    grad_self_in, attn_grad = self_backward(grad_resid, self_saved, attn_low, dec_seg, True)
    grad_start = grad_resid + grad_self_in
    return (
        result.astype(HALF_TYPE),
        grad_start,
        grad_pairs,
        attn_grad,
        cross_grad,
        ffn_grad,
        jnp.stack([gain_first, gain_middle, gain_last]),
        jnp.stack([bias_first, bias_middle, bias_last]),
    )


def per_device(
    enc_input,
    dec_input,
    dec_cotangent,
    enc_lengths,
    dec_lengths,
    attn_weights,
    cross_weights,
    ffn_weights,
    norm_gains,
    norm_biases,
):
    is_encoder = lax.axis_index("pipe") == 0
    tensor_count = lax.axis_size("tensor")
    batch_count, enc_shard, row_width = enc_input.shape
    dec_shard = dec_input.shape[1]
    enc_full = enc_shard * tensor_count
    dec_full = dec_shard * tensor_count
    local_width = attn_weights.shape[3]
    enc_seg = segments(enc_lengths, enc_full)
    dec_seg = segments(dec_lengths, dec_full)
    attn_low = attn_weights[0].astype(HALF_TYPE)
    cross_low = cross_weights[0].astype(HALF_TYPE)
    ffn_low = ffn_weights[0].astype(HALF_TYPE)
    gain_vecs = norm_gains[0]
    bias_vecs = norm_biases[0]
    pair_grad_spec = ((row_width, 2, local_width), WIDE_TYPE)
    memory, stash = encoder_forward(enc_input, enc_seg, attn_low, ffn_low, gain_vecs, bias_vecs)
    memory_full = gather_rows(memory.astype(HALF_TYPE))
    forward_out = (project_memory(memory_full, cross_low), memory_full) + stash
    received = shifted(forward_out[0], "pipe", 1)
    outcome = decoder_pass(
        dec_input,
        dec_cotangent,
        dec_seg,
        enc_seg,
        received[:, :, 0],
        received[:, :, 1],
        attn_low,
        cross_low,
        ffn_low,
        gain_vecs,
        bias_vecs,
    )
    decoder_out = (outcome[2],) + outcome[:2] + outcome[3:] + blanks([pair_grad_spec])
    returned = shifted(decoder_out[0], "pipe", -1)
    stash = forward_out[1:]
    grad_memory, grad_pair_w = project_back(returned, stash[0], cross_low)
    outcome = encoder_backward(
        grad_memory, stash[1:], enc_input, enc_seg, attn_low, ffn_low, gain_vecs, bias_vecs
    )
    encoder_out = (outcome[0], outcome[1], grad_pair_w, outcome[2], outcome[3], outcome[4])
    enc_grad = encoder_out[0]
    enc_wgrads = encoder_out[1:6]
    dec_result = decoder_out[1]
    dec_grad = decoder_out[2]
    dec_wgrads = decoder_out[3:8]

    def by_section(first, second):
        return jnp.where(is_encoder, first, second)

    attn_total = by_section(enc_wgrads[0], dec_wgrads[0])[None]
    cross_total = by_section(enc_wgrads[1], dec_wgrads[1])[None]
    ffn_total = by_section(enc_wgrads[2], dec_wgrads[2])[None]
    gain_total = by_section(enc_wgrads[3], dec_wgrads[3])[None]
    bias_total = by_section(enc_wgrads[4], dec_wgrads[4])[None]
    attn_sum, cross_sum, ffn_sum = (
        lax.psum_scatter(
            attn_total.astype(jnp.bfloat16), "dp", scatter_dimension=1, tiled=True
        ).astype(jnp.float32),
        lax.psum_scatter(
            cross_total.astype(jnp.bfloat16), "dp", scatter_dimension=1, tiled=True
        ).astype(jnp.float32),
        lax.psum_scatter(
            ffn_total.astype(jnp.bfloat16), "dp", scatter_dimension=1, tiled=True
        ).astype(jnp.float32),
    )
    gain_sum, bias_sum = (
        lax.psum_scatter(gain_total, ("dp", "tensor"), scatter_dimension=2, tiled=True),
        lax.psum_scatter(bias_total, ("dp", "tensor"), scatter_dimension=2, tiled=True),
    )
    half_width = row_width // 2
    sent_up = shifted(enc_grad[:, :, half_width:].astype(jnp.bfloat16), "pipe", 1).astype(
        jnp.float32
    )
    enc_input_grad = jnp.where(is_encoder, enc_grad[:, :, :half_width], sent_up)
    dec_wide = dec_result.astype(WIDE_TYPE)
    sent_down = shifted(
        jnp.stack([dec_wide[:, :, :half_width], dec_grad[:, :, :half_width]]).astype(jnp.bfloat16),
        "pipe",
        -1,
    ).astype(jnp.float32)
    dec_output = jnp.where(is_encoder, sent_down[0], dec_wide[:, :, half_width:]).astype(HALF_TYPE)
    dec_input_grad = jnp.where(is_encoder, sent_down[1], dec_grad[:, :, half_width:])
    return (
        dec_output,
        enc_input_grad,
        dec_input_grad,
        attn_sum,
        cross_sum,
        ffn_sum,
        gain_sum,
        bias_sum,
    )


def solution(mesh):
    placed = (
        P("dp", "tensor", None),
        P("dp", "tensor", None),
        P("dp", "tensor", None),
        P("dp", None),
        P("dp", None),
        P("pipe", None, None, "tensor"),
        P("pipe", None, None, "tensor"),
        P("pipe", None, None, "tensor"),
        P("pipe", None, None),
        P("pipe", None, None),
    )
    return jax.shard_map(
        per_device,
        mesh=mesh,
        in_specs=placed,
        out_specs=(
            P("dp", "tensor", "pipe"),
            P("dp", "tensor", "pipe"),
            P("dp", "tensor", "pipe"),
            P("pipe", "dp", None, "tensor"),
            P("pipe", "dp", None, "tensor"),
            P("pipe", "dp", None, "tensor"),
            P("pipe", None, ("dp", "tensor")),
            P("pipe", None, ("dp", "tensor")),
        ),
        check_vma=False,
    )
```

profile of v0, /device:TPU:0, one launch (start us, length us, event | category | flops | bytes accessed | tf_op | source)
XLA Modules:
  0.0 3695.8 jit_solution(9210290951905105065)
XLA Ops:
  18.9 149.2 %all-gather.14.cloned.1.call-done = bf16[2,2048,1024]{2,1,0:T(8,128)(2,1)} async-done(((bf16[2,512,1024]{2,1,0:T(8,128)(2,1)}), bf16[2,2048,1024]{2,1,0:T(8,128)(2,1)}) %all-gather.14.cloned.1.call-update) | async-done | bytes 8388624 | tf_op jit(solution)/shard_map/all_gather | solution.py:24
  192.4 165.4 %while.95 = (s32[]{:T(128)}, bf16[8,512,256]{2,1,0:T(8,128)(2,1)}, f32[8,512,4]{1,2,0:T(4,128)}, s32[8]{0:T(128)S(1)}, bf16[2,2048,256]{1,2,0:T(8,128)(2,1)}, /*...) while((s32[]{:T(128)}, bf16[8,512,256]{2,1,0:T(8,128)(2,1)}, ...), condition=%wide.region_16.17_spmd, body=%wide.region_13.16_spmd.sunk | while | flops 1125120000 | bytes 63011320 | solution.py:121
  366.1 142.8 %reduce-scatter.23.cloned.1.call-done = bf16[2,512,1024]{2,1,0:T(8,128)(2,1)} async-done(((bf16[2,2048,1024]{2,1,0:T(8,128)(2,1)}), bf16[2,512,1024]{2,1,0:T(8,128)(2,1)}) %reduce-scatter.23.cloned.1.call-update) | async-done | bytes 2097168 | tf_op jit(solution)/shard_map/reduce_scatter | solution.py:28
  526.7 142.8 %all-gather.16.cloned.1.call-done = bf16[2,2048,1024]{2,1,0:T(8,128)(2,1)} async-done(((bf16[2,512,1024]{2,1,0:T(8,128)(2,1)}), bf16[2,2048,1024]{2,1,0:T(8,128)(2,1)}) %all-gather.16.cloned.1.call-update) | async-done | bytes 8388624 | tf_op jit(solution)/shard_map/all_gather | solution.py:24
  694.0 40.8 %multiply_convert_fusion.2 = (bf16[2,2048,1024]{2,1,0:T(8,128)(2,1)S(1)}, f32[2,2048,1024]{2,1,0:T(8,128)}) fusion(f32[2,2048,1024]{2,1,0:T(8,128)} %get-tuple-element.1380, u8[2048,1024]{1,0:T(8,128)(4,1)} %get-tuple-element.1187, u8[2048,1024]{1,0:T(8,128)(4,1)} %get-tuple-element.1186), kind=kLoop, calls=%fused_computation.173 | loop fusion | flops 293601280 | bytes 46137344 | tf_op jit(solution)/shard_map/convert_element_type | solution.py:268
  749.8 142.2 %reduce-scatter.25.cloned.1.call-done = bf16[2,512,1024]{2,1,0:T(8,128)(2,1)} async-done(((bf16[2,2048,1024]{2,1,0:T(8,128)(2,1)}), bf16[2,512,1024]{2,1,0:T(8,128)(2,1)}) %reduce-scatter.25.cloned.1.call-update) | async-done | bytes 2097168 | tf_op jit(solution)/shard_map/reduce_scatter | solution.py:28
  933.9 138.8 %all-gather.18.cloned.1.call-done = bf16[2,2048,1024]{2,1,0:T(8,128)(2,1)} async-done(((bf16[2,512,1024]{2,1,0:T(8,128)(2,1)}), bf16[2,2048,1024]{2,1,0:T(8,128)(2,1)}) %all-gather.18.cloned.1.call-update) | async-done | bytes 8388624 | tf_op jit(solution)/shard_map/all_gather | solution.py:24
  1369.5 167.0 %while.97 = (s32[]{:T(128)}, f32[2,2048,256]{2,1,0:T(8,128)}, f32[2,2048,256]{2,1,0:T(8,128)}, bf16[2,256,256]{1,2,0:T(8,128)(2,1)}, s32[2]{0:T(128)S(1)}, /*ind...) while((s32[]{:T(128)}, f32[2,2048,256]{2,1,0:T(8,128)}, ...), condition=%wide.region_40.41_spmd, body=%wide.region_38.40_spmd.sunk | while | flops 1398282240 | bytes 183254800 | solution.py:181
  1559.4 144.1 %reduce-scatter.37.cloned.1.call-done = bf16[2,512,1024]{2,1,0:T(8,128)(2,1)} async-done(((bf16[2,2048,1024]{2,1,0:T(8,128)(2,1)}), bf16[2,512,1024]{2,1,0:T(8,128)(2,1)}) %reduce-scatter.37.cloned.1.call-update) | async-done | bytes 2097168 | tf_op jit(solution)/shard_map/reduce_scatter | solution.py:28
  1712.2 148.9 %all-gather.30.cloned.1.call-done = bf16[2,2048,1024]{2,1,0:T(8,128)(2,1)} async-done(((bf16[2,512,1024]{2,1,0:T(8,128)(2,1)}), bf16[2,2048,1024]{2,1,0:T(8,128)(2,1)}) %all-gather.30.cloned.1.call-update) | async-done | bytes 8388624 | tf_op jit(solution)/shard_map/all_gather | solution.py:24
  1901.0 137.7 %reduce-scatter.39.cloned.1.call-done = bf16[2,512,1024]{2,1,0:T(8,128)(2,1)} async-done(((bf16[2,2048,1024]{2,1,0:T(8,128)(2,1)}), bf16[2,512,1024]{2,1,0:T(8,128)(2,1)}) %reduce-scatter.39.cloned.1.call-update) | async-done | bytes 2097168 | tf_op jit(solution)/shard_map/reduce_scatter | solution.py:28
  2072.2 38.2 %while.98 = (s32[]{:T(128)}, f32[2,256,256]{2,1,0:T(8,128)}, f32[2,256,256]{2,1,0:T(8,128)S(1)}, bf16[2,256,256]{2,1,0:T(8,128)(2,1)}, s32[2]{0:T(128)S(1)}, /*i...) while((s32[]{:T(128)}, f32[2,256,256]{2,1,0:T(8,128)}, ...), condition=%wide.region_46.47_spmd, body=%wide.region_44.46_spmd.sunk | while | flops 171772416 | bytes 20856268 | solution.py:181
  2115.9 104.3 %all-gather.32.cloned.1.call-done = bf16[2,2048,1024]{2,1,0:T(8,128)(2,1)} async-done(((bf16[2,512,1024]{2,1,0:T(8,128)(2,1)}), bf16[2,2048,1024]{2,1,0:T(8,128)(2,1)}) %all-gather.32.cloned.1.call-update) | async-done | bytes 8388624 | tf_op jit(solution)/shard_map/all_gather | solution.py:24
  2230.6 1008.4 %while.99 = (s32[]{:T(128)}, f32[2,2048,256]{2,1,0:T(8,128)}, f32[2,2048,256]{2,1,0:T(8,128)}, bf16[8,512,256]{1,2,0:T(8,128)(2,1)}, s32[8]{0:T(128)S(1)}, /*ind...) while((s32[]{:T(128)}, f32[2,2048,256]{2,1,0:T(8,128)}, ...), condition=%wide.region_56.57_spmd, body=%wide.region_54.56_spmd.sunk | while | flops 2795511808 | bytes 247798896 | solution.py:181
  2300.6 33.3 fusion.431
  2426.5 33.3 fusion.431
  2552.4 33.3 fusion.431
  2678.3 33.3 fusion.431
  2804.2 33.3 fusion.431
  3330.1 69.7 %reduce-scatter.41.cloned.1.call-done = bf16[2,512,1024]{2,1,0:T(8,128)(2,1)} async-done(((bf16[2,2048,1024]{2,1,0:T(8,128)(2,1)}), bf16[2,512,1024]{2,1,0:T(8,128)(2,1)}) %reduce-scatter.41.cloned.1.call-update) | async-done | bytes 2097168 | tf_op jit(solution)/shard_map/reduce_scatter | solution.py:28
  3433.1 53.8 %reduce-scatter.47.cloned.1.call-done = bf16[1,256,2,1024]{3,1,2,0:T(8,128)(2,1)} async-done(((bf16[1,1024,2,1024]{3,1,2,0:T(8,128)(2,1)}), bf16[1,256,2,1024]{3,1,2,0:T(8,128)(2,1)}) %reduce-scatter.47.cloned.1.call-update) | async-done | bytes 1048592 | tf_op jit(solution)/shard_map/reduce_scatter | solution.py:479
  3490.6 35.1 reduce-scatter.43.cloned.1.call-done
  3534.1 74.1 %reduce-scatter.49.cloned.1.call-done = f32[64,3]{1,0:T(8,128)} async-done(((f32[1024,3]{1,0:T(8,128)}), f32[64,3]{1,0:T(8,128)}) %reduce-scatter.49.cloned.1.call-update) | async-done | bytes 784
  3609.7 73.9 %reduce-scatter.51.cloned.1.call-done = f32[64,3]{1,0:T(8,128)} async-done(((f32[1024,3]{1,0:T(8,128)}), f32[64,3]{1,0:T(8,128)}) %reduce-scatter.51.cloned.1.call-update) | async-done | bytes 784
  (1221 shorter events, 1882.5 us)
Async XLA Ops:
  7.2 160.9 %all-gather.14.cloned.1.call-start = ((), (), s32[]{:S(2)}) async-start(), calls=%async_computation.18 | async-start | bytes 10485760 | tf_op jit(solution)/shard_map/all_gather | solution.py:24
  15.6 493.2 %reduce-scatter.23.cloned.1.call-start = ((), (), s32[]{:S(2)}) async-start(), calls=%async_computation.19 | async-start | bytes 10485760 | tf_op jit(solution)/shard_map/reduce_scatter | solution.py:28
  366.0 303.4 %all-gather.16.cloned.1.call-start = ((), (), s32[]{:S(2)}) async-start(), calls=%async_computation.20 | async-start | bytes 10485760 | tf_op jit(solution)/shard_map/all_gather | solution.py:24
  518.9 373.0 %reduce-scatter.25.cloned.1.call-start = ((), (), s32[]{:S(2)}) async-start(), calls=%async_computation.21 | async-start | bytes 10485760 | tf_op jit(solution)/shard_map/reduce_scatter | solution.py:28
  749.1 173.0 %all-gather.12.cloned.1.call-start = ((), (), s32[]{:S(2)}) async-start(), calls=%async_computation.16 | async-start | bytes 1310720 | tf_op jit(solution)/shard_map/all_gather | solution.py:24
  749.7 323.0 %all-gather.18.cloned.1.call-start = ((), (), s32[]{:S(2)}) async-start(), calls=%async_computation.22 | async-start | bytes 10485760 | tf_op jit(solution)/shard_map/all_gather | solution.py:24
  900.1 200.8 %reduce-scatter.21.cloned.1.call-start = ((), (), s32[]{:S(2)}) async-start(), calls=%async_computation.17 | async-start | bytes 1310720 | tf_op jit(solution)/shard_map/reduce_scatter | solution.py:28
  933.6 198.2 %all-gather.20.cloned.1.call-start = ((), (), s32[]{:S(2)}) async-start(), calls=%async_computation.23 | async-start | bytes 1310720 | tf_op jit(solution)/shard_map/all_gather | solution.py:24
  1105.1 92.0 %reduce-scatter.27.cloned.1.call-start = ((), (), s32[]{:S(2)}) async-start(), calls=%async_computation.24 | async-start | bytes 1310720 | tf_op jit(solution)/shard_map/reduce_scatter | solution.py:28
  1199.4 66.4 %reduce-scatter.29.cloned.1.call-start = ((), (), s32[]{:S(2)}) async-start(), calls=%async_computation.26 | async-start | bytes 1310720 | tf_op jit(solution)/shard_map/reduce_scatter | solution.py:28
  1334.8 368.6 %reduce-scatter.37.cloned.1.call-start = ((), (), s32[]{:S(2)}) async-start(), calls=%async_computation.33 | async-start | bytes 10485760 | tf_op jit(solution)/shard_map/reduce_scatter | solution.py:28
  1559.4 301.8 %all-gather.30.cloned.1.call-start = ((), (), s32[]{:S(2)}) async-start(), calls=%async_computation.34 | async-start | bytes 10485760 | tf_op jit(solution)/shard_map/all_gather | solution.py:24
  1710.6 185.3 %reduce-scatter.33.cloned.1.call-start = ((), (), s32[]{:S(2)}) async-start(), calls=%async_computation.30 | async-start | bytes 1310720 | tf_op jit(solution)/shard_map/reduce_scatter | solution.py:28
  1712.2 326.5 %reduce-scatter.39.cloned.1.call-start = ((), (), s32[]{:S(2)}) async-start(), calls=%async_computation.35 | async-start | bytes 10485760 | tf_op jit(solution)/shard_map/reduce_scatter | solution.py:28
  1895.9 173.7 %all-gather.28.cloned.1.call-start = ((), (), s32[]{:S(2)}) async-start(), calls=%async_computation.31 | async-start | bytes 1310720 | tf_op jit(solution)/shard_map/all_gather | solution.py:24
  1900.9 319.3 %all-gather.32.cloned.1.call-start = ((), (), s32[]{:S(2)}) async-start(), calls=%async_computation.36 | async-start | bytes 10485760 | tf_op jit(solution)/shard_map/all_gather | solution.py:24
  2052.2 1272.2 %reduce-scatter.35.cloned.1.call-start = ((), (), s32[]{:S(2)}) async-start(), calls=%async_computation.32 | async-start | bytes 1310720 | tf_op jit(solution)/shard_map/reduce_scatter | solution.py:28
  2115.9 1283.9 %reduce-scatter.41.cloned.1.call-start = ((), (), s32[]{:S(2)}) async-start(), calls=%async_computation.37 | async-start | bytes 10485760 | tf_op jit(solution)/shard_map/reduce_scatter | solution.py:28
  3256.9 174.2 %reduce-scatter.45.cloned.1.call-start = ((), (), s32[]{:S(2)}) async-start(), calls=%async_computation.39 | async-start | bytes 1310720 | tf_op jit(solution)/shard_map/reduce_scatter | solution.py:476
  3274.9 212.0 %reduce-scatter.47.cloned.1.call-start = ((), (), s32[]{:S(2)}) async-start(), calls=%async_computation.40 | async-start | bytes 5242880 | tf_op jit(solution)/shard_map/reduce_scatter | solution.py:479
  3305.5 220.2 %reduce-scatter.43.cloned.1.call-start = ((), (), s32[]{:S(2)}) async-start(), calls=%async_computation.38 | async-start | bytes 2621440 | tf_op jit(solution)/shard_map/reduce_scatter | solution.py:473
  3324.3 283.9 %reduce-scatter.49.cloned.1.call-start = ((), (), s32[]{:S(2)}) async-start(), calls=%async_computation.41 | async-start | bytes 557056
  3410.9 274.2 %collective-permute-start.3 = (bf16[2,512,512]{2,1,0:T(8,128)(2,1)}, bf16[2,512,512]{2,1,0:T(8,128)(2,1)}, u32[]{:S(2)}, u32[]{:S(2)}) collective-permute-start(bf16[2,512,512]{2,1,0:T(8,128)(2,1)} %slice.230), channel_id=1, source_target_pairs={{0,16},{1,17},{2,18},{3,19},{4,20},{5,21},{6,22},{7,23},{8,24},{9,... | collective-permute-start | bytes 3145736 | tf_op jit(solution)/shard_map/ppermute | solution.py:20
  3531.1 152.5 %reduce-scatter.51.cloned.1.call-start = ((), (), s32[]{:S(2)}) async-start(), calls=%async_computation.42 | async-start | bytes 557056
  (281 other events, 8148.4 us)
Sparse Core Ops, SparseCore 0:
  15.7 152.3 all-gather.13
  366.1 142.6 reduce-scatter.22
  519.1 150.3 all-gather.15
  749.3 142.6 reduce-scatter.24
  893.4 28.6 all-gather.11
  923.5 149.1 all-gather.17
  1105.2 26.5 all-gather.19
  1170.4 26.6 reduce-scatter.26
  1199.5 26.5 all-gather.21
  1239.2 26.6 reduce-scatter.28
  1269.3 26.5 all-gather.23
  1304.4 26.6 reduce-scatter.30
  1335.0 26.5 all-gather.25
  1559.5 143.9 reduce-scatter.36
  1710.7 150.3 all-gather.29
  1896.0 142.6 reduce-scatter.38
  2040.9 28.6 all-gather.27
  2071.1 149.1 all-gather.31
  3257.0 142.6 reduce-scatter.40
  3402.7 28.4 reduce-scatter.44
  3434.2 52.6 reduce-scatter.46
  3490.5 35.1 reduce-scatter.42
  3531.2 76.9 reduce-scatter.48
  3610.2 73.3 reduce-scatter.50
  (3 shorter events, 75.8 us)
where the time goes:
time: 3700 us
  waiting for transfers between devices  1820 us (49%)
  matrix products  1120 us (30%)
  local copies, waits for them, and re-layouts  426 us (12%)
  other arithmetic  235 us (6%)
  loops' own time  62 us (2%)
    all_gather x11, waiting for transfers between devices, gather_rows(): return lax.all_gather(values, 'tensor', axis=1, tiled=True)  828 us
    reduce_scatter x11, waiting for transfers between devices, sum_rows(): lax.psum_scatter(terms.astype(jnp.bfloat16), 'tensor', scatter_dimension=...  730 us
    dot_general x12, matrix products, one_block(): jnp.einsum('hqk,qhd->khd', grad_raw, query_part, preferred_element_type=j...  307 us
    dot_general x12, matrix products, one_block(): jnp.einsum('hqk,khd->qhd', grad_raw, key_here, preferred_element_type=jnp...  286 us
    unnamed x29, waiting for transfers between devices  149 us
    dot_general x24, matrix products, block_scores(): jnp.einsum('qhd,khd->hqk', query_part, key_here, preferred_element_type=j...  108 us
    dynamic_update_slice x36, local copies, waits for them, and re-layouts, add_batch(): lax.dynamic_update_index_in_dim(totals, current + addition, batch_index, 0)  97.5 us
    dynamic_slice x48, local copies, waits for them, and re-layouts, add_batch(): current = lax.dynamic_index_in_dim(totals, batch_index, 0, False)  95.6 us
  transfers between devices with their start and end apart: 31, of which 27 were waited for; matrix products, arithmetic and copies ran while one was open for 33% of the time, Pallas kernels for 0%

commit v1 on v0

v1 whole, which is shorter than its diff:
```python
from functools import partial

import jax
import jax.numpy as jnp
from jax import lax
from jax.experimental import pallas as pl
from jax.experimental.pallas import tpu as pltpu
from jax.sharding import PartitionSpec as P

HEAD = 64
LANES = 128
EPSILON = 1e-05
NEGATIVE = -1e30
HALF = jnp.bfloat16
WIDE = jnp.float32
VMEM_LIMIT = 56 << 20
MESH = pl.DeviceIdType.MESH
TILE_Q = 512
TILE_K = 512


def dot(left, right):
    return jnp.dot(left, right, preferred_element_type=WIDE)


def dot_bt(left, right):
    return lax.dot_general(left, right, (((1,), (1,)), ((), ())), preferred_element_type=WIDE)


def dot_ta(left, right):
    return lax.dot_general(left, right, (((0,), (0,)), ((), ())), preferred_element_type=WIDE)


def swap(value, axis, mask):
    return lax.ppermute(value, axis, [(i, i ^ mask) for i in range(lax.axis_size(axis))])


def joint(value, pairs):
    count = lax.axis_size("tensor")
    return lax.ppermute(
        value,
        ("pipe", "tensor"),
        [(a[0] * count + a[1], b[0] * count + b[1]) for a, b in pairs],
    )


def after(value, *earlier):
    return lax.optimization_barrier((value, *earlier))[0]


def swap_columns(value, axis, mask, difference):
    got = swap(value, axis, mask).reshape(value.shape[0], -1, LANES)
    order = [b ^ difference for b in range(got.shape[1])]
    return jnp.concatenate([got[:, b] for b in order], axis=1)


def table_of(places, lengths):
    total = jnp.zeros((), jnp.int32)
    table = jnp.zeros(places.shape, jnp.int32)
    for j in range(lengths.shape[0]):
        total = total + lengths[j]
        table = table + (places >= total).astype(jnp.int32)
    return table


def norm_forward(values, gain, bias):
    center = values - jnp.mean(values, axis=-1, keepdims=True)
    inv_scale = lax.rsqrt(jnp.mean(center * center, axis=-1, keepdims=True) + EPSILON)
    normed = center * inv_scale
    return normed * gain + bias, normed, inv_scale


def norm_backward(grad_out, normed, inv_scale, gain):
    grad_gain = jnp.sum(grad_out * normed, axis=0)
    grad_bias = jnp.sum(grad_out, axis=0)
    grad_normed = grad_out * gain
    grad_in = inv_scale * (
        grad_normed
        - jnp.mean(grad_normed, axis=-1, keepdims=True)
        - normed * jnp.mean(grad_normed * normed, axis=-1, keepdims=True)
    )
    return grad_in, grad_gain, grad_bias


def gelu(hidden):
    return 0.5 * hidden * (1.0 + lax.erf(hidden * (2.0**-0.5)))


def gelu_slope(hidden):
    density = jnp.exp(-0.5 * hidden * hidden) * 0.3989422804014327
    return 0.5 * (1.0 + lax.erf(hidden * (2.0**-0.5))) + hidden * density


def _allowed(seg_k, seg_q, causal, col0, row0):
    ok = seg_k == seg_q
    if causal:
        keys = col0 + lax.broadcasted_iota(jnp.int32, ok.shape, 0)
        queries = row0 + lax.broadcasted_iota(jnp.int32, ok.shape, 1)
        ok = ok & (queries >= keys)
    return ok


def _tile_loop(act, chunks, c, nq, nk, tq, tk, body):
    def step(i, carry):
        iq, ik = i // nk, i % nk

        @pl.when(act[iq * (chunks * nk) + c * nk + ik] > 0)
        def _():
            body(iq * tq, ik * tk, pl.ds(pl.multiple_of(iq * tq, tq), tq), pl.ds(pl.multiple_of(ik * tk, tk), tk))

        return carry

    lax.fori_loop(0, nq * nk, step, 0)


def _head_lanes(shape, head):
    lanes = lax.broadcasted_iota(jnp.int32, shape, 1)
    return (lanes < HEAD) if head == 0 else (lanes >= HEAD)


def _attend_kernel(chunks, tq, tk, causal, act, seg_q, seg_k, q, *refs):
    keys, values = refs[:chunks], refs[chunks : 2 * chunks]
    out, lse, top, total, acc = refs[2 * chunks :]
    rows = q.shape[0]
    nq, nk = rows // tq, keys[0].shape[0] // tk
    top[...] = jnp.full(top.shape, NEGATIVE, WIDE)
    total[...] = jnp.zeros(total.shape, WIDE)
    acc[...] = jnp.zeros(acc.shape, WIDE)
    for c in range(chunks):

        def tile(row0, col0, r, s, c=c):
            qs = q[r, :] * jnp.asarray(HEAD**-0.5, HALF)
            kk, vt = keys[c][s, :], values[c][s, :].T
            ok = _allowed(seg_k[c, s, 0:1], seg_q[0:1, r], causal, col0, row0)
            for h in range(2):
                qh = jnp.where(_head_lanes(qs.shape, h), qs, jnp.zeros_like(qs))
                sc = jnp.where(ok, dot_bt(kk, qh), NEGATIVE)
                before = top[h : h + 1, r]
                after = jnp.maximum(before, jnp.max(sc, axis=0, keepdims=True))
                pr = jnp.exp(sc - after).astype(HALF)
                fade = jnp.exp(before - after)
                total[h : h + 1, r] = total[h : h + 1, r] * fade + jnp.sum(
                    pr.astype(WIDE), axis=0, keepdims=True
                )
                span = slice(h * HEAD, (h + 1) * HEAD)
                acc[span, r] = acc[span, r] * fade + dot(vt[span, :], pr)
                top[h : h + 1, r] = after

        _tile_loop(act, chunks, c, nq, nk, tq, tk, tile)
    count = total[...]
    count = jnp.where(count > 0.0, count, 1.0)
    lse[0] = top[...] + jnp.log(count)
    whole = jnp.concatenate([acc[:HEAD, :] / count[0:1, :], acc[HEAD:, :] / count[1:2, :]], axis=0)
    out[...] = whole.T.astype(out.dtype)


def _attend_back_kernel(chunks, tq, tk, causal, own_delta, act, seg_q, seg_k, q, *refs):
    keys, values = refs[:chunks], refs[chunks : 2 * chunks]
    grad_out, stats = refs[2 * chunks : 2 * chunks + 2]
    refs = refs[2 * chunks + 2 :]
    extra, grad_q, *refs = refs
    grad_kv, (delta, dq, dkv) = refs[:chunks], refs[chunks:]
    rows = q.shape[0]
    nq, nk = rows // tq, keys[0].shape[0] // tk
    if own_delta:
        product = grad_out[...].astype(WIDE) * extra[...].astype(WIDE)
        pick = (
            lax.broadcasted_iota(jnp.int32, (8, LANES), 1) // HEAD
            == lax.broadcasted_iota(jnp.int32, (8, LANES), 0)
        ).astype(WIDE)
        delta[...] = lax.dot_general(
            pick, product, (((1,), (1,)), ((), ())), precision=lax.Precision.HIGHEST, preferred_element_type=WIDE
        )
    else:
        delta[0:2, :] = stats[0, 2:4, :]
    dq[...] = jnp.zeros(dq.shape, WIDE)
    for c in range(chunks):
        dkv[...] = jnp.zeros(dkv.shape, WIDE)

        def tile(row0, col0, r, s, c=c):
            qs = q[r, :] * jnp.asarray(HEAD**-0.5, HALF)
            go = grad_out[r, :]
            kk, vv = keys[c][s, :], values[c][s, :]
            ok = _allowed(seg_k[c, s, 0:1], seg_q[0:1, r], causal, col0, row0)
            for h in range(2):
                mine, mine_k = _head_lanes(qs.shape, h), _head_lanes(kk.shape, h)
                qh = jnp.where(mine, qs, jnp.zeros_like(qs))
                gh = jnp.where(mine, go, jnp.zeros_like(go))
                kh = jnp.where(mine_k, kk if own_delta else extra[s, :], jnp.zeros_like(kk))
                sc = jnp.where(ok, dot_bt(kk, qh), NEGATIVE)
                pr = jnp.exp(sc - stats[0, h : h + 1, r])
                ds = (pr * (dot_bt(vv, gh) - delta[h : h + 1, r])).astype(HALF)
                pr = pr.astype(HALF)
                dq[r, :] = dq[r, :] + dot_ta(ds, kh)
                dkv[0, s, :] = dkv[0, s, :] + dot(ds, qh)
                dkv[1, s, :] = dkv[1, s, :] + dot(pr, gh)

        _tile_loop(act, chunks, c, nq, nk, tq, tk, tile)
        grad_kv[c][...] = dkv[...].astype(grad_kv[c].dtype)
    grad_q[...] = (dq[...] * HEAD**-0.5).astype(grad_q.dtype)


def _tile_sizes(rows, keys):
    return min(TILE_Q, rows), min(TILE_K, keys)


def _activity(seg_q, seg_k, tq, tk):
    qt = seg_q.reshape(-1, tq)
    kt = seg_k.reshape(-1, tk)
    hit = (qt[:, :1] <= kt[:, -1][None]) & (kt[:, 0][None] <= qt[:, -1:])
    return hit.astype(jnp.int32).reshape(-1)


def tables(seg_q, seg_k):
    rows, (chunks, span) = seg_q.shape[0], seg_k.shape
    tq, tk = _tile_sizes(rows, span)
    return (
        _activity(seg_q, seg_k, tq, tk),
        jnp.broadcast_to(seg_q[None], (8, rows)),
        jnp.broadcast_to(seg_k[:, :, None], (chunks, span, LANES)),
    )


def _specs(rows, span, chunks, masks, blocked):
    row_block = pl.BlockSpec((rows, LANES), lambda h, act: (0, h))
    if blocked:
        row_block = pl.BlockSpec((None, rows, LANES), lambda h, act: (h, 0, 0))
    stat_block = pl.BlockSpec((1, 8, rows), lambda h, act: (h, 0, 0))
    heads = [
        pl.BlockSpec((8, rows), lambda h, act: (0, 0)),
        pl.BlockSpec((chunks, span, LANES), lambda h, act: (0, 0, 0)),
        row_block,
    ]
    for part in range(2):
        heads += [
            pl.BlockSpec((None, span, LANES), lambda h, act, m=m, part=part: (part, 0, h ^ m)) for m in masks
        ]
    return row_block, stat_block, heads


def attend(q, key_values, segs, masks, causal=False, out_type=WIDE):
    blocked = q.ndim == 3
    rows, width = (q.shape[1], q.shape[0] * LANES) if blocked else q.shape
    span = key_values[0].shape[1]
    chunks, blocks = len(key_values), width // LANES
    tq, tk = _tile_sizes(rows, span)
    row_block, stat_block, specs = _specs(rows, span, chunks, masks, blocked)
    pairs = rows * span * chunks
    return pl.pallas_call(
        partial(_attend_kernel, chunks, tq, tk, causal),
        out_shape=(
            jax.ShapeDtypeStruct(q.shape, out_type),
            jax.ShapeDtypeStruct((blocks, 8, rows), WIDE),
        ),
        grid_spec=pltpu.PrefetchScalarGridSpec(
            num_scalar_prefetch=1,
            grid=(blocks,),
            in_specs=specs,
            out_specs=[row_block, stat_block],
            scratch_shapes=[
                pltpu.VMEM((8, rows), WIDE),
                pltpu.VMEM((8, rows), WIDE),
                pltpu.VMEM((LANES, rows), WIDE),
            ],
        ),
        compiler_params=pltpu.CompilerParams(vmem_limit_bytes=VMEM_LIMIT),
        cost_estimate=pl.CostEstimate(
            flops=4 * pairs * width, transcendentals=pairs * width // HEAD, bytes_accessed=rows * width * 20
        ),
        name="attend",
    )(*segs, q, *key_values, *key_values)


def attend_back(q, key_values, grad_out, stats, extra, segs, masks, causal=False, own_delta=True):
    blocked = q.ndim == 3
    rows, width = (q.shape[1], q.shape[0] * LANES) if blocked else q.shape
    span = key_values[0].shape[1]
    chunks, blocks = len(key_values), width // LANES
    tq, tk = _tile_sizes(rows, span)
    row_block, stat_block, specs = _specs(rows, span, chunks, masks, blocked)
    kv_out = [pl.BlockSpec((2, span, LANES), lambda h, act, m=m: (0, 0, h ^ m)) for m in masks]
    pairs = rows * span * chunks
    extra_block = row_block if own_delta else pl.BlockSpec((span, LANES), lambda h, act: (0, h))
    outs = pl.pallas_call(
        partial(_attend_back_kernel, chunks, tq, tk, causal, own_delta),
        out_shape=[jax.ShapeDtypeStruct(q.shape, HALF)]
        + [jax.ShapeDtypeStruct((2, span, width), HALF)] * chunks,
        grid_spec=pltpu.PrefetchScalarGridSpec(
            num_scalar_prefetch=1,
            grid=(blocks,),
            in_specs=specs + [row_block, stat_block, extra_block],
            out_specs=[row_block] + kv_out,
            scratch_shapes=[
                pltpu.VMEM((8, rows), WIDE),
                pltpu.VMEM((rows, LANES), WIDE),
                pltpu.VMEM((2, span, LANES), WIDE),
            ],
        ),
        compiler_params=pltpu.CompilerParams(vmem_limit_bytes=VMEM_LIMIT),
        cost_estimate=pl.CostEstimate(
            flops=10 * pairs * width, transcendentals=pairs * width // HEAD, bytes_accessed=rows * width * 40
        ),
        name="attend_back",
    )(*segs, q, *key_values, *key_values, grad_out, stats, extra)
    return outs[0], outs[1:]


def _row_mean(values):
    return jnp.mean(values, axis=-1, keepdims=True)


def _norm_rows(values, gain, bias):
    center = values - _row_mean(values)
    inv_scale = lax.rsqrt(_row_mean(center * center) + EPSILON)
    normed = center * inv_scale
    return normed * gain + bias, normed, inv_scale


def _norm_rows_back(grad_out, normed, inv_scale, gain):
    grad_normed = grad_out * gain
    grad_in = inv_scale * (
        grad_normed - _row_mean(grad_normed) - normed * _row_mean(grad_normed * normed)
    )
    return (
        grad_in,
        jnp.sum(grad_out * normed, axis=0, keepdims=True),
        jnp.sum(grad_out, axis=0, keepdims=True),
    )


def _forward_rows(total, ins, outs):
    resid, gain, bias = ins
    value, normed, inv_scale = _norm_rows(total + resid[...], gain[...], bias[...])
    outs[0][...] = value
    outs[1][...] = normed
    outs[2][...] = jnp.broadcast_to(inv_scale, outs[2].shape)
    return value


def _turn_rows(total, ins, outs):
    resid, gain, bias, cotangent = ins
    value, normed, inv_scale = _norm_rows(total + resid[...], gain[...], bias[...])
    outs[0][...] = value.astype(outs[0].dtype)
    grad, grad_gain, grad_bias = _norm_rows_back(
        cotangent[...].astype(WIDE), normed, inv_scale, gain[...]
    )
    outs[1][...] = grad
    outs[2][0:1, :] = grad_gain
    outs[2][1:2, :] = grad_bias
    return grad


def _backward_rows(total, ins, outs):
    resid, normed, inv_scale, gain = ins
    grad, grad_gain, grad_bias = _norm_rows_back(
        total + resid[...], normed[...], inv_scale[:, 0:1], gain[...]
    )
    outs[0][...] = grad
    outs[1][0:1, :] = grad_gain
    outs[1][1:2, :] = grad_bias
    return grad


def _last_rows(total, ins, outs):
    outs[0][...] = total + ins[0][...]


def _rows_kernel(count, scatter, gather, middle, n_in, n_out, *refs):
    refs = list(refs)
    part = refs.pop(0) if scatter else None
    ins, refs = refs[:n_in], refs[n_in:]
    outs, refs = refs[:n_out], refs[n_out:]
    full = refs.pop(0) if gather else None
    landed = refs.pop(0) if scatter else None
    send_sem, recv_sem = refs[:2]
    me = lax.axis_index("tensor")
    steps = range(1, count)
    peers = [lax.rem(me + s, count) for s in steps]
    barrier = pltpu.get_barrier_semaphore()
    for peer in peers:
        pl.semaphore_signal(barrier, inc=1, device_id={"tensor": peer}, device_id_type=MESH)
    pl.semaphore_wait(barrier, count - 1)
    total = None
    if scatter:
        rows = part.shape[0] // count
        copies = []
        for s, peer in zip(steps, peers):
            copy = pltpu.make_async_remote_copy(
                src_ref=part.at[pl.ds(pl.multiple_of(peer * rows, rows), rows)],
                dst_ref=landed.at[s - 1],
                send_sem=send_sem.at[0, s - 1],
                recv_sem=recv_sem.at[0, s - 1],
                device_id={"tensor": peer},
                device_id_type=MESH,
            )
            copy.start()
            copies.append(copy)
        total = part[pl.ds(pl.multiple_of(me * rows, rows), rows), :].astype(WIDE)
        for s, copy in zip(steps, copies):
            copy.wait_recv()
            total = total + landed[s - 1].astype(WIDE)
        for copy in copies:
            copy.wait_send()
    sent = middle(total, ins, outs)
    if gather:
        rows = full.shape[0] // count
        own = pl.ds(pl.multiple_of(me * rows, rows), rows)
        full[own, :] = sent.astype(full.dtype)
        copies = []
        for s, peer in zip(steps, peers):
            copy = pltpu.make_async_remote_copy(
                src_ref=full.at[own],
                dst_ref=full.at[own],
                send_sem=send_sem.at[1, s - 1],
                recv_sem=recv_sem.at[1, s - 1],
                device_id={"tensor": peer},
                device_id_type=MESH,
            )
            copy.start()
            copies.append(copy)
        for copy in copies:
            copy.wait()


def rows_call(middle, number, part, ins, outs, gather=True):
    count = lax.axis_size("tensor")
    scatter = part is not None
    width = (part if scatter else ins[0]).shape[1]
    rows = part.shape[0] // count if scatter else ins[0].shape[0]
    shapes = [jax.ShapeDtypeStruct(shape, kind) for shape, kind in outs]
    if gather:
        shapes.append(jax.ShapeDtypeStruct((rows * count, width), HALF))
    whole = pl.BlockSpec(memory_space=pltpu.VMEM)
    operands = ([part] if scatter else []) + list(ins)
    got = pl.pallas_call(
        partial(_rows_kernel, count, scatter, gather, middle, len(ins), len(outs)),
        out_shape=shapes,
        in_specs=[whole] * len(operands),
        out_specs=[whole] * len(shapes),
        scratch_shapes=([pltpu.VMEM((count - 1, rows, width), HALF)] if scatter else [])
        + [pltpu.SemaphoreType.DMA((2, count - 1))] * 2,
        compiler_params=pltpu.CompilerParams(
            collective_id=number, has_side_effects=True, vmem_limit_bytes=VMEM_LIMIT
        ),
        cost_estimate=pl.CostEstimate(
            flops=10 * rows * width, transcendentals=0, bytes_accessed=64 * rows * width
        ),
        name=middle.__name__.strip("_"),
    )(*operands)
    return got


def _differ(a, b, count):
    total, bit = 0, 1
    while bit < count:
        total = total + lax.rem(lax.rem(a // bit, 2) + lax.rem(b // bit, 2), 2) * bit
        bit *= 2
    return total


def _slot(difference, count):
    top = count // 2
    return 2 * lax.rem(difference, top) + difference // top


def _enter(peers):
    barrier = pltpu.get_barrier_semaphore()
    for peer in peers:
        pl.semaphore_signal(barrier, inc=1, device_id=peer, device_id_type=MESH)
    pl.semaphore_wait(barrier, len(peers))


def _send(source, dest, send_sem, recv_sem, peer):
    copy = pltpu.make_async_remote_copy(
        src_ref=source,
        dst_ref=dest,
        send_sem=send_sem,
        recv_sem=recv_sem,
        device_id=peer,
        device_id_type=MESH,
    )
    copy.start()
    return copy


def _to_encoder_kernel(count, with_stats, *refs):
    if with_stats:
        value, out, lse, full, stats, own, own_stats, held, other, other_stats, send_sem, recv_sem = refs
    else:
        value, full, own, other, send_sem, recv_sem = refs
    core, me = lax.axis_index("pipe"), lax.axis_index("tensor")
    group = me // (count // 2)
    chips = [lax.rem(me + s, count) for s in range(1, count)]
    _enter([{"tensor": chip} for chip in chips] + [{"pipe": 1 - core}])
    sets = [(value, own, other, full)]
    if with_stats:
        for h in range(2):
            product = value[h].astype(WIDE) * out[h]
            pick = (
                lax.broadcasted_iota(jnp.int32, (8, product.shape[1]), 1) // HEAD
                == lax.broadcasted_iota(jnp.int32, (8, product.shape[1]), 0) - 2
            ).astype(WIDE)
            held[h] = lax.dot_general(
                pick,
                product,
                (((1,), (1,)), ((), ())),
                precision=lax.Precision.HIGHEST,
                preferred_element_type=WIDE,
            )
            held[h, 0:2, :] = lse[h, 0:2, :]
        sets.append((held, own_stats, other_stats, stats))
    copies = []
    for s, chip in enumerate(chips):
        place = _slot(_differ(chip, me, count), count)
        for h in range(2):
            at = lax.rem(h + core, 2) * count + place
            for i, (source, dest, _, _) in enumerate(sets):
                sems = (send_sem.at[i, s, h], recv_sem.at[i, s, h])
                copies.append(_send(source.at[h], dest.at[at], *sems, {"tensor": chip}))
    for h in range(2):
        for source, dest, _, _ in sets:
            dest[lax.rem(h + core, 2) * count] = source[h]
    for copy in copies:
        copy.wait()
    copies = []
    for g in range(2):
        for i, (_, source, dest, _) in enumerate(sets):
            here, there = pl.ds(g * count, count), pl.ds((1 - g) * count, count)
            sems = (send_sem.at[i, count - 1, g], recv_sem.at[i, count - 1, g])
            copies.append(_send(source.at[here], dest.at[there], *sems, {"pipe": 1 - core}))
    for copy in copies:
        copy.wait()
    for _, mine, theirs, dest in sets:

        @pl.when(core == group)
        def _(mine=mine, dest=dest):
            dest[...] = mine[...]

        @pl.when(core != group)
        def _(theirs=theirs, dest=dest):
            dest[...] = theirs[...]


def to_encoder(value, number, out=None, lse=None):
    count = lax.axis_size("tensor")
    _, rows, wide = value.shape
    shapes = [((2 * count, rows, wide), HALF)]
    if out is not None:
        shapes.append(((2 * count, 8, rows), WIDE))
    scratch = [pltpu.VMEM(*s) for s in shapes]
    if out is not None:
        scratch.append(pltpu.VMEM((2, 8, rows), WIDE))
    scratch += [pltpu.VMEM(*s) for s in shapes]
    whole = pl.BlockSpec(memory_space=pltpu.VMEM)
    operands = (value,) if out is None else (value, out, lse)
    return pl.pallas_call(
        partial(_to_encoder_kernel, count, out is not None),
        out_shape=[jax.ShapeDtypeStruct(*s) for s in shapes],
        in_specs=[whole] * len(operands),
        out_specs=[whole] * len(shapes),
        scratch_shapes=scratch + [pltpu.SemaphoreType.DMA((len(shapes), count, 2))] * 2,
        compiler_params=pltpu.CompilerParams(
            collective_id=number, has_side_effects=True, vmem_limit_bytes=VMEM_LIMIT
        ),
        name="to_encoder",
    )(*operands)


def _over_lanes(weights, wide):
    lanes = lax.broadcasted_iota(jnp.int32, (8, wide), 1) // HEAD
    pick = (lanes == lax.broadcasted_iota(jnp.int32, (8, wide), 0)).astype(HALF)
    high = weights.astype(HALF)
    low = (weights - high.astype(WIDE)).astype(HALF)
    return dot_ta(jnp.concatenate([high, low], axis=0), jnp.concatenate([pick, pick], axis=0))


def _to_decoder_kernel(count, *refs):
    part, lse, heads, out, out_lse = refs[:5]
    other, other_lse, both, both_lse, landed, landed_lse, send_sem, recv_sem = refs[5:]
    core, me = lax.axis_index("pipe"), lax.axis_index("tensor")
    top = count // 2
    chips = [lax.rem(me + s, count) for s in range(1, count)]
    _enter([{"tensor": chip} for chip in chips] + [{"pipe": 1 - core}])
    copies = []
    for g in range(2):
        here, there = pl.ds(g * count, count), pl.ds((1 - g) * count, count)
        for i, (source, dest) in enumerate(((part, other), (lse, other_lse))):
            sems = (send_sem.at[i, count - 1, g], recv_sem.at[i, count - 1, g])
            copies.append(_send(source.at[here], dest.at[there], *sems, {"pipe": 1 - core}))
    for copy in copies:
        copy.wait()
    wide = part.shape[2]
    for i in range(2 * count):
        first, second = lse[i], other_lse[i]
        peak = jnp.maximum(first, second)
        a, b = jnp.exp(first - peak), jnp.exp(second - peak)
        both_lse[i] = peak + jnp.log(a + b)
        share = _over_lanes(b / (a + b), wide)
        mine = part[i].astype(WIDE)
        both[i] = (mine + share * (other[i].astype(WIDE) - mine)).astype(HALF)
    copies = []
    for s, chip in enumerate(chips):
        place = _slot(_differ(chip, me, count), count)
        for h in range(2):
            at = lax.rem(h + core, 2) * count + place
            for i, (source, dest) in enumerate(((both, landed), (both_lse, landed_lse))):
                sems = (send_sem.at[i, s, h], recv_sem.at[i, s, h])
                copies.append(_send(source.at[at], dest.at[s, h], *sems, {"tensor": chip}))
    for copy in copies:
        copy.wait()
    for h in range(2):
        at = lax.rem(h + core, 2) * count
        terms = [(me, both[at], both_lse[at])]
        for s in range(count - 1):
            terms.append((lax.rem(me - s - 1 + count, count), landed[s, h], landed_lse[s, h]))
        logs = [jnp.where(chip // top == core, log, NEGATIVE) for chip, _, log in terms]
        peak = logs[0]
        for log in logs[1:]:
            peak = jnp.maximum(peak, log)
        weights = [jnp.exp(log - peak) for log in logs]
        weights = [
            jnp.where(chip // top == core, w, 0.0) for (chip, _, _), w in zip(terms, weights)
        ]
        total = sum(weights)
        out_lse[h] = peak + jnp.log(total)
        shares = [_over_lanes(w / total, wide) for w in weights]
        value = sum(c * term.astype(WIDE) for c, (_, term, _) in zip(shares, terms)) / sum(shares)
        out[h] = value
        heads[:, h * wide : (h + 1) * wide] = value.astype(HALF)


def to_decoder(part, lse, number):
    count = lax.axis_size("tensor")
    slots, rows, wide = part.shape
    whole = pl.BlockSpec(memory_space=pltpu.VMEM)
    return pl.pallas_call(
        partial(_to_decoder_kernel, count),
        out_shape=[
            jax.ShapeDtypeStruct((rows, 2 * wide), HALF),
            jax.ShapeDtypeStruct((2, rows, wide), WIDE),
            jax.ShapeDtypeStruct((2, 8, rows), WIDE),
        ],
        in_specs=[whole] * 2,
        out_specs=[whole] * 3,
        scratch_shapes=[
            pltpu.VMEM((slots, rows, wide), HALF),
            pltpu.VMEM((slots, 8, rows), WIDE),
            pltpu.VMEM((slots, rows, wide), HALF),
            pltpu.VMEM((slots, 8, rows), WIDE),
            pltpu.VMEM((count - 1, 2, rows, wide), HALF),
            pltpu.VMEM((count - 1, 2, 8, rows), WIDE),
        ]
        + [pltpu.SemaphoreType.DMA((2, count, 2))] * 2,
        compiler_params=pltpu.CompilerParams(
            collective_id=number, has_side_effects=True, vmem_limit_bytes=VMEM_LIMIT
        ),
        name="to_decoder",
    )(part, lse)


def to_pairs(value):
    slots, rows, wide = value.shape
    each = LANES // wide
    if each == 1:
        return value
    value = value.reshape(slots // each, each, rows, wide)
    return value.transpose(0, 2, 1, 3).reshape(slots // each, rows, LANES)


def from_pairs(value, wide):
    blocks, rows, _ = value.shape
    each = LANES // wide
    if each == 1:
        return value
    value = value.reshape(blocks, rows, each, wide)
    return value.transpose(0, 2, 1, 3).reshape(blocks * each, rows, wide)


def stats_to_pairs(stats, wide):
    each = LANES // wide
    if each == 1:
        return stats
    slots, _, rows = stats.shape
    stats = stats.reshape(slots // each, each, 8, rows)
    return jnp.concatenate(
        [stats[:, :, 0], stats[:, :, 2], jnp.zeros((slots // each, 4, rows), WIDE)], axis=1
    )


def stats_from_pairs(stats, wide):
    each = LANES // wide
    if each == 1:
        return stats
    blocks, _, rows = stats.shape
    value = stats[:, :each].reshape(blocks * each, 1, rows)
    return jnp.concatenate([value, jnp.zeros((blocks * each, 7, rows), WIDE)], axis=1)


def slot_bits():
    count = lax.axis_size("tensor")
    bits, bit = [count // 2], 1
    while bit < count // 2:
        bits.append(bit)
        bit *= 2
    return [b for b in bits if b > 0]


def in_column_halves(values):
    wide = values.shape[2] // 2
    return jnp.stack(
        [
            jnp.concatenate(
                [values[:, k, h * wide : (h + 1) * wide] for k in range(values.shape[1])], axis=1
            ).astype(HALF)
            for h in range(2)
        ]
    )


def _gather_kernel(bits, count, planes, *refs):
    own, refs = refs[:3], refs[3:]
    leaving, dec_rows, *refs = refs
    full, enc_cross, enc_ffn, *refs = refs
    dec, refs = refs[:3], refs[3:]
    rests, refs = refs[:2], refs[2:]
    coming, dec_full, send_sem, recv_sem, local_sem = refs
    core, place, me = lax.axis_index("pipe"), lax.axis_index("dp"), lax.axis_index("tensor")
    wide = own[0].shape[2]
    block = own[0].shape[1] // planes
    sibling = {"pipe": 1 - core}
    chips = {bit: {"tensor": _differ(me, bit, count)} for bit in bits}
    line = [{"tensor": _differ(me, s, count)} for s in range(1, count)]
    dp_bits = [1 << i for i in range(planes.bit_length() - 1)]
    others = {bit: {"dp": _differ(place, bit, planes)} for bit in dp_bits}
    _enter([sibling, *line, *others.values()])
    made = [0]

    def push(source, dest, peer):
        i = made[0]
        made[0] += 1
        return _send(source, dest, send_sem.at[i], recv_sem.at[i], peer)

    def rows_of(difference):
        return pl.ds(pl.multiple_of(_differ(place, difference, planes) * block, block), block)

    enc = [full.at[:, :, pl.ds(0, wide)], enc_cross, enc_ffn]
    shown = []
    for a in range(3):
        i = made[0]
        made[0] += 2
        shown.append(i)

        @pl.when(core == 0)
        def _(a=a, i=i):
            for h in range(2):
                _send(own[a].at[h], enc[a].at[1 - h], send_sem.at[i + h], recv_sem.at[i + h], sibling)
                pltpu.make_async_copy(own[a].at[h], enc[a].at[h], local_sem.at[a, h]).start()

        @pl.when(core == 1)
        def _(a=a, i=i):
            for h in range(2):
                _send(own[a].at[h], dec[a].at[h], send_sem.at[i + h], recv_sem.at[i + h], sibling)
                pltpu.make_async_copy(own[a].at[h], dec[a].at[h], local_sem.at[a, h]).start()

    def arrived(a):
        i = shown[a]
        for h in range(2):
            pltpu.make_async_copy(own[a].at[h], enc[a].at[h], local_sem.at[a, h]).wait()
            pltpu.make_async_copy(own[a].at[h], enc[a].at[h], recv_sem.at[i + h]).wait()

    def line_step(a, n, bit):
        here, size = rows_of(0), own[a].shape[2]
        if a == 0:
            source = full.at[0, here, pl.ds(0, n * size)]
            return [push(source, full.at[0, here, pl.ds(n * size, n * size)], chips[bit])]
        rest = rests[a - 1]
        copies = [
            push(enc[a].at[0, here], rest.at[:, pl.ds((n - 1) * size, size)], chips[bit])
        ]
        if n > 1:
            source = rest.at[:, pl.ds(0, (n - 1) * size)]
            copies.append(push(source, rest.at[:, pl.ds(n * size, (n - 1) * size)], chips[bit]))
        return copies

    def wait(copies):
        for copy in copies:
            copy.wait()

    def advance(chain):
        wait(chain["now"])
        chain["now"] = line_step(chain["array"], *chain["todo"].pop(0)) if chain["todo"] else []

    def columns(part):
        return pl.ds(wide + part * half, half)

    def plane_step(j):
        copies = []
        for part, order in enumerate(orders):
            for m in held[part]:
                at = full.at[0, rows_of(m), columns(part)]
                copies.append((part, m ^ order[j], push(at, at, others[order[j]])))
        return copies

    def share(part, m):
        here = rows_of(m)
        source = full.at[0, here, columns(part)]
        return push(source, full.at[1, here, columns(part)], sibling)

    steps = [(1 << i, bit) for i, bit in enumerate(bits)]
    for_attn, for_cross, for_ffn = [{"array": a, "todo": list(steps), "now": []} for a in range(3)]
    arrived(0)
    advance(for_attn)
    arrived(2)
    advance(for_attn)
    advance(for_ffn)
    while for_attn["now"]:
        advance(for_attn)
    token_sem = made[0]
    made[0] += 1

    @pl.when(core == 1)
    def _():
        _send(leaving, coming, send_sem.at[token_sem], recv_sem.at[token_sem], chips[bits[0]])

    at = pl.ds(pl.multiple_of(me * dec_rows.shape[0], dec_rows.shape[0]), dec_rows.shape[0])
    dec_full[at, :] = dec_rows[...]
    dec_sent = [push(dec_full.at[at], dec_full.at[at], peer) for peer in line]
    half = (count - 1) * wide // 2
    orders, held = (dp_bits, dp_bits[::-1]), ([0], [0])
    moving = plane_step(0)
    shared = [share(part, 0) for part in range(2)]
    advance(for_ffn)
    arrived(1)
    for j in range(len(dp_bits)):
        for _, _, copy in moving:
            copy.wait()
        for part, order in enumerate(orders):
            held[part].extend([m ^ order[j] for m in held[part]])
        following = plane_step(j + 1) if j + 1 < len(dp_bits) else []
        shared += [share(part, m) for part, m, _ in moving]
        moving = following
        advance(for_cross)
    while for_ffn["now"]:
        advance(for_ffn)
    while for_cross["now"]:
        advance(for_cross)

    @pl.when(core == 1)
    def _():
        pltpu.make_async_copy(leaving, leaving, send_sem.at[token_sem]).wait()
        pltpu.make_async_copy(leaving, coming, recv_sem.at[token_sem]).wait()

    wait(dec_sent)
    wait(shared)
    for a in range(3):
        for h in range(2):
            pltpu.make_async_copy(own[a].at[h], own[a].at[h], send_sem.at[shown[a] + h]).wait()


def gather_weights(attn, cross, ffn, leaving, dec_rows):
    own = (attn, cross, ffn)
    count, planes = lax.axis_size("tensor"), lax.axis_size("dp")
    depth = attn.shape[1]
    shapes = [(2, depth, count * attn.shape[2]), cross.shape, ffn.shape]
    shapes += [v.shape for v in own]
    shapes += [(depth // planes, (count - 1) * v.shape[2]) for v in (cross, ffn)]
    shapes += [leaving.shape, (count * dec_rows.shape[0], dec_rows.shape[1])]
    hbm, vmem = pl.BlockSpec(memory_space=pl.ANY), pl.BlockSpec(memory_space=pltpu.VMEM)
    return pl.pallas_call(
        partial(_gather_kernel, slot_bits(), count, planes),
        out_shape=[jax.ShapeDtypeStruct(shape, HALF) for shape in shapes],
        in_specs=[vmem] * 3 + [hbm, vmem],
        out_specs=[hbm] * (len(shapes) - 1) + [vmem],
        scratch_shapes=[pltpu.SemaphoreType.DMA((64,))] * 2 + [pltpu.SemaphoreType.DMA((3, 2))],
        compiler_params=pltpu.CompilerParams(
            collective_id=9, has_side_effects=True, vmem_limit_bytes=VMEM_LIMIT
        ),
        name="gather_weights",
    )(*own, leaving, dec_rows)


def gather_planes(rest):
    return lax.all_gather(rest, "dp", axis=0, tiled=True)


def fold_cores(mine, other):
    return (mine.astype(WIDE) + swap(other, "pipe", 1).astype(WIDE)).astype(HALF)


def fold_planes(term):
    return lax.psum_scatter(term, "dp", scatter_dimension=0, tiled=True)


def fold_chips(rows, kinds):
    for bit in reversed(slot_bits()):
        keep, send = jnp.split(rows, 2, axis=1)
        rows = (keep.astype(WIDE) + swap(send, "tensor", bit).astype(WIDE)).astype(HALF)
    return rows.reshape(rows.shape[0], kinds, -1)


def scatter_local(terms):
    core = lax.axis_index("pipe")
    wide = terms[0].shape[1] // 2
    pick = partial(lax.dynamic_slice_in_dim, slice_size=wide, axis=1)
    mine = jnp.concatenate([pick(v.astype(HALF), core * wide) for v in terms], axis=1)
    other = jnp.concatenate([pick(v.astype(HALF), (1 - core) * wide) for v in terms], axis=1)
    term = fold_cores(mine, other)
    rows = fold_planes(term)
    return rows.reshape(rows.shape[0], len(terms), wide), term


def reduce_norms(enc_terms, dec_terms):
    core = lax.axis_index("pipe")
    value = jnp.where(core == 0, enc_terms, dec_terms) + swap(
        jnp.where(core == 0, dec_terms, enc_terms), "pipe", 1
    )
    for axis in ("dp", "tensor"):
        bit = lax.axis_size(axis) // 2
        while bit >= 1:
            parts = value.reshape(value.shape[0], 2, -1)
            mine = lax.rem(lax.axis_index(axis) // bit, 2)
            keep = lax.dynamic_index_in_dim(parts, mine, 1, False)
            send = lax.dynamic_index_in_dim(parts, 1 - mine, 1, False)
            value = keep + swap(send, axis, bit)
            bit //= 2
    return value


def _blocks_of(weights, kinds):
    wide = weights.shape[2] // (lax.axis_size("tensor") * kinds)
    each = LANES // wide
    blocks = lax.axis_size("tensor") // each
    spec = pl.BlockSpec(
        (None, weights.shape[1], each * kinds * wide), lambda i: (i // blocks, 0, lax.rem(i, blocks))
    )
    return wide, each, blocks, spec


def _piece(weights, kinds, wide, each, k):
    parts = [weights[:, (j * kinds + k) * wide : (j * kinds + k + 1) * wide] for j in range(each)]
    return parts[0] if each == 1 else jnp.concatenate(parts, axis=1)


def _store_grads(refs, i, blocks, pieces, wide, each):
    columns = [p[:, j * wide : (j + 1) * wide] for j in range(each) for p in pieces]
    for ref, when in zip(refs, (i < blocks, i >= blocks)):

        @pl.when(when)
        def _(ref=ref):
            for n, column in enumerate(columns):
                ref[:, n * wide : (n + 1) * wide] = column.astype(ref.dtype)


def _grad_specs(depth, columns, blocks):
    return [
        pl.BlockSpec((depth, columns), lambda i: (0, jnp.minimum(i, blocks - 1))),
        pl.BlockSpec((depth, columns), lambda i: (0, jnp.maximum(i - blocks, 0))),
    ]


def _spread_kernel(kinds, use, wide, each, blocks, with_grad, pair, x, weights, *refs):
    left = x[...]
    values = [dot(left, _piece(weights, kinds, wide, each, k)) for k in use]
    if with_grad:
        y, *refs = refs
        i = pl.program_id(0)
        _store_grads(refs[-2:], i, blocks, [dot_ta(left, y[...].astype(HALF))], wide, each)
    if pair:
        refs[-1][0] = values[-2].astype(HALF)
        refs[-1][1] = values[-1].astype(HALF)
        values = values[:-2]
    for ref, value in zip(refs, values):
        ref[...] = value.astype(HALF)


def spread(x, weights, kinds, use, y=None, pair=False):
    rows, width = x.shape
    wide, each, blocks, spec = _blocks_of(weights, kinds)
    column = pl.BlockSpec((rows, LANES), lambda i: (0, i))
    single = len(use) - (2 if pair else 0)
    shapes, specs = [((rows, width), HALF)] * single, [column] * single
    if pair:
        shapes.append(((2, rows, width), HALF))
        specs.append(pl.BlockSpec((2, rows, LANES), lambda i: (0, 0, i)))
    if y is not None:
        shapes += [((width, width // 2), HALF)] * 2
        specs += _grad_specs(width, LANES, blocks)
    return pl.pallas_call(
        partial(_spread_kernel, kinds, use, wide, each, blocks, y is not None, pair),
        out_shape=[jax.ShapeDtypeStruct(*s) for s in shapes],
        grid=(2 * blocks,),
        in_specs=[pl.BlockSpec((rows, width), lambda i: (0, 0)), spec] + [column] * (y is not None),
        out_specs=specs,
        compiler_params=pltpu.CompilerParams(vmem_limit_bytes=VMEM_LIMIT),
        cost_estimate=pl.CostEstimate(
            flops=2 * rows * width * width * (len(use) + (y is not None)),
            transcendentals=0,
            bytes_accessed=2 * width * width * kinds,
        ),
        name="spread",
    )(x, weights, *([] if y is None else [y]))


def _collect_kernel(kinds, use, wide, each, blocks, n_y, with_grad, ending, n_extra, *refs):
    refs = list(refs)
    ys, refs = refs[:n_y], refs[n_y:]
    weights, refs = refs[0], refs[1:]
    x = refs.pop(0) if with_grad else None
    extra, refs = refs[:n_extra], refs[n_extra:]
    acc = refs.pop()
    grads = [refs.pop(), refs.pop()][::-1] if with_grad else []
    i = pl.program_id(0)

    @pl.when(i == 0)
    def _():
        acc[...] = jnp.zeros(acc.shape, WIDE)

    values = []
    for y in ys:
        values += [y[...]] if len(y.shape) == 2 else [y[0], y[1]]
    values = [v.astype(HALF) for v in values]
    for value, k in zip(values, use):
        acc[...] += dot_bt(value, _piece(weights, kinds, wide, each, k))
    if with_grad:
        left = x[...]
        _store_grads(grads, i, blocks, [dot_ta(left, v) for v in values], wide, each)

    @pl.when(i == 2 * blocks - 1)
    def _():
        ending(acc[...], extra, refs)


def collect(ys, weights, kinds, use, ending, extra, outs, x=None):
    rows, width = ys[0].shape[-2:]
    wide, each, blocks, spec = _blocks_of(weights, kinds)
    y_specs = [
        pl.BlockSpec((rows, LANES), lambda i: (0, i))
        if y.ndim == 2
        else pl.BlockSpec((2, rows, LANES), lambda i: (0, 0, i))
        for y in ys
    ]
    fixed = [pl.BlockSpec(v.shape, lambda i: (0, 0)) for v in ([] if x is None else [x]) + extra]
    shapes = list(outs)
    specs = [pl.BlockSpec(shape, lambda i: (0, 0)) for shape, _ in outs]
    if x is not None:
        shapes += [((width, len(use) * width // 2), HALF)] * 2
        specs += _grad_specs(width, len(use) * LANES, blocks)
    return pl.pallas_call(
        partial(
            _collect_kernel, kinds, use, wide, each, blocks, len(ys), x is not None, ending, len(extra)
        ),
        out_shape=[jax.ShapeDtypeStruct(*s) for s in shapes],
        grid=(2 * blocks,),
        in_specs=y_specs + [spec] + fixed,
        out_specs=specs,
        scratch_shapes=[pltpu.VMEM((rows, width), WIDE)],
        compiler_params=pltpu.CompilerParams(vmem_limit_bytes=VMEM_LIMIT),
        cost_estimate=pl.CostEstimate(
            flops=2 * rows * width * width * len(use) * (1 + (x is not None)),
            transcendentals=0,
            bytes_accessed=2 * width * width * kinds,
        ),
        name="collect",
    )(*ys, weights, *([] if x is None else [x]), *extra)


def _end_norm(total, ins, outs):
    resid, gain, bias = ins
    value, normed, inv_scale = _norm_rows(total + resid[...], gain[...], bias[...])
    outs[0][...] = value
    outs[1][...] = value.astype(HALF)
    outs[2][...] = normed
    outs[3][...] = jnp.broadcast_to(inv_scale, outs[3].shape)


def _end_norm_back(total, ins, outs):
    *resid, normed, inv_scale, gain = ins
    total = total + resid[0][...] if resid else total
    grad, grad_gain, grad_bias = _norm_rows_back(total, normed[...], inv_scale[:, 0:1], gain[...])
    outs[0][...] = grad
    outs[1][...] = grad.astype(HALF)
    outs[2][0:1, :] = grad_gain
    outs[2][1:2, :] = grad_bias


def _ffn_parts(count, own, mine, other):
    depth, wide = own.shape[1], own.shape[2] // 2
    specs = []
    for k in range(2):
        specs.append(pl.BlockSpec((None, depth, wide), lambda i, k=k: (i // count, 0, k)))
        for first in (0, count):
            specs.append(
                pl.BlockSpec(
                    (depth, wide),
                    lambda i, k=k, first=first: (0, 2 * jnp.clip(i - first - 1, 0, count - 2) + k),
                )
            )
    return wide, specs


def _ffn_cases(count, i, ins, outs):
    local = lax.rem(i, count) == 0
    return [
        (local, ins[0], outs[0]),
        (jnp.logical_and(~local, i < count), ins[1], outs[1]),
        (jnp.logical_and(~local, i > count), ins[2], outs[2]),
    ]


def _ffn_kernel(count, x, resid, gain, bias, *refs):
    ins, outs, refs = refs[:3], refs[3:6], refs[6:]
    value, value_low, normed, inv_scale, active, slope, acc = refs
    i = pl.program_id(0)

    @pl.when(i == 0)
    def _():
        acc[...] = jnp.zeros(acc.shape, WIDE)

    for condition, first, second in _ffn_cases(count, i, ins, outs):

        @pl.when(condition)
        def _(first=first, second=second):
            hidden = dot(x[...], first[...])
            below = 0.5 * (1.0 + lax.erf(hidden * (2.0**-0.5)))
            density = jnp.exp(-0.5 * hidden * hidden) * 0.3989422804014327
            act = (hidden * below).astype(HALF)
            active[...] = act
            slope[...] = (below + hidden * density).astype(HALF)
            acc[...] += dot_bt(act, second[...])

    @pl.when(i == 2 * count - 1)
    def _():
        _end_norm(acc[...], (resid, gain, bias), (value, value_low, normed, inv_scale))


def feed_forward(x, resid, gain, bias, own, mine, other):
    count = lax.axis_size("tensor")
    rows, width = x.shape
    wide, specs = _ffn_parts(count, own, mine, other)
    units = 2 * count * wide
    fixed = [pl.BlockSpec(v.shape, lambda i: (0, 0)) for v in (x, resid, gain, bias)]
    shapes = [((rows, width), WIDE), ((rows, width), HALF), ((rows, width), WIDE), ((rows, LANES), WIDE)]
    column = pl.BlockSpec((rows, wide), lambda i: (0, i))
    return pl.pallas_call(
        partial(_ffn_kernel, count),
        out_shape=[jax.ShapeDtypeStruct(*s) for s in shapes]
        + [jax.ShapeDtypeStruct((rows, units), HALF)] * 2,
        grid=(2 * count,),
        in_specs=fixed + specs,
        out_specs=[pl.BlockSpec(s, lambda i: (0, 0)) for s, _ in shapes] + [column] * 2,
        scratch_shapes=[pltpu.VMEM((rows, width), WIDE)],
        compiler_params=pltpu.CompilerParams(vmem_limit_bytes=VMEM_LIMIT),
        cost_estimate=pl.CostEstimate(
            flops=4 * rows * width * units, transcendentals=2 * rows * units, bytes_accessed=4 * width * units
        ),
        name="feed_forward",
    )(x, resid, gain, bias, own, mine, other, own, mine, other)


def _ffn_back_kernel(count, x, grad, resid, normed, inv_scale, gain, active, slope, *refs):
    ins, outs, refs = refs[:3], refs[3:6], refs[6:]
    result, result_low, terms, *grads, acc = refs
    i = pl.program_id(0)

    @pl.when(i == 0)
    def _():
        acc[...] = jnp.zeros(acc.shape, WIDE)

    for condition, first, second in _ffn_cases(count, i, ins, outs):

        @pl.when(condition)
        def _(first=first, second=second):
            hidden = (dot(grad[...], second[...]) * slope[...].astype(WIDE)).astype(HALF)
            acc[...] += dot_bt(hidden, first[...])
            f1 = dot_ta(x[...], hidden).astype(HALF)
            f2 = dot_ta(grad[...], active[...]).astype(HALF)
            for half, when in enumerate((i < count, i >= count)):

                @pl.when(when)
                def _(half=half):
                    grads[half][...] = f1
                    grads[2 + half][...] = f2

    @pl.when(i == 2 * count - 1)
    def _():
        _end_norm_back(acc[...], (resid, normed, inv_scale, gain), (result, result_low, terms))


def feed_forward_back(x, grad, resid, normed, inv_scale, gain, active, slope, own, mine, other):
    count = lax.axis_size("tensor")
    rows, width = x.shape
    wide, specs = _ffn_parts(count, own, mine, other)
    column = pl.BlockSpec((rows, wide), lambda i: (0, i))
    fixed = [pl.BlockSpec(v.shape, lambda i: (0, 0)) for v in (x, grad, resid, normed, inv_scale, gain)]
    shapes = [((rows, width), WIDE), ((rows, width), HALF), ((8, width), WIDE)]
    grad_specs = [
        pl.BlockSpec((width, wide), lambda i: (0, jnp.minimum(i, count - 1))),
        pl.BlockSpec((width, wide), lambda i: (0, jnp.maximum(i - count, 0))),
    ]
    return pl.pallas_call(
        partial(_ffn_back_kernel, count),
        out_shape=[jax.ShapeDtypeStruct(*s) for s in shapes]
        + [jax.ShapeDtypeStruct((width, count * wide), HALF)] * 4,
        grid=(2 * count,),
        in_specs=fixed + [column] * 2 + specs,
        out_specs=[pl.BlockSpec(s, lambda i: (0, 0)) for s, _ in shapes] + grad_specs * 2,
        scratch_shapes=[pltpu.VMEM((rows, width), WIDE)],
        compiler_params=pltpu.CompilerParams(vmem_limit_bytes=VMEM_LIMIT),
        cost_estimate=pl.CostEstimate(
            flops=16 * rows * width * count * wide, transcendentals=0, bytes_accessed=16 * width * count * wide
        ),
        name="feed_forward_back",
    )(x, grad, resid, normed, inv_scale, gain, active, slope, own, mine, other, own, mine, other)


def per_device(
    enc_input,
    dec_input,
    dec_cotangent,
    enc_lengths,
    dec_lengths,
    attn_weights,
    cross_weights,
    ffn_weights,
    norm_gains,
    norm_biases,
):
    core, place = lax.axis_index("pipe"), lax.axis_index("tensor")
    count = lax.axis_size("tensor")
    top_bit = count // 2
    group = place // top_bit
    block = jnp.where(core == 0, place, place ^ top_bit)
    span, width = enc_input.shape[1:]
    dec_span = dec_input.shape[1]
    local_width = attn_weights.shape[3]
    is_first = core == 0
    chips = range(count)
    half = width // 2
    half_local = local_width // 2

    def owner(t):
        return t // top_bit

    pick = partial(lax.dynamic_index_in_dim, index=core, axis=0, keepdims=False)
    start_low = pick(dec_input)
    (
        w_attn,
        own_cross,
        own_ffn,
        dec_attn_halves,
        dec_cross_halves,
        dec_ffn_halves,
        cross_rest,
        ffn_rest,
        got,
        start_full,
    ) = gather_weights(
        *[in_column_halves(v[0]) for v in (attn_weights, cross_weights, ffn_weights)],
        lax.dynamic_index_in_dim(enc_input, 1 - group, 0, False),
        start_low,
    )
    kept = lax.dynamic_index_in_dim(enc_input, group, 0, False)
    tokens = jnp.where(is_first, kept, got).astype(WIDE)
    mine_ffn = gather_planes(ffn_rest)

    def natural(halves, kinds):
        wide = halves.shape[2] // kinds
        return [
            jnp.concatenate([halves[h][:, k * wide : (k + 1) * wide] for h in range(2)], axis=1)
            for k in range(kinds)
        ]

    dec_attn, dec_cross, dec_ffn = [
        natural(v, k) for v, k in ((dec_attn_halves, 4), (dec_cross_halves, 2), (dec_ffn_halves, 2))
    ]
    norms = jnp.concatenate([norm_gains[0], norm_biases[0]], axis=0)
    norms_other = swap(norms, "pipe", 1)
    enc_norms = jnp.where(is_first, norms, norms_other)
    dec_norms = jnp.where(is_first, norms_other, norms)
    eg, eb, dg, db = enc_norms[:3], enc_norms[3:], dec_norms[:3], dec_norms[3:]

    enc_row = lax.dynamic_index_in_dim(enc_lengths, group, 0, False)
    dec_row_of_group = lax.dynamic_index_in_dim(dec_lengths, group, 0, False)
    dec_row = lax.dynamic_index_in_dim(dec_lengths, core, 0, False)
    spots = jnp.arange(span, dtype=jnp.int32)
    sources = [(s // top_bit, s % top_bit) for s in range(2 * top_bit)]
    own_seg = table_of(block * span + spots, enc_row)
    key_seg = jnp.stack(
        [table_of((block ^ (a * top_bit) ^ c) * span + spots, enc_row) for a, c in sources]
    )
    blocks = width // LANES
    masks = [a * (blocks // 2) + c * (blocks // 2 // top_bit) for a, c in sources]
    dec_spots = jnp.arange(dec_span * count, dtype=jnp.int32)
    dec_seg = table_of(dec_spots, dec_row)
    enc_segs = tables(own_seg, key_seg)
    dec_segs = tables(dec_seg, dec_seg[None])
    cross_segs = tables(table_of(dec_spots, dec_row_of_group), own_seg[None])

    def gain_of(i):
        return enc_norms[i : i + 1]

    def bias_of(i):
        return enc_norms[3 + i : 4 + i]

    embed, start_normed, start_scale = norm_forward(tokens, eg[0], eb[0])
    start_scale = jnp.broadcast_to(start_scale, (span, LANES))
    embed_low = embed.astype(HALF)
    query, key_value = spread(embed_low, w_attn, 4, (0, 1, 2), pair=True)

    def exchange(value):
        held = [value]
        bit = 1
        while bit < top_bit:
            held = held + [swap(v, "tensor", bit) for v in held]
            bit *= 2
        return held + [swap(v, "pipe", 1) for v in held]

    key_values = exchange(key_value)
    mine_cross = gather_planes(after(cross_rest, query))

    start_full = after(start_full, key_value)
    start = start_low.astype(WIDE)
    rows_full = dec_span * count
    wide_rows = ((dec_span, width), WIDE)
    kept_rows = [wide_rows, wide_rows, ((dec_span, LANES), WIDE)]
    norm_terms = ((8, width), WIDE)
    dec_in_w = [dec_attn[k] for k in range(3)]
    dec_query = dot(start_full, dec_in_w[0]).astype(HALF)
    dec_kv = jnp.stack([dot(start_full, w).astype(HALF) for w in dec_in_w[1:]])
    dec_heads_wide, dec_lse = attend(dec_query, [dec_kv], dec_segs, [0], True)
    dec_heads = dec_heads_wide.astype(HALF)
    self_norm, self_normed, self_scale, self_full = rows_call(
        _forward_rows,
        2,
        dot_bt(dec_heads, dec_attn[3]).astype(HALF),
        [start, dg[0:1], db[0:1]],
        kept_rows,
    )
    cross_query = dot(self_full, dec_cross[0]).astype(HALF)

    def in_halves(value):
        return jnp.stack([value[:, :half_local], value[:, half_local:]])

    [cross_q_enc] = to_encoder(in_halves(cross_query), 6)
    cross_q_enc = to_pairs(cross_q_enc)
    mine_ffn = after(mine_ffn, cross_q_enc)
    other_ffn = swap(mine_ffn, "pipe", 1)

    heads_wide, lse = attend(query, key_values, enc_segs, masks)
    heads = heads_wide.astype(HALF)
    mine_cross = after(mine_cross, heads)
    w_cross = jnp.stack(
        [
            jnp.concatenate([own_cross[0], mine_cross], axis=1),
            jnp.concatenate([own_cross[1], swap(mine_cross, "pipe", 1)], axis=1),
        ]
    )
    kept_tokens = [((span, width), WIDE), ((span, width), HALF), ((span, width), WIDE), ((span, LANES), WIDE)]
    attn_norm, attn_norm_low, attn_normed, attn_scale = collect(
        [heads], w_attn, 4, (3,), _end_norm, [embed, gain_of(1), bias_of(1)], kept_tokens
    )
    _, memory_low, mem_normed, mem_scale, active, slope = feed_forward(
        attn_norm_low, attn_norm, gain_of(2), bias_of(2), own_ffn, mine_ffn, other_ffn
    )
    [cross_kv] = spread(memory_low, w_cross, 2, (0, 1), pair=True)

    tables_of_keys = enc_lengths.shape[1]
    at_table = (own_seg[:, None] == jnp.arange(tables_of_keys)[None]).astype(HALF)
    sums = dot_ta(at_table, cross_kv[0])
    bit = 1
    while bit < top_bit:
        sums = sums + swap_columns(sums, "tensor", bit, masks[bit])
        bit *= 2
    sums = sums + swap_columns(sums, "pipe", 1, masks[top_bit])
    means = sums / enc_row.astype(WIDE)[:, None]
    centers = sum(
        jnp.where((own_seg == j)[:, None], means[j : j + 1], 0.0) for j in range(tables_of_keys)
    )
    centered = (cross_kv[0].astype(WIDE) - centers).astype(HALF)

    part_out, part_lse = attend(cross_q_enc, [cross_kv], cross_segs, [0], False, HALF)
    cross_heads, cross_out_wide, cross_lse = to_decoder(
        from_pairs(part_out, half_local), stats_from_pairs(part_lse, half_local), 7
    )
    cross_norm, cross_normed, cross_scale, cross_full = rows_call(
        _forward_rows,
        2,
        dot_bt(cross_heads, dec_cross[1]).astype(HALF),
        [self_norm, dg[1:2], db[1:2]],
        kept_rows,
    )
    dec_hidden = dot(cross_full, dec_ffn[0])
    dec_active = gelu(dec_hidden).astype(HALF)
    result, resid, dec_terms2, grad_full = rows_call(
        _turn_rows,
        3,
        dot_bt(dec_active, dec_ffn[1]).astype(HALF),
        [cross_norm, dg[2:3], db[2:3], pick(dec_cotangent)],
        [((dec_span, width), HALF), wide_rows, norm_terms],
    )
    grad_hidden = (dot(grad_full, dec_ffn[1]) * gelu_slope(dec_hidden)).astype(HALF)
    resid, dec_terms1, cross_grad_full = rows_call(
        _backward_rows,
        4,
        dot_bt(grad_hidden, dec_ffn[0]).astype(HALF),
        [resid, cross_normed, cross_scale, dg[1:2]],
        [wide_rows, norm_terms],
    )
    cross_heads_grad = dot(cross_grad_full, dec_cross[1]).astype(HALF)
    heads_grad_enc, stats_enc = to_encoder(
        in_halves(cross_heads_grad), 8, cross_out_wide, cross_lse
    )
    cross_q_term, [cross_kv_grad] = attend_back(
        cross_q_enc,
        [cross_kv],
        to_pairs(heads_grad_enc),
        stats_to_pairs(stats_enc, half_local),
        centered,
        cross_segs,
        [0],
        False,
        False,
    )
    dec_f2_grad = dot_ta(grad_full, dec_active)
    dec_f1_grad = dot_ta(cross_full, grad_hidden)
    dec_ffn_half, _ = scatter_local([dec_f1_grad, dec_f2_grad])

    back_tokens = [((span, width), WIDE), ((span, width), HALF), ((8, width), WIDE)]
    resid_enc, resid_low, enc_terms2, *cross_grads = collect(
        [cross_kv_grad],
        w_cross,
        2,
        (0, 1),
        _end_norm_back,
        [mem_normed, mem_scale, gain_of(2)],
        back_tokens,
        memory_low,
    )
    enc_ckv = fold_planes(fold_cores(*cross_grads))
    resid_enc, resid_low, enc_terms1, *ffn_grads = feed_forward_back(
        attn_norm_low,
        resid_low,
        resid_enc,
        attn_normed,
        attn_scale,
        gain_of(1),
        active,
        slope,
        own_ffn,
        mine_ffn,
        other_ffn,
    )
    enc_f2 = fold_planes(after(fold_cores(*ffn_grads[2:]), dec_ffn_half, enc_ckv))
    enc_f1 = fold_planes(fold_cores(*ffn_grads[:2]))
    heads_grad, *out_grads = spread(resid_low, w_attn, 4, (3,), heads)
    q_grad, kv_grads = attend_back(
        query, key_values, heads_grad, lse, heads_wide, enc_segs, masks
    )

    def join(a, b):
        return (a.astype(WIDE) + b.astype(WIDE)).astype(HALF)

    held = [join(a, swap(b, "pipe", 1)) for a, b in zip(kv_grads[:top_bit], kv_grads[top_bit:])]
    bit = top_bit // 2
    while bit >= 1:
        held = [join(a, swap(b, "tensor", bit)) for a, b in zip(held[:bit], held[bit:])]
        bit //= 2
    kv_grad = held[0]

    def to_owner(value):
        theirs = joint(value, [((1 - owner(t), t), (owner(t), t)) for t in chips])
        theirs = theirs.reshape(2, count, *theirs.shape[1:])
        chip = value.reshape(theirs.shape).astype(WIDE) + theirs[::-1].astype(WIDE)
        chip = jnp.where(is_first, chip, chip[::-1]).astype(HALF)
        terms = []
        for s in range(top_bit):
            near, far = 2 * s, 2 * s + 1
            near_pairs = [((owner(t), t), (owner(t), t ^ s)) for t in chips]
            far_pairs = [((owner(t), t), (owner(t), t ^ s ^ top_bit)) for t in chips]
            near_got = chip[:, near] if s == 0 else joint(chip[:, near], near_pairs)
            far_got = joint(chip[:, far], far_pairs)
            terms.append(jnp.where(core == group, near_got, far_got).astype(WIDE))
        return sum(terms)

    cross_q_grad = after(to_owner(from_pairs(cross_q_term, half_local)).astype(HALF), q_grad)
    cross_q_grad = jnp.concatenate([cross_q_grad[0], cross_q_grad[1]], axis=1)
    resid, dec_terms0, self_grad_full = rows_call(
        _backward_rows,
        4,
        dot_bt(cross_q_grad, dec_cross[0]).astype(HALF),
        [resid, self_normed, self_scale, dg[0:1]],
        [wide_rows, norm_terms],
    )
    dec_heads_grad = dot(self_grad_full, dec_attn[3]).astype(HALF)
    dec_q_grad, [dec_kv_grad] = attend_back(
        dec_query, [dec_kv], dec_heads_grad, dec_lse, dec_heads_wide, dec_segs, [0], True
    )
    dec_proj_grad = [dec_q_grad, dec_kv_grad[0], dec_kv_grad[1]]
    [dec_grad] = rows_call(
        _last_rows,
        5,
        sum(dot_bt(g, w) for g, w in zip(dec_proj_grad, dec_in_w)).astype(HALF),
        [resid],
        [wide_rows],
        False,
    )
    dec_left = [start_full] * 3 + [self_grad_full, self_full, cross_grad_full]
    dec_right = dec_proj_grad + [dec_heads, cross_q_grad, cross_heads]
    dec_small = [dot_ta(a, b) for a, b in zip(dec_left, dec_right)]
    dec_small_half, dec_small_term = scatter_local(dec_small)
    kv_grad = after(kv_grad, dec_small_term)

    enc_grad, _, enc_terms0, *in_grads = collect(
        [q_grad, kv_grad],
        w_attn,
        4,
        (0, 1, 2),
        _end_norm_back,
        [resid_enc, start_normed, start_scale, gain_of(0)],
        back_tokens,
        embed_low,
    )
    enc_in, enc_out = fold_cores(*in_grads), fold_cores(*out_grads)
    enc_attn_rows = fold_planes(jnp.concatenate([enc_in, enc_out], axis=1))
    enc_ffn_half = jnp.concatenate([fold_chips(enc_f1, 1), fold_chips(enc_f2, 1)], axis=1)
    enc_cross_half = fold_chips(enc_ckv, 2)
    enc_terms = [enc_terms0, enc_terms1, enc_terms2]

    def section(enc_half, dec_half):
        keep = jnp.where(is_first, enc_half, dec_half)
        got = swap(jnp.where(is_first, dec_half, enc_half), "pipe", 1)
        pair = jnp.where(is_first, jnp.stack([keep, got], axis=2), jnp.stack([got, keep], axis=2))
        return pair.reshape(*pair.shape[:2], -1)[None].astype(WIDE)

    ffn_out_grad = section(enc_ffn_half, dec_ffn_half)
    enc_attn_rows = after(enc_attn_rows, ffn_out_grad, enc_cross_half, dec_grad)
    in_columns = enc_in.shape[1]
    enc_attn_half = jnp.concatenate(
        [fold_chips(enc_attn_rows[:, :in_columns], 3), fold_chips(enc_attn_rows[:, in_columns:], 1)], axis=1
    )
    attn_out = section(enc_attn_half, dec_small_half[:, :4])
    cross_out = section(enc_cross_half, dec_small_half[:, 4:])
    dec_terms = [dec_terms0, dec_terms1, dec_terms2]
    norm_sums = reduce_norms(
        jnp.stack([v[i] for i in range(2) for v in enc_terms]),
        jnp.stack([v[i] for i in range(2) for v in dec_terms]),
    )

    dec_pair = jnp.stack([result, dec_grad.astype(HALF)])
    dec_halves = dec_pair.reshape(2, dec_span, 2, half)
    dec_got = swap(lax.dynamic_index_in_dim(dec_halves, 1 - core, 2, False), "pipe", 1)
    own_result = lax.dynamic_slice_in_dim(result, core * half, half, 1)
    own_grad = lax.dynamic_slice_in_dim(dec_grad, core * half, half, 1)
    dec_output = jnp.where(
        is_first, jnp.stack([own_result, dec_got[0]]), jnp.stack([dec_got[0], own_result])
    )
    got_grad = dec_got[1].astype(WIDE)
    dec_input_grad = jnp.where(
        is_first, jnp.stack([own_grad, got_grad]), jnp.stack([got_grad, own_grad])
    )

    enc_low = enc_grad.astype(HALF)
    far_first = joint(enc_low[:, :half], [((1, t), (0, t ^ top_bit)) for t in chips])
    far_second = joint(enc_low[:, half:], [((1, t), (1, t ^ top_bit)) for t in chips])
    near_second = joint(enc_low[:, half:], [((0, t), (1, t)) for t in chips])
    here = jnp.where(is_first, enc_grad[:, :half], near_second.astype(WIDE))
    there = jnp.where(is_first, far_first, far_second).astype(WIDE)
    enc_input_grad = jnp.where(group == 0, jnp.stack([here, there]), jnp.stack([there, here]))
    return (
        dec_output,
        enc_input_grad,
        dec_input_grad,
        attn_out,
        cross_out,
        ffn_out_grad,
        norm_sums[None, :3],
        norm_sums[None, 3:],
    )


def solution(mesh):
    rows = P("dp", "tensor", None)
    weights = P("pipe", None, None, "tensor")
    half_rows = P("dp", "tensor", "pipe")
    weight_grads = P("pipe", "dp", None, "tensor")
    norm_grads = P("pipe", None, ("dp", "tensor"))
    return jax.shard_map(
        per_device,
        mesh=mesh,
        in_specs=(rows, rows, rows, P("dp", None), P("dp", None))
        + (weights,) * 3
        + (P("pipe", None, None),) * 2,
        out_specs=(half_rows,) * 3 + (weight_grads,) * 3 + (norm_grads,) * 2,
        check_vma=False,
    )
```

time: 3700 us -> 1000 us (0.27)
  waiting for transfers between devices: 1820 us -> 131 us
  matrix products: 1120 us -> 29.2 us
  Pallas kernels: 0 us -> 630 us
  local copies, waits for them, and re-layouts: 426 us -> 66.1 us
  other arithmetic: 235 us -> 88.9 us
  loops' own time: 62 us -> 0 us
    dot_general x117 -> x25, matrix products: 1120 us -> 29.2 us  [the longest x8 11.1 us: dot(): return jnp.dot(left, right, preferred_element_type=WIDE)]
    reduce_scatter x14 -> x6, waiting for transfers between devices: 836 us -> 0.05 us  [fold_planes(): return lax.psum_scatter(term, 'dp', scatter_dimension=0, tiled=True)]
    all_gather x11 -> x2, waiting for transfers between devices: 828 us -> 0.02 us  [gather_planes(): return lax.all_gather(rest, 'dp', axis=0, tiled=True)]
    pallas_call x0 -> x24, Pallas kernels: none -> 630 us  [the longest x6 219 us: rows_call(): pl.pallas_call(partial(_rows_kernel, count, scatter, gather, middle, len(...]
    dynamic_slice x200 -> x5, local copies, waits for them, and re-layouts: 199 us -> 0.41 us  [the longest x2 0.35 us: scatter_local(): pick(v.astype(HALF), core * wide)]
    unnamed x29 -> x8, waiting for transfers between devices: 149 us -> 0.13 us
    ppermute x4 -> x44, waiting for transfers between devices: 9.89 us -> 131 us  [the longest x37 131 us: swap(): lax.ppermute(value, axis, [(i, i ^ mask) for i in range(lax.axis_size(axi...]
    dynamic_update_slice x70 -> x0, local copies, waits for them, and re-layouts: 112 us -> none  [the longest x36 97.5 us: add_batch(): lax.dynamic_update_index_in_dim(totals, current + addition, batch_index, 0)]
  transfers between devices with their start and end apart: 31 -> 52, of which waited for: 27 -> 19; matrix products, arithmetic and copies ran while one was open for 33% -> 14% of each run, Pallas kernels for 0% -> 35%
where the time goes in v1:
time: 1000 us; the launch traced here: 1020 us
  Pallas kernels  630 us (63%)
  waiting for transfers between devices  131 us (13%)
  other arithmetic  88.9 us (9%)
  local copies, waits for them, and re-layouts  66.1 us (7%)
  starting transfers between devices  46.1 us (5%)
  matrix products  29.2 us (3%)
  between operations  25.8 us (3%)
    pallas_call x6, Pallas kernels, rows_call(): pl.pallas_call(partial(_rows_kernel, count, scatter, gather, middle, len(...  219 us
    ppermute x37, waiting for transfers between devices, swap(): lax.ppermute(value, axis, [(i, i ^ mask) for i in range(lax.axis_size(axi...  131 us
    pallas_call x1, Pallas kernels, gather_weights(): pl.pallas_call(partial(_gather_kernel, slot_bits(), count, planes), out_s...  99.1 us
    pallas_call x3, Pallas kernels, attend_back(): pl.pallas_call(partial(_attend_back_kernel, chunks, tq, tk, causal, own_d...  58.2 us
    pallas_call x3, Pallas kernels, collect(): pl.pallas_call(partial(_collect_kernel, kinds, use, wide, each, blocks, l...  51.7 us
    pallas_call x3, Pallas kernels, attend(): pl.pallas_call(partial(_attend_kernel, chunks, tq, tk, causal), out_shape...  40.8 us
    pallas_call x1, Pallas kernels, to_decoder(): pl.pallas_call(partial(_to_decoder_kernel, count), out_shape=[jax.ShapeDt...  40.5 us
    pallas_call x2, Pallas kernels, to_encoder(): pl.pallas_call(partial(_to_encoder_kernel, count, out is not None), out_s...  35.8 us
  transfers between devices with their start and end apart: 52, of which 19 were waited for; matrix products, arithmetic and copies ran while one was open for 14% of the time, Pallas kernels for 35%

profile of v1, /device:TPU:0, one launch (start us, length us, event | category | flops | bytes accessed | tf_op | source)
XLA Modules:
  0.0 1017.2 jit_solution(14311034371068050785)
XLA Ops:
  26.7 99.1 %gather_weights.1 = (bf16[2,1024,2048]{2,1,0:T(8,128)(2,1)}, bf16[2,1024,256]{2,1,0:T(8,128)(2,1)}, bf16[2,1024,1024]{2,1,0:T(8,128)(2,1)}, bf16[2,1024,512]{2,1...) custom-call(bf16[2,1024,512]{2,1,0:T(8,128)(2,1)} %maximum_maximum_f, ...), custom_call_target="tpu_custom_call" | custom-call | tf_op jit(solution)/shard_map/gather_weights/pallas_call | solution.py:869
  145.3 11.5 %spread.3 = (bf16[512,1024]{1,0:T(8,128)(2,1)}, bf16[2,512,1024]{2,1,0:T(8,128)(2,1)}) custom-call(bf16[512,1024]{1,0:T(8,128)(2,1)} %get-tuple-element.243.x.refs_3_, bf16[2,1024,2048]{2,1,0:T(8,128)(2,1)} %get-tuple-element.96.weights.refs_1_.refs_2_), custom_call_target="tpu_custom_call" | custom-call | flops 3221225472 | bytes 8388608 | tf_op jit(solution)/shard_map/spread/pallas_call | solution.py:988
  166.7 58.4 %forward_rows.2 = (f32[64,1024]{1,0:T(8,128)}, f32[64,1024]{1,0:T(8,128)}, f32[64,128]{1,0:T(8,128)}, bf16[256,1024]{1,0:T(8,128)(2,1)}) custom-call(bf16[256,1024]{1,0:T(8,128)(2,1)} %convolution_convert_fusion.10.refs_0_, f32[64,1024]{1,0:T(8,128)} %get-tuple-element.214.refs_1_, f32[1,1024]{1,0:T(1,128)} %get-tuple-element.317.refs_2_.refs_4_, ...), custom_call_target="tpu_custom_call" | custom-call | flops 655360 | bytes 4194304 | tf_op jit(solution)/shard_map/forward_rows/pallas_call | solution.py:435
  227.2 16.6 %to_encoder.2.q = bf16[8,256,128]{2,1,0:T(8,128)(2,1)} custom-call(bf16[2,256,128]{2,1,0:T(8,128)(2,1)} %pad_maximum_fusion.35.refs_0_), custom_call_target="tpu_custom_call" | custom-call | tf_op jit(solution)/shard_map/to_encoder/pallas_call | solution.py:556
  262.3 26.1 %attend.4 = (f32[512,1024]{1,0:T(8,128)}, f32[8,8,512]{2,1,0:T(8,128)}) custom-call(s32[4]{0:T(128)} %convert_reduce_fusion.1.act, s32[8,512]{1,0:T(8,128)} %broadcast_in_dim.107.seg_q, s32[4,512,128]{2,1,0:T(8,128)} %broadcast_in_dim.108.seg_k, bf16[512,1024]{1,0:T(8,128)(2,1)} %get-tuple-element.103.q, ...), custom_call_target="tpu_custom_call" | custom-call | flops 4294967296 | bytes 10485760 | tf_op jit(solution)/shard_map/attend/pallas_call | solution.py:249
  298.8 11.9 %collect.3 = (f32[512,1024]{1,0:T(8,128)}, bf16[512,1024]{1,0:T(8,128)(2,1)}, f32[512,1024]{1,0:T(8,128)}, f32[512,128]{1,0:T(8,128)}) custom-call(bf16[512,1024]{1,0:T(8,128)(2,1)} %convert_element_type.733.refs_0_, bf16[2,1024,2048]{2,1,0:T(8,128)(2,1)} %get-tuple-element.96.weights.refs_1_.refs_2_, f32[512,1024]{1,0:T(8,128)} %get-tuple-element.242.refs_2_, ...), custom_call_target="tpu_custom_call" | custom-call | flops 1073741824 | bytes 8388608 | tf_op jit(solution)/shard_map/collect/pallas_call | solution.py:1048
  313.6 21.3 %feed_forward.1 = (f32[512,1024]{1,0:T(8,128)}, bf16[512,1024]{1,0:T(8,128)(2,1)}, f32[512,1024]{1,0:T(8,128)}, f32[512,128]{1,0:T(8,128)}, bf16[512,4096]{1,0:T(8,128)(2,1)}, /*index=5*/bf16[512,4096]{1,0:T(8,128)(2,1)}) custom-call(bf16[512,1024]{1,0:T(8,128)(2,1)} %get-tuple-element.105.x, f32[512,1024]{1,0:T(8,128)} %get-tuple-element.106.resid, ...), custom_call_target="tpu_custom_call" | custom-call | flops 8589934592 | bytes 16777216 | tf_op jit(solution)/shard_map/feed_forward/pallas_call | solution.py:1144
  347.2 11.3 %attend.5 = (bf16[8,256,128]{2,1,0:T(8,128)(2,1)}, f32[8,8,256]{2,1,0:T(8,128)}) custom-call(s32[1]{0:T(128)} %bitcast.6.act, s32[8,256]{1,0:T(8,128)} %broadcast_in_dim.103.seg_q, s32[1,512,128]{2,1,0:T(8,128)} %broadcast_in_dim.104.seg_k, bf16[8,256,128]{2,1,0:T(8,128)(2,1)} %to_encoder.2.q, bf16[2,512,1024]{2,1,0:T(8,128)(2,1)} %spread.4.refs_0_.refs_1_, ...), custom_call_target="tpu_custom_call" | custom-call | flops 536870912 | bytes 5242880 | tf_op jit(solution)/shard_map/attend/pallas_call | solution.py:249
  358.5 40.5 %to_decoder.1 = (bf16[256,256]{1,0:T(8,128)(2,1)}, f32[2,256,128]{2,1,0:T(8,128)}, f32[2,8,256]{2,1,0:T(8,128)}) custom-call(bf16[8,256,128]{2,1,0:T(8,128)(2,1)} %get-tuple-element.115.refs_0_, f32[8,8,256]{2,1,0:T(8,128)} %get-tuple-element.116.refs_1_), custom_call_target="tpu_custom_call" | custom-call | tf_op jit(solution)/shard_map/to_decoder/pallas_call | solution.py:636
  401.1 30.5 %forward_rows.3 = (f32[64,1024]{1,0:T(8,128)}, f32[64,1024]{1,0:T(8,128)}, f32[64,128]{1,0:T(8,128)}, bf16[256,1024]{1,0:T(8,128)(2,1)}) custom-call(bf16[256,1024]{1,0:T(8,128)(2,1)} %convolution_convert_fusion.9.refs_0_, f32[64,1024]{1,0:T(8,128)} %get-tuple-element.118.refs_1_, f32[1,1024]{1,0:T(1,128)} %get-tuple-element.315.refs_2_.refs_4_, ...), custom_call_target="tpu_custom_call" | custom-call | flops 655360 | bytes 4194304 | tf_op jit(solution)/shard_map/forward_rows/pallas_call | solution.py:435
  436.0 29.7 %turn_rows.1 = (bf16[64,1024]{1,0:T(8,128)(2,1)}, f32[64,1024]{1,0:T(8,128)}, f32[8,1024]{1,0:T(8,128)}, bf16[256,1024]{1,0:T(8,128)(2,1)}) custom-call(bf16[256,1024]{1,0:T(8,128)(2,1)} %fusion.9.refs_0_, f32[64,1024]{1,0:T(8,128)} %get-tuple-element.121.refs_1_, f32[1,1024]{1,0:T(1,128)} %get-tuple-element.313.refs_2_, ...), custom_call_target="tpu_custom_call" | custom-call | flops 655360 | bytes 4194304 | tf_op jit(solution)/shard_map/turn_rows/pallas_call | solution.py:435
  471.9 29.4 %backward_rows.2 = (f32[64,1024]{1,0:T(8,128)}, f32[8,1024]{1,0:T(8,128)}, bf16[256,1024]{1,0:T(8,128)(2,1)}) custom-call(bf16[256,1024]{1,0:T(8,128)(2,1)} %fusion.8.refs_0_, f32[64,1024]{1,0:T(8,128)} %get-tuple-element.124.refs_1_, f32[64,1024]{1,0:T(8,128)} %get-tuple-element.125.refs_2_, f32[64,128]{1,0:T(8,128)} %get-tuple-element.126.refs_3_, ...), custom_call_target="tpu_custom_call" | custom-call | flops 655360 | bytes 4194304 | tf_op jit(solution)/shard_map/backward_rows/pallas_call | solution.py:435
  508.0 19.1 %to_encoder.3 = (bf16[8,256,128]{2,1,0:T(8,128)(2,1)}, f32[8,8,256]{2,1,0:T(8,128)}) custom-call(bf16[2,256,128]{2,1,0:T(8,128)(2,1)} %pad_maximum_fusion.36.refs_0_, f32[2,256,128]{2,1,0:T(8,128)} %get-tuple-element.128.refs_1_, f32[2,8,256]{2,1,0:T(8,128)} %get-tuple-element.129.refs_2_), custom_call_target="tpu_custom_call" | custom-call | tf_op jit(solution)/shard_map/to_encoder/pallas_call | solution.py:556
  532.8 13.0 %attend_back.3 = (bf16[8,256,128]{2,1,0:T(8,128)(2,1)}, bf16[2,512,1024]{2,1,0:T(8,128)(2,1)}) custom-call(s32[1]{0:T(128)} %bitcast.6.act, s32[8,256]{1,0:T(8,128)} %broadcast_in_dim.103.seg_q, s32[1,512,128]{2,1,0:T(8,128)} %broadcast_in_dim.104.seg_k, bf16[8,256,128]{2,1,0:T(8,128)(2,1)} %to_encoder.2.q, bf16[2,512,1024]{2,1,0:T(8,128)(2,1)} %spread.4.refs_0_.refs_1_, ...), custom_call_target="tpu_custom_call" | custom-call | flops 1342177280 | bytes 10485760 | tf_op jit(solution)/shard_map/attend_back/pallas_call | solution.py:284
  545.8 16.9 %collect.4 = (f32[512,1024]{1,0:T(8,128)}, bf16[512,1024]{1,0:T(8,128)(2,1)}, f32[8,1024]{1,0:T(8,128)}, bf16[1024,1024]{1,0:T(8,128)(2,1)}, bf16[1024,1024]{1,0:T(8,128)(2,1)}) custom-call(bf16[2,512,1024]{2,1,0:T(8,128)(2,1)} %get-tuple-element.133.refs_0_, bf16[2,1024,1024]{2,1,0:T(8,128)(2,1)} %pad_maximum_fusion.weights.refs_1_, ...), custom_call_target="tpu_custom_call" | custom-call | flops 4294967296 | bytes 4194304 | tf_op jit(solution)/shard_map/collect/pallas_call | solution.py:1048
  563.0 32.1 %feed_forward_back.1 = (f32[512,1024]{1,0:T(8,128)}, bf16[512,1024]{1,0:T(8,128)(2,1)}, f32[8,1024]{1,0:T(8,128)}, bf16[1024,2048]{1,0:T(8,128)(2,1)}, bf16[1024...) custom-call(bf16[512,1024]{1,0:T(8,128)(2,1)} %get-tuple-element.105.x, ...), custom_call_target="tpu_custom_call" | custom-call | flops 17179869184 | bytes 33554432 | tf_op jit(solution)/shard_map/feed_forward_back/pallas_call | solution.py:1200
  637.0 40.9 %attend_back.4 = (bf16[512,1024]{1,0:T(8,128)(2,1)}, bf16[2,512,1024]{2,1,0:T(8,128)(2,1)}, bf16[2,512,1024]{2,1,0:T(8,128)(2,1)}, bf16[2,512,1024]{2,1,0:T(8,128)(2,1)}, bf16[2,512,1024]{2,1,0:T(8,128)(2,1)}) custom-call(s32[4]{0:T(128)} %convert_reduce_fusion.1.act, s32[8,512]{1,0:T(8,128)} %broadcast_in_dim.107.seg_q, ...), custom_call_target="tpu_custom_call" | custom-call | flops 10737418240 | bytes 20971520 | tf_op jit(solution)/shard_map/attend_back/pallas_call | solution.py:284
  679.7 54.9 %backward_rows.3 = (f32[64,1024]{1,0:T(8,128)}, f32[8,1024]{1,0:T(8,128)}, bf16[256,1024]{1,0:T(8,128)(2,1)}) custom-call(bf16[256,1024]{1,0:T(8,128)(2,1)} %convolution_convert_fusion.8.refs_0_, f32[64,1024]{1,0:T(8,128)} %get-tuple-element.147.refs_1_, f32[64,1024]{1,0:T(8,128)} %get-tuple-element.148.refs_2_, f32[64,128]{1,0:T(8,128)} %get-tuple-element.149.refs_3_, ...), custom_call_target="tpu_custom_call" | custom-call | flops 655360 | bytes 4194304 | tf_op jit(solution)/shard_map/backward_rows/pallas_call | solution.py:435
  765.4 40.4 %collective-permute-done.15 = bf16[2,512,1024]{2,1,0:T(8,128)(2,1)} collective-permute-done((bf16[2,512,1024]{2,1,0:T(8,128)(2,1)}, bf16[2,512,1024]{2,1,0:T(8,128)(2,1)}, u32[]{:S(2)}, u32[]{:S(2)}) %collective-permute-start.15) | collective-permute-done | bytes 2097184 | tf_op jit(solution)/shard_map/ppermute | solution.py:35
  812.3 22.9 %collect.5 = (f32[512,1024]{1,0:T(8,128)}, bf16[512,1024]{1,0:T(8,128)(2,1)}, f32[8,1024]{1,0:T(8,128)}, bf16[1024,1536]{1,0:T(8,128)(2,1)}, bf16[1024,1536]{1,0:T(8,128)(2,1)}) custom-call(bf16[512,1024]{1,0:T(8,128)(2,1)} %get-tuple-element.145.refs_0_, bf16[2,512,1024]{2,1,0:T(8,128)(2,1)} %add_convert_fusion.5.refs_1_, ...), custom_call_target="tpu_custom_call" | custom-call | flops 6442450944 | bytes 8388608 | tf_op jit(solution)/shard_map/collect/pallas_call | solution.py:1048
  852.6 16.3 %last_rows.1 = f32[64,1024]{1,0:T(8,128)} custom-call(bf16[256,1024]{1,0:T(8,128)(2,1)} %fusion.11.refs_0_, f32[64,1024]{1,0:T(8,128)} %get-tuple-element.154.refs_1_), custom_call_target="tpu_custom_call" | custom-call | flops 655360 | bytes 4194304 | tf_op jit(solution)/shard_map/last_rows/pallas_call | solution.py:435
  904.2 16.1 %collective-permute-done.23 = bf16[256,1024]{1,0:T(8,128)(2,1)} collective-permute-done((bf16[256,1024]{1,0:T(8,128)(2,1)}, bf16[256,1024]{1,0:T(8,128)(2,1)}, u32[]{:S(2)}, u32[]{:S(2)}) %collective-permute-start.23) | collective-permute-done | bytes 524320 | tf_op jit(solution)/shard_map/ppermute | solution.py:35
  921.7 15.4 %collective-permute-done.28 = bf16[256,1024]{1,0:T(8,128)(2,1)} collective-permute-done((bf16[256,1024]{1,0:T(8,128)(2,1)}, bf16[256,1024]{1,0:T(8,128)(2,1)}, u32[]{:S(2)}, u32[]{:S(2)}) %collective-permute-start.28) | collective-permute-done | bytes 524320 | tf_op jit(solution)/shard_map/ppermute | solution.py:35
  943.4 12.4 %collective-permute-done.29 = bf16[256,512]{1,0:T(8,128)(2,1)S(1)} collective-permute-done((bf16[256,512]{1,0:T(8,128)(2,1)S(1)}, bf16[256,512]{1,0:T(8,128)(2,1)S(1)}, u32[]{:S(2)}, u32[]{:S(2)}) %collective-permute-start.29) | collective-permute-done | bytes 262176 | tf_op jit(solution)/shard_map/ppermute | solution.py:35
  (484 shorter events, 304.8 us)
Async XLA Ops:
  7.2 236.7 %all-gather.3.cloned.1.call-start = ((), (), s32[]{:S(2)}) async-start(), calls=%async_computation.6 | async-start | bytes 7864320 | tf_op jit(solution)/shard_map/all_gather | solution.py:883
  125.8 165.5 %all-gather.5.cloned.1.call-start = ((), (), s32[]{:S(2)}) async-start(), calls=%async_computation.7 | async-start | bytes 1966080 | tf_op jit(solution)/shard_map/all_gather | solution.py:883
  156.8 87.6 %collective-permute-start.1 = (bf16[2,512,1024]{2,1,0:T(8,128)(2,1)}, bf16[2,512,1024]{2,1,0:T(8,128)(2,1)}, u32[]{:S(2)}, u32[]{:S(2)}) collective-permute-start(bf16[2,512,1024]{2,1,0:T(8,128)(2,1)} %get-tuple-element.97.refs_0_.refs_4_), channel_id=1, source_target_pairs={{0,1},{1,0},{2,3},{3,2},{4,5},{5,4},{6,7},{7,6},{8,9},{9,8},{10,11... | collective-permute-start | bytes 6291464 | tf_op jit(solution)/shard_map/ppermute | solution.py:35
  243.8 69.8 %collective-permute-start.4 = (bf16[1024,3072]{1,0:T(8,128)(2,1)}, bf16[1024,3072]{1,0:T(8,128)(2,1)}, u32[]{:S(2)}, u32[]{:S(2)}) collective-permute-start(bf16[1024,3072]{1,0:T(8,128)(2,1)} %all-gather.3.cloned.1.call-done.refs_1_.refs_4_), channel_id=1, source_target_pairs={{0,16},{16,0},{1,17},{17,1},{2,18},{18,2},{3,19},{19,3},{4,20},{20... | collective-permute-start | bytes 18874376 | tf_op jit(solution)/shard_map/ppermute | solution.py:35
  244.8 504.1 %reduce-scatter.11.cloned.1.call-start = ((), (), s32[]{:S(2)}) async-start(), calls=%async_computation.10 | async-start | bytes 2621440 | tf_op jit(solution)/shard_map/reduce_scatter | solution.py:891
  529.6 219.3 %reduce-scatter.13.cloned.1.call-start = ((), (), s32[]{:S(2)}) async-start(), calls=%async_computation.11 | async-start | bytes 2621440 | tf_op jit(solution)/shard_map/reduce_scatter | solution.py:891
  562.7 32.7 %collective-permute-start.27 = (bf16[1024,1024]{1,0:T(8,128)(2,1)}, bf16[1024,1024]{1,0:T(8,128)(2,1)S(1)}, u32[]{:S(2)}, u32[]{:S(2)}) collective-permute-start(bf16[1024,1024]{1,0:T(8,128)(2,1)} %get-tuple-element.171), channel_id=1, source_target_pairs={{0,16},{16,0},{1,17},{17,1},{2,18},{18,2},{3,19},{19,3},{4,20},{20... | collective-permute-start | bytes 6291464 | tf_op jit(solution)/shard_map/ppermute | solution.py:35
  597.7 295.9 %reduce-scatter.9.cloned.1.call-start = ((), (), s32[]{:S(2)}) async-start(), calls=%async_computation.9 | async-start | bytes 5242880 | tf_op jit(solution)/shard_map/reduce_scatter | solution.py:891
  610.6 286.1 %reduce-scatter.15.cloned.1.call-start = ((), (), s32[]{:S(2)}) async-start(), calls=%async_computation.12 | async-start | bytes 5242880 | tf_op jit(solution)/shard_map/reduce_scatter | solution.py:891
  612.9 132.1 %collective-permute-start.25 = (bf16[1024,2048]{1,0:T(8,128)(2,1)}, bf16[1024,2048]{1,0:T(8,128)(2,1)S(1)}, u32[]{:S(2)}, u32[]{:S(2)}) collective-permute-start(bf16[1024,2048]{1,0:T(8,128)(2,1)} %get-tuple-element.169), channel_id=1, source_target_pairs={{0,16},{16,0},{1,17},{17,1},{2,18},{18,2},{3,19},{19,3},{4,20},{20... | collective-permute-start | bytes 12582920 | tf_op jit(solution)/shard_map/ppermute | solution.py:35
  625.7 52.3 %collective-permute-start.9 = (bf16[2,256,128]{2,1,0:T(8,128)(2,1)S(1)}, bf16[2,256,128]{2,1,0:T(8,128)(2,1)S(1)}, u32[]{:S(2)}, u32[]{:S(2)}) collective-permute-start(bf16[2,256,128]{2,1,0:T(8,128)(2,1)S(1)} %get-tuple-element.284), channel_id=1, source_target_pairs={{0,2},{1,3},{18,16},{19,17},{4,6},{5,7},{22,20},{23,21},{8,10},{9,... | collective-permute-start | bytes 393224 | tf_op jit(solution)/shard_map/ppermute | solution.py:40
  629.9 48.5 %collective-permute-start.10 = (bf16[2,256,128]{2,1,0:T(8,128)(2,1)S(1)}, bf16[2,256,128]{2,1,0:T(8,128)(2,1)S(1)}, u32[]{:S(2)}, u32[]{:S(2)}) collective-permute-start(bf16[2,256,128]{2,1,0:T(8,128)(2,1)S(1)} %get-tuple-element.285), channel_id=1, source_target_pairs={{0,1},{1,0},{18,19},{19,18},{4,5},{5,4},{22,23},{23,22},{8,9},{9,8... | collective-permute-start | bytes 393224 | tf_op jit(solution)/shard_map/ppermute | solution.py:40
  635.7 42.8 %collective-permute-start.11 = (bf16[2,256,128]{2,1,0:T(8,128)(2,1)S(1)}, bf16[2,256,128]{2,1,0:T(8,128)(2,1)S(1)}, u32[]{:S(2)}, u32[]{:S(2)}) collective-permute-start(bf16[2,256,128]{2,1,0:T(8,128)(2,1)S(1)} %get-tuple-element.283), channel_id=1, source_target_pairs={{0,3},{1,2},{18,17},{19,16},{4,7},{5,6},{22,21},{23,20},{8,11},{9,... | collective-permute-start | bytes 393224 | tf_op jit(solution)/shard_map/ppermute | solution.py:40
  677.9 74.8 %collective-permute-start.14 = (bf16[2,512,1024]{2,1,0:T(8,128)(2,1)}, bf16[2,512,1024]{2,1,0:T(8,128)(2,1)}, u32[]{:S(2)}, u32[]{:S(2)}) collective-permute-start(bf16[2,512,1024]{2,1,0:T(8,128)(2,1)} %get-tuple-element.158), channel_id=1, source_target_pairs={{0,16},{16,0},{1,17},{17,1},{2,18},{18,2},{3,19},{19,3},{4,20},{20... | collective-permute-start | bytes 6291464 | tf_op jit(solution)/shard_map/ppermute | solution.py:35
  678.0 87.4 %collective-permute-start.13 = (bf16[2,512,1024]{2,1,0:T(8,128)(2,1)}, bf16[2,512,1024]{2,1,0:T(8,128)(2,1)}, u32[]{:S(2)}, u32[]{:S(2)}) collective-permute-start(bf16[2,512,1024]{2,1,0:T(8,128)(2,1)} %get-tuple-element.156), channel_id=1, source_target_pairs={{0,16},{16,0},{1,17},{17,1},{2,18},{18,2},{3,19},{19,3},{4,20},{20... | collective-permute-start | bytes 6291464 | tf_op jit(solution)/shard_map/ppermute | solution.py:35
  748.9 214.8 %reduce-scatter.7.cloned.1.call-start = ((), (), s32[]{:S(2)}) async-start(), calls=%async_computation.8 | async-start | bytes 5242880 | tf_op jit(solution)/shard_map/reduce_scatter | solution.py:891
  756.7 49.1 %collective-permute-start.15 = (bf16[2,512,1024]{2,1,0:T(8,128)(2,1)}, bf16[2,512,1024]{2,1,0:T(8,128)(2,1)}, u32[]{:S(2)}, u32[]{:S(2)}) collective-permute-start(bf16[2,512,1024]{2,1,0:T(8,128)(2,1)} %add_convert_fusion.6), channel_id=1, source_target_pairs={{0,1},{1,0},{2,3},{3,2},{4,5},{5,4},{6,7},{7,6},{8,9},{9,8},{10,11... | collective-permute-start | bytes 6291464 | tf_op jit(solution)/shard_map/ppermute | solution.py:35
  846.2 122.2 %reduce-scatter.17.cloned.1.call-start = ((), (), s32[]{:S(2)}) async-start(), calls=%async_computation.13 | async-start | bytes 1966080 | tf_op jit(solution)/shard_map/reduce_scatter | solution.py:891
  891.6 65.5 %collective-permute-start.19 = (bf16[512,512]{1,0:T(8,128)(2,1)}, bf16[512,512]{1,0:T(8,128)(2,1)S(1)}, u32[]{:S(2)}, u32[]{:S(2)}) collective-permute-start(bf16[512,512]{1,0:T(8,128)(2,1)} %get-tuple-element.245), channel_id=1, source_target_pairs={{16,18},{17,19},{18,16},{19,17},{20,22},{21,23},{22,20},{23,21},{2... | collective-permute-start | bytes 1572872 | tf_op jit(solution)/shard_map/ppermute | solution.py:40
  892.3 64.8 %collective-permute-start.18 = (bf16[512,512]{1,0:T(8,128)(2,1)}, bf16[512,512]{1,0:T(8,128)(2,1)}, u32[]{:S(2)}, u32[]{:S(2)}) collective-permute-start(bf16[512,512]{1,0:T(8,128)(2,1)} %get-tuple-element.246), channel_id=1, source_target_pairs={{16,2},{17,3},{18,0},{19,1},{20,6},{21,7},{22,4},{23,5},{24,10},{2... | collective-permute-start | bytes 1572872 | tf_op jit(solution)/shard_map/ppermute | solution.py:40
  895.5 24.7 %collective-permute-start.23 = (bf16[256,1024]{1,0:T(8,128)(2,1)}, bf16[256,1024]{1,0:T(8,128)(2,1)}, u32[]{:S(2)}, u32[]{:S(2)}) collective-permute-start(bf16[256,1024]{1,0:T(8,128)(2,1)} %split.81), channel_id=1, source_target_pairs={{0,1},{1,0},{2,3},{3,2},{4,5},{5,4},{6,7},{7,6},{8,9},{9,8},{10,11... | collective-permute-start | bytes 1572872 | tf_op jit(solution)/shard_map/ppermute | solution.py:35
  898.6 38.5 %collective-permute-start.28 = (bf16[256,1024]{1,0:T(8,128)(2,1)}, bf16[256,1024]{1,0:T(8,128)(2,1)}, u32[]{:S(2)}, u32[]{:S(2)}) collective-permute-start(bf16[256,1024]{1,0:T(8,128)(2,1)} %split.85), channel_id=1, source_target_pairs={{0,1},{1,0},{2,3},{3,2},{4,5},{5,4},{6,7},{7,6},{8,9},{9,8},{10,11... | collective-permute-start | bytes 1572872 | tf_op jit(solution)/shard_map/ppermute | solution.py:35
  904.1 38.5 %collective-permute-start.31 = (bf16[256,512]{1,0:T(8,128)(2,1)S(1)}, bf16[256,512]{1,0:T(8,128)(2,1)S(1)}, u32[]{:S(2)}, u32[]{:S(2)}) collective-permute-start(bf16[256,512]{1,0:T(8,128)(2,1)S(1)} %split.89), channel_id=1, source_target_pairs={{0,1},{1,0},{2,3},{3,2},{4,5},{5,4},{6,7},{7,6},{8,9},{9,8},{10,11... | collective-permute-start | bytes 786440 | tf_op jit(solution)/shard_map/ppermute | solution.py:35
  970.1 33.1 %collective-permute-start.38 = (bf16[256,2,128]{0,2,1:T(8,128)(2,1)}, bf16[256,2,128]{0,2,1:T(8,128)(2,1)}, u32[]{:S(2)}, u32[]{:S(2)}) collective-permute-start(bf16[256,2,128]{0,2,1:T(8,128)(2,1)} %get-tuple-element.270), channel_id=1, source_target_pairs={{0,16},{16,0},{1,17},{17,1},{2,18},{18,2},{3,19},{19,3},{4,20},{20... | collective-permute-start | bytes 393224 | tf_op jit(solution)/shard_map/ppermute | solution.py:35
  (104 other events, 1865.9 us)
Sparse Core Ops, SparseCore 0:
  125.9 76.0 all-gather.2
  244.9 32.8 all-gather.4
  529.7 38.5 reduce-scatter.10
  597.8 38.4 reduce-scatter.12
  639.2 52.6 reduce-scatter.8
  749.1 56.4 reduce-scatter.14
  846.3 55.1 reduce-scatter.6
  904.8 30.8 reduce-scatter.16

commit v2 on v1

--- a/solution.py
+++ b/solution.py
@@ -120,7 +120,7 @@
 
 def _attend_kernel(chunks, tq, tk, causal, act, seg_q, seg_k, q, *refs):
     keys, values = refs[:chunks], refs[chunks : 2 * chunks]
-    out, lse, top, total, acc = refs[2 * chunks :]
+    out, lse, top, total, acc = refs[-5:]
     rows = q.shape[0]
     nq, nk = rows // tq, keys[0].shape[0] // tk
     top[...] = jnp.full(top.shape, NEGATIVE, WIDE)
@@ -158,8 +158,7 @@
     keys, values = refs[:chunks], refs[chunks : 2 * chunks]
     grad_out, stats = refs[2 * chunks : 2 * chunks + 2]
     refs = refs[2 * chunks + 2 :]
-    extra, grad_q, *refs = refs
-    grad_kv, (delta, dq, dkv) = refs[:chunks], refs[chunks:]
+    extra, (grad_q, *grad_kv, delta, dq, dkv) = refs[0], refs[-(chunks + 4) :]
     rows = q.shape[0]
     nq, nk = rows // tq, keys[0].shape[0] // tk
     if own_delta:
@@ -221,41 +220,53 @@
     )
 
 
-def _specs(rows, span, chunks, masks, blocked):
-    row_block = pl.BlockSpec((rows, LANES), lambda h, act: (0, h))
+def _specs(rows, span, chunks, masks, blocked, part):
+    def block(h):
+        return h if part is None else 2 * h + part
+
+    row_block = pl.BlockSpec((rows, LANES), lambda h, act: (0, block(h)))
     if blocked:
-        row_block = pl.BlockSpec((None, rows, LANES), lambda h, act: (h, 0, 0))
-    stat_block = pl.BlockSpec((1, 8, rows), lambda h, act: (h, 0, 0))
+        row_block = pl.BlockSpec((None, rows, LANES), lambda h, act: (block(h), 0, 0))
+    stat_block = pl.BlockSpec((1, 8, rows), lambda h, act: (block(h), 0, 0))
     heads = [
         pl.BlockSpec((8, rows), lambda h, act: (0, 0)),
         pl.BlockSpec((chunks, span, LANES), lambda h, act: (0, 0, 0)),
         row_block,
     ]
-    for part in range(2):
+    for side in range(2):
         heads += [
-            pl.BlockSpec((None, span, LANES), lambda h, act, m=m, part=part: (part, 0, h ^ m)) for m in masks
+            pl.BlockSpec((None, span, LANES), lambda h, act, m=m, side=side: (side, 0, h ^ m)) for m in masks
         ]
     return row_block, stat_block, heads
 
 
-def attend(q, key_values, segs, masks, causal=False, out_type=WIDE):
+def _dimensions(q, key_values, masks, part):
     blocked = q.ndim == 3
     rows, width = (q.shape[1], q.shape[0] * LANES) if blocked else q.shape
-    span = key_values[0].shape[1]
-    chunks, blocks = len(key_values), width // LANES
-    tq, tk = _tile_sizes(rows, span)
-    row_block, stat_block, specs = _specs(rows, span, chunks, masks, blocked)
-    pairs = rows * span * chunks
+    span, chunks, blocks = key_values[0].shape[1], len(key_values), width // LANES
+    if part is not None:
+        blocks, masks = blocks // 2, [m // 2 for m in masks]
+    row_block, stat_block, specs = _specs(rows, span, chunks, masks, blocked, part)
+    return rows, span, chunks, blocks, masks, _tile_sizes(rows, span), row_block, stat_block, specs
+
+
+def attend(q, key_values, segs, masks, causal=False, out_type=WIDE, part=None, into=()):
+    rows, span, chunks, blocks, masks, (tq, tk), row_block, stat_block, specs = _dimensions(
+        q, key_values, masks, part
+    )
+    pairs = rows * span * chunks * blocks * LANES
+    kept = 4 + 2 * chunks
+    stat_blocks = blocks if part is None else 2 * blocks
     return pl.pallas_call(
         partial(_attend_kernel, chunks, tq, tk, causal),
         out_shape=(
             jax.ShapeDtypeStruct(q.shape, out_type),
-            jax.ShapeDtypeStruct((blocks, 8, rows), WIDE),
+            jax.ShapeDtypeStruct((stat_blocks, 8, rows), WIDE),
         ),
         grid_spec=pltpu.PrefetchScalarGridSpec(
             num_scalar_prefetch=1,
             grid=(blocks,),
-            in_specs=specs,
+            in_specs=specs + [pl.BlockSpec(memory_space=pl.ANY)] * len(into),
             out_specs=[row_block, stat_block],
             scratch_shapes=[
                 pltpu.VMEM((8, rows), WIDE),
@@ -263,32 +274,35 @@
                 pltpu.VMEM((LANES, rows), WIDE),
             ],
         ),
+        input_output_aliases={kept + i: i for i in range(len(into))},
         compiler_params=pltpu.CompilerParams(vmem_limit_bytes=VMEM_LIMIT),
         cost_estimate=pl.CostEstimate(
-            flops=4 * pairs * width, transcendentals=pairs * width // HEAD, bytes_accessed=rows * width * 20
+            flops=48 * pairs, transcendentals=pairs // HEAD, bytes_accessed=rows * blocks * LANES * 20
         ),
         name="attend",
-    )(*segs, q, *key_values, *key_values)
-
-
-def attend_back(q, key_values, grad_out, stats, extra, segs, masks, causal=False, own_delta=True):
-    blocked = q.ndim == 3
-    rows, width = (q.shape[1], q.shape[0] * LANES) if blocked else q.shape
-    span = key_values[0].shape[1]
-    chunks, blocks = len(key_values), width // LANES
-    tq, tk = _tile_sizes(rows, span)
-    row_block, stat_block, specs = _specs(rows, span, chunks, masks, blocked)
+    )(*segs, q, *key_values, *key_values, *into)
+
+
+def attend_back(
+    q, key_values, grad_out, stats, extra, segs, masks, causal=False, own_delta=True, part=None, into=()
+):
+    rows, span, chunks, blocks, masks, (tq, tk), row_block, stat_block, specs = _dimensions(
+        q, key_values, masks, part
+    )
     kv_out = [pl.BlockSpec((2, span, LANES), lambda h, act, m=m: (0, 0, h ^ m)) for m in masks]
-    pairs = rows * span * chunks
+    pairs = rows * span * chunks * blocks * LANES
     extra_block = row_block if own_delta else pl.BlockSpec((span, LANES), lambda h, act: (0, h))
+    kept = 7 + 2 * chunks
     outs = pl.pallas_call(
         partial(_attend_back_kernel, chunks, tq, tk, causal, own_delta),
         out_shape=[jax.ShapeDtypeStruct(q.shape, HALF)]
-        + [jax.ShapeDtypeStruct((2, span, width), HALF)] * chunks,
+        + [jax.ShapeDtypeStruct((2, span, blocks * LANES), HALF)] * chunks,
         grid_spec=pltpu.PrefetchScalarGridSpec(
             num_scalar_prefetch=1,
             grid=(blocks,),
-            in_specs=specs + [row_block, stat_block, extra_block],
+            in_specs=specs
+            + [row_block, stat_block, extra_block]
+            + [pl.BlockSpec(memory_space=pl.ANY)] * len(into),
             out_specs=[row_block] + kv_out,
             scratch_shapes=[
                 pltpu.VMEM((8, rows), WIDE),
@@ -296,12 +310,13 @@
                 pltpu.VMEM((2, span, LANES), WIDE),
             ],
         ),
+        input_output_aliases={kept + i: i for i in range(len(into))},
         compiler_params=pltpu.CompilerParams(vmem_limit_bytes=VMEM_LIMIT),
         cost_estimate=pl.CostEstimate(
-            flops=10 * pairs * width, transcendentals=pairs * width // HEAD, bytes_accessed=rows * width * 40
+            flops=80 * pairs, transcendentals=pairs // HEAD, bytes_accessed=rows * blocks * LANES * 40
         ),
         name="attend_back",
-    )(*segs, q, *key_values, *key_values, grad_out, stats, extra)
+    )(*segs, q, *key_values, *key_values, grad_out, stats, extra, *into)
     return outs[0], outs[1:]
 
 
@@ -359,10 +374,6 @@
     outs[1][0:1, :] = grad_gain
     outs[1][1:2, :] = grad_bias
     return grad
-
-
-def _last_rows(total, ins, outs):
-    outs[0][...] = total + ins[0][...]
 
 
 def _rows_kernel(count, scatter, gather, middle, n_in, n_out, *refs):
@@ -443,7 +454,7 @@
             collective_id=number, has_side_effects=True, vmem_limit_bytes=VMEM_LIMIT
         ),
         cost_estimate=pl.CostEstimate(
-            flops=10 * rows * width, transcendentals=0, bytes_accessed=64 * rows * width
+            flops=0, transcendentals=0, bytes_accessed=1400 * rows * width
         ),
         name=middle.__name__.strip("_"),
     )(*operands)
@@ -562,6 +573,7 @@
         compiler_params=pltpu.CompilerParams(
             collective_id=number, has_side_effects=True, vmem_limit_bytes=VMEM_LIMIT
         ),
+        cost_estimate=pl.CostEstimate(flops=0, transcendentals=0, bytes_accessed=60 << 20),
         name="to_encoder",
     )(*operands)
 
@@ -654,6 +666,7 @@
         compiler_params=pltpu.CompilerParams(
             collective_id=number, has_side_effects=True, vmem_limit_bytes=VMEM_LIMIT
         ),
+        cost_estimate=pl.CostEstimate(flops=0, transcendentals=0, bytes_accessed=60 << 20),
         name="to_decoder",
     )(part, lse)
 
@@ -875,6 +888,7 @@
         compiler_params=pltpu.CompilerParams(
             collective_id=9, has_side_effects=True, vmem_limit_bytes=VMEM_LIMIT
         ),
+        cost_estimate=pl.CostEstimate(flops=0, transcendentals=0, bytes_accessed=280 << 20),
         name="gather_weights",
     )(*own, leaving, dec_rows)
 
@@ -887,15 +901,15 @@
     return (mine.astype(WIDE) + swap(other, "pipe", 1).astype(WIDE)).astype(HALF)
 
 
+def fold_line(rows, bits):
+    for bit in bits:
+        keep, send = jnp.split(rows, 2, axis=1)
+        rows = (keep.astype(WIDE) + swap(send, "tensor", bit).astype(WIDE)).astype(HALF)
+    return rows
+
+
 def fold_planes(term):
     return lax.psum_scatter(term, "dp", scatter_dimension=0, tiled=True)
-
-
-def fold_chips(rows, kinds):
-    for bit in reversed(slot_bits()):
-        keep, send = jnp.split(rows, 2, axis=1)
-        rows = (keep.astype(WIDE) + swap(send, "tensor", bit).astype(WIDE)).astype(HALF)
-    return rows.reshape(rows.shape[0], kinds, -1)
 
 
 def scatter_local(terms):
@@ -905,25 +919,7 @@
     mine = jnp.concatenate([pick(v.astype(HALF), core * wide) for v in terms], axis=1)
     other = jnp.concatenate([pick(v.astype(HALF), (1 - core) * wide) for v in terms], axis=1)
     term = fold_cores(mine, other)
-    rows = fold_planes(term)
-    return rows.reshape(rows.shape[0], len(terms), wide), term
-
-
-def reduce_norms(enc_terms, dec_terms):
-    core = lax.axis_index("pipe")
-    value = jnp.where(core == 0, enc_terms, dec_terms) + swap(
-        jnp.where(core == 0, dec_terms, enc_terms), "pipe", 1
-    )
-    for axis in ("dp", "tensor"):
-        bit = lax.axis_size(axis) // 2
-        while bit >= 1:
-            parts = value.reshape(value.shape[0], 2, -1)
-            mine = lax.rem(lax.axis_index(axis) // bit, 2)
-            keep = lax.dynamic_index_in_dim(parts, mine, 1, False)
-            send = lax.dynamic_index_in_dim(parts, 1 - mine, 1, False)
-            value = keep + swap(send, axis, bit)
-            bit //= 2
-    return value
+    return fold_planes(term), term
 
 
 def _blocks_of(weights, kinds):
@@ -965,23 +961,28 @@
         y, *refs = refs
         i = pl.program_id(0)
         _store_grads(refs[-2:], i, blocks, [dot_ta(left, y[...].astype(HALF))], wide, each)
-    if pair:
-        refs[-1][0] = values[-2].astype(HALF)
-        refs[-1][1] = values[-1].astype(HALF)
-        values = values[:-2]
+    for n in range(pair):
+        ref = refs[len(refs) - pair + n]
+
+        @pl.when(lax.rem(pl.program_id(0), pair) == n)
+        def _(ref=ref):
+            ref[0] = values[-2].astype(HALF)
+            ref[1] = values[-1].astype(HALF)
+
+    values = values[:-2] if pair else values
     for ref, value in zip(refs, values):
         ref[...] = value.astype(HALF)
 
 
-def spread(x, weights, kinds, use, y=None, pair=False):
+def spread(x, weights, kinds, use, y=None, pair=0):
     rows, width = x.shape
     wide, each, blocks, spec = _blocks_of(weights, kinds)
     column = pl.BlockSpec((rows, LANES), lambda i: (0, i))
     single = len(use) - (2 if pair else 0)
     shapes, specs = [((rows, width), HALF)] * single, [column] * single
-    if pair:
-        shapes.append(((2, rows, width), HALF))
-        specs.append(pl.BlockSpec((2, rows, LANES), lambda i: (0, 0, i)))
+    for _ in range(pair):
+        shapes.append(((2, rows, width // pair), HALF))
+        specs.append(pl.BlockSpec((2, rows, LANES), lambda i: (0, 0, i // pair)))
     if y is not None:
         shapes += [((width, width // 2), HALF)] * 2
         specs += _grad_specs(width, LANES, blocks)
@@ -993,7 +994,7 @@
         out_specs=specs,
         compiler_params=pltpu.CompilerParams(vmem_limit_bytes=VMEM_LIMIT),
         cost_estimate=pl.CostEstimate(
-            flops=2 * rows * width * width * (len(use) + (y is not None)),
+            flops=8 * rows * width * width * (len(use) + (y is not None)),
             transcendentals=0,
             bytes_accessed=2 * width * width * kinds,
         ),
@@ -1001,7 +1002,7 @@
     )(x, weights, *([] if y is None else [y]))
 
 
-def _collect_kernel(kinds, use, wide, each, blocks, n_y, with_grad, ending, n_extra, *refs):
+def _collect_kernel(kinds, use, wide, each, blocks, n_y, split, with_grad, ending, n_extra, *refs):
     refs = list(refs)
     ys, refs = refs[:n_y], refs[n_y:]
     weights, refs = refs[0], refs[1:]
@@ -1015,9 +1016,16 @@
     def _():
         acc[...] = jnp.zeros(acc.shape, WIDE)
 
-    values = []
-    for y in ys:
-        values += [y[...]] if len(y.shape) == 2 else [y[0], y[1]]
+    values, ys = [], list(ys)
+    while ys:
+        y = ys.pop(0)
+        if len(y.shape) == 2:
+            values.append(y[...])
+        elif split:
+            odd = ys.pop(0)
+            values += [jnp.where(lax.rem(i, 2) == 0, y[n], odd[n]) for n in range(2)]
+        else:
+            values += [y[0], y[1]]
     values = [v.astype(HALF) for v in values]
     for value, k in zip(values, use):
         acc[...] += dot_bt(value, _piece(weights, kinds, wide, each, k))
@@ -1031,12 +1039,13 @@
 
 
 def collect(ys, weights, kinds, use, ending, extra, outs, x=None):
-    rows, width = ys[0].shape[-2:]
+    rows, width = ys[0].shape[-2], weights.shape[1]
+    split = any(y.ndim == 3 and y.shape[2] < width for y in ys)
     wide, each, blocks, spec = _blocks_of(weights, kinds)
     y_specs = [
         pl.BlockSpec((rows, LANES), lambda i: (0, i))
         if y.ndim == 2
-        else pl.BlockSpec((2, rows, LANES), lambda i: (0, 0, i))
+        else pl.BlockSpec((2, rows, LANES), lambda i: (0, 0, i // (2 if split else 1)))
         for y in ys
     ]
     fixed = [pl.BlockSpec(v.shape, lambda i: (0, 0)) for v in ([] if x is None else [x]) + extra]
@@ -1047,7 +1056,7 @@
         specs += _grad_specs(width, len(use) * LANES, blocks)
     return pl.pallas_call(
         partial(
-            _collect_kernel, kinds, use, wide, each, blocks, len(ys), x is not None, ending, len(extra)
+            _collect_kernel, kinds, use, wide, each, blocks, len(ys), split, x is not None, ending, len(extra)
         ),
         out_shape=[jax.ShapeDtypeStruct(*s) for s in shapes],
         grid=(2 * blocks,),
@@ -1056,7 +1065,7 @@
         scratch_shapes=[pltpu.VMEM((rows, width), WIDE)],
         compiler_params=pltpu.CompilerParams(vmem_limit_bytes=VMEM_LIMIT),
         cost_estimate=pl.CostEstimate(
-            flops=2 * rows * width * width * len(use) * (1 + (x is not None)),
+            flops=8 * rows * width * width * len(use) * (1 + (x is not None)),
             transcendentals=0,
             bytes_accessed=2 * width * width * kinds,
         ),
@@ -1151,7 +1160,7 @@
         scratch_shapes=[pltpu.VMEM((rows, width), WIDE)],
         compiler_params=pltpu.CompilerParams(vmem_limit_bytes=VMEM_LIMIT),
         cost_estimate=pl.CostEstimate(
-            flops=4 * rows * width * units, transcendentals=2 * rows * units, bytes_accessed=4 * width * units
+            flops=12 * rows * width * units, transcendentals=2 * rows * units, bytes_accessed=4 * width * units
         ),
         name="feed_forward",
     )(x, resid, gain, bias, own, mine, other, own, mine, other)
@@ -1207,10 +1216,289 @@
         scratch_shapes=[pltpu.VMEM((rows, width), WIDE)],
         compiler_params=pltpu.CompilerParams(vmem_limit_bytes=VMEM_LIMIT),
         cost_estimate=pl.CostEstimate(
-            flops=16 * rows * width * count * wide, transcendentals=0, bytes_accessed=16 * width * count * wide
+            flops=32 * rows * width * count * wide, transcendentals=0, bytes_accessed=16 * width * count * wide
         ),
         name="feed_forward_back",
     )(x, grad, resid, normed, inv_scale, gain, active, slope, own, mine, other, own, mine, other)
+
+
+def _add_rows(dest, first, second):
+    rows = 64 if dest.shape[0] % 64 == 0 else dest.shape[0]
+
+    def step(i, carry):
+        at = pl.ds(pl.multiple_of(i * rows, rows), rows)
+        dest[at, :] = (first[at, :].astype(WIDE) + second[at, :].astype(WIDE)).astype(HALF)
+        return carry
+
+    lax.fori_loop(0, dest.shape[0] // rows, step, 0)
+
+
+def _finish_kernel(bits, count, planes, *refs):
+    in_mine, out_mine, in_other, out_other, f1, f2, ckv, dec_ffn, dec_small, tokens, part, resid = refs[:12]
+    norm_terms, refs = refs[12:18], refs[18:]
+    attn_out, cross_out, ffn_out, far, near, dec_grad, norm_sum = refs[:7]
+    land_in, land_out, term, *refs = refs[7:]
+    n_steps = planes.bit_length() - 1
+    land_planes, refs = refs[:n_steps], refs[n_steps:]
+    folded, landed, refs = refs[:3], refs[3:6], refs[6:]
+    enc_ffn, enc_small, got_ffn, got_small, land_dec, norm_other, norm_land, send_sem, recv_sem = refs
+    core, place, me = lax.axis_index("pipe"), lax.axis_index("dp"), lax.axis_index("tensor")
+    sibling = {"pipe": 1 - core}
+    line = {s: {"tensor": _differ(me, s, count)} for s in range(1, count)}
+    cross_over = {"pipe": 1 - core, "tensor": _differ(me, bits[0], count)}
+    dp_bits = [1 << i for i in range(n_steps)]
+    others = {bit: {"dp": _differ(place, bit, planes)} for bit in dp_bits}
+    _enter([sibling, cross_over, *line.values(), *others.values()])
+    made = [0]
+
+    def number():
+        made[0] += 1
+        return made[0] - 1
+
+    def push(source, dest, peer):
+        i = number()
+        return _send(source, dest, send_sem.at[i], recv_sem.at[i], peer)
+
+    def wait(copies):
+        for copy in copies:
+            copy.wait()
+
+    for i in range(3):
+        at = slice(2 * i, 2 * i + 2)
+        enc, dec = norm_terms[i][0:2, :], norm_terms[3 + i][0:2, :]
+        norm_sum[at, :] = jnp.where(core == 0, enc, dec)
+        norm_other[at, :] = jnp.where(core == 0, dec, enc)
+    norm_sum[6:8, :] = jnp.zeros((2, norm_sum.shape[1]), WIDE)
+    norm_other[6:8, :] = jnp.zeros((2, norm_sum.shape[1]), WIDE)
+    norm_peers = [*others.values(), *(line[bit] for bit in bits)]
+    norm_now = [push(norm_other, norm_land.at[0], sibling)]
+
+    def advance_norms():
+        if norm_now:
+            norm_now.pop().wait()
+            n = n_steps + len(bits) - len(norm_peers)
+            norm_sum[...] = norm_sum[...] + norm_land[n]
+            if norm_peers:
+                norm_now.append(push(norm_sum, norm_land.at[n + 1], norm_peers.pop(0)))
+
+    to_core = [push(in_other, land_in, sibling), push(out_other, land_out, sibling)]
+
+    def chain(source, a, at=slice(None)):
+        fold, land = (v if at == slice(None) else v.at[at] for v in (folded[a], landed[a]))
+        size = folded[a].shape[1] * 2 // count
+        return {
+            "source": source,
+            "fold": fold,
+            "land": land,
+            "size": size,
+            "slots": count,
+            "bits": list(reversed(bits)),
+            "now": [],
+        }
+
+    def advance(c):
+        land, size = c["land"], c["size"]
+        if c["now"]:
+            wait(c["now"])
+            c["now"] = []
+            kept = c["slots"] // 2 * size
+            offset = (count - c["slots"]) * size
+            at = pl.ds(0, kept)
+            _add_rows(c["fold"].at[:, at], c["source"].at[:, at], land.at[:, pl.ds(offset, kept)])
+            c["source"], c["slots"] = c["fold"], c["slots"] // 2
+        if c["bits"]:
+            kept = c["slots"] // 2 * size
+            offset = (count - c["slots"]) * size
+            source = c["source"].at[:, pl.ds(kept, kept)]
+            c["now"] = [push(source, land.at[:, pl.ds(offset, kept)], line[c["bits"].pop(0)])]
+
+    chains = [chain(f1, 0), chain(ckv, 1)]
+    advance(chains[0])
+
+    half = tokens.shape[1] // 2
+    far_sem, near_sem, same_sem = number(), number(), number()
+
+    @pl.when(core == 1)
+    def _():
+        _send(tokens.at[:, pl.ds(0, half)], far, send_sem.at[far_sem], recv_sem.at[far_sem], cross_over)
+        _send(
+            tokens.at[:, pl.ds(half, half)], far, send_sem.at[same_sem], recv_sem.at[far_sem], line[bits[0]]
+        )
+
+    @pl.when(core == 0)
+    def _():
+        _send(tokens.at[:, pl.ds(half, half)], near, send_sem.at[near_sem], recv_sem.at[near_sem], sibling)
+
+    rows = dec_grad.shape[0]
+
+    def rows_of_chip(chip):
+        return pl.ds(pl.multiple_of(chip * rows, rows), rows)
+
+    dec_sent = [
+        push(part.at[rows_of_chip(peer["tensor"])], land_dec.at[s - 1], peer) for s, peer in line.items()
+    ]
+
+    wait(to_core)
+    block = in_mine.shape[0] // planes
+    wide = term.shape[1] // count
+    inner = in_mine.shape[1] // count
+
+    def sum_step(i, carry):
+        at = pl.ds(pl.multiple_of(i * 64, 64), 64)
+        for s in range(count):
+            first = in_mine[at, s * inner : (s + 1) * inner].astype(WIDE)
+            second = land_in[at, s * inner : (s + 1) * inner].astype(WIDE)
+            term[at, s * wide : s * wide + inner] = (first + second).astype(HALF)
+            outer = wide - inner
+            first = out_mine[at, s * outer : (s + 1) * outer].astype(WIDE)
+            second = land_out[at, s * outer : (s + 1) * outer].astype(WIDE)
+            term[at, s * wide + inner : (s + 1) * wide] = (first + second).astype(HALF)
+        return carry
+
+    lax.fori_loop(0, in_mine.shape[0] // 64, sum_step, 0)
+
+    columns = term.shape[1] // 2
+    orders = (dp_bits, dp_bits[::-1])
+    held = [[list(range(planes)) for _ in orders] for _ in range(2)]
+    piece = block // 2
+
+    def rows_of(difference, r):
+        first = _differ(place, difference, planes) * block + r * piece
+        return pl.ds(pl.multiple_of(first, piece), piece)
+
+    def at_of(p, m, r):
+        return term.at[rows_of(m, r), pl.ds(p * columns, columns)]
+
+    def plane_start(j, r):
+        copies = []
+        for p, order in enumerate(orders):
+            bit = order[j]
+            kept = [m for m in held[r][p] if not m & bit]
+            for n, m in enumerate(kept):
+                dest = land_planes[j].at[p, n, pl.ds(r * piece, piece)]
+                copies.append((p, m, dest, push(at_of(p, m ^ bit, r), dest, others[bit])))
+            held[r][p] = kept
+        return copies
+
+    def plane_finish(copies, r):
+        for p, m, dest, copy in copies:
+            copy.wait()
+            _add_rows(at_of(p, m, r), at_of(p, m, r), dest)
+
+    moving = [plane_start(0, r) for r in range(2)]
+    for_attn = []
+    for j in range(n_steps):
+        for r in range(2):
+            advance(chains[min(2 * j + r, 1)])
+            advance_norms()
+            plane_finish(moving[r], r)
+            if j + 1 < n_steps:
+                moving[r] = plane_start(j + 1, r)
+            else:
+                for_attn.append(chain(term.at[rows_of(0, r)], 2, pl.ds(r * piece, piece)))
+                advance(for_attn[-1])
+    while any(c["now"] or c["bits"] for c in chains + for_attn):
+        for c in for_attn + chains:
+            advance(c)
+        advance_norms()
+    while norm_now:
+        advance_norms()
+
+    size = [fold.shape[1] * 2 // count for fold in folded]
+    enc_ffn[:, : size[0]] = folded[0][:, : size[0]]
+    enc_ffn[:, size[0] :] = f2[...]
+    enc_small[:, : size[2]] = folded[2][:, : size[2]]
+    enc_small[:, size[2] :] = folded[1][:, : size[1]]
+    swap_sem = [number(), number()]
+
+    @pl.when(core == 0)
+    def _():
+        _send(dec_ffn, got_ffn, send_sem.at[swap_sem[0]], recv_sem.at[swap_sem[0]], sibling)
+        _send(dec_small, got_small, send_sem.at[swap_sem[1]], recv_sem.at[swap_sem[1]], sibling)
+
+    @pl.when(core == 1)
+    def _():
+        _send(enc_ffn, got_ffn, send_sem.at[swap_sem[0]], recv_sem.at[swap_sem[0]], sibling)
+        _send(enc_small, got_small, send_sem.at[swap_sem[1]], recv_sem.at[swap_sem[1]], sibling)
+
+    wait(dec_sent)
+    total = part[rows_of_chip(me), :].astype(WIDE) + resid[...]
+    for s in range(count - 1):
+        total = total + land_dec[s].astype(WIDE)
+    dec_grad[...] = total
+    for i, (mine, got) in enumerate(((enc_ffn, got_ffn), (enc_small, got_small))):
+        pltpu.make_async_copy(mine, got, send_sem.at[swap_sem[i]]).wait()
+        pltpu.make_async_copy(mine, got, recv_sem.at[swap_sem[i]]).wait()
+
+    def write(first, second):
+        for h, (ffn, small) in enumerate((first, second)):
+            c = ffn.shape[1] // 2
+            for k in range(2):
+                ffn_out[k, :, h * c : (h + 1) * c] = ffn[:, k * c : (k + 1) * c].astype(WIDE)
+            c = small.shape[1] // 6
+            for k in range(6):
+                dest = attn_out.at[k] if k < 4 else cross_out.at[k - 4]
+                dest[:, h * c : (h + 1) * c] = small[:, k * c : (k + 1) * c].astype(WIDE)
+
+    @pl.when(core == 0)
+    def _():
+        write((enc_ffn, enc_small), (got_ffn, got_small))
+
+    @pl.when(core == 1)
+    def _():
+        write((got_ffn, got_small), (dec_ffn, dec_small))
+
+    pltpu.make_async_copy(far, far, recv_sem.at[far_sem]).wait()
+
+    @pl.when(core == 1)
+    def _():
+        pltpu.make_async_copy(far, far, send_sem.at[far_sem]).wait()
+        pltpu.make_async_copy(far, far, send_sem.at[same_sem]).wait()
+        pltpu.make_async_copy(near, near, recv_sem.at[near_sem]).wait()
+
+    @pl.when(core == 0)
+    def _():
+        pltpu.make_async_copy(near, near, send_sem.at[near_sem]).wait()
+
+
+def finish(in_grads, out_grads, f1, f2, ckv, dec_ffn, dec_small, tokens, part, resid, norm_terms):
+    count, planes = lax.axis_size("tensor"), lax.axis_size("dp")
+    depth = in_grads[0].shape[0]
+    rows = depth // planes
+    attn_columns = in_grads[0].shape[1] + out_grads[0].shape[1]
+    wide = 2 * dec_small.shape[1] // 6
+    vmem = pl.BlockSpec(memory_space=pltpu.VMEM)
+    operands = (in_grads[0], out_grads[0], in_grads[1], out_grads[1], f1, f2, ckv, dec_ffn, dec_small, tokens, part, resid)
+    operands += tuple(norm_terms)
+    lines = [f1.shape[1], ckv.shape[1], attn_columns]
+    scratch = [in_grads[0].shape, out_grads[0].shape, (depth, attn_columns)]
+    blocks = planes // 2
+    while blocks >= 1:
+        scratch.append((2, blocks, rows, attn_columns // 2))
+        blocks //= 2
+    scratch += [(rows, c // 2) for c in lines]
+    scratch += [(rows, c - c // count) for c in lines]
+    scratch += [dec_ffn.shape, dec_small.shape] * 2
+    scratch.append((count - 1, *resid.shape))
+    norm_steps = count.bit_length() + planes.bit_length() - 1
+    norm_shapes = [norm_terms[0].shape, (norm_steps, *norm_terms[0].shape)]
+    token_piece = ((tokens.shape[0], tokens.shape[1] // 2), HALF)
+    outs = [((4, rows, wide), WIDE), ((2, rows, wide), WIDE), ((2, rows, dec_ffn.shape[1]), WIDE)]
+    outs += [token_piece, token_piece, (resid.shape, WIDE), (norm_terms[0].shape, WIDE)]
+    return pl.pallas_call(
+        partial(_finish_kernel, slot_bits(), count, planes),
+        out_shape=[jax.ShapeDtypeStruct(*o) for o in outs],
+        in_specs=[vmem] * len(operands),
+        out_specs=[vmem] * len(outs),
+        scratch_shapes=[pltpu.VMEM(shape, HALF) for shape in scratch]
+        + [pltpu.VMEM(shape, WIDE) for shape in norm_shapes]
+        + [pltpu.SemaphoreType.DMA((64,))] * 2,
+        compiler_params=pltpu.CompilerParams(
+            collective_id=5, has_side_effects=True, vmem_limit_bytes=VMEM_LIMIT
+        ),
+        cost_estimate=pl.CostEstimate(flops=0, transcendentals=0, bytes_accessed=200 << 20),
+        name="finish",
+    )(*operands)
 
 
 def per_device(
@@ -1235,11 +1523,18 @@
     local_width = attn_weights.shape[3]
     is_first = core == 0
     chips = range(count)
+    sources = [(s // top_bit, s % top_bit) for s in range(2 * top_bit)]
     half = width // 2
     half_local = local_width // 2
 
     def owner(t):
         return t // top_bit
+
+    norms = jnp.concatenate([norm_gains[0], norm_biases[0]], axis=0)
+    norms_other = swap(norms, "pipe", 1)
+    enc_norms = jnp.where(is_first, norms, norms_other)
+    dec_norms = jnp.where(is_first, norms_other, norms)
+    eg, eb, dg, db = enc_norms[:3], enc_norms[3:], dec_norms[:3], dec_norms[3:]
 
     pick = partial(lax.dynamic_index_in_dim, index=core, axis=0, keepdims=False)
     start_low = pick(dec_input)
@@ -1255,7 +1550,7 @@
         got,
         start_full,
     ) = gather_weights(
-        *[in_column_halves(v[0]) for v in (attn_weights, cross_weights, ffn_weights)],
+        *[in_column_halves(v[0]) for v in (after(attn_weights, norms_other), cross_weights, ffn_weights)],
         lax.dynamic_index_in_dim(enc_input, 1 - group, 0, False),
         start_low,
     )
@@ -1273,50 +1568,50 @@
     dec_attn, dec_cross, dec_ffn = [
         natural(v, k) for v, k in ((dec_attn_halves, 4), (dec_cross_halves, 2), (dec_ffn_halves, 2))
     ]
-    norms = jnp.concatenate([norm_gains[0], norm_biases[0]], axis=0)
-    norms_other = swap(norms, "pipe", 1)
-    enc_norms = jnp.where(is_first, norms, norms_other)
-    dec_norms = jnp.where(is_first, norms_other, norms)
-    eg, eb, dg, db = enc_norms[:3], enc_norms[3:], dec_norms[:3], dec_norms[3:]
-
+    blocks = width // LANES
+    masks = [a * (blocks // 2) + c * (blocks // 2 // top_bit) for a, c in sources]
+
+    def gain_of(i):
+        return enc_norms[i : i + 1]
+
+    def bias_of(i):
+        return enc_norms[3 + i : 4 + i]
+
+    embed, start_normed, start_scale = norm_forward(tokens, eg[0], eb[0])
+    start_scale = jnp.broadcast_to(start_scale, (span, LANES))
+    embed_low = embed.astype(HALF)
+    parts = 2 if all(m % 2 == 0 for m in masks) else 1
+    query, *key_value = spread(embed_low, w_attn, 4, (0, 1, 2), pair=parts)
+
+    def across_chips(value):
+        held, bit = [value], 1
+        while bit < top_bit:
+            held = held + [swap(v, "tensor", bit) for v in held]
+            bit *= 2
+        return held
+
+    def exchange(held, *earlier):
+        if earlier:
+            held = after(tuple(held), *earlier)
+        return list(held) + [swap(v, "pipe", 1) for v in held]
+
+    key_values = [across_chips(v) for v in key_value]
+    mine_cross = gather_planes(after(cross_rest, query))
+
+    enc_lengths, dec_lengths = [after(v, query) for v in (enc_lengths, dec_lengths)]
     enc_row = lax.dynamic_index_in_dim(enc_lengths, group, 0, False)
     dec_row_of_group = lax.dynamic_index_in_dim(dec_lengths, group, 0, False)
     dec_row = lax.dynamic_index_in_dim(dec_lengths, core, 0, False)
     spots = jnp.arange(span, dtype=jnp.int32)
-    sources = [(s // top_bit, s % top_bit) for s in range(2 * top_bit)]
     own_seg = table_of(block * span + spots, enc_row)
     key_seg = jnp.stack(
         [table_of((block ^ (a * top_bit) ^ c) * span + spots, enc_row) for a, c in sources]
     )
-    blocks = width // LANES
-    masks = [a * (blocks // 2) + c * (blocks // 2 // top_bit) for a, c in sources]
     dec_spots = jnp.arange(dec_span * count, dtype=jnp.int32)
     dec_seg = table_of(dec_spots, dec_row)
     enc_segs = tables(own_seg, key_seg)
     dec_segs = tables(dec_seg, dec_seg[None])
     cross_segs = tables(table_of(dec_spots, dec_row_of_group), own_seg[None])
-
-    def gain_of(i):
-        return enc_norms[i : i + 1]
-
-    def bias_of(i):
-        return enc_norms[3 + i : 4 + i]
-
-    embed, start_normed, start_scale = norm_forward(tokens, eg[0], eb[0])
-    start_scale = jnp.broadcast_to(start_scale, (span, LANES))
-    embed_low = embed.astype(HALF)
-    query, key_value = spread(embed_low, w_attn, 4, (0, 1, 2), pair=True)
-
-    def exchange(value):
-        held = [value]
-        bit = 1
-        while bit < top_bit:
-            held = held + [swap(v, "tensor", bit) for v in held]
-            bit *= 2
-        return held + [swap(v, "pipe", 1) for v in held]
-
-    key_values = exchange(key_value)
-    mine_cross = gather_planes(after(cross_rest, query))
 
     start_full = after(start_full, key_value)
     start = start_low.astype(WIDE)
@@ -1329,26 +1624,32 @@
     dec_kv = jnp.stack([dot(start_full, w).astype(HALF) for w in dec_in_w[1:]])
     dec_heads_wide, dec_lse = attend(dec_query, [dec_kv], dec_segs, [0], True)
     dec_heads = dec_heads_wide.astype(HALF)
-    self_norm, self_normed, self_scale, self_full = rows_call(
-        _forward_rows,
-        2,
-        dot_bt(dec_heads, dec_attn[3]).astype(HALF),
-        [start, dg[0:1], db[0:1]],
-        kept_rows,
-    )
-    cross_query = dot(self_full, dec_cross[0]).astype(HALF)
-
-    def in_halves(value):
-        return jnp.stack([value[:, :half_local], value[:, half_local:]])
-
-    [cross_q_enc] = to_encoder(in_halves(cross_query), 6)
-    cross_q_enc = to_pairs(cross_q_enc)
-    mine_ffn = after(mine_ffn, cross_q_enc)
+    term = dot_bt(dec_heads, dec_attn[3]).astype(HALF)
+
+    attended = ()
+    for n in range(parts):
+        key_values[n] = exchange(key_values[n], *attended, *((term,) if n else ()))
+        attended = attend(
+            query, key_values[n], enc_segs, masks, part=n if parts == 2 else None, into=attended
+        )
+    heads_wide, lse = attended
+
+    def sum_to_owner(term):
+        total = after(start, lse)
+        for s in range(count):
+            rows = lax.dynamic_slice_in_dim(term, (place ^ s) * dec_span, dec_span, 0)
+            total = total + (swap(rows, "tensor", s) if s else rows).astype(WIDE)
+        return total
+
+    self_norm, self_normed, self_scale = norm_forward(sum_to_owner(term), dg[0:1], db[0:1])
+    self_scale = jnp.broadcast_to(self_scale, (dec_span, LANES))
+    self_low = self_norm.astype(HALF)
+    self_rows = [swap(self_low, "tensor", s) if s else self_low for s in range(count)]
+
+    heads = heads_wide.astype(HALF)
+    mine_ffn = after(mine_ffn, heads_wide)
     other_ffn = swap(mine_ffn, "pipe", 1)
-
-    heads_wide, lse = attend(query, key_values, enc_segs, masks)
-    heads = heads_wide.astype(HALF)
-    mine_cross = after(mine_cross, heads)
+    mine_cross = after(mine_cross, other_ffn)
     w_cross = jnp.stack(
         [
             jnp.concatenate([own_cross[0], mine_cross], axis=1),
@@ -1362,7 +1663,18 @@
     _, memory_low, mem_normed, mem_scale, active, slope = feed_forward(
         attn_norm_low, attn_norm, gain_of(2), bias_of(2), own_ffn, mine_ffn, other_ffn
     )
-    [cross_kv] = spread(memory_low, w_cross, 2, (0, 1), pair=True)
+    self_full = after(jnp.zeros((rows_full, width), HALF), mem_scale)
+    for s in range(count):
+        self_full = lax.dynamic_update_slice_in_dim(self_full, self_rows[s], (place ^ s) * dec_span, 0)
+    cross_query = dot(self_full, dec_cross[0]).astype(HALF)
+
+    def in_halves(value):
+        return jnp.stack([value[:, :half_local], value[:, half_local:]])
+
+    [cross_q_enc] = to_encoder(in_halves(cross_query), 6)
+    cross_q_enc = to_pairs(cross_q_enc)
+
+    [cross_kv] = spread(memory_low, w_cross, 2, (0, 1), pair=1)
 
     tables_of_keys = enc_lengths.shape[1]
     at_table = (own_seg[:, None] == jnp.arange(tables_of_keys)[None]).astype(HALF)
@@ -1423,7 +1735,28 @@
     )
     dec_f2_grad = dot_ta(grad_full, dec_active)
     dec_f1_grad = dot_ta(cross_full, grad_hidden)
-    dec_ffn_half, _ = scatter_local([dec_f1_grad, dec_f2_grad])
+    dec_ffn_rows, _ = scatter_local([dec_f1_grad, dec_f2_grad])
+
+    def to_chip(value):
+        theirs = joint(value, [((1 - owner(t), t), (owner(t), t)) for t in chips])
+        theirs = theirs.reshape(2, count, *theirs.shape[1:])
+        chip = value.reshape(theirs.shape).astype(WIDE) + theirs[::-1].astype(WIDE)
+        return jnp.where(is_first, chip, chip[::-1]).astype(HALF)
+
+    def to_owner(chip):
+        terms = []
+        for s in range(top_bit):
+            near, far = 2 * s, 2 * s + 1
+            near_pairs = [((owner(t), t), (owner(t), t ^ s)) for t in chips]
+            far_pairs = [((owner(t), t), (owner(t), t ^ s ^ top_bit)) for t in chips]
+            near_got = chip[:, near] if s == 0 else joint(chip[:, near], near_pairs)
+            far_got = joint(chip[:, far], far_pairs)
+            terms.append(jnp.where(core == group, near_got, far_got).astype(WIDE))
+        return sum(terms)
+
+    cross_q_chip = to_chip(from_pairs(cross_q_term, half_local))
+    cross_q_grad = to_owner(cross_q_chip).astype(HALF)
+    cross_q_grad = jnp.concatenate([cross_q_grad[0], cross_q_grad[1]], axis=1)
 
     back_tokens = [((span, width), WIDE), ((span, width), HALF), ((8, width), WIDE)]
     resid_enc, resid_low, enc_terms2, *cross_grads = collect(
@@ -1436,10 +1769,11 @@
         back_tokens,
         memory_low,
     )
-    enc_ckv = fold_planes(fold_cores(*cross_grads))
+    ckv_term = fold_cores(*cross_grads)
+    enc_ckv = fold_planes(ckv_term)
     resid_enc, resid_low, enc_terms1, *ffn_grads = feed_forward_back(
         attn_norm_low,
-        resid_low,
+        after(resid_low, dec_ffn_rows, cross_q_chip),
         resid_enc,
         attn_normed,
         attn_scale,
@@ -1450,40 +1784,53 @@
         mine_ffn,
         other_ffn,
     )
-    enc_f2 = fold_planes(after(fold_cores(*ffn_grads[2:]), dec_ffn_half, enc_ckv))
-    enc_f1 = fold_planes(fold_cores(*ffn_grads[:2]))
-    heads_grad, *out_grads = spread(resid_low, w_attn, 4, (3,), heads)
-    q_grad, kv_grads = attend_back(
-        query, key_values, heads_grad, lse, heads_wide, enc_segs, masks
-    )
+    f2_term = fold_cores(*ffn_grads[2:])
+    enc_f2 = fold_planes(f2_term)
+    f1_term = fold_cores(*ffn_grads[:2])
+    enc_f1 = fold_planes(f1_term)
+    heads_grad, *out_grads = spread(after(resid_low, cross_q_grad), w_attn, 4, (3,), heads)
+    line_bits = list(reversed(slot_bits()))
 
     def join(a, b):
         return (a.astype(WIDE) + b.astype(WIDE)).astype(HALF)
 
-    held = [join(a, swap(b, "pipe", 1)) for a, b in zip(kv_grads[:top_bit], kv_grads[top_bit:])]
-    bit = top_bit // 2
-    while bit >= 1:
-        held = [join(a, swap(b, "tensor", bit)) for a, b in zip(held[:bit], held[bit:])]
-        bit //= 2
-    kv_grad = held[0]
-
-    def to_owner(value):
-        theirs = joint(value, [((1 - owner(t), t), (owner(t), t)) for t in chips])
-        theirs = theirs.reshape(2, count, *theirs.shape[1:])
-        chip = value.reshape(theirs.shape).astype(WIDE) + theirs[::-1].astype(WIDE)
-        chip = jnp.where(is_first, chip, chip[::-1]).astype(HALF)
-        terms = []
-        for s in range(top_bit):
-            near, far = 2 * s, 2 * s + 1
-            near_pairs = [((owner(t), t), (owner(t), t ^ s)) for t in chips]
-            far_pairs = [((owner(t), t), (owner(t), t ^ s ^ top_bit)) for t in chips]
-            near_got = chip[:, near] if s == 0 else joint(chip[:, near], near_pairs)
-            far_got = joint(chip[:, far], far_pairs)
-            terms.append(jnp.where(core == group, near_got, far_got).astype(WIDE))
-        return sum(terms)
-
-    cross_q_grad = after(to_owner(from_pairs(cross_q_term, half_local)).astype(HALF), q_grad)
-    cross_q_grad = jnp.concatenate([cross_q_grad[0], cross_q_grad[1]], axis=1)
+    grads_in = after(heads_grad, f1_term, f2_term)
+    def send_chips(held):
+        pairs, bit = [(v,) for v in held], top_bit // 2
+        while bit >= 1:
+            held = [join(*v) if len(v) == 2 else v[0] for v in pairs]
+            pairs = [(a, swap(b, "tensor", bit)) for a, b in zip(held[:bit], held[bit:])]
+            bit //= 2
+        return pairs[0]
+
+    def sum_pair(pair, *earlier):
+        return join(after(pair[0], *earlier), pair[1]) if len(pair) == 2 else pair[0]
+
+    q_grad, moving, held = (), [], []
+    for n in range(parts):
+        q_grad, terms = attend_back(
+            query,
+            key_values[n],
+            after(grads_in, *held),
+            lse,
+            heads_wide,
+            enc_segs,
+            masks,
+            part=n if parts == 2 else None,
+            into=q_grad,
+        )
+        q_grad = (q_grad,)
+        if n == 0:
+            keep, send = jnp.split(after(enc_f2, terms[0]), 2, axis=1)
+            f2_pair = (keep, swap(send, "tensor", line_bits[0]))
+        held = [join(a, swap(b, "pipe", 1)) for a, b in zip(terms[:top_bit], terms[top_bit:])]
+        moving.append(send_chips(held))
+    kv_grad = [sum_pair(pair, terms[0]) for pair in moving[:-1]]
+    f2_rows = sum_pair(f2_pair, terms[0])
+    f2_half = fold_line(f2_rows, line_bits[1:])
+    [q_grad] = q_grad
+
+    cross_q_grad = after(cross_q_grad, *held, enc_f1, f2_rows)
     resid, dec_terms0, self_grad_full = rows_call(
         _backward_rows,
         4,
@@ -1496,22 +1843,15 @@
         dec_query, [dec_kv], dec_heads_grad, dec_lse, dec_heads_wide, dec_segs, [0], True
     )
     dec_proj_grad = [dec_q_grad, dec_kv_grad[0], dec_kv_grad[1]]
-    [dec_grad] = rows_call(
-        _last_rows,
-        5,
-        sum(dot_bt(g, w) for g, w in zip(dec_proj_grad, dec_in_w)).astype(HALF),
-        [resid],
-        [wide_rows],
-        False,
-    )
+    dec_part = sum(dot_bt(g, w) for g, w in zip(dec_proj_grad, dec_in_w)).astype(HALF)
     dec_left = [start_full] * 3 + [self_grad_full, self_full, cross_grad_full]
     dec_right = dec_proj_grad + [dec_heads, cross_q_grad, cross_heads]
     dec_small = [dot_ta(a, b) for a, b in zip(dec_left, dec_right)]
-    dec_small_half, dec_small_term = scatter_local(dec_small)
-    kv_grad = after(kv_grad, dec_small_term)
-
-    enc_grad, _, enc_terms0, *in_grads = collect(
-        [q_grad, kv_grad],
+    dec_small_rows, dec_small_term = scatter_local(dec_small)
+    kv_grad.append(sum_pair(moving[-1], dec_small_term, enc_ckv, f2_half))
+
+    enc_grad, enc_low, enc_terms0, *in_grads = collect(
+        [q_grad, *kv_grad],
         w_attn,
         4,
         (0, 1, 2),
@@ -1520,30 +1860,26 @@
         back_tokens,
         embed_low,
     )
-    enc_in, enc_out = fold_cores(*in_grads), fold_cores(*out_grads)
-    enc_attn_rows = fold_planes(jnp.concatenate([enc_in, enc_out], axis=1))
-    enc_ffn_half = jnp.concatenate([fold_chips(enc_f1, 1), fold_chips(enc_f2, 1)], axis=1)
-    enc_cross_half = fold_chips(enc_ckv, 2)
-    enc_terms = [enc_terms0, enc_terms1, enc_terms2]
-
-    def section(enc_half, dec_half):
-        keep = jnp.where(is_first, enc_half, dec_half)
-        got = swap(jnp.where(is_first, dec_half, enc_half), "pipe", 1)
-        pair = jnp.where(is_first, jnp.stack([keep, got], axis=2), jnp.stack([got, keep], axis=2))
-        return pair.reshape(*pair.shape[:2], -1)[None].astype(WIDE)
-
-    ffn_out_grad = section(enc_ffn_half, dec_ffn_half)
-    enc_attn_rows = after(enc_attn_rows, ffn_out_grad, enc_cross_half, dec_grad)
-    in_columns = enc_in.shape[1]
-    enc_attn_half = jnp.concatenate(
-        [fold_chips(enc_attn_rows[:, :in_columns], 3), fold_chips(enc_attn_rows[:, in_columns:], 1)], axis=1
-    )
-    attn_out = section(enc_attn_half, dec_small_half[:, :4])
-    cross_out = section(enc_cross_half, dec_small_half[:, 4:])
-    dec_terms = [dec_terms0, dec_terms1, dec_terms2]
-    norm_sums = reduce_norms(
-        jnp.stack([v[i] for i in range(2) for v in enc_terms]),
-        jnp.stack([v[i] for i in range(2) for v in dec_terms]),
+    attn_out, cross_out, ffn_out_grad, there, near_second, dec_grad, norm_sums = finish(
+        in_grads,
+        out_grads,
+        enc_f1,
+        f2_half,
+        enc_ckv,
+        dec_ffn_rows,
+        dec_small_rows,
+        enc_low,
+        dec_part,
+        resid,
+        [enc_terms0, enc_terms1, enc_terms2, dec_terms0, dec_terms1, dec_terms2],
+    )
+
+    attn_out, cross_out, ffn_out_grad = [
+        v.transpose(1, 0, 2)[None] for v in (attn_out, cross_out, ffn_out_grad)
+    ]
+    own_columns = width // (lax.axis_size("dp") * count)
+    norm_sums = lax.dynamic_slice_in_dim(
+        norm_sums[:6].reshape(3, 2, width), (lax.axis_index("dp") * count + place) * own_columns, own_columns, 2
     )
 
     dec_pair = jnp.stack([result, dec_grad.astype(HALF)])
@@ -1559,12 +1895,8 @@
         is_first, jnp.stack([own_grad, got_grad]), jnp.stack([got_grad, own_grad])
     )
 
-    enc_low = enc_grad.astype(HALF)
-    far_first = joint(enc_low[:, :half], [((1, t), (0, t ^ top_bit)) for t in chips])
-    far_second = joint(enc_low[:, half:], [((1, t), (1, t ^ top_bit)) for t in chips])
-    near_second = joint(enc_low[:, half:], [((0, t), (1, t)) for t in chips])
     here = jnp.where(is_first, enc_grad[:, :half], near_second.astype(WIDE))
-    there = jnp.where(is_first, far_first, far_second).astype(WIDE)
+    there = there.astype(WIDE)
     enc_input_grad = jnp.where(group == 0, jnp.stack([here, there]), jnp.stack([there, here]))
     return (
         dec_output,
@@ -1573,8 +1905,8 @@
         attn_out,
         cross_out,
         ffn_out_grad,
-        norm_sums[None, :3],
-        norm_sums[None, 3:],
+        norm_sums[None, :, 0],
+        norm_sums[None, :, 1],
     )
 
 

time: 1000 us -> 970 us (0.970); the launches traced: 1020 us -> 962 us
  waiting for transfers between devices: 131 us -> 89.6 us
  other arithmetic: 88.9 us -> 73.7 us
  starting transfers between devices: 46.1 us -> 61.3 us
    pallas_call x0 -> x1, Pallas kernels: none -> 85.2 us  [finish(): pl.pallas_call(partial(_finish_kernel, slot_bits(), count, planes), out_s...]
    pallas_call x6 -> x4, Pallas kernels: 219 us -> 142 us  [rows_call(): pl.pallas_call(partial(_rows_kernel, count, scatter, gather, middle, len(...]
    ppermute x37 -> x31, waiting for transfers between devices: 131 us -> 82.3 us  [swap(): lax.ppermute(value, axis, [(i, i ^ mask) for i in range(lax.axis_size(axi...]
    ppermute x37 -> x31, starting transfers between devices: 28.7 us -> 49.9 us  [swap(): lax.ppermute(value, axis, [(i, i ^ mask) for i in range(lax.axis_size(axi...]
    pallas_call x1, Pallas kernels: 40.5 us -> 20.9 us  [to_decoder(): pl.pallas_call(partial(_to_decoder_kernel, count), out_shape=[jax.ShapeDt...]
    pallas_call x3 -> x4, Pallas kernels: 58.2 us -> 62.5 us  [attend_back(): pl.pallas_call(partial(_attend_back_kernel, chunks, tq, tk, causal, own_d...]
    unnamed x181 -> x193, local copies, waits for them, and re-layouts: 19.7 us -> 23.3 us
    pallas_call x3 -> x4, Pallas kernels: 40.8 us -> 44.1 us  [attend(): pl.pallas_call(partial(_attend_kernel, chunks, tq, tk, causal), out_shape...]
  transfers between devices with their start and end apart: 52 -> 42, of which waited for: 19 -> 14; matrix products, arithmetic and copies ran while one was open for 14% -> 12% of each run, Pallas kernels for 35% -> 32%
where the time goes in v2:
time: 970 us; the launch traced here: 962 us
  Pallas kernels  628 us (65%)
  waiting for transfers between devices  89.6 us (9%)
  other arithmetic  73.7 us (8%)
  starting transfers between devices  61.3 us (6%)
  local copies, waits for them, and re-layouts  56.6 us (6%)
  matrix products  27.2 us (3%)
  between operations  25.5 us (3%)
    pallas_call x4, Pallas kernels, rows_call(): pl.pallas_call(partial(_rows_kernel, count, scatter, gather, middle, len(...  142 us
    pallas_call x1, Pallas kernels, gather_weights(): pl.pallas_call(partial(_gather_kernel, slot_bits(), count, planes), out_s...  98.7 us
    pallas_call x1, Pallas kernels, finish(): pl.pallas_call(partial(_finish_kernel, slot_bits(), count, planes), out_s...  85.2 us
    ppermute x31, waiting for transfers between devices, swap(): lax.ppermute(value, axis, [(i, i ^ mask) for i in range(lax.axis_size(axi...  82.3 us
    pallas_call x4, Pallas kernels, attend_back(): pl.pallas_call(partial(_attend_back_kernel, chunks, tq, tk, causal, own_d...  62.5 us
    pallas_call x3, Pallas kernels, collect(): pl.pallas_call(partial(_collect_kernel, kinds, use, wide, each, blocks, l...  51.8 us
    ppermute x31, starting transfers between devices, swap(): lax.ppermute(value, axis, [(i, i ^ mask) for i in range(lax.axis_size(axi...  49.9 us
    pallas_call x4, Pallas kernels, attend(): pl.pallas_call(partial(_attend_kernel, chunks, tq, tk, causal), out_shape...  44.1 us
  transfers between devices with their start and end apart: 42, of which 14 were waited for; matrix products, arithmetic and copies ran while one was open for 12% of the time, Pallas kernels for 32%

profile of v2, /device:TPU:0, one launch (start us, length us, event | category | flops | bytes accessed | tf_op | source)
XLA Modules:
  0.0 962.1 jit_solution(8334809777561344906)
XLA Ops:
  30.7 98.7 %gather_weights.1 = (bf16[2,1024,2048]{2,1,0:T(8,128)(2,1)}, bf16[2,1024,256]{2,1,0:T(8,128)(2,1)}, bf16[2,1024,1024]{2,1,0:T(8,128)(2,1)}, bf16[2,1024,512]{2,1...) custom-call(bf16[2,1024,512]{2,1,0:T(8,128)(2,1)} %maximum_maximum_f, ...), custom_call_target="tpu_custom_call" | custom-call | bytes 293601280 | tf_op jit(solution)/shard_map/gather_weights/pallas_call | solution.py:882
  134.4 12.5 %spread.3 = (bf16[512,1024]{1,0:T(8,128)(2,1)}, bf16[2,512,512]{2,1,0:T(8,128)(2,1)}, bf16[2,512,512]{2,1,0:T(8,128)(2,1)}) custom-call(bf16[512,1024]{1,0:T(8,128)(2,1)} %get-tuple-element.297.x.refs_4_, bf16[2,1024,2048]{2,1,0:T(8,128)(2,1)} %get-tuple-element.120.weights.refs_1_.refs_3_), custom_call_target="tpu_custom_call" | custom-call | flops 12884901888 | bytes 8388608 | tf_op jit(solution)/shard_map/spread/pallas_call | solution.py:989
  167.9 11.8 %collective-permute-done.2.refs_1_.refs_5_ = bf16[2,512,512]{2,1,0:T(8,128)(2,1)} collective-permute-done((bf16[2,512,512]{2,1,0:T(8,128)(2,1)}, bf16[2,512,512]{2,1,0:T(8,128)(2,1)}, u32[]{:S(2)}, u32[]{:S(2)}) %collective-permute-start.2) | collective-permute-done | bytes 1048608 | tf_op jit(solution)/shard_map/ppermute | solution.py:35
  193.0 14.9 %attend.4 = (f32[512,1024]{1,0:T(8,128)}, f32[8,8,512]{2,1,0:T(8,128)}) custom-call(s32[4]{0:T(128)} %convert_reduce_fusion.1.act, s32[8,512]{1,0:T(8,128)} %broadcast_in_dim.119.seg_q, s32[4,512,128]{2,1,0:T(8,128)} %broadcast_in_dim.120.seg_k, bf16[512,1024]{1,0:T(8,128)(2,1)} %get-tuple-element.121.q, ...), custom_call_target="tpu_custom_call" | custom-call | flops 25769803776 | bytes 5242880 | tf_op jit(solution)/shard_map/attend/pallas_call | solution.py:260
  213.5 14.9 %attend.6 = (f32[512,1024]{1,0:T(8,128)}, f32[8,8,512]{2,1,0:T(8,128)}) custom-call(s32[4]{0:T(128)} %convert_reduce_fusion.1.act, s32[8,512]{1,0:T(8,128)} %broadcast_in_dim.119.seg_q, s32[4,512,128]{2,1,0:T(8,128)} %broadcast_in_dim.120.seg_k, bf16[512,1024]{1,0:T(8,128)(2,1)} %get-tuple-element.121.q, ...), custom_call_target="tpu_custom_call", output_to_operand_aliasing={{0}: (12, {}), {1}: (13, {})} | custom-call | flops 25769803776 | bytes 5242880 | tf_op jit(solution)/shard_map/attend/pallas_call | solution.py:260
  229.7 22.7 %collective-permute-start.10 = (bf16[64,1024]{1,0:T(8,128)(2,1)S(1)}, bf16[64,1024]{1,0:T(8,128)(2,1)S(1)}, u32[]{:S(2)}, u32[]{:S(2)}) collective-permute-start(bf16[64,1024]{1,0:T(8,128)(2,1)S(1)} %get-tuple-element.337), channel_id=1, source_target_pairs={{0,3},{1,2},{2,1},{3,0},{4,7},{5,6},{6,5},{7,4},{8,11},{9,10},{10,... | collective-permute-start | bytes 393224 | tf_op jit(solution)/shard_map/ppermute | solution.py:35
  272.4 12.0 %collect.3 = (f32[512,1024]{1,0:T(8,128)}, bf16[512,1024]{1,0:T(8,128)(2,1)}, f32[512,1024]{1,0:T(8,128)}, f32[512,128]{1,0:T(8,128)}) custom-call(bf16[512,1024]{1,0:T(8,128)(2,1)} %convert_element_type.638.refs_0_, bf16[2,1024,2048]{2,1,0:T(8,128)(2,1)} %get-tuple-element.120.weights.refs_1_.refs_3_, f32[512,1024]{1,0:T(8,128)} %get-tuple-element.296.refs_2_, ...), custom_call_target="tpu_custom_call" | custom-call | flops 4294967296 | bytes 8388608 | tf_op jit(solution)/shard_map/collect/pallas_call | solution.py:1057
  284.5 21.2 %feed_forward.1 = (f32[512,1024]{1,0:T(8,128)}, bf16[512,1024]{1,0:T(8,128)(2,1)}, f32[512,1024]{1,0:T(8,128)}, f32[512,128]{1,0:T(8,128)}, bf16[512,4096]{1,0:T(8,128)(2,1)}, /*index=5*/bf16[512,4096]{1,0:T(8,128)(2,1)}) custom-call(bf16[512,1024]{1,0:T(8,128)(2,1)} %get-tuple-element.135.x, f32[512,1024]{1,0:T(8,128)} %get-tuple-element.136.resid, ...), custom_call_target="tpu_custom_call" | custom-call | flops 25769803776 | bytes 16777216 | tf_op jit(solution)/shard_map/feed_forward/pallas_call | solution.py:1153
  321.5 17.4 %to_encoder.2.q = bf16[8,256,128]{2,1,0:T(8,128)(2,1)} custom-call(bf16[2,256,128]{2,1,0:T(8,128)(2,1)} %pad_maximum_fusion.33.refs_0_), custom_call_target="tpu_custom_call" | custom-call | bytes 62914560 | tf_op jit(solution)/shard_map/to_encoder/pallas_call | solution.py:567
  365.2 20.9 %to_decoder.1 = (bf16[256,256]{1,0:T(8,128)(2,1)}, f32[2,256,128]{2,1,0:T(8,128)}, f32[2,8,256]{2,1,0:T(8,128)}) custom-call(bf16[8,256,128]{2,1,0:T(8,128)(2,1)} %get-tuple-element.150.refs_0_, f32[8,8,256]{2,1,0:T(8,128)} %get-tuple-element.151.refs_1_), custom_call_target="tpu_custom_call" | custom-call | bytes 62914560 | tf_op jit(solution)/shard_map/to_decoder/pallas_call | solution.py:648
  388.2 29.7 %forward_rows.1 = (f32[64,1024]{1,0:T(8,128)}, f32[64,1024]{1,0:T(8,128)}, f32[64,128]{1,0:T(8,128)}, bf16[256,1024]{1,0:T(8,128)(2,1)}) custom-call(bf16[256,1024]{1,0:T(8,128)(2,1)} %convolution_convert_fusion.9.refs_0_, f32[64,1024]{1,0:T(8,128)} %get-tuple-element.264.refs_1_, f32[1,1024]{1,0:T(1,128)} %get-tuple-element.352.refs_2_.refs_4_, ...), custom_call_target="tpu_custom_call" | custom-call | bytes 91750400 | tf_op jit(solution)/shard_map/forward_rows/pallas_call | solution.py:446
  421.5 29.7 %turn_rows.1 = (bf16[64,1024]{1,0:T(8,128)(2,1)}, f32[64,1024]{1,0:T(8,128)}, f32[8,1024]{1,0:T(8,128)}, bf16[256,1024]{1,0:T(8,128)(2,1)}) custom-call(bf16[256,1024]{1,0:T(8,128)(2,1)} %fusion.9.refs_0_, f32[64,1024]{1,0:T(8,128)} %get-tuple-element.155.refs_1_, f32[1,1024]{1,0:T(1,128)} %get-tuple-element.350.refs_2_, ...), custom_call_target="tpu_custom_call" | custom-call | bytes 91750400 | tf_op jit(solution)/shard_map/turn_rows/pallas_call | solution.py:446
  458.4 27.1 %backward_rows.2 = (f32[64,1024]{1,0:T(8,128)}, f32[8,1024]{1,0:T(8,128)}, bf16[256,1024]{1,0:T(8,128)(2,1)}) custom-call(bf16[256,1024]{1,0:T(8,128)(2,1)} %fusion.8.refs_0_, f32[64,1024]{1,0:T(8,128)} %get-tuple-element.158.refs_1_, f32[64,1024]{1,0:T(8,128)} %get-tuple-element.159.refs_2_, f32[64,128]{1,0:T(8,128)} %get-tuple-element.160.refs_3_, ...), custom_call_target="tpu_custom_call" | custom-call | bytes 91750400 | tf_op jit(solution)/shard_map/backward_rows/pallas_call | solution.py:446
  489.1 19.1 %to_encoder.3 = (bf16[8,256,128]{2,1,0:T(8,128)(2,1)}, f32[8,8,256]{2,1,0:T(8,128)}) custom-call(bf16[2,256,128]{2,1,0:T(8,128)(2,1)} %pad_maximum_fusion.34.refs_0_, f32[2,256,128]{2,1,0:T(8,128)} %get-tuple-element.162.refs_1_, f32[2,8,256]{2,1,0:T(8,128)} %get-tuple-element.163.refs_2_), custom_call_target="tpu_custom_call" | custom-call | bytes 62914560 | tf_op jit(solution)/shard_map/to_encoder/pallas_call | solution.py:567
  513.5 12.8 %attend_back.4 = (bf16[8,256,128]{2,1,0:T(8,128)(2,1)}, bf16[2,512,1024]{2,1,0:T(8,128)(2,1)}) custom-call(s32[1]{0:T(128)} %bitcast.30.act, s32[8,256]{1,0:T(8,128)} %broadcast_in_dim.116.seg_q, s32[1,512,128]{2,1,0:T(8,128)} %broadcast_in_dim.117.seg_k, bf16[8,256,128]{2,1,0:T(8,128)(2,1)} %to_encoder.2.q, bf16[2,512,1024]{2,1,0:T(8,128)(2,1)} %spread.4.refs_0_.refs_1_, ...), custom_call_target="tpu_custom_call" | custom-call | flops 10737418240 | bytes 10485760 | tf_op jit(solution)/shard_map/attend_back/pallas_call | solution.py:296
  527.8 16.8 %collect.4 = (f32[512,1024]{1,0:T(8,128)}, bf16[512,1024]{1,0:T(8,128)(2,1)}, f32[8,1024]{1,0:T(8,128)}, bf16[1024,1024]{1,0:T(8,128)(2,1)}, bf16[1024,1024]{1,0:T(8,128)(2,1)}) custom-call(bf16[2,512,1024]{2,1,0:T(8,128)(2,1)} %get-tuple-element.166.refs_0_, bf16[2,1024,1024]{2,1,0:T(8,128)(2,1)} %pad_maximum_fusion.weights.refs_1_, ...), custom_call_target="tpu_custom_call" | custom-call | flops 17179869184 | bytes 4194304 | tf_op jit(solution)/shard_map/collect/pallas_call | solution.py:1057
  547.7 31.7 %feed_forward_back.1 = (f32[512,1024]{1,0:T(8,128)}, bf16[512,1024]{1,0:T(8,128)(2,1)}, f32[8,1024]{1,0:T(8,128)}, bf16[1024,2048]{1,0:T(8,128)(2,1)}, bf16[1024...) custom-call(bf16[512,1024]{1,0:T(8,128)(2,1)} %get-tuple-element.135.x, ...), custom_call_target="tpu_custom_call" | custom-call | flops 34359738368 | bytes 33554432 | tf_op jit(solution)/shard_map/feed_forward_back/pallas_call | solution.py:1209
  624.5 22.3 %attend_back.5 = (bf16[512,1024]{1,0:T(8,128)(2,1)}, bf16[2,512,512]{2,1,0:T(8,128)(2,1)}, bf16[2,512,512]{2,1,0:T(8,128)(2,1)}, bf16[2,512,512]{2,1,0:T(8,128)(2,1)}, bf16[2,512,512]{2,1,0:T(8,128)(2,1)}) custom-call(s32[4]{0:T(128)} %convert_reduce_fusion.1.act, s32[8,512]{1,0:T(8,128)} %broadcast_in_dim.119.seg_q, ...), custom_call_target="tpu_custom_call" | custom-call | flops 42949672960 | bytes 10485760 | tf_op jit(solution)/shard_map/attend_back/pallas_call | solution.py:296
  654.1 23.0 %attend_back.6 = (bf16[512,1024]{1,0:T(8,128)(2,1)}, bf16[2,512,512]{2,1,0:T(8,128)(2,1)}, bf16[2,512,512]{2,1,0:T(8,128)(2,1)}, bf16[2,512,512]{2,1,0:T(8,128)(2,1)}, bf16[2,512,512]{2,1,0:T(8,128)(2,1)}) custom-call(s32[4]{0:T(128)} %convert_reduce_fusion.1.act, s32[8,512]{1,0:T(8,128)} %broadcast_in_dim.119.seg_q, ...), custom_call_target="tpu_custom_call", output_to_operand_aliasing={{0}: (15, {})} | custom-call | flops 42949672960 | bytes 10485760 | tf_op jit(solution)/shard_map/attend_back/pallas_call | solution.py:296
  691.4 29.3 %collective-permute-done.29 = bf16[256,1024]{1,0:T(8,128)(2,1)S(1)} collective-permute-done((bf16[256,1024]{1,0:T(8,128)(2,1)S(1)}, bf16[256,1024]{1,0:T(8,128)(2,1)S(1)}, u32[]{:S(2)}, u32[]{:S(2)}) %collective-permute-start.29) | collective-permute-done | bytes 524320 | tf_op jit(solution)/shard_map/ppermute | solution.py:35
  723.7 55.9 %backward_rows.3 = (f32[64,1024]{1,0:T(8,128)}, f32[8,1024]{1,0:T(8,128)}, bf16[256,1024]{1,0:T(8,128)(2,1)}) custom-call(bf16[256,1024]{1,0:T(8,128)(2,1)} %convolution_convert_fusion.8.refs_0_, f32[64,1024]{1,0:T(8,128)} %get-tuple-element.199.refs_1_, f32[64,1024]{1,0:T(8,128)} %get-tuple-element.265.refs_2_, f32[64,128]{1,0:T(8,128)} %broadcast_in_dim.133.refs_3_, ...), custom_call_target="tpu_custom_call" | custom-call | bytes 91750400 | tf_op jit(solution)/shard_map/backward_rows/pallas_call | solution.py:446
  811.4 17.0 %collective-permute-done.32 = bf16[256,512]{1,0:T(8,128)(2,1)} collective-permute-done((bf16[256,512]{1,0:T(8,128)(2,1)}, bf16[256,512]{1,0:T(8,128)(2,1)}, u32[]{:S(2)}, u32[]{:S(2)}) %collective-permute-start.32) | collective-permute-done | bytes 262176 | tf_op jit(solution)/shard_map/ppermute | solution.py:35
  833.7 23.0 %collect.5 = (f32[512,1024]{1,0:T(8,128)}, bf16[512,1024]{1,0:T(8,128)(2,1)}, f32[8,1024]{1,0:T(8,128)}, bf16[1024,1536]{1,0:T(8,128)(2,1)}, bf16[1024,1536]{1,0:T(8,128)(2,1)}) custom-call(bf16[512,1024]{1,0:T(8,128)(2,1)} %get-tuple-element.190.refs_0_, bf16[2,512,512]{2,1,0:T(8,128)(2,1)} %add_convert_fusion.8.refs_1_, ...), custom_call_target="tpu_custom_call" | custom-call | flops 25769803776 | bytes 8388608 | tf_op jit(solution)/shard_map/collect/pallas_call | solution.py:1057
  856.7 85.2 %finish.1 = (f32[4,256,256]{2,1,0:T(8,128)}, f32[2,256,256]{2,1,0:T(8,128)}, f32[2,256,1024]{2,1,0:T(8,128)}, bf16[512,512]{1,0:T(8,128)(2,1)}, bf16[512,512]{1,...) custom-call(bf16[1024,1536]{1,0:T(8,128)(2,1)} %get-tuple-element.208.refs_0_, ...), custom_call_target="tpu_custom_call" | custom-call | bytes 209715200 | tf_op jit(solution)/shard_map/finish/pallas_call | solution.py:1488
  (434 shorter events, 266.8 us)
Async XLA Ops:
  7.2 221.3 %all-gather.3.cloned.1.call-start = ((), (), s32[]{:S(2)}) async-start(), calls=%async_computation.5 | async-start | bytes 7864320 | tf_op jit(solution)/shard_map/all_gather | solution.py:897
  129.5 154.9 %all-gather.5.cloned.1.call-start = ((), (), s32[]{:S(2)}) async-start(), calls=%async_computation.6 | async-start | bytes 1966080 | tf_op jit(solution)/shard_map/all_gather | solution.py:897
  146.9 44.2 %collective-permute-start.3 = (bf16[2,512,512]{2,1,0:T(8,128)(2,1)}, bf16[2,512,512]{2,1,0:T(8,128)(2,1)}, u32[]{:S(2)}, u32[]{:S(2)}) collective-permute-start(bf16[2,512,512]{2,1,0:T(8,128)(2,1)} %get-tuple-element.125.refs_0_.refs_4_), channel_id=1, source_target_pairs={{0,16},{16,0},{1,17},{17,1},{2,18},{18,2},{3,19},{19,3},{4,20},{20... | collective-permute-start | bytes 3145736 | tf_op jit(solution)/shard_map/ppermute | solution.py:35
  153.4 26.3 %collective-permute-start.2 = (bf16[2,512,512]{2,1,0:T(8,128)(2,1)}, bf16[2,512,512]{2,1,0:T(8,128)(2,1)}, u32[]{:S(2)}, u32[]{:S(2)}) collective-permute-start(bf16[2,512,512]{2,1,0:T(8,128)(2,1)} %get-tuple-element.125.refs_0_.refs_4_), channel_id=1, source_target_pairs={{0,1},{1,0},{2,3},{3,2},{4,5},{5,4},{6,7},{7,6},{8,9},{9,8},{10,11... | collective-permute-start | bytes 3145736 | tf_op jit(solution)/shard_map/ppermute | solution.py:35
  153.4 54.5 %collective-permute-start.1 = (bf16[2,512,512]{2,1,0:T(8,128)(2,1)}, bf16[2,512,512]{2,1,0:T(8,128)(2,1)}, u32[]{:S(2)}, u32[]{:S(2)}) collective-permute-start(bf16[2,512,512]{2,1,0:T(8,128)(2,1)} %get-tuple-element.132.refs_0_.refs_4_), channel_id=1, source_target_pairs={{0,1},{1,0},{2,3},{3,2},{4,5},{5,4},{6,7},{7,6},{8,9},{9,8},{10,11... | collective-permute-start | bytes 3145736 | tf_op jit(solution)/shard_map/ppermute | solution.py:35
  228.5 55.9 %collective-permute-start.7 = (bf16[1024,3072]{1,0:T(8,128)(2,1)}, bf16[1024,3072]{1,0:T(8,128)(2,1)}, u32[]{:S(2)}, u32[]{:S(2)}) collective-permute-start(bf16[1024,3072]{1,0:T(8,128)(2,1)} %all-gather.3.cloned.1.call-done.refs_1_.refs_4_), channel_id=1, source_target_pairs={{0,16},{16,0},{1,17},{17,1},{2,18},{18,2},{3,19},{19,3},{4,20},{20... | collective-permute-start | bytes 18874376 | tf_op jit(solution)/shard_map/ppermute | solution.py:35
  228.9 318.8 %reduce-scatter.6.cloned.1.call-start = ((), (), s32[]{:S(2)}) async-start(), calls=%async_computation.7 | async-start | bytes 2621440 | tf_op jit(solution)/shard_map/reduce_scatter | solution.py:912
  229.7 41.4 %collective-permute-start.10 = (bf16[64,1024]{1,0:T(8,128)(2,1)S(1)}, bf16[64,1024]{1,0:T(8,128)(2,1)S(1)}, u32[]{:S(2)}, u32[]{:S(2)}) collective-permute-start(bf16[64,1024]{1,0:T(8,128)(2,1)S(1)} %get-tuple-element.337), channel_id=1, source_target_pairs={{0,3},{1,2},{2,1},{3,0},{4,7},{5,6},{6,5},{7,4},{8,11},{9,10},{10,... | collective-permute-start | bytes 393224 | tf_op jit(solution)/shard_map/ppermute | solution.py:35
  252.4 18.7 %collective-permute-start.9 = (bf16[64,1024]{1,0:T(8,128)(2,1)S(1)}, bf16[64,1024]{1,0:T(8,128)(2,1)}, u32[]{:S(2)}, u32[]{:S(2)}) collective-permute-start(bf16[64,1024]{1,0:T(8,128)(2,1)S(1)} %get-tuple-element.338), channel_id=1, source_target_pairs={{0,2},{1,3},{2,0},{3,1},{4,6},{5,7},{6,4},{7,5},{8,10},{9,11},{10,... | collective-permute-start | bytes 393224 | tf_op jit(solution)/shard_map/ppermute | solution.py:35
  284.4 54.5 %collective-permute-start.14 = (bf16[1024,768]{1,0:T(8,128)(2,1)}, bf16[1024,768]{1,0:T(8,128)(2,1)S(1)}, u32[]{:S(2)}, u32[]{:S(2)}) collective-permute-start(bf16[1024,768]{1,0:T(8,128)(2,1)} %all-gather.5.cloned.1.call-done), channel_id=1, source_target_pairs={{0,16},{16,0},{1,17},{17,1},{2,18},{18,2},{3,19},{19,3},{4,20},{20... | collective-permute-start | bytes 4718600 | tf_op jit(solution)/shard_map/ppermute | solution.py:35
  456.4 31.4 %collective-permute-start.15 = (f32[3,1024]{1,0:T(4,128)S(1)}, f32[3,1024]{1,0:T(4,128)S(1)}, u32[]{:S(2)}, u32[]{:S(2)}) collective-permute-start(f32[3,1024]{1,0:T(4,128)S(1)} %fusion.20), channel_id=1, source_target_pairs={{0,1},{1,0},{2,3},{3,2},{4,5},{5,4},{6,7},{7,6},{8,9},{9,8},{10,11... | collective-permute-start | bytes 36872 | tf_op jit(solution)/shard_map/ppermute | solution.py:35
  487.7 20.6 %collective-permute-start.17 = (bf16[1024,1024]{1,0:T(8,128)(2,1)S(1)}, bf16[1024,1024]{1,0:T(8,128)(2,1)S(1)}, u32[]{:S(2)}, u32[]{:S(2)}) collective-permute-start(bf16[1024,1024]{1,0:T(8,128)(2,1)S(1)} %pad_maximum_fusion.3), channel_id=1, source_target_pairs={{0,16},{16,0},{1,17},{17,1},{2,18},{18,2},{3,19},{19,3},{4,20},{20... | collective-permute-start | bytes 6291464 | tf_op jit(solution)/shard_map/ppermute | solution.py:35
  487.9 20.3 %collective-permute-start.16 = (f32[3,1024]{1,0:T(4,128)S(1)}, f32[3,1024]{1,0:T(4,128)S(1)}, u32[]{:S(2)}, u32[]{:S(2)}) collective-permute-start(f32[3,1024]{1,0:T(4,128)S(1)} %add.547), channel_id=1, source_target_pairs={{0,16},{16,0},{1,17},{17,1},{2,18},{18,2},{3,19},{19,3},{4,20},{20... | collective-permute-start | bytes 36872 | tf_op jit(solution)/shard_map/ppermute | solution.py:35
  510.4 174.9 %reduce-scatter.10.cloned.1.call-start = ((), (), s32[]{:S(2)}) async-start(), calls=%async_computation.9 | async-start | bytes 5242880 | tf_op jit(solution)/shard_map/reduce_scatter | solution.py:912
  526.4 18.3 %collective-permute-start.18 = (bf16[8,256,128]{2,1,0:T(8,128)(2,1)}, bf16[8,256,128]{2,1,0:T(8,128)(2,1)S(1)}, u32[]{:S(2)}, u32[]{:S(2)}) collective-permute-start(bf16[8,256,128]{2,1,0:T(8,128)(2,1)} %get-tuple-element.169), channel_id=1, source_target_pairs={{16,0},{17,1},{2,18},{3,19},{20,4},{21,5},{6,22},{7,23},{24,8},{25... | collective-permute-start | bytes 1572872 | tf_op jit(solution)/shard_map/ppermute | solution.py:40
  593.0 127.9 %reduce-scatter.8.cloned.1.call-start = ((), (), s32[]{:S(2)}) async-start(), calls=%async_computation.8 | async-start | bytes 5242880 | tf_op jit(solution)/shard_map/reduce_scatter | solution.py:912
  593.1 24.9 %collective-permute-start.22 = (bf16[1024,2048]{1,0:T(8,128)(2,1)}, bf16[1024,2048]{1,0:T(8,128)(2,1)}, u32[]{:S(2)}, u32[]{:S(2)}) collective-permute-start(bf16[1024,2048]{1,0:T(8,128)(2,1)} %get-tuple-element.180), channel_id=1, source_target_pairs={{0,16},{16,0},{1,17},{17,1},{2,18},{18,2},{3,19},{19,3},{4,20},{20... | collective-permute-start | bytes 12582920 | tf_op jit(solution)/shard_map/ppermute | solution.py:35
  624.5 205.7 %reduce-scatter.12.cloned.1.call-start = ((), (), s32[]{:S(2)}) async-start(), calls=%async_computation.10 | async-start | bytes 2621440 | tf_op jit(solution)/shard_map/reduce_scatter | solution.py:912
  647.4 32.4 %collective-permute-start.31 = (bf16[1024,1024]{1,0:T(8,128)(2,1)}, bf16[1024,1024]{1,0:T(8,128)(2,1)}, u32[]{:S(2)}, u32[]{:S(2)}) collective-permute-start(bf16[1024,1024]{1,0:T(8,128)(2,1)} %get-tuple-element.205), channel_id=1, source_target_pairs={{0,16},{16,0},{1,17},{17,1},{2,18},{18,2},{3,19},{19,3},{4,20},{20... | collective-permute-start | bytes 6291464 | tf_op jit(solution)/shard_map/ppermute | solution.py:35
  683.8 172.9 %reduce-scatter.14.cloned.1.call-start = ((), (), s32[]{:S(2)}) async-start(), calls=%async_computation.11 | async-start | bytes 1966080 | tf_op jit(solution)/shard_map/reduce_scatter | solution.py:912
  683.8 115.6 %collective-permute-start.26 = (bf16[2,512,512]{2,1,0:T(8,128)(2,1)}, bf16[2,512,512]{2,1,0:T(8,128)(2,1)}, u32[]{:S(2)}, u32[]{:S(2)}) collective-permute-start(bf16[2,512,512]{2,1,0:T(8,128)(2,1)} %add_convert_fusion.9), channel_id=1, source_target_pairs={{0,1},{1,0},{2,3},{3,2},{4,5},{5,4},{6,7},{7,6},{8,9},{9,8},{10,11... | collective-permute-start | bytes 3145736 | tf_op jit(solution)/shard_map/ppermute | solution.py:35
  686.6 34.1 %collective-permute-start.29 = (bf16[256,1024]{1,0:T(8,128)(2,1)S(1)}, bf16[256,1024]{1,0:T(8,128)(2,1)S(1)}, u32[]{:S(2)}, u32[]{:S(2)}) collective-permute-start(bf16[256,1024]{1,0:T(8,128)(2,1)S(1)} %get-tuple-element.300), channel_id=1, source_target_pairs={{0,1},{1,0},{2,3},{3,2},{4,5},{5,4},{6,7},{7,6},{8,9},{9,8},{10,11... | collective-permute-start | bytes 1572872 | tf_op jit(solution)/shard_map/ppermute | solution.py:35
  797.4 32.8 %collective-permute-start.33 = (bf16[2,512,512]{2,1,0:T(8,128)(2,1)}, bf16[2,512,512]{2,1,0:T(8,128)(2,1)}, u32[]{:S(2)}, u32[]{:S(2)}) collective-permute-start(bf16[2,512,512]{2,1,0:T(8,128)(2,1)} %add_convert_fusion.6), channel_id=1, source_target_pairs={{0,1},{1,0},{2,3},{3,2},{4,5},{5,4},{6,7},{7,6},{8,9},{9,8},{10,11... | collective-permute-start | bytes 3145736 | tf_op jit(solution)/shard_map/ppermute | solution.py:35
  802.6 25.8 %collective-permute-start.32 = (bf16[256,512]{1,0:T(8,128)(2,1)}, bf16[256,512]{1,0:T(8,128)(2,1)}, u32[]{:S(2)}, u32[]{:S(2)}) collective-permute-start(bf16[256,512]{1,0:T(8,128)(2,1)} %split.17), channel_id=1, source_target_pairs={{0,2},{1,3},{2,0},{3,1},{4,6},{5,7},{6,4},{7,5},{8,10},{9,11},{10,... | collective-permute-start | bytes 786440 | tf_op jit(solution)/shard_map/ppermute | solution.py:35
  (102 other events, 1408.6 us)
Sparse Core Ops, SparseCore 0:
  129.6 75.6 all-gather.2
  229.0 50.3 all-gather.4
  510.5 37.1 reduce-scatter.5
  593.1 52.8 reduce-scatter.9
  648.9 52.6 reduce-scatter.7
  705.3 41.8 reduce-scatter.11
  810.4 28.1 reduce-scatter.13

commit v3 on v2

--- a/solution.py
+++ b/solution.py
@@ -15,7 +15,7 @@
 WIDE = jnp.float32
 VMEM_LIMIT = 56 << 20
 MESH = pl.DeviceIdType.MESH
-TILE_Q = 512
+TILE_Q = 256
 TILE_K = 512
 
 
@@ -132,19 +132,22 @@
             qs = q[r, :] * jnp.asarray(HEAD**-0.5, HALF)
             kk, vt = keys[c][s, :], values[c][s, :].T
             ok = _allowed(seg_k[c, s, 0:1], seg_q[0:1, r], causal, col0, row0)
-            for h in range(2):
-                qh = jnp.where(_head_lanes(qs.shape, h), qs, jnp.zeros_like(qs))
-                sc = jnp.where(ok, dot_bt(kk, qh), NEGATIVE)
-                before = top[h : h + 1, r]
-                after = jnp.maximum(before, jnp.max(sc, axis=0, keepdims=True))
-                pr = jnp.exp(sc - after).astype(HALF)
-                fade = jnp.exp(before - after)
-                total[h : h + 1, r] = total[h : h + 1, r] * fade + jnp.sum(
-                    pr.astype(WIDE), axis=0, keepdims=True
-                )
+            ones = jnp.ones((8, vt.shape[1]), HALF)
+            heads = range(2)
+            raw = [
+                dot_bt(kk, jnp.where(_head_lanes(qs.shape, h), qs, jnp.zeros_like(qs))) for h in heads
+            ]
+            scores = [jnp.where(ok, sc, NEGATIVE) for sc in raw]
+            before = [top[h : h + 1, r] for h in heads]
+            after_ = [jnp.maximum(b, jnp.max(sc, axis=0, keepdims=True)) for b, sc in zip(before, scores)]
+            terms = [jnp.exp(sc - a).astype(HALF) for sc, a in zip(scores, after_)]
+            for h in heads:
+                fade = jnp.exp(before[h] - after_[h])
                 span = slice(h * HEAD, (h + 1) * HEAD)
-                acc[span, r] = acc[span, r] * fade + dot(vt[span, :], pr)
-                top[h : h + 1, r] = after
+                sums = dot(jnp.concatenate([vt[span, :], ones], axis=0), terms[h])
+                acc[span, r] = acc[span, r] * fade + sums[:HEAD]
+                total[h : h + 1, r] = total[h : h + 1, r] * fade + sums[HEAD : HEAD + 1]
+                top[h : h + 1, r] = after_[h]
 
         _tile_loop(act, chunks, c, nq, nk, tq, tk, tile)
     count = total[...]
@@ -181,18 +184,21 @@
             go = grad_out[r, :]
             kk, vv = keys[c][s, :], values[c][s, :]
             ok = _allowed(seg_k[c, s, 0:1], seg_q[0:1, r], causal, col0, row0)
-            for h in range(2):
-                mine, mine_k = _head_lanes(qs.shape, h), _head_lanes(kk.shape, h)
-                qh = jnp.where(mine, qs, jnp.zeros_like(qs))
-                gh = jnp.where(mine, go, jnp.zeros_like(go))
-                kh = jnp.where(mine_k, kk if own_delta else extra[s, :], jnp.zeros_like(kk))
-                sc = jnp.where(ok, dot_bt(kk, qh), NEGATIVE)
-                pr = jnp.exp(sc - stats[0, h : h + 1, r])
-                ds = (pr * (dot_bt(vv, gh) - delta[h : h + 1, r])).astype(HALF)
-                pr = pr.astype(HALF)
-                dq[r, :] = dq[r, :] + dot_ta(ds, kh)
-                dkv[0, s, :] = dkv[0, s, :] + dot(ds, qh)
-                dkv[1, s, :] = dkv[1, s, :] + dot(pr, gh)
+            heads = range(2)
+            mine = [_head_lanes(qs.shape, h) for h in heads]
+            mine_k = [_head_lanes(kk.shape, h) for h in heads]
+            from_keys = kk if own_delta else extra[s, :]
+            qh = [jnp.where(m, qs, jnp.zeros_like(qs)) for m in mine]
+            gh = [jnp.where(m, go, jnp.zeros_like(go)) for m in mine]
+            kh = [jnp.where(m, from_keys, jnp.zeros_like(kk)) for m in mine_k]
+            raw = [dot_bt(kk, v) for v in qh]
+            grads = [dot_bt(vv, v) for v in gh]
+            pr = [jnp.exp(jnp.where(ok, raw[h], NEGATIVE) - stats[0, h : h + 1, r]) for h in heads]
+            ds = [(pr[h] * (grads[h] - delta[h : h + 1, r])).astype(HALF) for h in heads]
+            pr = [v.astype(HALF) for v in pr]
+            dkv[1, s, :] += dot(pr[0], gh[0]) + dot(pr[1], gh[1])
+            dkv[0, s, :] += dot(ds[0], qh[0]) + dot(ds[1], qh[1])
+            dq[r, :] += dot_ta(ds[0], kh[0]) + dot_ta(ds[1], kh[1])
 
         _tile_loop(act, chunks, c, nq, nk, tq, tk, tile)
         grad_kv[c][...] = dkv[...].astype(grad_kv[c].dtype)
@@ -901,13 +907,6 @@
     return (mine.astype(WIDE) + swap(other, "pipe", 1).astype(WIDE)).astype(HALF)
 
 
-def fold_line(rows, bits):
-    for bit in bits:
-        keep, send = jnp.split(rows, 2, axis=1)
-        rows = (keep.astype(WIDE) + swap(send, "tensor", bit).astype(WIDE)).astype(HALF)
-    return rows
-
-
 def fold_planes(term):
     return lax.psum_scatter(term, "dp", scatter_dimension=0, tiled=True)
 
@@ -1234,14 +1233,14 @@
 
 
 def _finish_kernel(bits, count, planes, *refs):
-    in_mine, out_mine, in_other, out_other, f1, f2, ckv, dec_ffn, dec_small, tokens, part, resid = refs[:12]
-    norm_terms, refs = refs[12:18], refs[18:]
-    attn_out, cross_out, ffn_out, far, near, dec_grad, norm_sum = refs[:7]
-    land_in, land_out, term, *refs = refs[7:]
+    in_mine, out_mine, in_other, out_other, f1, f2, ckv, dec_ffn, dec_small, tokens = refs[:10]
+    norm_terms, refs = refs[10:16], refs[16:]
+    attn_out, cross_out, ffn_out, far, near, norm_sum = refs[:6]
+    land_in, land_out, term, *refs = refs[6:]
     n_steps = planes.bit_length() - 1
     land_planes, refs = refs[:n_steps], refs[n_steps:]
-    folded, landed, refs = refs[:3], refs[3:6], refs[6:]
-    enc_ffn, enc_small, got_ffn, got_small, land_dec, norm_other, norm_land, send_sem, recv_sem = refs
+    folded, landed, refs = refs[:4], refs[4:8], refs[8:]
+    enc_ffn, enc_small, got_ffn, got_small, norm_other, norm_land, send_sem, recv_sem = refs
     core, place, me = lax.axis_index("pipe"), lax.axis_index("dp"), lax.axis_index("tensor")
     sibling = {"pipe": 1 - core}
     line = {s: {"tensor": _differ(me, s, count)} for s in range(1, count)}
@@ -1312,7 +1311,7 @@
             source = c["source"].at[:, pl.ds(kept, kept)]
             c["now"] = [push(source, land.at[:, pl.ds(offset, kept)], line[c["bits"].pop(0)])]
 
-    chains = [chain(f1, 0), chain(ckv, 1)]
+    chains = [chain(f2, 0), chain(f1, 1), chain(ckv, 2)]
     advance(chains[0])
 
     half = tokens.shape[1] // 2
@@ -1328,15 +1327,6 @@
     @pl.when(core == 0)
     def _():
         _send(tokens.at[:, pl.ds(half, half)], near, send_sem.at[near_sem], recv_sem.at[near_sem], sibling)
-
-    rows = dec_grad.shape[0]
-
-    def rows_of_chip(chip):
-        return pl.ds(pl.multiple_of(chip * rows, rows), rows)
-
-    dec_sent = [
-        push(part.at[rows_of_chip(peer["tensor"])], land_dec.at[s - 1], peer) for s, peer in line.items()
-    ]
 
     wait(to_core)
     block = in_mine.shape[0] // planes
@@ -1389,13 +1379,13 @@
     for_attn = []
     for j in range(n_steps):
         for r in range(2):
-            advance(chains[min(2 * j + r, 1)])
+            advance(chains[min(2 * j + r, 2)])
             advance_norms()
             plane_finish(moving[r], r)
             if j + 1 < n_steps:
                 moving[r] = plane_start(j + 1, r)
             else:
-                for_attn.append(chain(term.at[rows_of(0, r)], 2, pl.ds(r * piece, piece)))
+                for_attn.append(chain(term.at[rows_of(0, r)], 3, pl.ds(r * piece, piece)))
                 advance(for_attn[-1])
     while any(c["now"] or c["bits"] for c in chains + for_attn):
         for c in for_attn + chains:
@@ -1405,10 +1395,10 @@
         advance_norms()
 
     size = [fold.shape[1] * 2 // count for fold in folded]
-    enc_ffn[:, : size[0]] = folded[0][:, : size[0]]
-    enc_ffn[:, size[0] :] = f2[...]
-    enc_small[:, : size[2]] = folded[2][:, : size[2]]
-    enc_small[:, size[2] :] = folded[1][:, : size[1]]
+    enc_ffn[:, : size[1]] = folded[1][:, : size[1]]
+    enc_ffn[:, size[1] :] = folded[0][:, : size[0]]
+    enc_small[:, : size[3]] = folded[3][:, : size[3]]
+    enc_small[:, size[3] :] = folded[2][:, : size[2]]
     swap_sem = [number(), number()]
 
     @pl.when(core == 0)
@@ -1421,11 +1411,6 @@
         _send(enc_ffn, got_ffn, send_sem.at[swap_sem[0]], recv_sem.at[swap_sem[0]], sibling)
         _send(enc_small, got_small, send_sem.at[swap_sem[1]], recv_sem.at[swap_sem[1]], sibling)
 
-    wait(dec_sent)
-    total = part[rows_of_chip(me), :].astype(WIDE) + resid[...]
-    for s in range(count - 1):
-        total = total + land_dec[s].astype(WIDE)
-    dec_grad[...] = total
     for i, (mine, got) in enumerate(((enc_ffn, got_ffn), (enc_small, got_small))):
         pltpu.make_async_copy(mine, got, send_sem.at[swap_sem[i]]).wait()
         pltpu.make_async_copy(mine, got, recv_sem.at[swap_sem[i]]).wait()
@@ -1461,16 +1446,16 @@
         pltpu.make_async_copy(near, near, send_sem.at[near_sem]).wait()
 
 
-def finish(in_grads, out_grads, f1, f2, ckv, dec_ffn, dec_small, tokens, part, resid, norm_terms):
+def finish(in_grads, out_grads, f1, f2, ckv, dec_ffn, dec_small, tokens, norm_terms):
     count, planes = lax.axis_size("tensor"), lax.axis_size("dp")
     depth = in_grads[0].shape[0]
     rows = depth // planes
     attn_columns = in_grads[0].shape[1] + out_grads[0].shape[1]
     wide = 2 * dec_small.shape[1] // 6
     vmem = pl.BlockSpec(memory_space=pltpu.VMEM)
-    operands = (in_grads[0], out_grads[0], in_grads[1], out_grads[1], f1, f2, ckv, dec_ffn, dec_small, tokens, part, resid)
+    operands = (in_grads[0], out_grads[0], in_grads[1], out_grads[1], f1, f2, ckv, dec_ffn, dec_small, tokens)
     operands += tuple(norm_terms)
-    lines = [f1.shape[1], ckv.shape[1], attn_columns]
+    lines = [f2.shape[1], f1.shape[1], ckv.shape[1], attn_columns]
     scratch = [in_grads[0].shape, out_grads[0].shape, (depth, attn_columns)]
     blocks = planes // 2
     while blocks >= 1:
@@ -1479,12 +1464,11 @@
     scratch += [(rows, c // 2) for c in lines]
     scratch += [(rows, c - c // count) for c in lines]
     scratch += [dec_ffn.shape, dec_small.shape] * 2
-    scratch.append((count - 1, *resid.shape))
     norm_steps = count.bit_length() + planes.bit_length() - 1
     norm_shapes = [norm_terms[0].shape, (norm_steps, *norm_terms[0].shape)]
     token_piece = ((tokens.shape[0], tokens.shape[1] // 2), HALF)
     outs = [((4, rows, wide), WIDE), ((2, rows, wide), WIDE), ((2, rows, dec_ffn.shape[1]), WIDE)]
-    outs += [token_piece, token_piece, (resid.shape, WIDE), (norm_terms[0].shape, WIDE)]
+    outs += [token_piece, token_piece, (norm_terms[0].shape, WIDE)]
     return pl.pallas_call(
         partial(_finish_kernel, slot_bits(), count, planes),
         out_shape=[jax.ShapeDtypeStruct(*o) for o in outs],
@@ -1634,14 +1618,14 @@
         )
     heads_wide, lse = attended
 
-    def sum_to_owner(term):
-        total = after(start, lse)
+    def sum_to_owner(term, resid, *earlier):
+        total = after(resid, *earlier)
         for s in range(count):
             rows = lax.dynamic_slice_in_dim(term, (place ^ s) * dec_span, dec_span, 0)
             total = total + (swap(rows, "tensor", s) if s else rows).astype(WIDE)
         return total
 
-    self_norm, self_normed, self_scale = norm_forward(sum_to_owner(term), dg[0:1], db[0:1])
+    self_norm, self_normed, self_scale = norm_forward(sum_to_owner(term, start, lse), dg[0:1], db[0:1])
     self_scale = jnp.broadcast_to(self_scale, (dec_span, LANES))
     self_low = self_norm.astype(HALF)
     self_rows = [swap(self_low, "tensor", s) if s else self_low for s in range(count)]
@@ -1784,17 +1768,15 @@
         mine_ffn,
         other_ffn,
     )
-    f2_term = fold_cores(*ffn_grads[2:])
+    heads_grad, *out_grads = spread(resid_low, w_attn, 4, (3,), heads)
+    f2_term = fold_cores(after(ffn_grads[2], heads_grad), ffn_grads[3])
     enc_f2 = fold_planes(f2_term)
     f1_term = fold_cores(*ffn_grads[:2])
     enc_f1 = fold_planes(f1_term)
-    heads_grad, *out_grads = spread(after(resid_low, cross_q_grad), w_attn, 4, (3,), heads)
-    line_bits = list(reversed(slot_bits()))
-
     def join(a, b):
         return (a.astype(WIDE) + b.astype(WIDE)).astype(HALF)
 
-    grads_in = after(heads_grad, f1_term, f2_term)
+    grads_in = after(heads_grad, f1_term, f2_term, cross_q_grad)
     def send_chips(held):
         pairs, bit = [(v,) for v in held], top_bit // 2
         while bit >= 1:
@@ -1820,17 +1802,12 @@
             into=q_grad,
         )
         q_grad = (q_grad,)
-        if n == 0:
-            keep, send = jnp.split(after(enc_f2, terms[0]), 2, axis=1)
-            f2_pair = (keep, swap(send, "tensor", line_bits[0]))
         held = [join(a, swap(b, "pipe", 1)) for a, b in zip(terms[:top_bit], terms[top_bit:])]
         moving.append(send_chips(held))
     kv_grad = [sum_pair(pair, terms[0]) for pair in moving[:-1]]
-    f2_rows = sum_pair(f2_pair, terms[0])
-    f2_half = fold_line(f2_rows, line_bits[1:])
     [q_grad] = q_grad
 
-    cross_q_grad = after(cross_q_grad, *held, enc_f1, f2_rows)
+    cross_q_grad = after(cross_q_grad, *held, enc_f1)
     resid, dec_terms0, self_grad_full = rows_call(
         _backward_rows,
         4,
@@ -1838,7 +1815,8 @@
         [resid, self_normed, self_scale, dg[0:1]],
         [wide_rows, norm_terms],
     )
-    dec_heads_grad = dot(self_grad_full, dec_attn[3]).astype(HALF)
+    kv_grad.append(sum_pair(moving[-1], self_grad_full))
+    dec_heads_grad = dot(after(self_grad_full, kv_grad[-1]), dec_attn[3]).astype(HALF)
     dec_q_grad, [dec_kv_grad] = attend_back(
         dec_query, [dec_kv], dec_heads_grad, dec_lse, dec_heads_wide, dec_segs, [0], True
     )
@@ -1848,7 +1826,7 @@
     dec_right = dec_proj_grad + [dec_heads, cross_q_grad, cross_heads]
     dec_small = [dot_ta(a, b) for a, b in zip(dec_left, dec_right)]
     dec_small_rows, dec_small_term = scatter_local(dec_small)
-    kv_grad.append(sum_pair(moving[-1], dec_small_term, enc_ckv, f2_half))
+    kv_grad[-1] = after(kv_grad[-1], dec_small_term, enc_ckv)
 
     enc_grad, enc_low, enc_terms0, *in_grads = collect(
         [q_grad, *kv_grad],
@@ -1860,17 +1838,16 @@
         back_tokens,
         embed_low,
     )
-    attn_out, cross_out, ffn_out_grad, there, near_second, dec_grad, norm_sums = finish(
+    dec_grad = sum_to_owner(dec_part, resid, enc_low)
+    attn_out, cross_out, ffn_out_grad, there, near_second, norm_sums = finish(
         in_grads,
         out_grads,
         enc_f1,
-        f2_half,
+        enc_f2,
         enc_ckv,
         dec_ffn_rows,
         dec_small_rows,
-        enc_low,
-        dec_part,
-        resid,
+        after(enc_low, dec_grad),
         [enc_terms0, enc_terms1, enc_terms2, dec_terms0, dec_terms1, dec_terms2],
     )
 

time: 970 us -> 942 us (0.971)
  waiting for transfers between devices: 89.6 us -> 37.4 us
  Pallas kernels: 628 us -> 644 us
  starting transfers between devices: 61.3 us -> 77.3 us
    ppermute x31 -> x32, waiting for transfers between devices: 82.3 us -> 27.3 us  [swap(): lax.ppermute(value, axis, [(i, i ^ mask) for i in range(lax.axis_size(axi...]
    ppermute x31 -> x32, starting transfers between devices: 49.9 us -> 65.7 us  [swap(): lax.ppermute(value, axis, [(i, i ^ mask) for i in range(lax.axis_size(axi...]
    pallas_call x4, Pallas kernels: 142 us -> 156 us  [rows_call(): pl.pallas_call(partial(_rows_kernel, count, scatter, gather, middle, len(...]
    pallas_call x1, Pallas kernels: 85.2 us -> 95.5 us  [finish(): pl.pallas_call(partial(_finish_kernel, slot_bits(), count, planes), out_s...]
    unnamed x193 -> x173, local copies, waits for them, and re-layouts: 23.3 us -> 24.6 us
  transfers between devices with their start and end apart: 42 -> 43, of which waited for: 14 -> 11; matrix products, arithmetic and copies ran while one was open for 12% -> 10% of each run, Pallas kernels for 32% -> 33%
where the time goes in v3:
time: 942 us; the launch traced here: 932 us
  Pallas kernels  644 us (68%)
  starting transfers between devices  77.3 us (8%)
  other arithmetic  68.7 us (7%)
  local copies, waits for them, and re-layouts  54.9 us (6%)
  waiting for transfers between devices  37.4 us (4%)
  between operations  25.8 us (3%)
  matrix products  24.5 us (3%)
    pallas_call x4, Pallas kernels, rows_call(): pl.pallas_call(partial(_rows_kernel, count, scatter, gather, middle, len(...  156 us
    pallas_call x1, Pallas kernels, gather_weights(): pl.pallas_call(partial(_gather_kernel, slot_bits(), count, planes), out_s...  98.8 us
    pallas_call x1, Pallas kernels, finish(): pl.pallas_call(partial(_finish_kernel, slot_bits(), count, planes), out_s...  95.5 us
    ppermute x32, starting transfers between devices, swap(): lax.ppermute(value, axis, [(i, i ^ mask) for i in range(lax.axis_size(axi...  65.7 us
    pallas_call x4, Pallas kernels, attend_back(): pl.pallas_call(partial(_attend_back_kernel, chunks, tq, tk, causal, own_d...  58 us
    pallas_call x3, Pallas kernels, collect(): pl.pallas_call(partial(_collect_kernel, kinds, use, wide, each, blocks, l...  51.8 us
    pallas_call x4, Pallas kernels, attend(): pl.pallas_call(partial(_attend_kernel, chunks, tq, tk, causal), out_shape...  40.7 us
    pallas_call x2, Pallas kernels, to_encoder(): pl.pallas_call(partial(_to_encoder_kernel, count, out is not None), out_s...  36.7 us
  transfers between devices with their start and end apart: 43, of which 11 were waited for; matrix products, arithmetic and copies ran while one was open for 10% of the time, Pallas kernels for 33%

profile of v3, /device:TPU:0, one launch (start us, length us, event | category | flops | bytes accessed | tf_op | source)
XLA Modules:
  0.0 932.3 jit_solution(5195725700824087696)
XLA Ops:
  29.5 98.8 %gather_weights.1 = (bf16[2,1024,2048]{2,1,0:T(8,128)(2,1)}, bf16[2,1024,256]{2,1,0:T(8,128)(2,1)}, bf16[2,1024,1024]{2,1,0:T(8,128)(2,1)}, bf16[2,1024,512]{2,1...) custom-call(bf16[2,1024,512]{2,1,0:T(8,128)(2,1)} %maximum_maximum_f, ...), custom_call_target="tpu_custom_call" | custom-call | bytes 293601280 | tf_op jit(solution)/shard_map/gather_weights/pallas_call | solution.py:888
  132.7 12.2 %spread.3 = (bf16[512,1024]{1,0:T(8,128)(2,1)}, bf16[2,512,512]{2,1,0:T(8,128)(2,1)}, bf16[2,512,512]{2,1,0:T(8,128)(2,1)}) custom-call(bf16[512,1024]{1,0:T(8,128)(2,1)} %get-tuple-element.321.x.refs_4_, bf16[2,1024,2048]{2,1,0:T(8,128)(2,1)} %get-tuple-element.121.weights.refs_1_.refs_3_), custom_call_target="tpu_custom_call" | custom-call | flops 12884901888 | bytes 8388608 | tf_op jit(solution)/shard_map/spread/pallas_call | solution.py:988
  168.6 9.3 %collective-permute-start.4 = (bf16[2,512,512]{2,1,0:T(8,128)(2,1)}, bf16[2,512,512]{2,1,0:T(8,128)(2,1)S(1)}, u32[]{:S(2)}, u32[]{:S(2)}) collective-permute-start(bf16[2,512,512]{2,1,0:T(8,128)(2,1)} %collective-permute-done.2.refs_1_.refs_5_), channel_id=1, source_target_pairs={{0,16},{16,0},{1,17},{17,1},{2,18},{18,2},{3,19},{19,3},{4,20},{20... | collective-permute-start | bytes 3145736 | tf_op jit(solution)/shard_map/ppermute | solution.py:35
  188.9 14.5 %attend.4 = (f32[512,1024]{1,0:T(8,128)}, f32[8,8,512]{2,1,0:T(8,128)}) custom-call(s32[8]{0:T(128)} %reshape.627.act, s32[8,512]{1,0:T(8,128)} %broadcast_in_dim.119.seg_q, s32[4,512,128]{2,1,0:T(8,128)} %broadcast_in_dim.120.seg_k, bf16[512,1024]{1,0:T(8,128)(2,1)} %get-tuple-element.122.q, bf16[2,512,512]{2,1,0:T(8,128)(2,1)} %get-tuple-element.126.refs_0_.refs_4_, ...), custom_call_target="tpu_custom_call" | custom-call | flops 25769803776 | bytes 5242880 | tf_op jit(solution)/shard_map/attend/pallas_call | solution.py:266
  213.3 14.4 %attend.6 = (f32[512,1024]{1,0:T(8,128)}, f32[8,8,512]{2,1,0:T(8,128)}) custom-call(s32[8]{0:T(128)} %reshape.627.act, s32[8,512]{1,0:T(8,128)} %broadcast_in_dim.119.seg_q, s32[4,512,128]{2,1,0:T(8,128)} %broadcast_in_dim.120.seg_k, bf16[512,1024]{1,0:T(8,128)(2,1)} %get-tuple-element.122.q, ...), custom_call_target="tpu_custom_call", output_to_operand_aliasing={{0}: (12, {}), {1}: (13, {})} | custom-call | flops 25769803776 | bytes 5242880 | tf_op jit(solution)/shard_map/attend/pallas_call | solution.py:266
  257.9 11.8 %collect.3 = (f32[512,1024]{1,0:T(8,128)}, bf16[512,1024]{1,0:T(8,128)(2,1)}, f32[512,1024]{1,0:T(8,128)}, f32[512,128]{1,0:T(8,128)}) custom-call(bf16[512,1024]{1,0:T(8,128)(2,1)} %convert_element_type.642.refs_0_, bf16[2,1024,2048]{2,1,0:T(8,128)(2,1)} %get-tuple-element.121.weights.refs_1_.refs_3_, f32[512,1024]{1,0:T(8,128)} %get-tuple-element.320.refs_2_, ...), custom_call_target="tpu_custom_call" | custom-call | flops 4294967296 | bytes 8388608 | tf_op jit(solution)/shard_map/collect/pallas_call | solution.py:1056
  269.7 21.2 %feed_forward.1 = (f32[512,1024]{1,0:T(8,128)}, bf16[512,1024]{1,0:T(8,128)(2,1)}, f32[512,1024]{1,0:T(8,128)}, f32[512,128]{1,0:T(8,128)}, bf16[512,4096]{1,0:T(8,128)(2,1)}, /*index=5*/bf16[512,4096]{1,0:T(8,128)(2,1)}) custom-call(bf16[512,1024]{1,0:T(8,128)(2,1)} %get-tuple-element.136.x, f32[512,1024]{1,0:T(8,128)} %get-tuple-element.137.resid, ...), custom_call_target="tpu_custom_call" | custom-call | flops 25769803776 | bytes 16777216 | tf_op jit(solution)/shard_map/feed_forward/pallas_call | solution.py:1152
  307.5 17.6 %to_encoder.2.q = bf16[8,256,128]{2,1,0:T(8,128)(2,1)} custom-call(bf16[2,256,128]{2,1,0:T(8,128)(2,1)} %pad_maximum_fusion.33.refs_0_), custom_call_target="tpu_custom_call" | custom-call | bytes 62914560 | tf_op jit(solution)/shard_map/to_encoder/pallas_call | solution.py:573
  327.8 9.3 spread.4.refs_0_.refs_1_
  340.1 8.9 attend.7
  349.0 20.5 %to_decoder.1 = (bf16[256,256]{1,0:T(8,128)(2,1)}, f32[2,256,128]{2,1,0:T(8,128)}, f32[2,8,256]{2,1,0:T(8,128)}) custom-call(bf16[8,256,128]{2,1,0:T(8,128)(2,1)} %get-tuple-element.151.refs_0_, f32[8,8,256]{2,1,0:T(8,128)} %get-tuple-element.152.refs_1_), custom_call_target="tpu_custom_call" | custom-call | bytes 62914560 | tf_op jit(solution)/shard_map/to_decoder/pallas_call | solution.py:654
  371.5 29.7 %forward_rows.1 = (f32[64,1024]{1,0:T(8,128)}, f32[64,1024]{1,0:T(8,128)}, f32[64,128]{1,0:T(8,128)}, bf16[256,1024]{1,0:T(8,128)(2,1)}) custom-call(bf16[256,1024]{1,0:T(8,128)(2,1)} %convolution_convert_fusion.9.refs_0_, f32[64,1024]{1,0:T(8,128)} %get-tuple-element.288.refs_1_, f32[1,1024]{1,0:T(1,128)} %get-tuple-element.377.refs_2_.refs_4_, ...), custom_call_target="tpu_custom_call" | custom-call | bytes 91750400 | tf_op jit(solution)/shard_map/forward_rows/pallas_call | solution.py:452
  404.7 29.8 %turn_rows.1 = (bf16[64,1024]{1,0:T(8,128)(2,1)}, f32[64,1024]{1,0:T(8,128)}, f32[8,1024]{1,0:T(8,128)}, bf16[256,1024]{1,0:T(8,128)(2,1)}) custom-call(bf16[256,1024]{1,0:T(8,128)(2,1)} %fusion.9.refs_0_, f32[64,1024]{1,0:T(8,128)} %get-tuple-element.156.refs_1_, f32[1,1024]{1,0:T(1,128)} %get-tuple-element.375.refs_2_, ...), custom_call_target="tpu_custom_call" | custom-call | bytes 91750400 | tf_op jit(solution)/shard_map/turn_rows/pallas_call | solution.py:452
  441.7 27.1 %backward_rows.2 = (f32[64,1024]{1,0:T(8,128)}, f32[8,1024]{1,0:T(8,128)}, bf16[256,1024]{1,0:T(8,128)(2,1)}) custom-call(bf16[256,1024]{1,0:T(8,128)(2,1)} %fusion.8.refs_0_, f32[64,1024]{1,0:T(8,128)} %get-tuple-element.159.refs_1_, f32[64,1024]{1,0:T(8,128)} %get-tuple-element.160.refs_2_, f32[64,128]{1,0:T(8,128)} %get-tuple-element.161.refs_3_, ...), custom_call_target="tpu_custom_call" | custom-call | bytes 91750400 | tf_op jit(solution)/shard_map/backward_rows/pallas_call | solution.py:452
  472.4 19.1 %to_encoder.3 = (bf16[8,256,128]{2,1,0:T(8,128)(2,1)}, f32[8,8,256]{2,1,0:T(8,128)}) custom-call(bf16[2,256,128]{2,1,0:T(8,128)(2,1)} %pad_maximum_fusion.34.refs_0_, f32[2,256,128]{2,1,0:T(8,128)} %get-tuple-element.163.refs_1_, f32[2,8,256]{2,1,0:T(8,128)} %get-tuple-element.164.refs_2_), custom_call_target="tpu_custom_call" | custom-call | bytes 62914560 | tf_op jit(solution)/shard_map/to_encoder/pallas_call | solution.py:573
  496.8 11.1 %attend_back.4 = (bf16[8,256,128]{2,1,0:T(8,128)(2,1)}, bf16[2,512,1024]{2,1,0:T(8,128)(2,1)}) custom-call(s32[1]{0:T(128)} %bitcast.30.act, s32[8,256]{1,0:T(8,128)} %broadcast_in_dim.116.seg_q, s32[1,512,128]{2,1,0:T(8,128)} %broadcast_in_dim.117.seg_k, bf16[8,256,128]{2,1,0:T(8,128)(2,1)} %to_encoder.2.q, bf16[2,512,1024]{2,1,0:T(8,128)(2,1)} %spread.4.refs_0_.refs_1_, ...), custom_call_target="tpu_custom_call" | custom-call | flops 10737418240 | bytes 10485760 | tf_op jit(solution)/shard_map/attend_back/pallas_call | solution.py:302
  509.3 16.9 %collect.4 = (f32[512,1024]{1,0:T(8,128)}, bf16[512,1024]{1,0:T(8,128)(2,1)}, f32[8,1024]{1,0:T(8,128)}, bf16[1024,1024]{1,0:T(8,128)(2,1)}, bf16[1024,1024]{1,0:T(8,128)(2,1)}) custom-call(bf16[2,512,1024]{2,1,0:T(8,128)(2,1)} %get-tuple-element.168.refs_0_, bf16[2,1024,1024]{2,1,0:T(8,128)(2,1)} %pad_maximum_fusion.weights.refs_1_, ...), custom_call_target="tpu_custom_call" | custom-call | flops 17179869184 | bytes 4194304 | tf_op jit(solution)/shard_map/collect/pallas_call | solution.py:1056
  530.9 31.7 %feed_forward_back.1 = (f32[512,1024]{1,0:T(8,128)}, bf16[512,1024]{1,0:T(8,128)(2,1)}, f32[8,1024]{1,0:T(8,128)}, bf16[1024,2048]{1,0:T(8,128)(2,1)}, bf16[1024...) custom-call(bf16[512,1024]{1,0:T(8,128)(2,1)} %get-tuple-element.136.x, ...), custom_call_target="tpu_custom_call" | custom-call | flops 34359738368 | bytes 33554432 | tf_op jit(solution)/shard_map/feed_forward_back/pallas_call | solution.py:1208
  593.6 11.2 %spread.5 = (bf16[512,1024]{1,0:T(8,128)(2,1)}, bf16[1024,512]{1,0:T(8,128)(2,1)}, bf16[1024,512]{1,0:T(8,128)(2,1)}) custom-call(bf16[512,1024]{1,0:T(8,128)(2,1)} %get-tuple-element.177.x, bf16[2,1024,2048]{2,1,0:T(8,128)(2,1)} %get-tuple-element.121.weights.refs_1_.refs_3_, bf16[512,1024]{1,0:T(8,128)(2,1)} %convert_element_type.642.refs_0_), custom_call_target="tpu_custom_call" | custom-call | flops 8589934592 | bytes 8388608 | tf_op jit(solution)/shard_map/spread/pallas_call | solution.py:988
  611.4 21.4 %attend_back.5 = (bf16[512,1024]{1,0:T(8,128)(2,1)}, bf16[2,512,512]{2,1,0:T(8,128)(2,1)}, bf16[2,512,512]{2,1,0:T(8,128)(2,1)}, bf16[2,512,512]{2,1,0:T(8,128)(2,1)}, bf16[2,512,512]{2,1,0:T(8,128)(2,1)}) custom-call(s32[8]{0:T(128)} %reshape.627.act, s32[8,512]{1,0:T(8,128)} %broadcast_in_dim.119.seg_q, s32[4,512,128]{2,1,0:T(8,128)} %broadcast_in_dim.120.seg_k, ...), custom_call_target="tpu_custom_call" | custom-call | flops 42949672960 | bytes 10485760 | tf_op jit(solution)/shard_map/attend_back/pallas_call | solution.py:302
  644.8 21.8 %attend_back.6 = (bf16[512,1024]{1,0:T(8,128)(2,1)}, bf16[2,512,512]{2,1,0:T(8,128)(2,1)}, bf16[2,512,512]{2,1,0:T(8,128)(2,1)}, bf16[2,512,512]{2,1,0:T(8,128)(2,1)}, bf16[2,512,512]{2,1,0:T(8,128)(2,1)}) custom-call(s32[8]{0:T(128)} %reshape.627.act, s32[8,512]{1,0:T(8,128)} %broadcast_in_dim.119.seg_q, ...), custom_call_target="tpu_custom_call", output_to_operand_aliasing={{0}: (15, {})} | custom-call | flops 42949672960 | bytes 10485760 | tf_op jit(solution)/shard_map/attend_back/pallas_call | solution.py:302
  687.7 69.7 %backward_rows.3 = (f32[64,1024]{1,0:T(8,128)}, f32[8,1024]{1,0:T(8,128)}, bf16[256,1024]{1,0:T(8,128)(2,1)}) custom-call(bf16[256,1024]{1,0:T(8,128)(2,1)} %convolution_convert_fusion.8.refs_0_, f32[64,1024]{1,0:T(8,128)} %get-tuple-element.196.refs_1_, f32[64,1024]{1,0:T(8,128)} %get-tuple-element.289.refs_2_, f32[64,128]{1,0:T(8,128)} %broadcast_in_dim.133.refs_3_, ...), custom_call_target="tpu_custom_call" | custom-call | bytes 91750400 | tf_op jit(solution)/shard_map/backward_rows/pallas_call | solution.py:452
  789.1 23.2 %collect.5 = (f32[512,1024]{1,0:T(8,128)}, bf16[512,1024]{1,0:T(8,128)(2,1)}, f32[8,1024]{1,0:T(8,128)}, bf16[1024,1536]{1,0:T(8,128)(2,1)}, bf16[1024,1536]{1,0:T(8,128)(2,1)}) custom-call(bf16[512,1024]{1,0:T(8,128)(2,1)} %get-tuple-element.198.refs_0_, bf16[2,512,512]{2,1,0:T(8,128)(2,1)} %add_convert_fusion.6.refs_1_, ...), custom_call_target="tpu_custom_call" | custom-call | flops 25769803776 | bytes 8388608 | tf_op jit(solution)/shard_map/collect/pallas_call | solution.py:1056
  817.4 95.5 %finish.1 = (f32[4,256,256]{2,1,0:T(8,128)}, f32[2,256,256]{2,1,0:T(8,128)}, f32[2,256,1024]{2,1,0:T(8,128)}, bf16[512,512]{1,0:T(8,128)(2,1)}, bf16[512,512]{1,0:T(8,128)(2,1)}, /*index=5*/f32[8,1024]{1,0:T(8,128)}) custom-call(bf16[1024,1536]{1,0:T(8,128)(2,1)} %get-tuple-element.213.refs_0_, bf16[1024,512]{1,0:T(8,128)(2,1)} %get-tuple-element.214.refs_1_, ...), custom_call_target="tpu_custom_call" | custom-call | bytes 209715200 | tf_op jit(solution)/shard_map/finish/pallas_call | solution.py:1472
  (417 shorter events, 260.1 us)
Async XLA Ops:
  7.2 220.6 %all-gather.3.cloned.1.call-start = ((), (), s32[]{:S(2)}) async-start(), calls=%async_computation.5 | async-start | bytes 7864320 | tf_op jit(solution)/shard_map/all_gather | solution.py:903
  144.9 23.7 %collective-permute-start.2 = (bf16[2,512,512]{2,1,0:T(8,128)(2,1)}, bf16[2,512,512]{2,1,0:T(8,128)(2,1)}, u32[]{:S(2)}, u32[]{:S(2)}) collective-permute-start(bf16[2,512,512]{2,1,0:T(8,128)(2,1)} %get-tuple-element.126.refs_0_.refs_4_), channel_id=1, source_target_pairs={{0,1},{1,0},{2,3},{3,2},{4,5},{5,4},{6,7},{7,6},{8,9},{9,8},{10,11... | collective-permute-start | bytes 3145736 | tf_op jit(solution)/shard_map/ppermute | solution.py:35
  144.9 42.0 %collective-permute-start.3 = (bf16[2,512,512]{2,1,0:T(8,128)(2,1)}, bf16[2,512,512]{2,1,0:T(8,128)(2,1)}, u32[]{:S(2)}, u32[]{:S(2)}) collective-permute-start(bf16[2,512,512]{2,1,0:T(8,128)(2,1)} %get-tuple-element.126.refs_0_.refs_4_), channel_id=1, source_target_pairs={{0,16},{16,0},{1,17},{17,1},{2,18},{18,2},{3,19},{19,3},{4,20},{20... | collective-permute-start | bytes 3145736 | tf_op jit(solution)/shard_map/ppermute | solution.py:35
  153.1 116.6 %all-gather.5.cloned.1.call-start = ((), (), s32[]{:S(2)}) async-start(), calls=%async_computation.6 | async-start | bytes 1966080 | tf_op jit(solution)/shard_map/all_gather | solution.py:903
  153.7 49.7 %collective-permute-start.1 = (bf16[2,512,512]{2,1,0:T(8,128)(2,1)}, bf16[2,512,512]{2,1,0:T(8,128)(2,1)}, u32[]{:S(2)}, u32[]{:S(2)}) collective-permute-start(bf16[2,512,512]{2,1,0:T(8,128)(2,1)} %get-tuple-element.133.refs_0_.refs_4_), channel_id=1, source_target_pairs={{0,1},{1,0},{2,3},{3,2},{4,5},{5,4},{6,7},{7,6},{8,9},{9,8},{10,11... | collective-permute-start | bytes 3145736 | tf_op jit(solution)/shard_map/ppermute | solution.py:35
  168.6 18.4 %collective-permute-start.4 = (bf16[2,512,512]{2,1,0:T(8,128)(2,1)}, bf16[2,512,512]{2,1,0:T(8,128)(2,1)S(1)}, u32[]{:S(2)}, u32[]{:S(2)}) collective-permute-start(bf16[2,512,512]{2,1,0:T(8,128)(2,1)} %collective-permute-done.2.refs_1_.refs_5_), channel_id=1, source_target_pairs={{0,16},{16,0},{1,17},{17,1},{2,18},{18,2},{3,19},{19,3},{4,20},{20... | collective-permute-start | bytes 3145736 | tf_op jit(solution)/shard_map/ppermute | solution.py:35
  227.8 41.9 %collective-permute-start.7 = (bf16[1024,3072]{1,0:T(8,128)(2,1)}, bf16[1024,3072]{1,0:T(8,128)(2,1)}, u32[]{:S(2)}, u32[]{:S(2)}) collective-permute-start(bf16[1024,3072]{1,0:T(8,128)(2,1)} %all-gather.3.cloned.1.call-done.refs_1_.refs_4_), channel_id=1, source_target_pairs={{0,16},{16,0},{1,17},{17,1},{2,18},{18,2},{3,19},{19,3},{4,20},{20... | collective-permute-start | bytes 18874376 | tf_op jit(solution)/shard_map/ppermute | solution.py:35
  233.1 297.8 %reduce-scatter.6.cloned.1.call-start = ((), (), s32[]{:S(2)}) async-start(), calls=%async_computation.7 | async-start | bytes 2621440 | tf_op jit(solution)/shard_map/reduce_scatter | solution.py:911
  233.4 24.1 %collective-permute-start.10 = (bf16[64,1024]{1,0:T(8,128)(2,1)S(1)}, bf16[64,1024]{1,0:T(8,128)(2,1)S(1)}, u32[]{:S(2)}, u32[]{:S(2)}) collective-permute-start(bf16[64,1024]{1,0:T(8,128)(2,1)S(1)} %get-tuple-element.362), channel_id=1, source_target_pairs={{0,3},{1,2},{2,1},{3,0},{4,7},{5,6},{6,5},{7,4},{8,11},{9,10},{10,... | collective-permute-start | bytes 393224 | tf_op jit(solution)/shard_map/ppermute | solution.py:35
  235.8 21.6 %collective-permute-start.8 = (bf16[64,1024]{1,0:T(8,128)(2,1)S(1)}, bf16[64,1024]{1,0:T(8,128)(2,1)S(1)}, u32[]{:S(2)}, u32[]{:S(2)}) collective-permute-start(bf16[64,1024]{1,0:T(8,128)(2,1)S(1)} %get-tuple-element.361), channel_id=1, source_target_pairs={{0,1},{1,0},{2,3},{3,2},{4,5},{5,4},{6,7},{7,6},{8,9},{9,8},{10,11... | collective-permute-start | bytes 393224 | tf_op jit(solution)/shard_map/ppermute | solution.py:35
  269.6 55.5 %collective-permute-start.14 = (bf16[1024,768]{1,0:T(8,128)(2,1)}, bf16[1024,768]{1,0:T(8,128)(2,1)S(1)}, u32[]{:S(2)}, u32[]{:S(2)}) collective-permute-start(bf16[1024,768]{1,0:T(8,128)(2,1)} %all-gather.5.cloned.1.call-done), channel_id=1, source_target_pairs={{0,16},{16,0},{1,17},{17,1},{2,18},{18,2},{3,19},{19,3},{4,20},{20... | collective-permute-start | bytes 4718600 | tf_op jit(solution)/shard_map/ppermute | solution.py:35
  439.7 31.4 %collective-permute-start.15 = (f32[3,1024]{1,0:T(4,128)S(1)}, f32[3,1024]{1,0:T(4,128)S(1)}, u32[]{:S(2)}, u32[]{:S(2)}) collective-permute-start(f32[3,1024]{1,0:T(4,128)S(1)} %fusion.20), channel_id=1, source_target_pairs={{0,1},{1,0},{2,3},{3,2},{4,5},{5,4},{6,7},{7,6},{8,9},{9,8},{10,11... | collective-permute-start | bytes 36872 | tf_op jit(solution)/shard_map/ppermute | solution.py:35
  471.0 20.6 %collective-permute-start.21 = (bf16[1024,1024]{1,0:T(8,128)(2,1)S(1)}, bf16[1024,1024]{1,0:T(8,128)(2,1)S(1)}, u32[]{:S(2)}, u32[]{:S(2)}) collective-permute-start(bf16[1024,1024]{1,0:T(8,128)(2,1)S(1)} %pad_maximum_fusion.3), channel_id=1, source_target_pairs={{0,16},{16,0},{1,17},{17,1},{2,18},{18,2},{3,19},{19,3},{4,20},{20... | collective-permute-start | bytes 6291464 | tf_op jit(solution)/shard_map/ppermute | solution.py:35
  471.2 20.3 %collective-permute-start.16 = (f32[3,1024]{1,0:T(4,128)S(1)}, f32[3,1024]{1,0:T(4,128)S(1)}, u32[]{:S(2)}, u32[]{:S(2)}) collective-permute-start(f32[3,1024]{1,0:T(4,128)S(1)} %add.573), channel_id=1, source_target_pairs={{0,16},{16,0},{1,17},{17,1},{2,18},{18,2},{3,19},{19,3},{4,20},{20... | collective-permute-start | bytes 36872 | tf_op jit(solution)/shard_map/ppermute | solution.py:35
  493.7 192.2 %reduce-scatter.8.cloned.1.call-start = ((), (), s32[]{:S(2)}) async-start(), calls=%async_computation.8 | async-start | bytes 5242880 | tf_op jit(solution)/shard_map/reduce_scatter | solution.py:911
  576.3 212.0 %reduce-scatter.10.cloned.1.call-start = ((), (), s32[]{:S(2)}) async-start(), calls=%async_computation.9 | async-start | bytes 2621440 | tf_op jit(solution)/shard_map/reduce_scatter | solution.py:911
  576.3 28.5 %collective-permute-start.23 = (bf16[1024,2048]{1,0:T(8,128)(2,1)}, bf16[1024,2048]{1,0:T(8,128)(2,1)}, u32[]{:S(2)}, u32[]{:S(2)}) collective-permute-start(bf16[1024,2048]{1,0:T(8,128)(2,1)} %get-tuple-element.183), channel_id=1, source_target_pairs={{0,16},{16,0},{1,17},{17,1},{2,18},{18,2},{3,19},{19,3},{4,20},{20... | collective-permute-start | bytes 12582920 | tf_op jit(solution)/shard_map/ppermute | solution.py:35
  593.5 221.9 %reduce-scatter.12.cloned.1.call-start = ((), (), s32[]{:S(2)}) async-start(), calls=%async_computation.10 | async-start | bytes 5242880 | tf_op jit(solution)/shard_map/reduce_scatter | solution.py:911
  638.9 178.5 %reduce-scatter.14.cloned.1.call-start = ((), (), s32[]{:S(2)}) async-start(), calls=%async_computation.11 | async-start | bytes 1966080 | tf_op jit(solution)/shard_map/reduce_scatter | solution.py:911
  679.6 77.8 %collective-permute-start.29 = (bf16[2,512,512]{2,1,0:T(8,128)(2,1)}, bf16[2,512,512]{2,1,0:T(8,128)(2,1)}, u32[]{:S(2)}, u32[]{:S(2)}) collective-permute-start(bf16[2,512,512]{2,1,0:T(8,128)(2,1)} %add_convert_fusion.7), channel_id=1, source_target_pairs={{0,1},{1,0},{2,3},{3,2},{4,5},{5,4},{6,7},{7,6},{8,9},{9,8},{10,11... | collective-permute-start | bytes 3145736 | tf_op jit(solution)/shard_map/ppermute | solution.py:35
  682.7 92.3 %collective-permute-start.28 = (bf16[2,512,512]{2,1,0:T(8,128)(2,1)}, bf16[2,512,512]{2,1,0:T(8,128)(2,1)}, u32[]{:S(2)}, u32[]{:S(2)}) collective-permute-start(bf16[2,512,512]{2,1,0:T(8,128)(2,1)} %add_convert_fusion.9), channel_id=1, source_target_pairs={{0,1},{1,0},{2,3},{3,2},{4,5},{5,4},{6,7},{7,6},{8,9},{9,8},{10,11... | collective-permute-start | bytes 3145736 | tf_op jit(solution)/shard_map/ppermute | solution.py:35
  779.6 32.7 %collective-permute-start.32 = (bf16[64,1024]{1,0:T(8,128)(2,1)S(1)}, bf16[64,1024]{1,0:T(8,128)(2,1)S(1)}, u32[]{:S(2)}, u32[]{:S(2)}) collective-permute-start(bf16[64,1024]{1,0:T(8,128)(2,1)S(1)} %get-tuple-element.351), channel_id=1, source_target_pairs={{0,1},{1,0},{2,3},{3,2},{4,5},{5,4},{6,7},{7,6},{8,9},{9,8},{10,11... | collective-permute-start | bytes 393224 | tf_op jit(solution)/shard_map/ppermute | solution.py:35
  782.9 29.5 %collective-permute-start.33 = (bf16[64,1024]{1,0:T(8,128)(2,1)S(1)}, bf16[64,1024]{1,0:T(8,128)(2,1)S(1)}, u32[]{:S(2)}, u32[]{:S(2)}) collective-permute-start(bf16[64,1024]{1,0:T(8,128)(2,1)S(1)} %get-tuple-element.353), channel_id=1, source_target_pairs={{0,2},{1,3},{2,0},{3,1},{4,6},{5,7},{6,4},{7,5},{8,10},{9,11},{10,... | collective-permute-start | bytes 393224 | tf_op jit(solution)/shard_map/ppermute | solution.py:35
  782.9 29.5 %collective-permute-start.34 = (bf16[64,1024]{1,0:T(8,128)(2,1)S(1)}, bf16[64,1024]{1,0:T(8,128)(2,1)S(1)}, u32[]{:S(2)}, u32[]{:S(2)}) collective-permute-start(bf16[64,1024]{1,0:T(8,128)(2,1)S(1)} %get-tuple-element.352), channel_id=1, source_target_pairs={{0,3},{1,2},{2,1},{3,0},{4,7},{5,6},{6,5},{7,4},{8,11},{9,10},{10,... | collective-permute-start | bytes 393224 | tf_op jit(solution)/shard_map/ppermute | solution.py:35
  (93 other events, 1158.1 us)
Sparse Core Ops, SparseCore 0:
  153.2 70.0 all-gather.2
  233.2 33.9 all-gather.4
  493.8 37.0 reduce-scatter.5
  576.4 52.6 reduce-scatter.7
  632.5 35.1 reduce-scatter.9
  670.8 52.6 reduce-scatter.11
  788.4 28.9 reduce-scatter.13

commit v4 on v3

--- a/solution.py
+++ b/solution.py
@@ -1754,7 +1754,6 @@
         memory_low,
     )
     ckv_term = fold_cores(*cross_grads)
-    enc_ckv = fold_planes(ckv_term)
     resid_enc, resid_low, enc_terms1, *ffn_grads = feed_forward_back(
         attn_norm_low,
         after(resid_low, dec_ffn_rows, cross_q_chip),
@@ -1773,10 +1772,29 @@
     enc_f2 = fold_planes(f2_term)
     f1_term = fold_cores(*ffn_grads[:2])
     enc_f1 = fold_planes(f1_term)
+    enc_ckv = fold_planes(ckv_term)
     def join(a, b):
         return (a.astype(WIDE) + b.astype(WIDE)).astype(HALF)
 
-    grads_in = after(heads_grad, f1_term, f2_term, cross_q_grad)
+    cross_q_grad = after(cross_q_grad, f2_term)
+    resid, dec_terms0, self_grad_full = rows_call(
+        _backward_rows,
+        4,
+        dot_bt(cross_q_grad, dec_cross[0]).astype(HALF),
+        [resid, self_normed, self_scale, dg[0:1]],
+        [wide_rows, norm_terms],
+    )
+    dec_heads_grad = dot(self_grad_full, dec_attn[3]).astype(HALF)
+    dec_q_grad, [dec_kv_grad] = attend_back(
+        dec_query, [dec_kv], dec_heads_grad, dec_lse, dec_heads_wide, dec_segs, [0], True
+    )
+    dec_proj_grad = [dec_q_grad, dec_kv_grad[0], dec_kv_grad[1]]
+    dec_part = sum(dot_bt(g, w) for g, w in zip(dec_proj_grad, dec_in_w)).astype(HALF)
+    dec_left = [start_full] * 3 + [self_grad_full, self_full, cross_grad_full]
+    dec_right = dec_proj_grad + [dec_heads, cross_q_grad, cross_heads]
+    dec_small = [dot_ta(a, b) for a, b in zip(dec_left, dec_right)]
+    dec_small_rows, dec_small_term = scatter_local(dec_small)
+    grads_in = after(heads_grad, f1_term, dec_small_term)
     def send_chips(held):
         pairs, bit = [(v,) for v in held], top_bit // 2
         while bit >= 1:
@@ -1788,7 +1806,7 @@
     def sum_pair(pair, *earlier):
         return join(after(pair[0], *earlier), pair[1]) if len(pair) == 2 else pair[0]
 
-    q_grad, moving, held = (), [], []
+    q_grad, kv_grad, held = (), [], []
     for n in range(parts):
         q_grad, terms = attend_back(
             query,
@@ -1802,31 +1820,14 @@
             into=q_grad,
         )
         q_grad = (q_grad,)
+        if n:
+            kv_grad.append(sum_pair(moving, terms[0]))
+            terms = after(tuple(terms), kv_grad[0])
         held = [join(a, swap(b, "pipe", 1)) for a, b in zip(terms[:top_bit], terms[top_bit:])]
-        moving.append(send_chips(held))
-    kv_grad = [sum_pair(pair, terms[0]) for pair in moving[:-1]]
+        moving = send_chips(held)
     [q_grad] = q_grad
 
-    cross_q_grad = after(cross_q_grad, *held, enc_f1)
-    resid, dec_terms0, self_grad_full = rows_call(
-        _backward_rows,
-        4,
-        dot_bt(cross_q_grad, dec_cross[0]).astype(HALF),
-        [resid, self_normed, self_scale, dg[0:1]],
-        [wide_rows, norm_terms],
-    )
-    kv_grad.append(sum_pair(moving[-1], self_grad_full))
-    dec_heads_grad = dot(after(self_grad_full, kv_grad[-1]), dec_attn[3]).astype(HALF)
-    dec_q_grad, [dec_kv_grad] = attend_back(
-        dec_query, [dec_kv], dec_heads_grad, dec_lse, dec_heads_wide, dec_segs, [0], True
-    )
-    dec_proj_grad = [dec_q_grad, dec_kv_grad[0], dec_kv_grad[1]]
-    dec_part = sum(dot_bt(g, w) for g, w in zip(dec_proj_grad, dec_in_w)).astype(HALF)
-    dec_left = [start_full] * 3 + [self_grad_full, self_full, cross_grad_full]
-    dec_right = dec_proj_grad + [dec_heads, cross_q_grad, cross_heads]
-    dec_small = [dot_ta(a, b) for a, b in zip(dec_left, dec_right)]
-    dec_small_rows, dec_small_term = scatter_local(dec_small)
-    kv_grad[-1] = after(kv_grad[-1], dec_small_term, enc_ckv)
+    kv_grad.append(after(sum_pair(moving), enc_ckv, enc_f1, enc_f2))
 
     enc_grad, enc_low, enc_terms0, *in_grads = collect(
         [q_grad, *kv_grad],
@@ -1838,7 +1839,7 @@
         back_tokens,
         embed_low,
     )
-    dec_grad = sum_to_owner(dec_part, resid, enc_low)
+    dec_grad = sum_to_owner(after(dec_part, kv_grad[-1]), resid, enc_low)
     attn_out, cross_out, ffn_out_grad, there, near_second, norm_sums = finish(
         in_grads,
         out_grads,

time: 942 us -> 918 us (0.975)
  waiting for transfers between devices: 37.4 us -> 66.3 us
  Pallas kernels: 644 us -> 617 us
  starting transfers between devices: 77.3 us -> 55.9 us
    pallas_call x4, Pallas kernels: 156 us -> 113 us  [rows_call(): pl.pallas_call(partial(_rows_kernel, count, scatter, gather, middle, len(...]
    ppermute x32, starting transfers between devices: 65.7 us -> 43.6 us  [swap(): lax.ppermute(value, axis, [(i, i ^ mask) for i in range(lax.axis_size(axi...]
    ppermute x32, waiting for transfers between devices: 27.3 us -> 47.4 us  [swap(): lax.ppermute(value, axis, [(i, i ^ mask) for i in range(lax.axis_size(axi...]
    pallas_call x1, Pallas kernels: 95.5 us -> 113 us  [finish(): pl.pallas_call(partial(_finish_kernel, slot_bits(), count, planes), out_s...]
    unnamed x173 -> x165, local copies, waits for them, and re-layouts: 24.6 us -> 23.3 us
  transfers between devices with their start and end apart: 43 -> 43, of which waited for: 11 -> 14; matrix products, arithmetic and copies ran while one was open for 10% -> 12% of each run, Pallas kernels for 33% -> 45%
where the time goes in v4:
time: 918 us; the launch traced here: 908 us
  Pallas kernels  617 us (67%)
  waiting for transfers between devices  66.3 us (7%)
  other arithmetic  65.4 us (7%)
  starting transfers between devices  55.9 us (6%)
  local copies, waits for them, and re-layouts  53.2 us (6%)
  between operations  25.5 us (3%)
  matrix products  24.7 us (3%)
    pallas_call x1, Pallas kernels, finish(): pl.pallas_call(partial(_finish_kernel, slot_bits(), count, planes), out_s...  113 us
    pallas_call x4, Pallas kernels, rows_call(): pl.pallas_call(partial(_rows_kernel, count, scatter, gather, middle, len(...  113 us
    pallas_call x1, Pallas kernels, gather_weights(): pl.pallas_call(partial(_gather_kernel, slot_bits(), count, planes), out_s...  98.8 us
    pallas_call x4, Pallas kernels, attend_back(): pl.pallas_call(partial(_attend_back_kernel, chunks, tq, tk, causal, own_d...  57.4 us
    pallas_call x3, Pallas kernels, collect(): pl.pallas_call(partial(_collect_kernel, kinds, use, wide, each, blocks, l...  51.8 us
    ppermute x32, waiting for transfers between devices, swap(): lax.ppermute(value, axis, [(i, i ^ mask) for i in range(lax.axis_size(axi...  47.4 us
    ppermute x32, starting transfers between devices, swap(): lax.ppermute(value, axis, [(i, i ^ mask) for i in range(lax.axis_size(axi...  43.6 us
    pallas_call x4, Pallas kernels, attend(): pl.pallas_call(partial(_attend_kernel, chunks, tq, tk, causal), out_shape...  40.7 us
  transfers between devices with their start and end apart: 43, of which 14 were waited for; matrix products, arithmetic and copies ran while one was open for 12% of the time, Pallas kernels for 45%

profile of v4, /device:TPU:0, one launch (start us, length us, event | category | flops | bytes accessed | tf_op | source)
XLA Modules:
  0.0 907.8 jit_solution(16272713991240077076)
XLA Ops:
  29.5 98.8 %gather_weights.1 = (bf16[2,1024,2048]{2,1,0:T(8,128)(2,1)}, bf16[2,1024,256]{2,1,0:T(8,128)(2,1)}, bf16[2,1024,1024]{2,1,0:T(8,128)(2,1)}, bf16[2,1024,512]{2,1...) custom-call(bf16[2,1024,512]{2,1,0:T(8,128)(2,1)} %maximum_maximum_f, ...), custom_call_target="tpu_custom_call" | custom-call | bytes 293601280 | tf_op jit(solution)/shard_map/gather_weights/pallas_call | solution.py:888
  132.7 12.2 %spread.3 = (bf16[512,1024]{1,0:T(8,128)(2,1)}, bf16[2,512,512]{2,1,0:T(8,128)(2,1)}, bf16[2,512,512]{2,1,0:T(8,128)(2,1)}) custom-call(bf16[512,1024]{1,0:T(8,128)(2,1)} %get-tuple-element.327.x.refs_4_, bf16[2,1024,2048]{2,1,0:T(8,128)(2,1)} %get-tuple-element.124.weights.refs_1_.refs_3_), custom_call_target="tpu_custom_call" | custom-call | flops 12884901888 | bytes 8388608 | tf_op jit(solution)/shard_map/spread/pallas_call | solution.py:988
  168.1 9.8 %collective-permute-start.4 = (bf16[2,512,512]{2,1,0:T(8,128)(2,1)}, bf16[2,512,512]{2,1,0:T(8,128)(2,1)S(1)}, u32[]{:S(2)}, u32[]{:S(2)}) collective-permute-start(bf16[2,512,512]{2,1,0:T(8,128)(2,1)} %collective-permute-done.2.refs_1_.refs_5_), channel_id=1, source_target_pairs={{0,16},{16,0},{1,17},{17,1},{2,18},{18,2},{3,19},{19,3},{4,20},{20... | collective-permute-start | bytes 3145736 | tf_op jit(solution)/shard_map/ppermute | solution.py:35
  188.8 14.5 %attend.4 = (f32[512,1024]{1,0:T(8,128)}, f32[8,8,512]{2,1,0:T(8,128)}) custom-call(s32[8]{0:T(128)} %reshape.627.act, s32[8,512]{1,0:T(8,128)} %broadcast_in_dim.119.seg_q, s32[4,512,128]{2,1,0:T(8,128)} %broadcast_in_dim.120.seg_k, bf16[512,1024]{1,0:T(8,128)(2,1)} %get-tuple-element.125.q, bf16[2,512,512]{2,1,0:T(8,128)(2,1)} %get-tuple-element.129.refs_0_.refs_4_, ...), custom_call_target="tpu_custom_call" | custom-call | flops 25769803776 | bytes 5242880 | tf_op jit(solution)/shard_map/attend/pallas_call | solution.py:266
  208.8 14.4 %attend.6 = (f32[512,1024]{1,0:T(8,128)}, f32[8,8,512]{2,1,0:T(8,128)}) custom-call(s32[8]{0:T(128)} %reshape.627.act, s32[8,512]{1,0:T(8,128)} %broadcast_in_dim.119.seg_q, s32[4,512,128]{2,1,0:T(8,128)} %broadcast_in_dim.120.seg_k, bf16[512,1024]{1,0:T(8,128)(2,1)} %get-tuple-element.125.q, ...), custom_call_target="tpu_custom_call", output_to_operand_aliasing={{0}: (12, {}), {1}: (13, {})} | custom-call | flops 25769803776 | bytes 5242880 | tf_op jit(solution)/shard_map/attend/pallas_call | solution.py:266
  246.7 11.8 %collect.3 = (f32[512,1024]{1,0:T(8,128)}, bf16[512,1024]{1,0:T(8,128)(2,1)}, f32[512,1024]{1,0:T(8,128)}, f32[512,128]{1,0:T(8,128)}) custom-call(bf16[512,1024]{1,0:T(8,128)(2,1)} %convert_element_type.642.refs_0_, bf16[2,1024,2048]{2,1,0:T(8,128)(2,1)} %get-tuple-element.124.weights.refs_1_.refs_3_, f32[512,1024]{1,0:T(8,128)} %get-tuple-element.326.refs_2_, ...), custom_call_target="tpu_custom_call" | custom-call | flops 4294967296 | bytes 8388608 | tf_op jit(solution)/shard_map/collect/pallas_call | solution.py:1056
  266.3 21.2 %feed_forward.1 = (f32[512,1024]{1,0:T(8,128)}, bf16[512,1024]{1,0:T(8,128)(2,1)}, f32[512,1024]{1,0:T(8,128)}, f32[512,128]{1,0:T(8,128)}, bf16[512,4096]{1,0:T(8,128)(2,1)}, /*index=5*/bf16[512,4096]{1,0:T(8,128)(2,1)}) custom-call(bf16[512,1024]{1,0:T(8,128)(2,1)} %get-tuple-element.139.x, f32[512,1024]{1,0:T(8,128)} %get-tuple-element.140.resid, ...), custom_call_target="tpu_custom_call" | custom-call | flops 25769803776 | bytes 16777216 | tf_op jit(solution)/shard_map/feed_forward/pallas_call | solution.py:1152
  303.9 17.2 %to_encoder.2.q = bf16[8,256,128]{2,1,0:T(8,128)(2,1)} custom-call(bf16[2,256,128]{2,1,0:T(8,128)(2,1)} %pad_maximum_fusion.33.refs_0_), custom_call_target="tpu_custom_call" | custom-call | bytes 62914560 | tf_op jit(solution)/shard_map/to_encoder/pallas_call | solution.py:573
  325.0 9.3 %spread.4.refs_0_.refs_1_ = bf16[2,512,1024]{2,1,0:T(8,128)(2,1)} custom-call(bf16[512,1024]{1,0:T(8,128)(2,1)} %get-tuple-element.149.x.refs_2_, bf16[2,1024,1024]{2,1,0:T(8,128)(2,1)} %pad_maximum_fusion.weights.refs_1_), custom_call_target="tpu_custom_call" | custom-call | flops 8589934592 | bytes 4194304 | tf_op jit(solution)/shard_map/spread/pallas_call | solution.py:988
  346.2 20.4 %to_decoder.1 = (bf16[256,256]{1,0:T(8,128)(2,1)}, f32[2,256,128]{2,1,0:T(8,128)}, f32[2,8,256]{2,1,0:T(8,128)}) custom-call(bf16[8,256,128]{2,1,0:T(8,128)(2,1)} %get-tuple-element.154.refs_0_, f32[8,8,256]{2,1,0:T(8,128)} %get-tuple-element.155.refs_1_), custom_call_target="tpu_custom_call" | custom-call | bytes 62914560 | tf_op jit(solution)/shard_map/to_decoder/pallas_call | solution.py:654
  368.7 29.7 %forward_rows.1 = (f32[64,1024]{1,0:T(8,128)}, f32[64,1024]{1,0:T(8,128)}, f32[64,128]{1,0:T(8,128)}, bf16[256,1024]{1,0:T(8,128)(2,1)}) custom-call(bf16[256,1024]{1,0:T(8,128)(2,1)} %convolution_convert_fusion.9.refs_0_, f32[64,1024]{1,0:T(8,128)} %get-tuple-element.294.refs_1_, f32[1,1024]{1,0:T(1,128)} %get-tuple-element.383.refs_2_.refs_4_, ...), custom_call_target="tpu_custom_call" | custom-call | bytes 91750400 | tf_op jit(solution)/shard_map/forward_rows/pallas_call | solution.py:452
  402.0 29.8 %turn_rows.1 = (bf16[64,1024]{1,0:T(8,128)(2,1)}, f32[64,1024]{1,0:T(8,128)}, f32[8,1024]{1,0:T(8,128)}, bf16[256,1024]{1,0:T(8,128)(2,1)}) custom-call(bf16[256,1024]{1,0:T(8,128)(2,1)} %fusion.9.refs_0_, f32[64,1024]{1,0:T(8,128)} %get-tuple-element.159.refs_1_, f32[1,1024]{1,0:T(1,128)} %get-tuple-element.381.refs_2_, ...), custom_call_target="tpu_custom_call" | custom-call | bytes 91750400 | tf_op jit(solution)/shard_map/turn_rows/pallas_call | solution.py:452
  439.1 27.0 %backward_rows.2 = (f32[64,1024]{1,0:T(8,128)}, f32[8,1024]{1,0:T(8,128)}, bf16[256,1024]{1,0:T(8,128)(2,1)}) custom-call(bf16[256,1024]{1,0:T(8,128)(2,1)} %fusion.8.refs_0_, f32[64,1024]{1,0:T(8,128)} %get-tuple-element.162.refs_1_, f32[64,1024]{1,0:T(8,128)} %get-tuple-element.163.refs_2_, f32[64,128]{1,0:T(8,128)} %get-tuple-element.164.refs_3_, ...), custom_call_target="tpu_custom_call" | custom-call | bytes 91750400 | tf_op jit(solution)/shard_map/backward_rows/pallas_call | solution.py:452
  469.7 19.1 %to_encoder.3 = (bf16[8,256,128]{2,1,0:T(8,128)(2,1)}, f32[8,8,256]{2,1,0:T(8,128)}) custom-call(bf16[2,256,128]{2,1,0:T(8,128)(2,1)} %pad_maximum_fusion.34.refs_0_, f32[2,256,128]{2,1,0:T(8,128)} %get-tuple-element.166.refs_1_, f32[2,8,256]{2,1,0:T(8,128)} %get-tuple-element.167.refs_2_), custom_call_target="tpu_custom_call" | custom-call | bytes 62914560 | tf_op jit(solution)/shard_map/to_encoder/pallas_call | solution.py:573
  494.2 10.9 %attend_back.4 = (bf16[8,256,128]{2,1,0:T(8,128)(2,1)}, bf16[2,512,1024]{2,1,0:T(8,128)(2,1)}) custom-call(s32[1]{0:T(128)} %bitcast.30.act, s32[8,256]{1,0:T(8,128)} %broadcast_in_dim.116.seg_q, s32[1,512,128]{2,1,0:T(8,128)} %broadcast_in_dim.117.seg_k, bf16[8,256,128]{2,1,0:T(8,128)(2,1)} %to_encoder.2.q, bf16[2,512,1024]{2,1,0:T(8,128)(2,1)} %spread.4.refs_0_.refs_1_, ...), custom_call_target="tpu_custom_call" | custom-call | flops 10737418240 | bytes 10485760 | tf_op jit(solution)/shard_map/attend_back/pallas_call | solution.py:302
  506.6 16.8 %collect.4 = (f32[512,1024]{1,0:T(8,128)}, bf16[512,1024]{1,0:T(8,128)(2,1)}, f32[8,1024]{1,0:T(8,128)}, bf16[1024,1024]{1,0:T(8,128)(2,1)}, bf16[1024,1024]{1,0:T(8,128)(2,1)}) custom-call(bf16[2,512,1024]{2,1,0:T(8,128)(2,1)} %get-tuple-element.171.refs_0_, bf16[2,1024,1024]{2,1,0:T(8,128)(2,1)} %pad_maximum_fusion.weights.refs_1_, ...), custom_call_target="tpu_custom_call" | custom-call | flops 17179869184 | bytes 4194304 | tf_op jit(solution)/shard_map/collect/pallas_call | solution.py:1056
  532.6 31.7 %feed_forward_back.1 = (f32[512,1024]{1,0:T(8,128)}, bf16[512,1024]{1,0:T(8,128)(2,1)}, f32[8,1024]{1,0:T(8,128)}, bf16[1024,2048]{1,0:T(8,128)(2,1)}, bf16[1024...) custom-call(bf16[512,1024]{1,0:T(8,128)(2,1)} %get-tuple-element.139.x, ...), custom_call_target="tpu_custom_call" | custom-call | flops 34359738368 | bytes 33554432 | tf_op jit(solution)/shard_map/feed_forward_back/pallas_call | solution.py:1208
  593.0 10.9 %spread.5 = (bf16[512,1024]{1,0:T(8,128)(2,1)}, bf16[1024,512]{1,0:T(8,128)(2,1)}, bf16[1024,512]{1,0:T(8,128)(2,1)}) custom-call(bf16[512,1024]{1,0:T(8,128)(2,1)} %get-tuple-element.181.x, bf16[2,1024,2048]{2,1,0:T(8,128)(2,1)} %get-tuple-element.124.weights.refs_1_.refs_3_, bf16[512,1024]{1,0:T(8,128)(2,1)} %convert_element_type.642.refs_0_), custom_call_target="tpu_custom_call" | custom-call | flops 8589934592 | bytes 8388608 | tf_op jit(solution)/shard_map/spread/pallas_call | solution.py:988
  612.2 26.3 %backward_rows.3 = (f32[64,1024]{1,0:T(8,128)}, f32[8,1024]{1,0:T(8,128)}, bf16[256,1024]{1,0:T(8,128)(2,1)}) custom-call(bf16[256,1024]{1,0:T(8,128)(2,1)} %convolution_convert_fusion.8.refs_0_, f32[64,1024]{1,0:T(8,128)} %get-tuple-element.186.refs_1_, f32[64,1024]{1,0:T(8,128)} %get-tuple-element.295.refs_2_, f32[64,128]{1,0:T(8,128)} %broadcast_in_dim.133.refs_3_, ...), custom_call_target="tpu_custom_call" | custom-call | bytes 91750400 | tf_op jit(solution)/shard_map/backward_rows/pallas_call | solution.py:452
  658.6 21.4 %attend_back.6 = (bf16[512,1024]{1,0:T(8,128)(2,1)}, bf16[2,512,512]{2,1,0:T(8,128)(2,1)}, bf16[2,512,512]{2,1,0:T(8,128)(2,1)}, bf16[2,512,512]{2,1,0:T(8,128)(2,1)}, bf16[2,512,512]{2,1,0:T(8,128)(2,1)}) custom-call(s32[8]{0:T(128)} %reshape.627.act, s32[8,512]{1,0:T(8,128)} %broadcast_in_dim.119.seg_q, s32[4,512,128]{2,1,0:T(8,128)} %broadcast_in_dim.120.seg_k, ...), custom_call_target="tpu_custom_call" | custom-call | flops 42949672960 | bytes 10485760 | tf_op jit(solution)/shard_map/attend_back/pallas_call | solution.py:302
  686.8 21.4 %attend_back.7 = (bf16[512,1024]{1,0:T(8,128)(2,1)}, bf16[2,512,512]{2,1,0:T(8,128)(2,1)}, bf16[2,512,512]{2,1,0:T(8,128)(2,1)}, bf16[2,512,512]{2,1,0:T(8,128)(2,1)}, bf16[2,512,512]{2,1,0:T(8,128)(2,1)}) custom-call(s32[8]{0:T(128)} %reshape.627.act, s32[8,512]{1,0:T(8,128)} %broadcast_in_dim.119.seg_q, ...), custom_call_target="tpu_custom_call", output_to_operand_aliasing={{0}: (15, {})} | custom-call | flops 42949672960 | bytes 10485760 | tf_op jit(solution)/shard_map/attend_back/pallas_call | solution.py:302
  720.5 20.4 %collective-permute-done.30 = bf16[2,512,512]{2,1,0:T(8,128)(2,1)} collective-permute-done((bf16[2,512,512]{2,1,0:T(8,128)(2,1)}, bf16[2,512,512]{2,1,0:T(8,128)(2,1)}, u32[]{:S(2)}, u32[]{:S(2)}) %collective-permute-start.30) | collective-permute-done | bytes 1048608 | tf_op jit(solution)/shard_map/ppermute | solution.py:35
  749.3 23.2 %collect.5 = (f32[512,1024]{1,0:T(8,128)}, bf16[512,1024]{1,0:T(8,128)(2,1)}, f32[8,1024]{1,0:T(8,128)}, bf16[1024,1536]{1,0:T(8,128)(2,1)}, bf16[1024,1536]{1,0:T(8,128)(2,1)}) custom-call(bf16[512,1024]{1,0:T(8,128)(2,1)} %get-tuple-element.201.refs_0_, bf16[2,512,512]{2,1,0:T(8,128)(2,1)} %add_convert_fusion.8.refs_1_, ...), custom_call_target="tpu_custom_call" | custom-call | flops 25769803776 | bytes 8388608 | tf_op jit(solution)/shard_map/collect/pallas_call | solution.py:1056
  773.5 113.3 %finish.1 = (f32[4,256,256]{2,1,0:T(8,128)}, f32[2,256,256]{2,1,0:T(8,128)}, f32[2,256,1024]{2,1,0:T(8,128)}, bf16[512,512]{1,0:T(8,128)(2,1)}, bf16[512,512]{1,0:T(8,128)(2,1)}, /*index=5*/f32[8,1024]{1,0:T(8,128)}) custom-call(bf16[1024,1536]{1,0:T(8,128)(2,1)} %get-tuple-element.219.refs_0_, bf16[1024,512]{1,0:T(8,128)(2,1)} %get-tuple-element.220.refs_1_, ...), custom_call_target="tpu_custom_call" | custom-call | bytes 209715200 | tf_op jit(solution)/shard_map/finish/pallas_call | solution.py:1472
  (409 shorter events, 250.7 us)
Async XLA Ops:
  7.2 216.1 %all-gather.3.cloned.1.call-start = ((), (), s32[]{:S(2)}) async-start(), calls=%async_computation.5 | async-start | bytes 7864320 | tf_op jit(solution)/shard_map/all_gather | solution.py:903
  144.9 23.2 %collective-permute-start.2 = (bf16[2,512,512]{2,1,0:T(8,128)(2,1)}, bf16[2,512,512]{2,1,0:T(8,128)(2,1)}, u32[]{:S(2)}, u32[]{:S(2)}) collective-permute-start(bf16[2,512,512]{2,1,0:T(8,128)(2,1)} %get-tuple-element.129.refs_0_.refs_4_), channel_id=1, source_target_pairs={{0,1},{1,0},{2,3},{3,2},{4,5},{5,4},{6,7},{7,6},{8,9},{9,8},{10,11... | collective-permute-start | bytes 3145736 | tf_op jit(solution)/shard_map/ppermute | solution.py:35
  144.9 42.0 %collective-permute-start.3 = (bf16[2,512,512]{2,1,0:T(8,128)(2,1)}, bf16[2,512,512]{2,1,0:T(8,128)(2,1)}, u32[]{:S(2)}, u32[]{:S(2)}) collective-permute-start(bf16[2,512,512]{2,1,0:T(8,128)(2,1)} %get-tuple-element.129.refs_0_.refs_4_), channel_id=1, source_target_pairs={{0,16},{16,0},{1,17},{17,1},{2,18},{18,2},{3,19},{19,3},{4,20},{20... | collective-permute-start | bytes 3145736 | tf_op jit(solution)/shard_map/ppermute | solution.py:35
  153.1 113.2 %all-gather.5.cloned.1.call-start = ((), (), s32[]{:S(2)}) async-start(), calls=%async_computation.6 | async-start | bytes 1966080 | tf_op jit(solution)/shard_map/all_gather | solution.py:903
  153.4 49.9 %collective-permute-start.1 = (bf16[2,512,512]{2,1,0:T(8,128)(2,1)}, bf16[2,512,512]{2,1,0:T(8,128)(2,1)}, u32[]{:S(2)}, u32[]{:S(2)}) collective-permute-start(bf16[2,512,512]{2,1,0:T(8,128)(2,1)} %get-tuple-element.136.refs_0_.refs_4_), channel_id=1, source_target_pairs={{0,1},{1,0},{2,3},{3,2},{4,5},{5,4},{6,7},{7,6},{8,9},{9,8},{10,11... | collective-permute-start | bytes 3145736 | tf_op jit(solution)/shard_map/ppermute | solution.py:35
  223.2 43.1 %collective-permute-start.7 = (bf16[1024,3072]{1,0:T(8,128)(2,1)}, bf16[1024,3072]{1,0:T(8,128)(2,1)}, u32[]{:S(2)}, u32[]{:S(2)}) collective-permute-start(bf16[1024,3072]{1,0:T(8,128)(2,1)} %all-gather.3.cloned.1.call-done.refs_1_.refs_4_), channel_id=1, source_target_pairs={{0,16},{16,0},{1,17},{17,1},{2,18},{18,2},{3,19},{19,3},{4,20},{20... | collective-permute-start | bytes 18874376 | tf_op jit(solution)/shard_map/ppermute | solution.py:35
  223.4 309.2 %reduce-scatter.6.cloned.1.call-start = ((), (), s32[]{:S(2)}) async-start(), calls=%async_computation.7 | async-start | bytes 2621440 | tf_op jit(solution)/shard_map/reduce_scatter | solution.py:911
  224.1 22.2 %collective-permute-start.10 = (bf16[64,1024]{1,0:T(8,128)(2,1)S(1)}, bf16[64,1024]{1,0:T(8,128)(2,1)S(1)}, u32[]{:S(2)}, u32[]{:S(2)}) collective-permute-start(bf16[64,1024]{1,0:T(8,128)(2,1)S(1)} %get-tuple-element.368), channel_id=1, source_target_pairs={{0,3},{1,2},{2,1},{3,0},{4,7},{5,6},{6,5},{7,4},{8,11},{9,10},{10,... | collective-permute-start | bytes 393224 | tf_op jit(solution)/shard_map/ppermute | solution.py:35
  266.3 54.8 %collective-permute-start.14 = (bf16[1024,768]{1,0:T(8,128)(2,1)}, bf16[1024,768]{1,0:T(8,128)(2,1)}, u32[]{:S(2)}, u32[]{:S(2)}) collective-permute-start(bf16[1024,768]{1,0:T(8,128)(2,1)} %all-gather.5.cloned.1.call-done), channel_id=1, source_target_pairs={{0,16},{16,0},{1,17},{17,1},{2,18},{18,2},{3,19},{19,3},{4,20},{20... | collective-permute-start | bytes 4718600 | tf_op jit(solution)/shard_map/ppermute | solution.py:35
  437.0 31.3 %collective-permute-start.15 = (f32[3,1024]{1,0:T(4,128)S(1)}, f32[3,1024]{1,0:T(4,128)S(1)}, u32[]{:S(2)}, u32[]{:S(2)}) collective-permute-start(f32[3,1024]{1,0:T(4,128)S(1)} %fusion.20), channel_id=1, source_target_pairs={{0,1},{1,0},{2,3},{3,2},{4,5},{5,4},{6,7},{7,6},{8,9},{9,8},{10,11... | collective-permute-start | bytes 36872 | tf_op jit(solution)/shard_map/ppermute | solution.py:35
  468.2 20.6 %collective-permute-start.21 = (bf16[1024,1024]{1,0:T(8,128)(2,1)S(1)}, bf16[1024,1024]{1,0:T(8,128)(2,1)S(1)}, u32[]{:S(2)}, u32[]{:S(2)}) collective-permute-start(bf16[1024,1024]{1,0:T(8,128)(2,1)S(1)} %pad_maximum_fusion.3), channel_id=1, source_target_pairs={{0,16},{16,0},{1,17},{17,1},{2,18},{18,2},{3,19},{19,3},{4,20},{20... | collective-permute-start | bytes 6291464 | tf_op jit(solution)/shard_map/ppermute | solution.py:35
  468.4 20.3 %collective-permute-start.16 = (f32[3,1024]{1,0:T(4,128)S(1)}, f32[3,1024]{1,0:T(4,128)S(1)}, u32[]{:S(2)}, u32[]{:S(2)}) collective-permute-start(f32[3,1024]{1,0:T(4,128)S(1)} %add.573), channel_id=1, source_target_pairs={{0,16},{16,0},{1,17},{17,1},{2,18},{18,2},{3,19},{19,3},{4,20},{20... | collective-permute-start | bytes 36872 | tf_op jit(solution)/shard_map/ppermute | solution.py:35
  491.0 252.5 %reduce-scatter.8.cloned.1.call-start = ((), (), s32[]{:S(2)}) async-start(), calls=%async_computation.8 | async-start | bytes 2621440 | tf_op jit(solution)/shard_map/reduce_scatter | solution.py:911
  523.4 41.0 %collective-permute-start.31 = (bf16[1024,1024]{1,0:T(8,128)(2,1)}, bf16[1024,1024]{1,0:T(8,128)(2,1)S(1)}, u32[]{:S(2)}, u32[]{:S(2)}) collective-permute-start(bf16[1024,1024]{1,0:T(8,128)(2,1)} %get-tuple-element.212), channel_id=1, source_target_pairs={{0,16},{16,0},{1,17},{17,1},{2,18},{18,2},{3,19},{19,3},{4,20},{20... | collective-permute-start | bytes 6291464 | tf_op jit(solution)/shard_map/ppermute | solution.py:35
  566.7 176.8 %reduce-scatter.10.cloned.1.call-start = ((), (), s32[]{:S(2)}) async-start(), calls=%async_computation.9 | async-start | bytes 5242880 | tf_op jit(solution)/shard_map/reduce_scatter | solution.py:911
  567.2 36.8 %collective-permute-start.22 = (bf16[1024,2048]{1,0:T(8,128)(2,1)}, bf16[1024,2048]{1,0:T(8,128)(2,1)}, u32[]{:S(2)}, u32[]{:S(2)}) collective-permute-start(bf16[1024,2048]{1,0:T(8,128)(2,1)} %get-tuple-element.184), channel_id=1, source_target_pairs={{0,16},{16,0},{1,17},{17,1},{2,18},{18,2},{3,19},{19,3},{4,20},{20... | collective-permute-start | bytes 12582920 | tf_op jit(solution)/shard_map/ppermute | solution.py:35
  580.1 163.5 %reduce-scatter.12.cloned.1.call-start = ((), (), s32[]{:S(2)}) async-start(), calls=%async_computation.10 | async-start | bytes 5242880 | tf_op jit(solution)/shard_map/reduce_scatter | solution.py:911
  652.0 121.5 %reduce-scatter.14.cloned.1.call-start = ((), (), s32[]{:S(2)}) async-start(), calls=%async_computation.11 | async-start | bytes 1966080 | tf_op jit(solution)/shard_map/reduce_scatter | solution.py:911
  684.5 25.5 %collective-permute-start.27 = (bf16[2,512,512]{2,1,0:T(8,128)(2,1)S(1)}, bf16[2,512,512]{2,1,0:T(8,128)(2,1)S(1)}, u32[]{:S(2)}, u32[]{:S(2)}) collective-permute-start(bf16[2,512,512]{2,1,0:T(8,128)(2,1)S(1)} %add_convert_fusion.9), channel_id=1, source_target_pairs={{0,1},{1,0},{2,3},{3,2},{4,5},{5,4},{6,7},{7,6},{8,9},{9,8},{10,11... | collective-permute-start | bytes 3145736 | tf_op jit(solution)/shard_map/ppermute | solution.py:35
  715.4 25.5 %collective-permute-start.30 = (bf16[2,512,512]{2,1,0:T(8,128)(2,1)}, bf16[2,512,512]{2,1,0:T(8,128)(2,1)}, u32[]{:S(2)}, u32[]{:S(2)}) collective-permute-start(bf16[2,512,512]{2,1,0:T(8,128)(2,1)} %add_convert_fusion.6), channel_id=1, source_target_pairs={{0,1},{1,0},{2,3},{3,2},{4,5},{5,4},{6,7},{7,6},{8,9},{9,8},{10,11... | collective-permute-start | bytes 3145736 | tf_op jit(solution)/shard_map/ppermute | solution.py:35
  743.5 29.0 %collective-permute-start.32 = (bf16[64,1024]{1,0:T(8,128)(2,1)S(1)}, bf16[64,1024]{1,0:T(8,128)(2,1)S(1)}, u32[]{:S(2)}, u32[]{:S(2)}) collective-permute-start(bf16[64,1024]{1,0:T(8,128)(2,1)S(1)} %get-tuple-element.345), channel_id=1, source_target_pairs={{0,1},{1,0},{2,3},{3,2},{4,5},{5,4},{6,7},{7,6},{8,9},{9,8},{10,11... | collective-permute-start | bytes 393224 | tf_op jit(solution)/shard_map/ppermute | solution.py:35
  745.4 27.1 %collective-permute-start.33 = (bf16[64,1024]{1,0:T(8,128)(2,1)S(1)}, bf16[64,1024]{1,0:T(8,128)(2,1)S(1)}, u32[]{:S(2)}, u32[]{:S(2)}) collective-permute-start(bf16[64,1024]{1,0:T(8,128)(2,1)S(1)} %get-tuple-element.347), channel_id=1, source_target_pairs={{0,2},{1,3},{2,0},{3,1},{4,6},{5,7},{6,4},{7,5},{8,10},{9,11},{10,... | collective-permute-start | bytes 393224 | tf_op jit(solution)/shard_map/ppermute | solution.py:35
  748.5 24.1 %collective-permute-start.34 = (bf16[64,1024]{1,0:T(8,128)(2,1)S(1)}, bf16[64,1024]{1,0:T(8,128)(2,1)S(1)}, u32[]{:S(2)}, u32[]{:S(2)}) collective-permute-start(bf16[64,1024]{1,0:T(8,128)(2,1)S(1)} %get-tuple-element.346), channel_id=1, source_target_pairs={{0,3},{1,2},{2,1},{3,0},{4,7},{5,6},{6,5},{7,4},{8,11},{9,10},{10,... | collective-permute-start | bytes 393224 | tf_op jit(solution)/shard_map/ppermute | solution.py:35
  773.5 125.8 %collective-permute-start.35 = (bf16[2,64,512]{2,1,0:T(8,128)(2,1)}, bf16[2,64,512]{2,1,0:T(8,128)(2,1)S(1)}, u32[]{:S(2)}, u32[]{:S(2)}) collective-permute-start(bf16[2,64,512]{2,1,0:T(8,128)(2,1)} %fusion.23), channel_id=1, source_target_pairs={{0,16},{16,0},{1,17},{17,1},{2,18},{18,2},{3,19},{19,3},{4,20},{20... | collective-permute-start | bytes 393224 | tf_op jit(solution)/shard_map/ppermute | solution.py:35
  (89 other events, 1381.6 us)
Sparse Core Ops, SparseCore 0:
  153.2 69.9 all-gather.2
  225.1 41.1 all-gather.4
  491.1 41.4 reduce-scatter.5
  566.8 35.2 reduce-scatter.7
  605.0 52.6 reduce-scatter.9
  660.8 52.7 reduce-scatter.11
  719.5 46.3 reduce-scatter.13

commit v5 on v4

--- a/solution.py
+++ b/solution.py
@@ -1314,20 +1314,6 @@
     chains = [chain(f2, 0), chain(f1, 1), chain(ckv, 2)]
     advance(chains[0])
 
-    half = tokens.shape[1] // 2
-    far_sem, near_sem, same_sem = number(), number(), number()
-
-    @pl.when(core == 1)
-    def _():
-        _send(tokens.at[:, pl.ds(0, half)], far, send_sem.at[far_sem], recv_sem.at[far_sem], cross_over)
-        _send(
-            tokens.at[:, pl.ds(half, half)], far, send_sem.at[same_sem], recv_sem.at[far_sem], line[bits[0]]
-        )
-
-    @pl.when(core == 0)
-    def _():
-        _send(tokens.at[:, pl.ds(half, half)], near, send_sem.at[near_sem], recv_sem.at[near_sem], sibling)
-
     wait(to_core)
     block = in_mine.shape[0] // planes
     wide = term.shape[1] // count
@@ -1377,16 +1363,33 @@
 
     moving = [plane_start(0, r) for r in range(2)]
     for_attn = []
+    advance(chains[1])
+    advance(chains[2])
+
+    half = tokens.shape[1] // 2
+    far_sem, near_sem, same_sem = number(), number(), number()
+
+    @pl.when(core == 1)
+    def _():
+        _send(tokens.at[:, pl.ds(0, half)], far, send_sem.at[far_sem], recv_sem.at[far_sem], cross_over)
+        _send(
+            tokens.at[:, pl.ds(half, half)], far, send_sem.at[same_sem], recv_sem.at[far_sem], line[bits[0]]
+        )
+
+    @pl.when(core == 0)
+    def _():
+        _send(tokens.at[:, pl.ds(half, half)], near, send_sem.at[near_sem], recv_sem.at[near_sem], sibling)
+
     for j in range(n_steps):
         for r in range(2):
-            advance(chains[min(2 * j + r, 2)])
-            advance_norms()
             plane_finish(moving[r], r)
             if j + 1 < n_steps:
                 moving[r] = plane_start(j + 1, r)
             else:
                 for_attn.append(chain(term.at[rows_of(0, r)], 3, pl.ds(r * piece, piece)))
                 advance(for_attn[-1])
+            advance(chains[(2 * j + r) % 3])
+            advance_norms()
     while any(c["now"] or c["bits"] for c in chains + for_attn):
         for c in for_attn + chains:
             advance(c)
@@ -1703,8 +1706,11 @@
         [wide_rows, norm_terms],
     )
     cross_heads_grad = dot(cross_grad_full, dec_cross[1]).astype(HALF)
+    dec_f2_grad = dot_ta(grad_full, dec_active)
+    dec_f1_grad = dot_ta(cross_full, grad_hidden)
+    dec_ffn_rows, dec_ffn_term = scatter_local([dec_f1_grad, dec_f2_grad])
     heads_grad_enc, stats_enc = to_encoder(
-        in_halves(cross_heads_grad), 8, cross_out_wide, cross_lse
+        in_halves(after(cross_heads_grad, dec_ffn_term)), 8, cross_out_wide, cross_lse
     )
     cross_q_term, [cross_kv_grad] = attend_back(
         cross_q_enc,
@@ -1717,9 +1723,6 @@
         False,
         False,
     )
-    dec_f2_grad = dot_ta(grad_full, dec_active)
-    dec_f1_grad = dot_ta(cross_full, grad_hidden)
-    dec_ffn_rows, _ = scatter_local([dec_f1_grad, dec_f2_grad])
 
     def to_chip(value):
         theirs = joint(value, [((1 - owner(t), t), (owner(t), t)) for t in chips])

time: 918 us -> 913 us (level)
  starting transfers between devices: 55.9 us -> 88 us
  Pallas kernels: 617 us -> 597 us
  waiting for transfers between devices: 66.3 us -> 50.7 us
    ppermute x32, starting transfers between devices: 43.6 us -> 73 us  [swap(): lax.ppermute(value, axis, [(i, i ^ mask) for i in range(lax.axis_size(axi...]
    pallas_call x1, Pallas kernels: 113 us -> 91.1 us  [finish(): pl.pallas_call(partial(_finish_kernel, slot_bits(), count, planes), out_s...]
    unnamed x165 -> x159, local copies, waits for them, and re-layouts: 23.3 us -> 23.1 us
  transfers between devices with their start and end apart: 43 -> 43, of which waited for: 14 -> 11; matrix products, arithmetic and copies ran while one was open for 12% -> 12% of each run, Pallas kernels for 45% -> 43%
where the time goes in v5:
time: 913 us; the launch traced here: 903 us
  Pallas kernels  597 us (65%)
  starting transfers between devices  88 us (10%)
  other arithmetic  64.3 us (7%)
  local copies, waits for them, and re-layouts  53 us (6%)
  waiting for transfers between devices  50.7 us (6%)
  between operations  25.4 us (3%)
  matrix products  24.9 us (3%)
    pallas_call x4, Pallas kernels, rows_call(): pl.pallas_call(partial(_rows_kernel, count, scatter, gather, middle, len(...  113 us
    pallas_call x1, Pallas kernels, gather_weights(): pl.pallas_call(partial(_gather_kernel, slot_bits(), count, planes), out_s...  98.7 us
    pallas_call x1, Pallas kernels, finish(): pl.pallas_call(partial(_finish_kernel, slot_bits(), count, planes), out_s...  91.1 us
    ppermute x32, starting transfers between devices, swap(): lax.ppermute(value, axis, [(i, i ^ mask) for i in range(lax.axis_size(axi...  73 us
    pallas_call x4, Pallas kernels, attend_back(): pl.pallas_call(partial(_attend_back_kernel, chunks, tq, tk, causal, own_d...  57.8 us
    pallas_call x3, Pallas kernels, collect(): pl.pallas_call(partial(_collect_kernel, kinds, use, wide, each, blocks, l...  51.8 us
    ppermute x32, waiting for transfers between devices, swap(): lax.ppermute(value, axis, [(i, i ^ mask) for i in range(lax.axis_size(axi...  47.9 us
    pallas_call x4, Pallas kernels, attend(): pl.pallas_call(partial(_attend_kernel, chunks, tq, tk, causal), out_shape...  40.7 us
  transfers between devices with their start and end apart: 43, of which 11 were waited for; matrix products, arithmetic and copies ran while one was open for 12% of the time, Pallas kernels for 43%

profile of v5, /device:TPU:0, one launch (start us, length us, event | category | flops | bytes accessed | tf_op | source)
XLA Modules:
  0.0 902.9 jit_solution(7593217672619753310)
XLA Ops:
  29.5 98.7 %gather_weights.1 = (bf16[2,1024,2048]{2,1,0:T(8,128)(2,1)}, bf16[2,1024,256]{2,1,0:T(8,128)(2,1)}, bf16[2,1024,1024]{2,1,0:T(8,128)(2,1)}, bf16[2,1024,512]{2,1...) custom-call(bf16[2,1024,512]{2,1,0:T(8,128)(2,1)} %maximum_maximum_f, ...), custom_call_target="tpu_custom_call" | custom-call | bytes 293601280 | tf_op jit(solution)/shard_map/gather_weights/pallas_call | solution.py:888
  132.6 12.2 %spread.3 = (bf16[512,1024]{1,0:T(8,128)(2,1)}, bf16[2,512,512]{2,1,0:T(8,128)(2,1)}, bf16[2,512,512]{2,1,0:T(8,128)(2,1)}) custom-call(bf16[512,1024]{1,0:T(8,128)(2,1)} %get-tuple-element.329.x.refs_4_, bf16[2,1024,2048]{2,1,0:T(8,128)(2,1)} %get-tuple-element.125.weights.refs_1_.refs_3_), custom_call_target="tpu_custom_call" | custom-call | flops 12884901888 | bytes 8388608 | tf_op jit(solution)/shard_map/spread/pallas_call | solution.py:988
  167.6 10.3 %collective-permute-start.4 = (bf16[2,512,512]{2,1,0:T(8,128)(2,1)}, bf16[2,512,512]{2,1,0:T(8,128)(2,1)S(1)}, u32[]{:S(2)}, u32[]{:S(2)}) collective-permute-start(bf16[2,512,512]{2,1,0:T(8,128)(2,1)} %collective-permute-done.2.refs_1_.refs_5_), channel_id=1, source_target_pairs={{0,16},{16,0},{1,17},{17,1},{2,18},{18,2},{3,19},{19,3},{4,20},{20... | collective-permute-start | bytes 3145736 | tf_op jit(solution)/shard_map/ppermute | solution.py:35
  188.7 14.5 %attend.4 = (f32[512,1024]{1,0:T(8,128)}, f32[8,8,512]{2,1,0:T(8,128)}) custom-call(s32[8]{0:T(128)} %reshape.627.act, s32[8,512]{1,0:T(8,128)} %broadcast_in_dim.119.seg_q, s32[4,512,128]{2,1,0:T(8,128)} %broadcast_in_dim.120.seg_k, bf16[512,1024]{1,0:T(8,128)(2,1)} %get-tuple-element.126.q, bf16[2,512,512]{2,1,0:T(8,128)(2,1)} %get-tuple-element.130.refs_0_.refs_4_, ...), custom_call_target="tpu_custom_call" | custom-call | flops 25769803776 | bytes 5242880 | tf_op jit(solution)/shard_map/attend/pallas_call | solution.py:266
  213.2 14.4 %attend.6 = (f32[512,1024]{1,0:T(8,128)}, f32[8,8,512]{2,1,0:T(8,128)}) custom-call(s32[8]{0:T(128)} %reshape.627.act, s32[8,512]{1,0:T(8,128)} %broadcast_in_dim.119.seg_q, s32[4,512,128]{2,1,0:T(8,128)} %broadcast_in_dim.120.seg_k, bf16[512,1024]{1,0:T(8,128)(2,1)} %get-tuple-element.126.q, ...), custom_call_target="tpu_custom_call", output_to_operand_aliasing={{0}: (12, {}), {1}: (13, {})} | custom-call | flops 25769803776 | bytes 5242880 | tf_op jit(solution)/shard_map/attend/pallas_call | solution.py:266
  258.0 11.8 %collect.3 = (f32[512,1024]{1,0:T(8,128)}, bf16[512,1024]{1,0:T(8,128)(2,1)}, f32[512,1024]{1,0:T(8,128)}, f32[512,128]{1,0:T(8,128)}) custom-call(bf16[512,1024]{1,0:T(8,128)(2,1)} %convert_element_type.642.refs_0_, bf16[2,1024,2048]{2,1,0:T(8,128)(2,1)} %get-tuple-element.125.weights.refs_1_.refs_3_, f32[512,1024]{1,0:T(8,128)} %get-tuple-element.328.refs_2_, ...), custom_call_target="tpu_custom_call" | custom-call | flops 4294967296 | bytes 8388608 | tf_op jit(solution)/shard_map/collect/pallas_call | solution.py:1056
  269.9 21.2 %feed_forward.1 = (f32[512,1024]{1,0:T(8,128)}, bf16[512,1024]{1,0:T(8,128)(2,1)}, f32[512,1024]{1,0:T(8,128)}, f32[512,128]{1,0:T(8,128)}, bf16[512,4096]{1,0:T(8,128)(2,1)}, /*index=5*/bf16[512,4096]{1,0:T(8,128)(2,1)}) custom-call(bf16[512,1024]{1,0:T(8,128)(2,1)} %get-tuple-element.140.x, f32[512,1024]{1,0:T(8,128)} %get-tuple-element.141.resid, ...), custom_call_target="tpu_custom_call" | custom-call | flops 25769803776 | bytes 16777216 | tf_op jit(solution)/shard_map/feed_forward/pallas_call | solution.py:1152
  308.0 17.2 %to_encoder.2.q = bf16[8,256,128]{2,1,0:T(8,128)(2,1)} custom-call(bf16[2,256,128]{2,1,0:T(8,128)(2,1)} %pad_maximum_fusion.33.refs_0_), custom_call_target="tpu_custom_call" | custom-call | bytes 62914560 | tf_op jit(solution)/shard_map/to_encoder/pallas_call | solution.py:573
  329.2 9.3 %spread.4.refs_0_.refs_1_ = bf16[2,512,1024]{2,1,0:T(8,128)(2,1)} custom-call(bf16[512,1024]{1,0:T(8,128)(2,1)} %get-tuple-element.150.x.refs_2_, bf16[2,1024,1024]{2,1,0:T(8,128)(2,1)} %pad_maximum_fusion.weights.refs_1_), custom_call_target="tpu_custom_call" | custom-call | flops 8589934592 | bytes 4194304 | tf_op jit(solution)/shard_map/spread/pallas_call | solution.py:988
  350.4 20.2 %to_decoder.1 = (bf16[256,256]{1,0:T(8,128)(2,1)}, f32[2,256,128]{2,1,0:T(8,128)}, f32[2,8,256]{2,1,0:T(8,128)}) custom-call(bf16[8,256,128]{2,1,0:T(8,128)(2,1)} %get-tuple-element.155.refs_0_, f32[8,8,256]{2,1,0:T(8,128)} %get-tuple-element.156.refs_1_), custom_call_target="tpu_custom_call" | custom-call | bytes 62914560 | tf_op jit(solution)/shard_map/to_decoder/pallas_call | solution.py:654
  372.6 29.8 %forward_rows.1 = (f32[64,1024]{1,0:T(8,128)}, f32[64,1024]{1,0:T(8,128)}, f32[64,128]{1,0:T(8,128)}, bf16[256,1024]{1,0:T(8,128)(2,1)}) custom-call(bf16[256,1024]{1,0:T(8,128)(2,1)} %convolution_convert_fusion.9.refs_0_, f32[64,1024]{1,0:T(8,128)} %get-tuple-element.296.refs_1_, f32[1,1024]{1,0:T(1,128)} %get-tuple-element.385.refs_2_.refs_4_, ...), custom_call_target="tpu_custom_call" | custom-call | bytes 91750400 | tf_op jit(solution)/shard_map/forward_rows/pallas_call | solution.py:452
  406.0 29.6 %turn_rows.1 = (bf16[64,1024]{1,0:T(8,128)(2,1)}, f32[64,1024]{1,0:T(8,128)}, f32[8,1024]{1,0:T(8,128)}, bf16[256,1024]{1,0:T(8,128)(2,1)}) custom-call(bf16[256,1024]{1,0:T(8,128)(2,1)} %fusion.9.refs_0_, f32[64,1024]{1,0:T(8,128)} %get-tuple-element.160.refs_1_, f32[1,1024]{1,0:T(1,128)} %get-tuple-element.383.refs_2_, ...), custom_call_target="tpu_custom_call" | custom-call | bytes 91750400 | tf_op jit(solution)/shard_map/turn_rows/pallas_call | solution.py:452
  443.7 27.5 %backward_rows.2 = (f32[64,1024]{1,0:T(8,128)}, f32[8,1024]{1,0:T(8,128)}, bf16[256,1024]{1,0:T(8,128)(2,1)}) custom-call(bf16[256,1024]{1,0:T(8,128)(2,1)} %fusion.8.refs_0_, f32[64,1024]{1,0:T(8,128)} %get-tuple-element.163.refs_1_, f32[64,1024]{1,0:T(8,128)} %get-tuple-element.164.refs_2_, f32[64,128]{1,0:T(8,128)} %get-tuple-element.165.refs_3_, ...), custom_call_target="tpu_custom_call" | custom-call | bytes 91750400 | tf_op jit(solution)/shard_map/backward_rows/pallas_call | solution.py:452
  478.8 20.9 %to_encoder.3 = (bf16[8,256,128]{2,1,0:T(8,128)(2,1)}, f32[8,8,256]{2,1,0:T(8,128)}) custom-call(bf16[2,256,128]{2,1,0:T(8,128)(2,1)} %pad_maximum_fusion.34.refs_0_, f32[2,256,128]{2,1,0:T(8,128)} %get-tuple-element.168.refs_1_, f32[2,8,256]{2,1,0:T(8,128)} %get-tuple-element.169.refs_2_), custom_call_target="tpu_custom_call" | custom-call | bytes 62914560 | tf_op jit(solution)/shard_map/to_encoder/pallas_call | solution.py:573
  499.7 11.1 %attend_back.4 = (bf16[8,256,128]{2,1,0:T(8,128)(2,1)}, bf16[2,512,1024]{2,1,0:T(8,128)(2,1)}) custom-call(s32[1]{0:T(128)} %bitcast.30.act, s32[8,256]{1,0:T(8,128)} %broadcast_in_dim.116.seg_q, s32[1,512,128]{2,1,0:T(8,128)} %broadcast_in_dim.117.seg_k, bf16[8,256,128]{2,1,0:T(8,128)(2,1)} %to_encoder.2.q, bf16[2,512,1024]{2,1,0:T(8,128)(2,1)} %spread.4.refs_0_.refs_1_, ...), custom_call_target="tpu_custom_call" | custom-call | flops 10737418240 | bytes 10485760 | tf_op jit(solution)/shard_map/attend_back/pallas_call | solution.py:302
  512.3 16.8 %collect.4 = (f32[512,1024]{1,0:T(8,128)}, bf16[512,1024]{1,0:T(8,128)(2,1)}, f32[8,1024]{1,0:T(8,128)}, bf16[1024,1024]{1,0:T(8,128)(2,1)}, bf16[1024,1024]{1,0:T(8,128)(2,1)}) custom-call(bf16[2,512,1024]{2,1,0:T(8,128)(2,1)} %get-tuple-element.173.refs_0_, bf16[2,1024,1024]{2,1,0:T(8,128)(2,1)} %pad_maximum_fusion.weights.refs_1_, ...), custom_call_target="tpu_custom_call" | custom-call | flops 17179869184 | bytes 4194304 | tf_op jit(solution)/shard_map/collect/pallas_call | solution.py:1056
  530.6 31.6 %feed_forward_back.1 = (f32[512,1024]{1,0:T(8,128)}, bf16[512,1024]{1,0:T(8,128)(2,1)}, f32[8,1024]{1,0:T(8,128)}, bf16[1024,2048]{1,0:T(8,128)(2,1)}, bf16[1024...) custom-call(bf16[512,1024]{1,0:T(8,128)(2,1)} %get-tuple-element.140.x, ...), custom_call_target="tpu_custom_call" | custom-call | flops 34359738368 | bytes 33554432 | tf_op jit(solution)/shard_map/feed_forward_back/pallas_call | solution.py:1208
  592.6 10.9 %spread.5 = (bf16[512,1024]{1,0:T(8,128)(2,1)}, bf16[1024,512]{1,0:T(8,128)(2,1)}, bf16[1024,512]{1,0:T(8,128)(2,1)}) custom-call(bf16[512,1024]{1,0:T(8,128)(2,1)} %get-tuple-element.183.x, bf16[2,1024,2048]{2,1,0:T(8,128)(2,1)} %get-tuple-element.125.weights.refs_1_.refs_3_, bf16[512,1024]{1,0:T(8,128)(2,1)} %convert_element_type.642.refs_0_), custom_call_target="tpu_custom_call" | custom-call | flops 8589934592 | bytes 8388608 | tf_op jit(solution)/shard_map/spread/pallas_call | solution.py:988
  611.9 26.3 %backward_rows.3 = (f32[64,1024]{1,0:T(8,128)}, f32[8,1024]{1,0:T(8,128)}, bf16[256,1024]{1,0:T(8,128)(2,1)}) custom-call(bf16[256,1024]{1,0:T(8,128)(2,1)} %convolution_convert_fusion.8.refs_0_, f32[64,1024]{1,0:T(8,128)} %get-tuple-element.188.refs_1_, f32[64,1024]{1,0:T(8,128)} %get-tuple-element.297.refs_2_, f32[64,128]{1,0:T(8,128)} %broadcast_in_dim.133.refs_3_, ...), custom_call_target="tpu_custom_call" | custom-call | bytes 91750400 | tf_op jit(solution)/shard_map/backward_rows/pallas_call | solution.py:452
  658.3 21.4 %attend_back.6 = (bf16[512,1024]{1,0:T(8,128)(2,1)}, bf16[2,512,512]{2,1,0:T(8,128)(2,1)}, bf16[2,512,512]{2,1,0:T(8,128)(2,1)}, bf16[2,512,512]{2,1,0:T(8,128)(2,1)}, bf16[2,512,512]{2,1,0:T(8,128)(2,1)}) custom-call(s32[8]{0:T(128)} %reshape.627.act, s32[8,512]{1,0:T(8,128)} %broadcast_in_dim.119.seg_q, s32[4,512,128]{2,1,0:T(8,128)} %broadcast_in_dim.120.seg_k, ...), custom_call_target="tpu_custom_call" | custom-call | flops 42949672960 | bytes 10485760 | tf_op jit(solution)/shard_map/attend_back/pallas_call | solution.py:302
  697.4 21.6 %attend_back.7 = (bf16[512,1024]{1,0:T(8,128)(2,1)}, bf16[2,512,512]{2,1,0:T(8,128)(2,1)}, bf16[2,512,512]{2,1,0:T(8,128)(2,1)}, bf16[2,512,512]{2,1,0:T(8,128)(2,1)}, bf16[2,512,512]{2,1,0:T(8,128)(2,1)}) custom-call(s32[8]{0:T(128)} %reshape.627.act, s32[8,512]{1,0:T(8,128)} %broadcast_in_dim.119.seg_q, ...), custom_call_target="tpu_custom_call", output_to_operand_aliasing={{0}: (15, {})} | custom-call | flops 42949672960 | bytes 10485760 | tf_op jit(solution)/shard_map/attend_back/pallas_call | solution.py:302
  738.4 20.4 %collective-permute-done.30 = bf16[2,512,512]{2,1,0:T(8,128)(2,1)} collective-permute-done((bf16[2,512,512]{2,1,0:T(8,128)(2,1)}, bf16[2,512,512]{2,1,0:T(8,128)(2,1)}, u32[]{:S(2)}, u32[]{:S(2)}) %collective-permute-start.30) | collective-permute-done | bytes 1048608 | tf_op jit(solution)/shard_map/ppermute | solution.py:35
  766.7 23.1 %collect.5 = (f32[512,1024]{1,0:T(8,128)}, bf16[512,1024]{1,0:T(8,128)(2,1)}, f32[8,1024]{1,0:T(8,128)}, bf16[1024,1536]{1,0:T(8,128)(2,1)}, bf16[1024,1536]{1,0:T(8,128)(2,1)}) custom-call(bf16[512,1024]{1,0:T(8,128)(2,1)} %get-tuple-element.203.refs_0_, bf16[2,512,512]{2,1,0:T(8,128)(2,1)} %add_convert_fusion.8.refs_1_, ...), custom_call_target="tpu_custom_call" | custom-call | flops 25769803776 | bytes 8388608 | tf_op jit(solution)/shard_map/collect/pallas_call | solution.py:1056
  790.8 91.1 %finish.1 = (f32[4,256,256]{2,1,0:T(8,128)}, f32[2,256,256]{2,1,0:T(8,128)}, f32[2,256,1024]{2,1,0:T(8,128)}, bf16[512,512]{1,0:T(8,128)(2,1)}, bf16[512,512]{1,0:T(8,128)(2,1)}, /*index=5*/f32[8,1024]{1,0:T(8,128)}) custom-call(bf16[1024,1536]{1,0:T(8,128)(2,1)} %get-tuple-element.221.refs_0_, bf16[1024,512]{1,0:T(8,128)(2,1)} %get-tuple-element.222.refs_1_, ...), custom_call_target="tpu_custom_call" | custom-call | bytes 209715200 | tf_op jit(solution)/shard_map/finish/pallas_call | solution.py:1475
  (403 shorter events, 265.6 us)
Async XLA Ops:
  7.2 220.4 %all-gather.3.cloned.1.call-start = ((), (), s32[]{:S(2)}) async-start(), calls=%async_computation.5 | async-start | bytes 7864320 | tf_op jit(solution)/shard_map/all_gather | solution.py:903
  144.8 22.8 %collective-permute-start.2 = (bf16[2,512,512]{2,1,0:T(8,128)(2,1)}, bf16[2,512,512]{2,1,0:T(8,128)(2,1)}, u32[]{:S(2)}, u32[]{:S(2)}) collective-permute-start(bf16[2,512,512]{2,1,0:T(8,128)(2,1)} %get-tuple-element.130.refs_0_.refs_4_), channel_id=1, source_target_pairs={{0,1},{1,0},{2,3},{3,2},{4,5},{5,4},{6,7},{7,6},{8,9},{9,8},{10,11... | collective-permute-start | bytes 3145736 | tf_op jit(solution)/shard_map/ppermute | solution.py:35
  144.8 41.9 %collective-permute-start.3 = (bf16[2,512,512]{2,1,0:T(8,128)(2,1)}, bf16[2,512,512]{2,1,0:T(8,128)(2,1)}, u32[]{:S(2)}, u32[]{:S(2)}) collective-permute-start(bf16[2,512,512]{2,1,0:T(8,128)(2,1)} %get-tuple-element.130.refs_0_.refs_4_), channel_id=1, source_target_pairs={{0,16},{16,0},{1,17},{17,1},{2,18},{18,2},{3,19},{19,3},{4,20},{20... | collective-permute-start | bytes 3145736 | tf_op jit(solution)/shard_map/ppermute | solution.py:35
  153.0 116.8 %all-gather.5.cloned.1.call-start = ((), (), s32[]{:S(2)}) async-start(), calls=%async_computation.6 | async-start | bytes 1966080 | tf_op jit(solution)/shard_map/all_gather | solution.py:903
  153.4 49.9 %collective-permute-start.1 = (bf16[2,512,512]{2,1,0:T(8,128)(2,1)}, bf16[2,512,512]{2,1,0:T(8,128)(2,1)}, u32[]{:S(2)}, u32[]{:S(2)}) collective-permute-start(bf16[2,512,512]{2,1,0:T(8,128)(2,1)} %get-tuple-element.137.refs_0_.refs_4_), channel_id=1, source_target_pairs={{0,1},{1,0},{2,3},{3,2},{4,5},{5,4},{6,7},{7,6},{8,9},{9,8},{10,11... | collective-permute-start | bytes 3145736 | tf_op jit(solution)/shard_map/ppermute | solution.py:35
  227.6 42.3 %collective-permute-start.7 = (bf16[1024,3072]{1,0:T(8,128)(2,1)}, bf16[1024,3072]{1,0:T(8,128)(2,1)}, u32[]{:S(2)}, u32[]{:S(2)}) collective-permute-start(bf16[1024,3072]{1,0:T(8,128)(2,1)} %all-gather.3.cloned.1.call-done.refs_1_.refs_4_), channel_id=1, source_target_pairs={{0,16},{16,0},{1,17},{17,1},{2,18},{18,2},{3,19},{19,3},{4,20},{20... | collective-permute-start | bytes 18874376 | tf_op jit(solution)/shard_map/ppermute | solution.py:35
  232.9 297.6 %reduce-scatter.6.cloned.1.call-start = ((), (), s32[]{:S(2)}) async-start(), calls=%async_computation.7 | async-start | bytes 2621440 | tf_op jit(solution)/shard_map/reduce_scatter | solution.py:911
  233.5 24.1 %collective-permute-start.10 = (bf16[64,1024]{1,0:T(8,128)(2,1)S(1)}, bf16[64,1024]{1,0:T(8,128)(2,1)S(1)}, u32[]{:S(2)}, u32[]{:S(2)}) collective-permute-start(bf16[64,1024]{1,0:T(8,128)(2,1)S(1)} %get-tuple-element.370), channel_id=1, source_target_pairs={{0,3},{1,2},{2,1},{3,0},{4,7},{5,6},{6,5},{7,4},{8,11},{9,10},{10,... | collective-permute-start | bytes 393224 | tf_op jit(solution)/shard_map/ppermute | solution.py:35
  233.6 24.0 %collective-permute-start.8 = (bf16[64,1024]{1,0:T(8,128)(2,1)S(1)}, bf16[64,1024]{1,0:T(8,128)(2,1)S(1)}, u32[]{:S(2)}, u32[]{:S(2)}) collective-permute-start(bf16[64,1024]{1,0:T(8,128)(2,1)S(1)} %get-tuple-element.369), channel_id=1, source_target_pairs={{0,1},{1,0},{2,3},{3,2},{4,5},{5,4},{6,7},{7,6},{8,9},{9,8},{10,11... | collective-permute-start | bytes 393224 | tf_op jit(solution)/shard_map/ppermute | solution.py:35
  269.8 55.4 %collective-permute-start.14 = (bf16[1024,768]{1,0:T(8,128)(2,1)}, bf16[1024,768]{1,0:T(8,128)(2,1)}, u32[]{:S(2)}, u32[]{:S(2)}) collective-permute-start(bf16[1024,768]{1,0:T(8,128)(2,1)} %all-gather.5.cloned.1.call-done), channel_id=1, source_target_pairs={{0,16},{16,0},{1,17},{17,1},{2,18},{18,2},{3,19},{19,3},{4,20},{20... | collective-permute-start | bytes 4718600 | tf_op jit(solution)/shard_map/ppermute | solution.py:35
  440.8 30.3 %collective-permute-start.16 = (f32[3,1024]{1,0:T(4,128)S(1)}, f32[3,1024]{1,0:T(4,128)S(1)}, u32[]{:S(2)}, u32[]{:S(2)}) collective-permute-start(f32[3,1024]{1,0:T(4,128)S(1)} %fusion.20), channel_id=1, source_target_pairs={{0,1},{1,0},{2,3},{3,2},{4,5},{5,4},{6,7},{7,6},{8,9},{9,8},{10,11... | collective-permute-start | bytes 36872 | tf_op jit(solution)/shard_map/ppermute | solution.py:35
  443.6 29.2 %collective-permute-start.15 = (bf16[1024,1024]{1,0:T(8,128)(2,1)S(1)}, bf16[1024,1024]{1,0:T(8,128)(2,1)S(1)}, u32[]{:S(2)}, u32[]{:S(2)}) collective-permute-start(bf16[1024,1024]{1,0:T(8,128)(2,1)S(1)} %pad_maximum_fusion.3), channel_id=1, source_target_pairs={{0,16},{16,0},{1,17},{17,1},{2,18},{18,2},{3,19},{19,3},{4,20},{20... | collective-permute-start | bytes 6291464 | tf_op jit(solution)/shard_map/ppermute | solution.py:35
  475.0 286.4 %reduce-scatter.8.cloned.1.call-start = ((), (), s32[]{:S(2)}) async-start(), calls=%async_computation.8 | async-start | bytes 2621440 | tf_op jit(solution)/shard_map/reduce_scatter | solution.py:911
  529.2 33.1 %collective-permute-start.31 = (bf16[1024,1024]{1,0:T(8,128)(2,1)}, bf16[1024,1024]{1,0:T(8,128)(2,1)S(1)}, u32[]{:S(2)}, u32[]{:S(2)}) collective-permute-start(bf16[1024,1024]{1,0:T(8,128)(2,1)} %get-tuple-element.214), channel_id=1, source_target_pairs={{0,16},{16,0},{1,17},{17,1},{2,18},{18,2},{3,19},{19,3},{4,20},{20... | collective-permute-start | bytes 6291464 | tf_op jit(solution)/shard_map/ppermute | solution.py:35
  564.6 196.8 %reduce-scatter.10.cloned.1.call-start = ((), (), s32[]{:S(2)}) async-start(), calls=%async_computation.9 | async-start | bytes 5242880 | tf_op jit(solution)/shard_map/reduce_scatter | solution.py:911
  565.0 38.5 %collective-permute-start.22 = (bf16[1024,2048]{1,0:T(8,128)(2,1)}, bf16[1024,2048]{1,0:T(8,128)(2,1)}, u32[]{:S(2)}, u32[]{:S(2)}) collective-permute-start(bf16[1024,2048]{1,0:T(8,128)(2,1)} %get-tuple-element.186), channel_id=1, source_target_pairs={{0,16},{16,0},{1,17},{17,1},{2,18},{18,2},{3,19},{19,3},{4,20},{20... | collective-permute-start | bytes 12582920 | tf_op jit(solution)/shard_map/ppermute | solution.py:35
  577.6 183.8 %reduce-scatter.12.cloned.1.call-start = ((), (), s32[]{:S(2)}) async-start(), calls=%async_computation.10 | async-start | bytes 5242880 | tf_op jit(solution)/shard_map/reduce_scatter | solution.py:911
  651.6 139.1 %reduce-scatter.14.cloned.1.call-start = ((), (), s32[]{:S(2)}) async-start(), calls=%async_computation.11 | async-start | bytes 1966080 | tf_op jit(solution)/shard_map/reduce_scatter | solution.py:911
  691.2 29.3 %collective-permute-start.27 = (bf16[2,512,512]{2,1,0:T(8,128)(2,1)S(1)}, bf16[2,512,512]{2,1,0:T(8,128)(2,1)S(1)}, u32[]{:S(2)}, u32[]{:S(2)}) collective-permute-start(bf16[2,512,512]{2,1,0:T(8,128)(2,1)S(1)} %add_convert_fusion.9), channel_id=1, source_target_pairs={{0,1},{1,0},{2,3},{3,2},{4,5},{5,4},{6,7},{7,6},{8,9},{9,8},{10,11... | collective-permute-start | bytes 3145736 | tf_op jit(solution)/shard_map/ppermute | solution.py:35
  730.9 28.0 %collective-permute-start.30 = (bf16[2,512,512]{2,1,0:T(8,128)(2,1)}, bf16[2,512,512]{2,1,0:T(8,128)(2,1)}, u32[]{:S(2)}, u32[]{:S(2)}) collective-permute-start(bf16[2,512,512]{2,1,0:T(8,128)(2,1)} %add_convert_fusion.6), channel_id=1, source_target_pairs={{0,1},{1,0},{2,3},{3,2},{4,5},{5,4},{6,7},{7,6},{8,9},{9,8},{10,11... | collective-permute-start | bytes 3145736 | tf_op jit(solution)/shard_map/ppermute | solution.py:35
  761.4 28.4 %collective-permute-start.32 = (bf16[64,1024]{1,0:T(8,128)(2,1)S(1)}, bf16[64,1024]{1,0:T(8,128)(2,1)S(1)}, u32[]{:S(2)}, u32[]{:S(2)}) collective-permute-start(bf16[64,1024]{1,0:T(8,128)(2,1)S(1)} %get-tuple-element.347), channel_id=1, source_target_pairs={{0,1},{1,0},{2,3},{3,2},{4,5},{5,4},{6,7},{7,6},{8,9},{9,8},{10,11... | collective-permute-start | bytes 393224 | tf_op jit(solution)/shard_map/ppermute | solution.py:35
  763.2 26.6 %collective-permute-start.33 = (bf16[64,1024]{1,0:T(8,128)(2,1)S(1)}, bf16[64,1024]{1,0:T(8,128)(2,1)S(1)}, u32[]{:S(2)}, u32[]{:S(2)}) collective-permute-start(bf16[64,1024]{1,0:T(8,128)(2,1)S(1)} %get-tuple-element.349), channel_id=1, source_target_pairs={{0,2},{1,3},{2,0},{3,1},{4,6},{5,7},{6,4},{7,5},{8,10},{9,11},{10,... | collective-permute-start | bytes 393224 | tf_op jit(solution)/shard_map/ppermute | solution.py:35
  763.2 26.6 %collective-permute-start.34 = (bf16[64,1024]{1,0:T(8,128)(2,1)S(1)}, bf16[64,1024]{1,0:T(8,128)(2,1)S(1)}, u32[]{:S(2)}, u32[]{:S(2)}) collective-permute-start(bf16[64,1024]{1,0:T(8,128)(2,1)S(1)} %get-tuple-element.348), channel_id=1, source_target_pairs={{0,3},{1,2},{2,1},{3,0},{4,7},{5,6},{6,5},{7,4},{8,11},{9,10},{10,... | collective-permute-start | bytes 393224 | tf_op jit(solution)/shard_map/ppermute | solution.py:35
  790.7 103.7 %collective-permute-start.35 = (bf16[2,64,512]{2,1,0:T(8,128)(2,1)}, bf16[2,64,512]{2,1,0:T(8,128)(2,1)S(1)}, u32[]{:S(2)}, u32[]{:S(2)}) collective-permute-start(bf16[2,64,512]{2,1,0:T(8,128)(2,1)} %fusion.23), channel_id=1, source_target_pairs={{0,16},{16,0},{1,17},{17,1},{2,18},{18,2},{3,19},{19,3},{4,20},{20... | collective-permute-start | bytes 393224 | tf_op jit(solution)/shard_map/ppermute | solution.py:35
  (86 other events, 1210.4 us)
Sparse Core Ops, SparseCore 0:
  153.1 70.0 all-gather.2
  233.0 33.1 all-gather.4
  475.1 38.8 reduce-scatter.5
  564.7 38.7 reduce-scatter.7
  606.3 52.6 reduce-scatter.9
  662.1 52.7 reduce-scatter.11
  737.4 28.2 reduce-scatter.13

commit v6 on v5

--- a/solution.py
+++ b/solution.py
@@ -1809,12 +1809,12 @@
     def sum_pair(pair, *earlier):
         return join(after(pair[0], *earlier), pair[1]) if len(pair) == 2 else pair[0]
 
-    q_grad, kv_grad, held = (), [], []
+    q_grad, kv_grad, held = (), [], ()
     for n in range(parts):
         q_grad, terms = attend_back(
             query,
             key_values[n],
-            after(grads_in, *held),
+            after(grads_in, *held, dec_grad) if n else grads_in,
             lse,
             heads_wide,
             enc_segs,
@@ -1823,6 +1823,8 @@
             into=q_grad,
         )
         q_grad = (q_grad,)
+        if n == 0:
+            dec_grad = sum_to_owner(dec_part, resid, terms[0])
         if n:
             kv_grad.append(sum_pair(moving, terms[0]))
             terms = after(tuple(terms), kv_grad[0])
@@ -1842,7 +1844,6 @@
         back_tokens,
         embed_low,
     )
-    dec_grad = sum_to_owner(after(dec_part, kv_grad[-1]), resid, enc_low)
     attn_out, cross_out, ffn_out_grad, there, near_second, norm_sums = finish(
         in_grads,
         out_grads,
@@ -1851,7 +1852,7 @@
         enc_ckv,
         dec_ffn_rows,
         dec_small_rows,
-        after(enc_low, dec_grad),
+        enc_low,
         [enc_terms0, enc_terms1, enc_terms2, dec_terms0, dec_terms1, dec_terms2],
     )
 

time: 913 us -> 915 us (level)
  starting transfers between devices: 88 us -> 70.5 us
  Pallas kernels: 597 us -> 609 us
    ppermute x32, starting transfers between devices: 73 us -> 56.2 us  [swap(): lax.ppermute(value, axis, [(i, i ^ mask) for i in range(lax.axis_size(axi...]
    pallas_call x1, Pallas kernels: 91.1 us -> 102 us  [finish(): pl.pallas_call(partial(_finish_kernel, slot_bits(), count, planes), out_s...]
    unnamed x159 -> x181, local copies, waits for them, and re-layouts: 23.1 us -> 25 us
  transfers between devices with their start and end apart: 43 -> 43, of which waited for: 11 -> 15; matrix products, arithmetic and copies ran while one was open for 12% -> 11% of each run, Pallas kernels for 43% -> 33%
where the time goes in v6:
time: 915 us; the launch traced here: 905 us
  Pallas kernels  609 us (67%)
  starting transfers between devices  70.5 us (8%)
  other arithmetic  67.1 us (7%)
  waiting for transfers between devices  57.1 us (6%)
  local copies, waits for them, and re-layouts  53 us (6%)
  between operations  25.5 us (3%)
  matrix products  22.5 us (2%)
    pallas_call x4, Pallas kernels, rows_call(): pl.pallas_call(partial(_rows_kernel, count, scatter, gather, middle, len(...  114 us
    pallas_call x1, Pallas kernels, finish(): pl.pallas_call(partial(_finish_kernel, slot_bits(), count, planes), out_s...  102 us
    pallas_call x1, Pallas kernels, gather_weights(): pl.pallas_call(partial(_gather_kernel, slot_bits(), count, planes), out_s...  98.7 us
    pallas_call x4, Pallas kernels, attend_back(): pl.pallas_call(partial(_attend_back_kernel, chunks, tq, tk, causal, own_d...  57.9 us
    ppermute x32, starting transfers between devices, swap(): lax.ppermute(value, axis, [(i, i ^ mask) for i in range(lax.axis_size(axi...  56.2 us
    ppermute x32, waiting for transfers between devices, swap(): lax.ppermute(value, axis, [(i, i ^ mask) for i in range(lax.axis_size(axi...  53.2 us
    pallas_call x3, Pallas kernels, collect(): pl.pallas_call(partial(_collect_kernel, kinds, use, wide, each, blocks, l...  52.1 us
    pallas_call x4, Pallas kernels, attend(): pl.pallas_call(partial(_attend_kernel, chunks, tq, tk, causal), out_shape...  40.7 us
  transfers between devices with their start and end apart: 43, of which 15 were waited for; matrix products, arithmetic and copies ran while one was open for 11% of the time, Pallas kernels for 33%

profile of v6, /device:TPU:0, one launch (start us, length us, event | category | flops | bytes accessed | tf_op | source)
XLA Modules:
  0.0 904.8 jit_solution(1878641309982041040)
XLA Ops:
  31.1 98.7 %gather_weights.1 = (bf16[2,1024,2048]{2,1,0:T(8,128)(2,1)}, bf16[2,1024,256]{2,1,0:T(8,128)(2,1)}, bf16[2,1024,1024]{2,1,0:T(8,128)(2,1)}, bf16[2,1024,512]{2,1...) custom-call(bf16[2,1024,512]{2,1,0:T(8,128)(2,1)} %maximum_maximum_f, ...), custom_call_target="tpu_custom_call" | custom-call | bytes 293601280 | tf_op jit(solution)/shard_map/gather_weights/pallas_call | solution.py:888
  133.6 12.2 %spread.3 = (bf16[512,1024]{1,0:T(8,128)(2,1)}, bf16[2,512,512]{2,1,0:T(8,128)(2,1)}, bf16[2,512,512]{2,1,0:T(8,128)(2,1)}) custom-call(bf16[512,1024]{1,0:T(8,128)(2,1)} %get-tuple-element.325.x.refs_4_, bf16[2,1024,2048]{2,1,0:T(8,128)(2,1)} %get-tuple-element.123.weights.refs_1_.refs_3_), custom_call_target="tpu_custom_call" | custom-call | flops 12884901888 | bytes 8388608 | tf_op jit(solution)/shard_map/spread/pallas_call | solution.py:988
  189.8 14.5 %attend.4 = (f32[512,1024]{1,0:T(8,128)}, f32[8,8,512]{2,1,0:T(8,128)}) custom-call(s32[8]{0:T(128)} %reshape.627.act, s32[8,512]{1,0:T(8,128)} %broadcast_in_dim.119.seg_q, s32[4,512,128]{2,1,0:T(8,128)} %broadcast_in_dim.120.seg_k, bf16[512,1024]{1,0:T(8,128)(2,1)} %get-tuple-element.124.q, bf16[2,512,512]{2,1,0:T(8,128)(2,1)} %get-tuple-element.128.refs_0_.refs_4_, ...), custom_call_target="tpu_custom_call" | custom-call | flops 25769803776 | bytes 5242880 | tf_op jit(solution)/shard_map/attend/pallas_call | solution.py:266
  209.8 14.4 %attend.6 = (f32[512,1024]{1,0:T(8,128)}, f32[8,8,512]{2,1,0:T(8,128)}) custom-call(s32[8]{0:T(128)} %reshape.627.act, s32[8,512]{1,0:T(8,128)} %broadcast_in_dim.119.seg_q, s32[4,512,128]{2,1,0:T(8,128)} %broadcast_in_dim.120.seg_k, bf16[512,1024]{1,0:T(8,128)(2,1)} %get-tuple-element.124.q, ...), custom_call_target="tpu_custom_call", output_to_operand_aliasing={{0}: (12, {}), {1}: (13, {})} | custom-call | flops 25769803776 | bytes 5242880 | tf_op jit(solution)/shard_map/attend/pallas_call | solution.py:266
  224.7 11.4 %collective-permute-start.10 = (bf16[64,1024]{1,0:T(8,128)(2,1)S(1)}, bf16[64,1024]{1,0:T(8,128)(2,1)S(1)}, u32[]{:S(2)}, u32[]{:S(2)}) collective-permute-start(bf16[64,1024]{1,0:T(8,128)(2,1)S(1)} %get-tuple-element.366), channel_id=1, source_target_pairs={{0,3},{1,2},{2,1},{3,0},{4,7},{5,6},{6,5},{7,4},{8,11},{9,10},{10,... | collective-permute-start | bytes 393224 | tf_op jit(solution)/shard_map/ppermute | solution.py:35
  257.1 12.0 %collect.3 = (f32[512,1024]{1,0:T(8,128)}, bf16[512,1024]{1,0:T(8,128)(2,1)}, f32[512,1024]{1,0:T(8,128)}, f32[512,128]{1,0:T(8,128)}) custom-call(bf16[512,1024]{1,0:T(8,128)(2,1)} %convert_element_type.642.refs_0_, bf16[2,1024,2048]{2,1,0:T(8,128)(2,1)} %get-tuple-element.123.weights.refs_1_.refs_3_, f32[512,1024]{1,0:T(8,128)} %get-tuple-element.324.refs_2_, ...), custom_call_target="tpu_custom_call" | custom-call | flops 4294967296 | bytes 8388608 | tf_op jit(solution)/shard_map/collect/pallas_call | solution.py:1056
  269.6 21.2 %feed_forward.1 = (f32[512,1024]{1,0:T(8,128)}, bf16[512,1024]{1,0:T(8,128)(2,1)}, f32[512,1024]{1,0:T(8,128)}, f32[512,128]{1,0:T(8,128)}, bf16[512,4096]{1,0:T(8,128)(2,1)}, /*index=5*/bf16[512,4096]{1,0:T(8,128)(2,1)}) custom-call(bf16[512,1024]{1,0:T(8,128)(2,1)} %get-tuple-element.138.x, f32[512,1024]{1,0:T(8,128)} %get-tuple-element.139.resid, ...), custom_call_target="tpu_custom_call" | custom-call | flops 25769803776 | bytes 16777216 | tf_op jit(solution)/shard_map/feed_forward/pallas_call | solution.py:1152
  307.2 17.2 %to_encoder.2.q = bf16[8,256,128]{2,1,0:T(8,128)(2,1)} custom-call(bf16[2,256,128]{2,1,0:T(8,128)(2,1)} %pad_maximum_fusion.33.refs_0_), custom_call_target="tpu_custom_call" | custom-call | bytes 62914560 | tf_op jit(solution)/shard_map/to_encoder/pallas_call | solution.py:573
  347.9 20.5 %to_decoder.1 = (bf16[256,256]{1,0:T(8,128)(2,1)}, f32[2,256,128]{2,1,0:T(8,128)}, f32[2,8,256]{2,1,0:T(8,128)}) custom-call(bf16[8,256,128]{2,1,0:T(8,128)(2,1)} %get-tuple-element.153.refs_0_, f32[8,8,256]{2,1,0:T(8,128)} %get-tuple-element.154.refs_1_), custom_call_target="tpu_custom_call" | custom-call | bytes 62914560 | tf_op jit(solution)/shard_map/to_decoder/pallas_call | solution.py:654
  370.5 29.7 %forward_rows.1 = (f32[64,1024]{1,0:T(8,128)}, f32[64,1024]{1,0:T(8,128)}, f32[64,128]{1,0:T(8,128)}, bf16[256,1024]{1,0:T(8,128)(2,1)}) custom-call(bf16[256,1024]{1,0:T(8,128)(2,1)} %convolution_convert_fusion.9.refs_0_, f32[64,1024]{1,0:T(8,128)} %get-tuple-element.292.refs_1_, f32[1,1024]{1,0:T(1,128)} %get-tuple-element.381.refs_2_.refs_4_, ...), custom_call_target="tpu_custom_call" | custom-call | bytes 91750400 | tf_op jit(solution)/shard_map/forward_rows/pallas_call | solution.py:452
  403.7 29.8 %turn_rows.1 = (bf16[64,1024]{1,0:T(8,128)(2,1)}, f32[64,1024]{1,0:T(8,128)}, f32[8,1024]{1,0:T(8,128)}, bf16[256,1024]{1,0:T(8,128)(2,1)}) custom-call(bf16[256,1024]{1,0:T(8,128)(2,1)} %fusion.9.refs_0_, f32[64,1024]{1,0:T(8,128)} %get-tuple-element.158.refs_1_, f32[1,1024]{1,0:T(1,128)} %get-tuple-element.379.refs_2_, ...), custom_call_target="tpu_custom_call" | custom-call | bytes 91750400 | tf_op jit(solution)/shard_map/turn_rows/pallas_call | solution.py:452
  443.9 27.5 %backward_rows.2 = (f32[64,1024]{1,0:T(8,128)}, f32[8,1024]{1,0:T(8,128)}, bf16[256,1024]{1,0:T(8,128)(2,1)}) custom-call(bf16[256,1024]{1,0:T(8,128)(2,1)} %fusion.8.refs_0_, f32[64,1024]{1,0:T(8,128)} %get-tuple-element.161.refs_1_, f32[64,1024]{1,0:T(8,128)} %get-tuple-element.162.refs_2_, f32[64,128]{1,0:T(8,128)} %get-tuple-element.163.refs_3_, ...), custom_call_target="tpu_custom_call" | custom-call | bytes 91750400 | tf_op jit(solution)/shard_map/backward_rows/pallas_call | solution.py:452
  478.2 20.9 %to_encoder.3 = (bf16[8,256,128]{2,1,0:T(8,128)(2,1)}, f32[8,8,256]{2,1,0:T(8,128)}) custom-call(bf16[2,256,128]{2,1,0:T(8,128)(2,1)} %pad_maximum_fusion.34.refs_0_, f32[2,256,128]{2,1,0:T(8,128)} %get-tuple-element.166.refs_1_, f32[2,8,256]{2,1,0:T(8,128)} %get-tuple-element.167.refs_2_), custom_call_target="tpu_custom_call" | custom-call | bytes 62914560 | tf_op jit(solution)/shard_map/to_encoder/pallas_call | solution.py:573
  499.1 11.0 %attend_back.4 = (bf16[8,256,128]{2,1,0:T(8,128)(2,1)}, bf16[2,512,1024]{2,1,0:T(8,128)(2,1)}) custom-call(s32[1]{0:T(128)} %bitcast.30.act, s32[8,256]{1,0:T(8,128)} %broadcast_in_dim.116.seg_q, s32[1,512,128]{2,1,0:T(8,128)} %broadcast_in_dim.117.seg_k, bf16[8,256,128]{2,1,0:T(8,128)(2,1)} %to_encoder.2.q, bf16[2,512,1024]{2,1,0:T(8,128)(2,1)} %spread.4.refs_0_.refs_1_, ...), custom_call_target="tpu_custom_call" | custom-call | flops 10737418240 | bytes 10485760 | tf_op jit(solution)/shard_map/attend_back/pallas_call | solution.py:302
  511.6 16.8 %collect.4 = (f32[512,1024]{1,0:T(8,128)}, bf16[512,1024]{1,0:T(8,128)(2,1)}, f32[8,1024]{1,0:T(8,128)}, bf16[1024,1024]{1,0:T(8,128)(2,1)}, bf16[1024,1024]{1,0:T(8,128)(2,1)}) custom-call(bf16[2,512,1024]{2,1,0:T(8,128)(2,1)} %get-tuple-element.171.refs_0_, bf16[2,1024,1024]{2,1,0:T(8,128)(2,1)} %pad_maximum_fusion.weights.refs_1_, ...), custom_call_target="tpu_custom_call" | custom-call | flops 17179869184 | bytes 4194304 | tf_op jit(solution)/shard_map/collect/pallas_call | solution.py:1056
  529.9 31.7 %feed_forward_back.1 = (f32[512,1024]{1,0:T(8,128)}, bf16[512,1024]{1,0:T(8,128)(2,1)}, f32[8,1024]{1,0:T(8,128)}, bf16[1024,2048]{1,0:T(8,128)(2,1)}, bf16[1024...) custom-call(bf16[512,1024]{1,0:T(8,128)(2,1)} %get-tuple-element.138.x, ...), custom_call_target="tpu_custom_call" | custom-call | flops 34359738368 | bytes 33554432 | tf_op jit(solution)/shard_map/feed_forward_back/pallas_call | solution.py:1208
  591.7 10.9 %spread.5 = (bf16[512,1024]{1,0:T(8,128)(2,1)}, bf16[1024,512]{1,0:T(8,128)(2,1)}, bf16[1024,512]{1,0:T(8,128)(2,1)}) custom-call(bf16[512,1024]{1,0:T(8,128)(2,1)} %get-tuple-element.181.x, bf16[2,1024,2048]{2,1,0:T(8,128)(2,1)} %get-tuple-element.123.weights.refs_1_.refs_3_, bf16[512,1024]{1,0:T(8,128)(2,1)} %convert_element_type.642.refs_0_), custom_call_target="tpu_custom_call" | custom-call | flops 8589934592 | bytes 8388608 | tf_op jit(solution)/shard_map/spread/pallas_call | solution.py:988
  611.0 26.6 %backward_rows.3 = (f32[64,1024]{1,0:T(8,128)}, f32[8,1024]{1,0:T(8,128)}, bf16[256,1024]{1,0:T(8,128)(2,1)}) custom-call(bf16[256,1024]{1,0:T(8,128)(2,1)} %convolution_convert_fusion.8.refs_0_, f32[64,1024]{1,0:T(8,128)} %get-tuple-element.186.refs_1_, f32[64,1024]{1,0:T(8,128)} %get-tuple-element.293.refs_2_, f32[64,128]{1,0:T(8,128)} %broadcast_in_dim.133.refs_3_, ...), custom_call_target="tpu_custom_call" | custom-call | bytes 91750400 | tf_op jit(solution)/shard_map/backward_rows/pallas_call | solution.py:452
  657.7 21.7 %attend_back.6 = (bf16[512,1024]{1,0:T(8,128)(2,1)}, bf16[2,512,512]{2,1,0:T(8,128)(2,1)}, bf16[2,512,512]{2,1,0:T(8,128)(2,1)}, bf16[2,512,512]{2,1,0:T(8,128)(2,1)}, bf16[2,512,512]{2,1,0:T(8,128)(2,1)}) custom-call(s32[8]{0:T(128)} %reshape.627.act, s32[8,512]{1,0:T(8,128)} %broadcast_in_dim.119.seg_q, s32[4,512,128]{2,1,0:T(8,128)} %broadcast_in_dim.120.seg_k, ...), custom_call_target="tpu_custom_call" | custom-call | flops 42949672960 | bytes 10485760 | tf_op jit(solution)/shard_map/attend_back/pallas_call | solution.py:302
  681.2 11.8 %collective-permute-start.27 = (bf16[64,1024]{1,0:T(8,128)(2,1)S(1)}, bf16[64,1024]{1,0:T(8,128)(2,1)S(1)}, u32[]{:S(2)}, u32[]{:S(2)}) collective-permute-start(bf16[64,1024]{1,0:T(8,128)(2,1)S(1)} %get-tuple-element.356), channel_id=1, source_target_pairs={{0,3},{1,2},{2,1},{3,0},{4,7},{5,6},{6,5},{7,4},{8,11},{9,10},{10,... | collective-permute-start | bytes 393224 | tf_op jit(solution)/shard_map/ppermute | solution.py:35
  705.3 21.5 %attend_back.7 = (bf16[512,1024]{1,0:T(8,128)(2,1)}, bf16[2,512,512]{2,1,0:T(8,128)(2,1)}, bf16[2,512,512]{2,1,0:T(8,128)(2,1)}, bf16[2,512,512]{2,1,0:T(8,128)(2,1)}, bf16[2,512,512]{2,1,0:T(8,128)(2,1)}) custom-call(s32[8]{0:T(128)} %reshape.627.act, s32[8,512]{1,0:T(8,128)} %broadcast_in_dim.119.seg_q, ...), custom_call_target="tpu_custom_call", output_to_operand_aliasing={{0}: (15, {})} | custom-call | flops 42949672960 | bytes 10485760 | tf_op jit(solution)/shard_map/attend_back/pallas_call | solution.py:302
  740.0 19.2 %collective-permute-done.34 = bf16[2,512,512]{2,1,0:T(8,128)(2,1)S(1)} collective-permute-done((bf16[2,512,512]{2,1,0:T(8,128)(2,1)}, bf16[2,512,512]{2,1,0:T(8,128)(2,1)S(1)}, u32[]{:S(2)}, u32[]{:S(2)}) %collective-permute-start.34) | collective-permute-done | bytes 1048608 | tf_op jit(solution)/shard_map/ppermute | solution.py:35
  761.4 23.3 %collect.5 = (f32[512,1024]{1,0:T(8,128)}, bf16[512,1024]{1,0:T(8,128)(2,1)}, f32[8,1024]{1,0:T(8,128)}, bf16[1024,1536]{1,0:T(8,128)(2,1)}, bf16[1024,1536]{1,0:T(8,128)(2,1)}) custom-call(bf16[512,1024]{1,0:T(8,128)(2,1)} %get-tuple-element.202.refs_0_, bf16[2,512,512]{2,1,0:T(8,128)(2,1)} %add_convert_fusion.8.refs_1_, ...), custom_call_target="tpu_custom_call" | custom-call | flops 25769803776 | bytes 8388608 | tf_op jit(solution)/shard_map/collect/pallas_call | solution.py:1056
  784.7 102.4 %finish.1 = (f32[4,256,256]{2,1,0:T(8,128)}, f32[2,256,256]{2,1,0:T(8,128)}, f32[2,256,1024]{2,1,0:T(8,128)}, bf16[512,512]{1,0:T(8,128)(2,1)}, bf16[512,512]{1,0:T(8,128)(2,1)}, /*index=5*/f32[8,1024]{1,0:T(8,128)}) custom-call(bf16[1024,1536]{1,0:T(8,128)(2,1)} %get-tuple-element.217.refs_0_, bf16[1024,512]{1,0:T(8,128)(2,1)} %get-tuple-element.218.refs_1_, ...), custom_call_target="tpu_custom_call" | custom-call | bytes 209715200 | tf_op jit(solution)/shard_map/finish/pallas_call | solution.py:1475
  (425 shorter events, 252.4 us)
Async XLA Ops:
  7.2 217.5 %all-gather.3.cloned.1.call-start = ((), (), s32[]{:S(2)}) async-start(), calls=%async_computation.5 | async-start | bytes 7864320 | tf_op jit(solution)/shard_map/all_gather | solution.py:903
  145.8 23.5 %collective-permute-start.2 = (bf16[2,512,512]{2,1,0:T(8,128)(2,1)}, bf16[2,512,512]{2,1,0:T(8,128)(2,1)}, u32[]{:S(2)}, u32[]{:S(2)}) collective-permute-start(bf16[2,512,512]{2,1,0:T(8,128)(2,1)} %get-tuple-element.128.refs_0_.refs_4_), channel_id=1, source_target_pairs={{0,1},{1,0},{2,3},{3,2},{4,5},{5,4},{6,7},{7,6},{8,9},{9,8},{10,11... | collective-permute-start | bytes 3145736 | tf_op jit(solution)/shard_map/ppermute | solution.py:35
  145.8 42.0 %collective-permute-start.3 = (bf16[2,512,512]{2,1,0:T(8,128)(2,1)}, bf16[2,512,512]{2,1,0:T(8,128)(2,1)}, u32[]{:S(2)}, u32[]{:S(2)}) collective-permute-start(bf16[2,512,512]{2,1,0:T(8,128)(2,1)} %get-tuple-element.128.refs_0_.refs_4_), channel_id=1, source_target_pairs={{0,16},{16,0},{1,17},{17,1},{2,18},{18,2},{3,19},{19,3},{4,20},{20... | collective-permute-start | bytes 3145736 | tf_op jit(solution)/shard_map/ppermute | solution.py:35
  154.5 115.1 %all-gather.5.cloned.1.call-start = ((), (), s32[]{:S(2)}) async-start(), calls=%async_computation.6 | async-start | bytes 1966080 | tf_op jit(solution)/shard_map/all_gather | solution.py:903
  161.0 43.3 %collective-permute-start.1 = (bf16[2,512,512]{2,1,0:T(8,128)(2,1)}, bf16[2,512,512]{2,1,0:T(8,128)(2,1)}, u32[]{:S(2)}, u32[]{:S(2)}) collective-permute-start(bf16[2,512,512]{2,1,0:T(8,128)(2,1)} %get-tuple-element.135.refs_0_.refs_4_), channel_id=1, source_target_pairs={{0,1},{1,0},{2,3},{3,2},{4,5},{5,4},{6,7},{7,6},{8,9},{9,8},{10,11... | collective-permute-start | bytes 3145736 | tf_op jit(solution)/shard_map/ppermute | solution.py:35
  224.6 44.9 %collective-permute-start.7 = (bf16[1024,3072]{1,0:T(8,128)(2,1)}, bf16[1024,3072]{1,0:T(8,128)(2,1)}, u32[]{:S(2)}, u32[]{:S(2)}) collective-permute-start(bf16[1024,3072]{1,0:T(8,128)(2,1)} %all-gather.3.cloned.1.call-done.refs_1_.refs_4_), channel_id=1, source_target_pairs={{0,16},{16,0},{1,17},{17,1},{2,18},{18,2},{3,19},{19,3},{4,20},{20... | collective-permute-start | bytes 18874376 | tf_op jit(solution)/shard_map/ppermute | solution.py:35
  224.7 32.0 %collective-permute-start.10 = (bf16[64,1024]{1,0:T(8,128)(2,1)S(1)}, bf16[64,1024]{1,0:T(8,128)(2,1)S(1)}, u32[]{:S(2)}, u32[]{:S(2)}) collective-permute-start(bf16[64,1024]{1,0:T(8,128)(2,1)S(1)} %get-tuple-element.366), channel_id=1, source_target_pairs={{0,3},{1,2},{2,1},{3,0},{4,7},{5,6},{6,5},{7,4},{8,11},{9,10},{10,... | collective-permute-start | bytes 393224 | tf_op jit(solution)/shard_map/ppermute | solution.py:35
  236.1 20.5 %collective-permute-start.9 = (bf16[64,1024]{1,0:T(8,128)(2,1)S(1)}, bf16[64,1024]{1,0:T(8,128)(2,1)S(1)}, u32[]{:S(2)}, u32[]{:S(2)}) collective-permute-start(bf16[64,1024]{1,0:T(8,128)(2,1)S(1)} %get-tuple-element.367), channel_id=1, source_target_pairs={{0,2},{1,3},{2,0},{3,1},{4,6},{5,7},{6,4},{7,5},{8,10},{9,11},{10,... | collective-permute-start | bytes 393224 | tf_op jit(solution)/shard_map/ppermute | solution.py:35
  236.1 20.5 %collective-permute-start.8 = (bf16[64,1024]{1,0:T(8,128)(2,1)S(1)}, bf16[64,1024]{1,0:T(8,128)(2,1)S(1)}, u32[]{:S(2)}, u32[]{:S(2)}) collective-permute-start(bf16[64,1024]{1,0:T(8,128)(2,1)S(1)} %get-tuple-element.365), channel_id=1, source_target_pairs={{0,1},{1,0},{2,3},{3,2},{4,5},{5,4},{6,7},{7,6},{8,9},{9,8},{10,11... | collective-permute-start | bytes 393224 | tf_op jit(solution)/shard_map/ppermute | solution.py:35
  236.8 293.1 %reduce-scatter.6.cloned.1.call-start = ((), (), s32[]{:S(2)}) async-start(), calls=%async_computation.7 | async-start | bytes 2621440 | tf_op jit(solution)/shard_map/reduce_scatter | solution.py:911
  269.6 54.8 %collective-permute-start.14 = (bf16[1024,768]{1,0:T(8,128)(2,1)}, bf16[1024,768]{1,0:T(8,128)(2,1)}, u32[]{:S(2)}, u32[]{:S(2)}) collective-permute-start(bf16[1024,768]{1,0:T(8,128)(2,1)} %all-gather.5.cloned.1.call-done), channel_id=1, source_target_pairs={{0,16},{16,0},{1,17},{17,1},{2,18},{18,2},{3,19},{19,3},{4,20},{20... | collective-permute-start | bytes 4718600 | tf_op jit(solution)/shard_map/ppermute | solution.py:35
  440.2 31.2 %collective-permute-start.16 = (f32[3,1024]{1,0:T(4,128)S(1)}, f32[3,1024]{1,0:T(4,128)S(1)}, u32[]{:S(2)}, u32[]{:S(2)}) collective-permute-start(f32[3,1024]{1,0:T(4,128)S(1)} %fusion.20), channel_id=1, source_target_pairs={{0,1},{1,0},{2,3},{3,2},{4,5},{5,4},{6,7},{7,6},{8,9},{9,8},{10,11... | collective-permute-start | bytes 36872 | tf_op jit(solution)/shard_map/ppermute | solution.py:35
  443.9 29.2 %collective-permute-start.15 = (bf16[1024,1024]{1,0:T(8,128)(2,1)}, bf16[1024,1024]{1,0:T(8,128)(2,1)S(1)}, u32[]{:S(2)}, u32[]{:S(2)}) collective-permute-start(bf16[1024,1024]{1,0:T(8,128)(2,1)} %pad_maximum_fusion.3), channel_id=1, source_target_pairs={{0,16},{16,0},{1,17},{17,1},{2,18},{18,2},{3,19},{19,3},{4,20},{20... | collective-permute-start | bytes 6291464 | tf_op jit(solution)/shard_map/ppermute | solution.py:35
  475.3 285.2 %reduce-scatter.8.cloned.1.call-start = ((), (), s32[]{:S(2)}) async-start(), calls=%async_computation.8 | async-start | bytes 2621440 | tf_op jit(solution)/shard_map/reduce_scatter | solution.py:911
  510.1 19.5 %collective-permute-start.18 = (bf16[8,256,128]{2,1,0:T(8,128)(2,1)}, bf16[8,256,128]{2,1,0:T(8,128)(2,1)S(1)}, u32[]{:S(2)}, u32[]{:S(2)}) collective-permute-start(bf16[8,256,128]{2,1,0:T(8,128)(2,1)} %get-tuple-element.170), channel_id=1, source_target_pairs={{16,0},{17,1},{2,18},{3,19},{20,4},{21,5},{6,22},{7,23},{24,8},{25... | collective-permute-start | bytes 1572872 | tf_op jit(solution)/shard_map/ppermute | solution.py:40
  528.4 33.2 %collective-permute-start.35 = (bf16[1024,1024]{1,0:T(8,128)(2,1)}, bf16[1024,1024]{1,0:T(8,128)(2,1)S(1)}, u32[]{:S(2)}, u32[]{:S(2)}) collective-permute-start(bf16[1024,1024]{1,0:T(8,128)(2,1)} %get-tuple-element.213), channel_id=1, source_target_pairs={{0,16},{16,0},{1,17},{17,1},{2,18},{18,2},{3,19},{19,3},{4,20},{20... | collective-permute-start | bytes 6291464 | tf_op jit(solution)/shard_map/ppermute | solution.py:35
  564.0 196.6 %reduce-scatter.10.cloned.1.call-start = ((), (), s32[]{:S(2)}) async-start(), calls=%async_computation.9 | async-start | bytes 5242880 | tf_op jit(solution)/shard_map/reduce_scatter | solution.py:911
  564.4 38.2 %collective-permute-start.22 = (bf16[1024,2048]{1,0:T(8,128)(2,1)}, bf16[1024,2048]{1,0:T(8,128)(2,1)}, u32[]{:S(2)}, u32[]{:S(2)}) collective-permute-start(bf16[1024,2048]{1,0:T(8,128)(2,1)} %get-tuple-element.184), channel_id=1, source_target_pairs={{0,16},{16,0},{1,17},{17,1},{2,18},{18,2},{3,19},{19,3},{4,20},{20... | collective-permute-start | bytes 12582920 | tf_op jit(solution)/shard_map/ppermute | solution.py:35
  577.0 183.6 %reduce-scatter.12.cloned.1.call-start = ((), (), s32[]{:S(2)}) async-start(), calls=%async_computation.10 | async-start | bytes 5242880 | tf_op jit(solution)/shard_map/reduce_scatter | solution.py:911
  651.0 133.7 %reduce-scatter.14.cloned.1.call-start = ((), (), s32[]{:S(2)}) async-start(), calls=%async_computation.11 | async-start | bytes 1966080 | tf_op jit(solution)/shard_map/reduce_scatter | solution.py:911
  679.5 23.7 %collective-permute-start.30 = (bf16[2,512,512]{2,1,0:T(8,128)(2,1)}, bf16[2,512,512]{2,1,0:T(8,128)(2,1)S(1)}, u32[]{:S(2)}, u32[]{:S(2)}) collective-permute-start(bf16[2,512,512]{2,1,0:T(8,128)(2,1)} %get-tuple-element.199), channel_id=1, source_target_pairs={{0,16},{16,0},{1,17},{17,1},{2,18},{18,2},{3,19},{19,3},{4,20},{20... | collective-permute-start | bytes 3145736 | tf_op jit(solution)/shard_map/ppermute | solution.py:35
  680.7 24.3 %collective-permute-start.29 = (bf16[2,512,512]{2,1,0:T(8,128)(2,1)S(1)}, bf16[2,512,512]{2,1,0:T(8,128)(2,1)S(1)}, u32[]{:S(2)}, u32[]{:S(2)}) collective-permute-start(bf16[2,512,512]{2,1,0:T(8,128)(2,1)S(1)} %copy-done.77), channel_id=1, source_target_pairs={{0,16},{16,0},{1,17},{17,1},{2,18},{18,2},{3,19},{19,3},{4,20},{20... | collective-permute-start | bytes 3145736 | tf_op jit(solution)/shard_map/ppermute | solution.py:35
  703.5 25.0 %collective-permute-start.31 = (bf16[2,512,512]{2,1,0:T(8,128)(2,1)S(1)}, bf16[2,512,512]{2,1,0:T(8,128)(2,1)S(1)}, u32[]{:S(2)}, u32[]{:S(2)}) collective-permute-start(bf16[2,512,512]{2,1,0:T(8,128)(2,1)S(1)} %add_convert_fusion.9), channel_id=1, source_target_pairs={{0,1},{1,0},{2,3},{3,2},{4,5},{5,4},{6,7},{7,6},{8,9},{9,8},{10,11... | collective-permute-start | bytes 3145736 | tf_op jit(solution)/shard_map/ppermute | solution.py:35
  733.9 25.4 %collective-permute-start.34 = (bf16[2,512,512]{2,1,0:T(8,128)(2,1)}, bf16[2,512,512]{2,1,0:T(8,128)(2,1)S(1)}, u32[]{:S(2)}, u32[]{:S(2)}) collective-permute-start(bf16[2,512,512]{2,1,0:T(8,128)(2,1)} %add_convert_fusion.6), channel_id=1, source_target_pairs={{0,1},{1,0},{2,3},{3,2},{4,5},{5,4},{6,7},{7,6},{8,9},{9,8},{10,11... | collective-permute-start | bytes 3145736 | tf_op jit(solution)/shard_map/ppermute | solution.py:35
  (97 other events, 1436.6 us)
Sparse Core Ops, SparseCore 0:
  154.6 69.9 all-gather.2
  236.9 32.6 all-gather.4
  475.4 39.6 reduce-scatter.5
  564.1 39.6 reduce-scatter.7
  606.6 52.6 reduce-scatter.9
  662.4 52.6 reduce-scatter.11
  736.7 43.8 reduce-scatter.13

commit v7 on v5

--- a/solution.py
+++ b/solution.py
@@ -827,6 +827,9 @@
 
     steps = [(1 << i, bit) for i, bit in enumerate(bits)]
     for_attn, for_cross, for_ffn = [{"array": a, "todo": list(steps), "now": []} for a in range(3)]
+    at = pl.ds(pl.multiple_of(me * dec_rows.shape[0], dec_rows.shape[0]), dec_rows.shape[0])
+    dec_full[at, :] = dec_rows[...]
+    dec_sent = [push(dec_full.at[at], dec_full.at[at], peer) for peer in line]
     arrived(0)
     advance(for_attn)
     arrived(2)
@@ -841,9 +844,6 @@
     def _():
         _send(leaving, coming, send_sem.at[token_sem], recv_sem.at[token_sem], chips[bits[0]])
 
-    at = pl.ds(pl.multiple_of(me * dec_rows.shape[0], dec_rows.shape[0]), dec_rows.shape[0])
-    dec_full[at, :] = dec_rows[...]
-    dec_sent = [push(dec_full.at[at], dec_full.at[at], peer) for peer in line]
     half = (count - 1) * wide // 2
     orders, held = (dp_bits, dp_bits[::-1]), ([0], [0])
     moving = plane_step(0)
@@ -1363,8 +1363,6 @@
 
     moving = [plane_start(0, r) for r in range(2)]
     for_attn = []
-    advance(chains[1])
-    advance(chains[2])
 
     half = tokens.shape[1] // 2
     far_sem, near_sem, same_sem = number(), number(), number()
@@ -1379,6 +1377,9 @@
     @pl.when(core == 0)
     def _():
         _send(tokens.at[:, pl.ds(half, half)], near, send_sem.at[near_sem], recv_sem.at[near_sem], sibling)
+
+    advance(chains[1])
+    advance(chains[2])
 
     for j in range(n_steps):
         for r in range(2):

time: 913 us -> 909 us (level)
  starting transfers between devices: 88 us -> 52.8 us
  Pallas kernels: 597 us -> 616 us
  waiting for transfers between devices: 50.7 us -> 64 us
    ppermute x32, starting transfers between devices: 73 us -> 38.1 us  [swap(): lax.ppermute(value, axis, [(i, i ^ mask) for i in range(lax.axis_size(axi...]
    pallas_call x1, Pallas kernels: 91.1 us -> 109 us  [finish(): pl.pallas_call(partial(_finish_kernel, slot_bits(), count, planes), out_s...]
    all_gather x2, waiting for transfers between devices: 0.02 us -> 11.5 us  [gather_planes(): return lax.all_gather(rest, 'dp', axis=0, tiled=True)]
  transfers between devices with their start and end apart: 43 -> 43, of which waited for: 11 -> 14; matrix products, arithmetic and copies ran while one was open for 12% -> 12% of each run, Pallas kernels for 43% -> 45%
where the time goes in v7:
time: 909 us; the launch traced here: 901 us
  Pallas kernels  616 us (68%)
  other arithmetic  64.3 us (7%)
  waiting for transfers between devices  64 us (7%)
  local copies, waits for them, and re-layouts  53 us (6%)
  starting transfers between devices  52.8 us (6%)
  between operations  25.3 us (3%)
  matrix products  24.8 us (3%)
    pallas_call x4, Pallas kernels, rows_call(): pl.pallas_call(partial(_rows_kernel, count, scatter, gather, middle, len(...  113 us
    pallas_call x1, Pallas kernels, finish(): pl.pallas_call(partial(_finish_kernel, slot_bits(), count, planes), out_s...  109 us
    pallas_call x1, Pallas kernels, gather_weights(): pl.pallas_call(partial(_gather_kernel, slot_bits(), count, planes), out_s...  99.9 us
    pallas_call x4, Pallas kernels, attend_back(): pl.pallas_call(partial(_attend_back_kernel, chunks, tq, tk, causal, own_d...  57.6 us
    pallas_call x3, Pallas kernels, collect(): pl.pallas_call(partial(_collect_kernel, kinds, use, wide, each, blocks, l...  51.8 us
    ppermute x32, waiting for transfers between devices, swap(): lax.ppermute(value, axis, [(i, i ^ mask) for i in range(lax.axis_size(axi...  49.7 us
    pallas_call x4, Pallas kernels, attend(): pl.pallas_call(partial(_attend_kernel, chunks, tq, tk, causal), out_shape...  40.7 us
    ppermute x32, starting transfers between devices, swap(): lax.ppermute(value, axis, [(i, i ^ mask) for i in range(lax.axis_size(axi...  38.1 us
  transfers between devices with their start and end apart: 43, of which 14 were waited for; matrix products, arithmetic and copies ran while one was open for 12% of the time, Pallas kernels for 45%

profile of v7, /device:TPU:0, one launch (start us, length us, event | category | flops | bytes accessed | tf_op | source)
XLA Modules:
  0.0 900.6 jit_solution(16665815165037752420)
XLA Ops:
  29.5 99.9 %gather_weights.1 = (bf16[2,1024,2048]{2,1,0:T(8,128)(2,1)}, bf16[2,1024,256]{2,1,0:T(8,128)(2,1)}, bf16[2,1024,1024]{2,1,0:T(8,128)(2,1)}, bf16[2,1024,512]{2,1...) custom-call(bf16[2,1024,512]{2,1,0:T(8,128)(2,1)} %maximum_maximum_f, ...), custom_call_target="tpu_custom_call" | custom-call | bytes 293601280 | tf_op jit(solution)/shard_map/gather_weights/pallas_call | solution.py:888
  133.8 12.2 %spread.3 = (bf16[512,1024]{1,0:T(8,128)(2,1)}, bf16[2,512,512]{2,1,0:T(8,128)(2,1)}, bf16[2,512,512]{2,1,0:T(8,128)(2,1)}) custom-call(bf16[512,1024]{1,0:T(8,128)(2,1)} %get-tuple-element.329.x.refs_4_, bf16[2,1024,2048]{2,1,0:T(8,128)(2,1)} %get-tuple-element.125.weights.refs_1_.refs_3_), custom_call_target="tpu_custom_call" | custom-call | flops 12884901888 | bytes 8388608 | tf_op jit(solution)/shard_map/spread/pallas_call | solution.py:988
  187.1 14.5 %attend.4 = (f32[512,1024]{1,0:T(8,128)}, f32[8,8,512]{2,1,0:T(8,128)}) custom-call(s32[8]{0:T(128)} %reshape.627.act, s32[8,512]{1,0:T(8,128)} %broadcast_in_dim.119.seg_q, s32[4,512,128]{2,1,0:T(8,128)} %broadcast_in_dim.120.seg_k, bf16[512,1024]{1,0:T(8,128)(2,1)} %get-tuple-element.126.q, bf16[2,512,512]{2,1,0:T(8,128)(2,1)} %get-tuple-element.130.refs_0_.refs_4_, ...), custom_call_target="tpu_custom_call" | custom-call | flops 25769803776 | bytes 5242880 | tf_op jit(solution)/shard_map/attend/pallas_call | solution.py:266
  207.1 14.4 %attend.6 = (f32[512,1024]{1,0:T(8,128)}, f32[8,8,512]{2,1,0:T(8,128)}) custom-call(s32[8]{0:T(128)} %reshape.627.act, s32[8,512]{1,0:T(8,128)} %broadcast_in_dim.119.seg_q, s32[4,512,128]{2,1,0:T(8,128)} %broadcast_in_dim.120.seg_k, bf16[512,1024]{1,0:T(8,128)(2,1)} %get-tuple-element.126.q, ...), custom_call_target="tpu_custom_call", output_to_operand_aliasing={{0}: (12, {}), {1}: (13, {})} | custom-call | flops 25769803776 | bytes 5242880 | tf_op jit(solution)/shard_map/attend/pallas_call | solution.py:266
  244.5 11.8 %collect.3 = (f32[512,1024]{1,0:T(8,128)}, bf16[512,1024]{1,0:T(8,128)(2,1)}, f32[512,1024]{1,0:T(8,128)}, f32[512,128]{1,0:T(8,128)}) custom-call(bf16[512,1024]{1,0:T(8,128)(2,1)} %convert_element_type.642.refs_0_, bf16[2,1024,2048]{2,1,0:T(8,128)(2,1)} %get-tuple-element.125.weights.refs_1_.refs_3_, f32[512,1024]{1,0:T(8,128)} %get-tuple-element.328.refs_2_, ...), custom_call_target="tpu_custom_call" | custom-call | flops 4294967296 | bytes 8388608 | tf_op jit(solution)/shard_map/collect/pallas_call | solution.py:1056
  256.3 11.2 %all-gather.5.cloned.1.call-done = bf16[1024,768]{1,0:T(8,128)(2,1)} async-done(((bf16[256,768]{1,0:T(8,128)(2,1)}), bf16[1024,768]{1,0:T(8,128)(2,1)}) %all-gather.5.cloned.1.call-update) | async-done | bytes 1572880 | tf_op jit(solution)/shard_map/all_gather | solution.py:903
  267.5 21.2 %feed_forward.1 = (f32[512,1024]{1,0:T(8,128)}, bf16[512,1024]{1,0:T(8,128)(2,1)}, f32[512,1024]{1,0:T(8,128)}, f32[512,128]{1,0:T(8,128)}, bf16[512,4096]{1,0:T(8,128)(2,1)}, /*index=5*/bf16[512,4096]{1,0:T(8,128)(2,1)}) custom-call(bf16[512,1024]{1,0:T(8,128)(2,1)} %get-tuple-element.140.x, f32[512,1024]{1,0:T(8,128)} %get-tuple-element.141.resid, ...), custom_call_target="tpu_custom_call" | custom-call | flops 25769803776 | bytes 16777216 | tf_op jit(solution)/shard_map/feed_forward/pallas_call | solution.py:1152
  305.1 17.2 %to_encoder.2.q = bf16[8,256,128]{2,1,0:T(8,128)(2,1)} custom-call(bf16[2,256,128]{2,1,0:T(8,128)(2,1)} %pad_maximum_fusion.33.refs_0_), custom_call_target="tpu_custom_call" | custom-call | bytes 62914560 | tf_op jit(solution)/shard_map/to_encoder/pallas_call | solution.py:573
  326.3 9.3 %spread.4.refs_0_.refs_1_ = bf16[2,512,1024]{2,1,0:T(8,128)(2,1)} custom-call(bf16[512,1024]{1,0:T(8,128)(2,1)} %get-tuple-element.150.x.refs_2_, bf16[2,1024,1024]{2,1,0:T(8,128)(2,1)} %pad_maximum_fusion.weights.refs_1_), custom_call_target="tpu_custom_call" | custom-call | flops 8589934592 | bytes 4194304 | tf_op jit(solution)/shard_map/spread/pallas_call | solution.py:988
  347.5 20.4 %to_decoder.1 = (bf16[256,256]{1,0:T(8,128)(2,1)}, f32[2,256,128]{2,1,0:T(8,128)}, f32[2,8,256]{2,1,0:T(8,128)}) custom-call(bf16[8,256,128]{2,1,0:T(8,128)(2,1)} %get-tuple-element.155.refs_0_, f32[8,8,256]{2,1,0:T(8,128)} %get-tuple-element.156.refs_1_), custom_call_target="tpu_custom_call" | custom-call | bytes 62914560 | tf_op jit(solution)/shard_map/to_decoder/pallas_call | solution.py:654
  370.0 29.7 %forward_rows.1 = (f32[64,1024]{1,0:T(8,128)}, f32[64,1024]{1,0:T(8,128)}, f32[64,128]{1,0:T(8,128)}, bf16[256,1024]{1,0:T(8,128)(2,1)}) custom-call(bf16[256,1024]{1,0:T(8,128)(2,1)} %convolution_convert_fusion.9.refs_0_, f32[64,1024]{1,0:T(8,128)} %get-tuple-element.296.refs_1_, f32[1,1024]{1,0:T(1,128)} %get-tuple-element.385.refs_2_.refs_4_, ...), custom_call_target="tpu_custom_call" | custom-call | bytes 91750400 | tf_op jit(solution)/shard_map/forward_rows/pallas_call | solution.py:452
  403.2 29.8 %turn_rows.1 = (bf16[64,1024]{1,0:T(8,128)(2,1)}, f32[64,1024]{1,0:T(8,128)}, f32[8,1024]{1,0:T(8,128)}, bf16[256,1024]{1,0:T(8,128)(2,1)}) custom-call(bf16[256,1024]{1,0:T(8,128)(2,1)} %fusion.9.refs_0_, f32[64,1024]{1,0:T(8,128)} %get-tuple-element.160.refs_1_, f32[1,1024]{1,0:T(1,128)} %get-tuple-element.383.refs_2_, ...), custom_call_target="tpu_custom_call" | custom-call | bytes 91750400 | tf_op jit(solution)/shard_map/turn_rows/pallas_call | solution.py:452
  441.1 27.5 %backward_rows.2 = (f32[64,1024]{1,0:T(8,128)}, f32[8,1024]{1,0:T(8,128)}, bf16[256,1024]{1,0:T(8,128)(2,1)}) custom-call(bf16[256,1024]{1,0:T(8,128)(2,1)} %fusion.8.refs_0_, f32[64,1024]{1,0:T(8,128)} %get-tuple-element.163.refs_1_, f32[64,1024]{1,0:T(8,128)} %get-tuple-element.164.refs_2_, f32[64,128]{1,0:T(8,128)} %get-tuple-element.165.refs_3_, ...), custom_call_target="tpu_custom_call" | custom-call | bytes 91750400 | tf_op jit(solution)/shard_map/backward_rows/pallas_call | solution.py:452
  476.2 20.9 %to_encoder.3 = (bf16[8,256,128]{2,1,0:T(8,128)(2,1)}, f32[8,8,256]{2,1,0:T(8,128)}) custom-call(bf16[2,256,128]{2,1,0:T(8,128)(2,1)} %pad_maximum_fusion.34.refs_0_, f32[2,256,128]{2,1,0:T(8,128)} %get-tuple-element.168.refs_1_, f32[2,8,256]{2,1,0:T(8,128)} %get-tuple-element.169.refs_2_), custom_call_target="tpu_custom_call" | custom-call | bytes 62914560 | tf_op jit(solution)/shard_map/to_encoder/pallas_call | solution.py:573
  497.1 11.2 %attend_back.4 = (bf16[8,256,128]{2,1,0:T(8,128)(2,1)}, bf16[2,512,1024]{2,1,0:T(8,128)(2,1)}) custom-call(s32[1]{0:T(128)} %bitcast.30.act, s32[8,256]{1,0:T(8,128)} %broadcast_in_dim.116.seg_q, s32[1,512,128]{2,1,0:T(8,128)} %broadcast_in_dim.117.seg_k, bf16[8,256,128]{2,1,0:T(8,128)(2,1)} %to_encoder.2.q, bf16[2,512,1024]{2,1,0:T(8,128)(2,1)} %spread.4.refs_0_.refs_1_, ...), custom_call_target="tpu_custom_call" | custom-call | flops 10737418240 | bytes 10485760 | tf_op jit(solution)/shard_map/attend_back/pallas_call | solution.py:302
  509.8 16.8 %collect.4 = (f32[512,1024]{1,0:T(8,128)}, bf16[512,1024]{1,0:T(8,128)(2,1)}, f32[8,1024]{1,0:T(8,128)}, bf16[1024,1024]{1,0:T(8,128)(2,1)}, bf16[1024,1024]{1,0:T(8,128)(2,1)}) custom-call(bf16[2,512,1024]{2,1,0:T(8,128)(2,1)} %get-tuple-element.173.refs_0_, bf16[2,1024,1024]{2,1,0:T(8,128)(2,1)} %pad_maximum_fusion.weights.refs_1_, ...), custom_call_target="tpu_custom_call" | custom-call | flops 17179869184 | bytes 4194304 | tf_op jit(solution)/shard_map/collect/pallas_call | solution.py:1056
  528.1 31.6 %feed_forward_back.1 = (f32[512,1024]{1,0:T(8,128)}, bf16[512,1024]{1,0:T(8,128)(2,1)}, f32[8,1024]{1,0:T(8,128)}, bf16[1024,2048]{1,0:T(8,128)(2,1)}, bf16[1024...) custom-call(bf16[512,1024]{1,0:T(8,128)(2,1)} %get-tuple-element.140.x, ...), custom_call_target="tpu_custom_call" | custom-call | flops 34359738368 | bytes 33554432 | tf_op jit(solution)/shard_map/feed_forward_back/pallas_call | solution.py:1208
  589.8 10.9 %spread.5 = (bf16[512,1024]{1,0:T(8,128)(2,1)}, bf16[1024,512]{1,0:T(8,128)(2,1)}, bf16[1024,512]{1,0:T(8,128)(2,1)}) custom-call(bf16[512,1024]{1,0:T(8,128)(2,1)} %get-tuple-element.183.x, bf16[2,1024,2048]{2,1,0:T(8,128)(2,1)} %get-tuple-element.125.weights.refs_1_.refs_3_, bf16[512,1024]{1,0:T(8,128)(2,1)} %convert_element_type.642.refs_0_), custom_call_target="tpu_custom_call" | custom-call | flops 8589934592 | bytes 8388608 | tf_op jit(solution)/shard_map/spread/pallas_call | solution.py:988
  609.1 26.1 %backward_rows.3 = (f32[64,1024]{1,0:T(8,128)}, f32[8,1024]{1,0:T(8,128)}, bf16[256,1024]{1,0:T(8,128)(2,1)}) custom-call(bf16[256,1024]{1,0:T(8,128)(2,1)} %convolution_convert_fusion.8.refs_0_, f32[64,1024]{1,0:T(8,128)} %get-tuple-element.188.refs_1_, f32[64,1024]{1,0:T(8,128)} %get-tuple-element.297.refs_2_, f32[64,128]{1,0:T(8,128)} %broadcast_in_dim.133.refs_3_, ...), custom_call_target="tpu_custom_call" | custom-call | bytes 91750400 | tf_op jit(solution)/shard_map/backward_rows/pallas_call | solution.py:452
  655.3 21.4 %attend_back.6 = (bf16[512,1024]{1,0:T(8,128)(2,1)}, bf16[2,512,512]{2,1,0:T(8,128)(2,1)}, bf16[2,512,512]{2,1,0:T(8,128)(2,1)}, bf16[2,512,512]{2,1,0:T(8,128)(2,1)}, bf16[2,512,512]{2,1,0:T(8,128)(2,1)}) custom-call(s32[8]{0:T(128)} %reshape.627.act, s32[8,512]{1,0:T(8,128)} %broadcast_in_dim.119.seg_q, s32[4,512,128]{2,1,0:T(8,128)} %broadcast_in_dim.120.seg_k, ...), custom_call_target="tpu_custom_call" | custom-call | flops 42949672960 | bytes 10485760 | tf_op jit(solution)/shard_map/attend_back/pallas_call | solution.py:302
  683.8 21.4 %attend_back.7 = (bf16[512,1024]{1,0:T(8,128)(2,1)}, bf16[2,512,512]{2,1,0:T(8,128)(2,1)}, bf16[2,512,512]{2,1,0:T(8,128)(2,1)}, bf16[2,512,512]{2,1,0:T(8,128)(2,1)}, bf16[2,512,512]{2,1,0:T(8,128)(2,1)}) custom-call(s32[8]{0:T(128)} %reshape.627.act, s32[8,512]{1,0:T(8,128)} %broadcast_in_dim.119.seg_q, ...), custom_call_target="tpu_custom_call", output_to_operand_aliasing={{0}: (15, {})} | custom-call | flops 42949672960 | bytes 10485760 | tf_op jit(solution)/shard_map/attend_back/pallas_call | solution.py:302
  717.4 20.4 %collective-permute-done.30 = bf16[2,512,512]{2,1,0:T(8,128)(2,1)} collective-permute-done((bf16[2,512,512]{2,1,0:T(8,128)(2,1)}, bf16[2,512,512]{2,1,0:T(8,128)(2,1)}, u32[]{:S(2)}, u32[]{:S(2)}) %collective-permute-start.30) | collective-permute-done | bytes 1048608 | tf_op jit(solution)/shard_map/ppermute | solution.py:35
  746.0 23.2 %collect.5 = (f32[512,1024]{1,0:T(8,128)}, bf16[512,1024]{1,0:T(8,128)(2,1)}, f32[8,1024]{1,0:T(8,128)}, bf16[1024,1536]{1,0:T(8,128)(2,1)}, bf16[1024,1536]{1,0:T(8,128)(2,1)}) custom-call(bf16[512,1024]{1,0:T(8,128)(2,1)} %get-tuple-element.203.refs_0_, bf16[2,512,512]{2,1,0:T(8,128)(2,1)} %add_convert_fusion.8.refs_1_, ...), custom_call_target="tpu_custom_call" | custom-call | flops 25769803776 | bytes 8388608 | tf_op jit(solution)/shard_map/collect/pallas_call | solution.py:1056
  770.2 109.4 %finish.1 = (f32[4,256,256]{2,1,0:T(8,128)}, f32[2,256,256]{2,1,0:T(8,128)}, f32[2,256,1024]{2,1,0:T(8,128)}, bf16[512,512]{1,0:T(8,128)(2,1)}, bf16[512,512]{1,0:T(8,128)(2,1)}, /*index=5*/f32[8,1024]{1,0:T(8,128)}) custom-call(bf16[1024,1536]{1,0:T(8,128)(2,1)} %get-tuple-element.221.refs_0_, bf16[1024,512]{1,0:T(8,128)(2,1)} %get-tuple-element.222.refs_1_, ...), custom_call_target="tpu_custom_call" | custom-call | bytes 209715200 | tf_op jit(solution)/shard_map/finish/pallas_call | solution.py:1476
  (403 shorter events, 242.9 us)
Async XLA Ops:
  7.2 214.6 %all-gather.3.cloned.1.call-start = ((), (), s32[]{:S(2)}) async-start(), calls=%async_computation.5 | async-start | bytes 7864320 | tf_op jit(solution)/shard_map/all_gather | solution.py:903
  146.0 22.5 %collective-permute-start.2 = (bf16[2,512,512]{2,1,0:T(8,128)(2,1)}, bf16[2,512,512]{2,1,0:T(8,128)(2,1)}, u32[]{:S(2)}, u32[]{:S(2)}) collective-permute-start(bf16[2,512,512]{2,1,0:T(8,128)(2,1)} %get-tuple-element.130.refs_0_.refs_4_), channel_id=1, source_target_pairs={{0,1},{1,0},{2,3},{3,2},{4,5},{5,4},{6,7},{7,6},{8,9},{9,8},{10,11... | collective-permute-start | bytes 3145736 | tf_op jit(solution)/shard_map/ppermute | solution.py:35
  146.0 39.2 %collective-permute-start.3 = (bf16[2,512,512]{2,1,0:T(8,128)(2,1)}, bf16[2,512,512]{2,1,0:T(8,128)(2,1)}, u32[]{:S(2)}, u32[]{:S(2)}) collective-permute-start(bf16[2,512,512]{2,1,0:T(8,128)(2,1)} %get-tuple-element.130.refs_0_.refs_4_), channel_id=1, source_target_pairs={{0,16},{16,0},{1,17},{17,1},{2,18},{18,2},{3,19},{19,3},{4,20},{20... | collective-permute-start | bytes 3145736 | tf_op jit(solution)/shard_map/ppermute | solution.py:35
  151.4 116.1 %all-gather.5.cloned.1.call-start = ((), (), s32[]{:S(2)}) async-start(), calls=%async_computation.6 | async-start | bytes 1966080 | tf_op jit(solution)/shard_map/all_gather | solution.py:903
  151.8 49.9 %collective-permute-start.1 = (bf16[2,512,512]{2,1,0:T(8,128)(2,1)}, bf16[2,512,512]{2,1,0:T(8,128)(2,1)}, u32[]{:S(2)}, u32[]{:S(2)}) collective-permute-start(bf16[2,512,512]{2,1,0:T(8,128)(2,1)} %get-tuple-element.137.refs_0_.refs_4_), channel_id=1, source_target_pairs={{0,1},{1,0},{2,3},{3,2},{4,5},{5,4},{6,7},{7,6},{8,9},{9,8},{10,11... | collective-permute-start | bytes 3145736 | tf_op jit(solution)/shard_map/ppermute | solution.py:35
  221.8 45.7 %collective-permute-start.7 = (bf16[1024,3072]{1,0:T(8,128)(2,1)}, bf16[1024,3072]{1,0:T(8,128)(2,1)}, u32[]{:S(2)}, u32[]{:S(2)}) collective-permute-start(bf16[1024,3072]{1,0:T(8,128)(2,1)} %all-gather.3.cloned.1.call-done.refs_1_.refs_4_), channel_id=1, source_target_pairs={{0,16},{16,0},{1,17},{17,1},{2,18},{18,2},{3,19},{19,3},{4,20},{20... | collective-permute-start | bytes 18874376 | tf_op jit(solution)/shard_map/ppermute | solution.py:35
  221.8 306.2 %reduce-scatter.6.cloned.1.call-start = ((), (), s32[]{:S(2)}) async-start(), calls=%async_computation.7 | async-start | bytes 2621440 | tf_op jit(solution)/shard_map/reduce_scatter | solution.py:911
  222.4 21.7 %collective-permute-start.10 = (bf16[64,1024]{1,0:T(8,128)(2,1)S(1)}, bf16[64,1024]{1,0:T(8,128)(2,1)S(1)}, u32[]{:S(2)}, u32[]{:S(2)}) collective-permute-start(bf16[64,1024]{1,0:T(8,128)(2,1)S(1)} %get-tuple-element.370), channel_id=1, source_target_pairs={{0,3},{1,2},{2,1},{3,0},{4,7},{5,6},{6,5},{7,4},{8,11},{9,10},{10,... | collective-permute-start | bytes 393224 | tf_op jit(solution)/shard_map/ppermute | solution.py:35
  267.5 54.8 %collective-permute-start.14 = (bf16[1024,768]{1,0:T(8,128)(2,1)}, bf16[1024,768]{1,0:T(8,128)(2,1)}, u32[]{:S(2)}, u32[]{:S(2)}) collective-permute-start(bf16[1024,768]{1,0:T(8,128)(2,1)} %all-gather.5.cloned.1.call-done), channel_id=1, source_target_pairs={{0,16},{16,0},{1,17},{17,1},{2,18},{18,2},{3,19},{19,3},{4,20},{20... | collective-permute-start | bytes 4718600 | tf_op jit(solution)/shard_map/ppermute | solution.py:35
  438.2 30.3 %collective-permute-start.16 = (f32[3,1024]{1,0:T(4,128)S(1)}, f32[3,1024]{1,0:T(4,128)S(1)}, u32[]{:S(2)}, u32[]{:S(2)}) collective-permute-start(f32[3,1024]{1,0:T(4,128)S(1)} %fusion.20), channel_id=1, source_target_pairs={{0,1},{1,0},{2,3},{3,2},{4,5},{5,4},{6,7},{7,6},{8,9},{9,8},{10,11... | collective-permute-start | bytes 36872 | tf_op jit(solution)/shard_map/ppermute | solution.py:35
  441.0 29.2 %collective-permute-start.15 = (bf16[1024,1024]{1,0:T(8,128)(2,1)S(1)}, bf16[1024,1024]{1,0:T(8,128)(2,1)S(1)}, u32[]{:S(2)}, u32[]{:S(2)}) collective-permute-start(bf16[1024,1024]{1,0:T(8,128)(2,1)S(1)} %pad_maximum_fusion.3), channel_id=1, source_target_pairs={{0,16},{16,0},{1,17},{17,1},{2,18},{18,2},{3,19},{19,3},{4,20},{20... | collective-permute-start | bytes 6291464 | tf_op jit(solution)/shard_map/ppermute | solution.py:35
  472.4 267.9 %reduce-scatter.8.cloned.1.call-start = ((), (), s32[]{:S(2)}) async-start(), calls=%async_computation.8 | async-start | bytes 2621440 | tf_op jit(solution)/shard_map/reduce_scatter | solution.py:911
  508.3 19.5 %collective-permute-start.18 = (bf16[8,256,128]{2,1,0:T(8,128)(2,1)}, bf16[8,256,128]{2,1,0:T(8,128)(2,1)S(1)}, u32[]{:S(2)}, u32[]{:S(2)}) collective-permute-start(bf16[8,256,128]{2,1,0:T(8,128)(2,1)} %get-tuple-element.172), channel_id=1, source_target_pairs={{16,0},{17,1},{2,18},{3,19},{20,4},{21,5},{6,22},{7,23},{24,8},{25... | collective-permute-start | bytes 1572872 | tf_op jit(solution)/shard_map/ppermute | solution.py:40
  526.6 33.2 %collective-permute-start.31 = (bf16[1024,1024]{1,0:T(8,128)(2,1)}, bf16[1024,1024]{1,0:T(8,128)(2,1)S(1)}, u32[]{:S(2)}, u32[]{:S(2)}) collective-permute-start(bf16[1024,1024]{1,0:T(8,128)(2,1)} %get-tuple-element.214), channel_id=1, source_target_pairs={{0,16},{16,0},{1,17},{17,1},{2,18},{18,2},{3,19},{19,3},{4,20},{20... | collective-permute-start | bytes 6291464 | tf_op jit(solution)/shard_map/ppermute | solution.py:35
  562.1 178.2 %reduce-scatter.10.cloned.1.call-start = ((), (), s32[]{:S(2)}) async-start(), calls=%async_computation.9 | async-start | bytes 5242880 | tf_op jit(solution)/shard_map/reduce_scatter | solution.py:911
  562.5 38.2 %collective-permute-start.22 = (bf16[1024,2048]{1,0:T(8,128)(2,1)}, bf16[1024,2048]{1,0:T(8,128)(2,1)}, u32[]{:S(2)}, u32[]{:S(2)}) collective-permute-start(bf16[1024,2048]{1,0:T(8,128)(2,1)} %get-tuple-element.186), channel_id=1, source_target_pairs={{0,16},{16,0},{1,17},{17,1},{2,18},{18,2},{3,19},{19,3},{4,20},{20... | collective-permute-start | bytes 12582920 | tf_op jit(solution)/shard_map/ppermute | solution.py:35
  575.1 165.2 %reduce-scatter.12.cloned.1.call-start = ((), (), s32[]{:S(2)}) async-start(), calls=%async_computation.10 | async-start | bytes 5242880 | tf_op jit(solution)/shard_map/reduce_scatter | solution.py:911
  648.6 121.5 %reduce-scatter.14.cloned.1.call-start = ((), (), s32[]{:S(2)}) async-start(), calls=%async_computation.11 | async-start | bytes 1966080 | tf_op jit(solution)/shard_map/reduce_scatter | solution.py:911
  681.3 25.6 %collective-permute-start.27 = (bf16[2,512,512]{2,1,0:T(8,128)(2,1)S(1)}, bf16[2,512,512]{2,1,0:T(8,128)(2,1)S(1)}, u32[]{:S(2)}, u32[]{:S(2)}) collective-permute-start(bf16[2,512,512]{2,1,0:T(8,128)(2,1)S(1)} %add_convert_fusion.9), channel_id=1, source_target_pairs={{0,1},{1,0},{2,3},{3,2},{4,5},{5,4},{6,7},{7,6},{8,9},{9,8},{10,11... | collective-permute-start | bytes 3145736 | tf_op jit(solution)/shard_map/ppermute | solution.py:35
  712.2 25.5 %collective-permute-start.30 = (bf16[2,512,512]{2,1,0:T(8,128)(2,1)}, bf16[2,512,512]{2,1,0:T(8,128)(2,1)}, u32[]{:S(2)}, u32[]{:S(2)}) collective-permute-start(bf16[2,512,512]{2,1,0:T(8,128)(2,1)} %add_convert_fusion.6), channel_id=1, source_target_pairs={{0,1},{1,0},{2,3},{3,2},{4,5},{5,4},{6,7},{7,6},{8,9},{9,8},{10,11... | collective-permute-start | bytes 3145736 | tf_op jit(solution)/shard_map/ppermute | solution.py:35
  740.3 29.0 %collective-permute-start.32 = (bf16[64,1024]{1,0:T(8,128)(2,1)S(1)}, bf16[64,1024]{1,0:T(8,128)(2,1)S(1)}, u32[]{:S(2)}, u32[]{:S(2)}) collective-permute-start(bf16[64,1024]{1,0:T(8,128)(2,1)S(1)} %get-tuple-element.347), channel_id=1, source_target_pairs={{0,1},{1,0},{2,3},{3,2},{4,5},{5,4},{6,7},{7,6},{8,9},{9,8},{10,11... | collective-permute-start | bytes 393224 | tf_op jit(solution)/shard_map/ppermute | solution.py:35
  742.1 27.2 %collective-permute-start.33 = (bf16[64,1024]{1,0:T(8,128)(2,1)S(1)}, bf16[64,1024]{1,0:T(8,128)(2,1)S(1)}, u32[]{:S(2)}, u32[]{:S(2)}) collective-permute-start(bf16[64,1024]{1,0:T(8,128)(2,1)S(1)} %get-tuple-element.349), channel_id=1, source_target_pairs={{0,2},{1,3},{2,0},{3,1},{4,6},{5,7},{6,4},{7,5},{8,10},{9,11},{10,... | collective-permute-start | bytes 393224 | tf_op jit(solution)/shard_map/ppermute | solution.py:35
  745.2 24.1 %collective-permute-start.34 = (bf16[64,1024]{1,0:T(8,128)(2,1)S(1)}, bf16[64,1024]{1,0:T(8,128)(2,1)S(1)}, u32[]{:S(2)}, u32[]{:S(2)}) collective-permute-start(bf16[64,1024]{1,0:T(8,128)(2,1)S(1)} %get-tuple-element.348), channel_id=1, source_target_pairs={{0,3},{1,2},{2,1},{3,0},{4,7},{5,6},{6,5},{7,4},{8,11},{9,10},{10,... | collective-permute-start | bytes 393224 | tf_op jit(solution)/shard_map/ppermute | solution.py:35
  770.2 121.9 %collective-permute-start.35 = (bf16[2,64,512]{2,1,0:T(8,128)(2,1)}, bf16[2,64,512]{2,1,0:T(8,128)(2,1)S(1)}, u32[]{:S(2)}, u32[]{:S(2)}) collective-permute-start(bf16[2,64,512]{2,1,0:T(8,128)(2,1)} %fusion.23), channel_id=1, source_target_pairs={{0,16},{16,0},{1,17},{17,1},{2,18},{18,2},{3,19},{19,3},{4,20},{20... | collective-permute-start | bytes 393224 | tf_op jit(solution)/shard_map/ppermute | solution.py:35
  (86 other events, 1173.9 us)
Sparse Core Ops, SparseCore 0:
  151.5 70.2 all-gather.2
  223.6 43.7 all-gather.4
  472.5 41.2 reduce-scatter.5
  562.2 41.2 reduce-scatter.7
  606.3 52.6 reduce-scatter.9
  662.1 52.6 reduce-scatter.11
  717.8 50.6 reduce-scatter.13
